TPU v7x, 32 devices: a whole 2x2x4 slice. The times are simulated.
32 devices in a mesh: req: 4 (over y, core), exp: 8 (over z, x).
Axes of the slice: x: 2, y: 2, z: 4, core: 2. Of those that a mesh axis runs over, the one named last changes fastest.
Arguments:
- hidden_in: bfloat16 [8, 256, 2880], P('exp', 'req'), may hold values from -6 to 6
- queries: bfloat16 [8, 256, 4096], P('exp', 'req'), may hold values from -115 to 115
- new_kv: bfloat16 [8, 256, 1024], P('exp', 'req'), may hold values from -6 to 6
- kv_pool: bfloat16 [8, 32, 16, 1024], P('exp', 'req'), may hold values from -6 to 6
- page_table: int32 [8, 16], P('exp'), may hold values from 0 to 31, as said below
- new_slots: int32 [8, 16], P('exp'), may hold values from 0 to 31
- cached_pages: int32 [8], P('exp'), may hold values from 1 to 16, as said below
- sinks: float32 [64], replicated, may hold values from 2 to 8
- out_weight: bfloat16 [4096, 2880], P('req', 'exp'), may hold values from -0.375 to 0.375
Outputs:
- layer_out: bfloat16 [8, 256, 2880], P('exp', 'req')
- pool_out: bfloat16 [8, 32, 16, 1024], P('exp', 'req')
Inputs may be any that keep to these rules, and one draw needn't show every extreme that they name: For each request the entries of page_table and new_slots are 32 distinct slots. `cached_pages`: some request has exactly 16 cached pages.
All inputs are finite; a program needn't handle non-finite values.
Results may differ from a plain program's by a relative error of at most 0.009.
The roundings to bfloat16 on the way count: a program that leaves them out, or rounds other values in their place, can miss the bound.
Values may be sent and summed in bfloat16 or wider, within the bound.
No kernel may reach another device: no remote copies, remote signals or barrier semaphores. Data moves between devices by JAX's collectives and lax.ppermute only.
A program may use at most 64 MiB of HBM per device.

v0:
```python
import math

import jax
import jax.numpy as jnp
from jax import lax
from jax.sharding import PartitionSpec as P

HD = 64


THETA = 150000.0
NEGATIVE = -1e30


def rotate(values, positions):
    half_width = values.shape[-1] // 2
    frequency = THETA ** (-2.0 * jnp.arange(half_width).astype(jnp.float32) / values.shape[-1])
    angles = positions.astype(jnp.float32)[:, None] * frequency[None, :]
    cosine = jnp.cos(angles)[:, None, :]
    sine_part = jnp.sin(angles)[:, None, :]
    lower_half = values[..., :half_width]
    upper_half = values[..., half_width:]
    return jnp.concatenate(
        [
            lower_half * cosine - upper_half * sine_part,
            upper_half * cosine + lower_half * sine_part,
        ],
        axis=-1,
    )


def spread_heads(rows, head_total, kv_heads, dev_count):
    per_dev = head_total // dev_count
    per_kv = head_total // kv_heads
    repeat = max(1, per_kv // per_dev)
    kv_dev = max(1, per_dev // per_kv)
    count = rows.shape[0]
    split = jnp.repeat(rows.reshape(count, 2, kv_heads, HD), repeat, axis=2)
    split = split.reshape(count, 2, dev_count, kv_dev * HD)
    return jnp.transpose(split, (0, 2, 1, 3)).reshape(count, dev_count, 2 * kv_dev * HD)


def per_device(
    hidden_in, queries, new_kv, kv_pool, page_table, new_slots, cached_pages, sinks, out_weight
):
    tok_dev = hidden_in.shape[1]
    n_req = lax.axis_size("req")
    own_index = lax.axis_index("req")
    fresh_count = tok_dev * n_req
    head_count = sinks.shape[0]
    kv_width = new_kv.shape[2] // 2
    kv_heads = kv_width // HD
    per_kv = head_count // kv_heads
    heads_dev = head_count // n_req
    kv_dev = max(1, heads_dev // per_kv)
    per_dev_group = heads_dev // kv_dev
    head_width = 2 * kv_dev * HD
    slots_dev = kv_pool.shape[1]
    page_size = kv_pool.shape[2]
    slot_total = slots_dev * n_req
    page_limit = page_table.shape[1]
    fresh_pages = new_slots.shape[1]
    page_count = cached_pages[0]
    start_pos = page_count * page_size
    own_pos = start_pos + own_index * tok_dev + jnp.arange(tok_dev)
    q_rot = rotate(queries[0].reshape(tok_dev, head_count, HD).astype(jnp.float32), own_pos).astype(
        jnp.bfloat16
    )
    k_rot = rotate(
        new_kv[0, :, :kv_width].reshape(tok_dev, kv_heads, HD).astype(jnp.float32), own_pos
    ).astype(jnp.bfloat16)
    kv_rot = jnp.concatenate([k_rot.reshape(tok_dev, kv_width), new_kv[0, :, kv_width:]], axis=1)
    slot_all = jnp.arange(slot_total)
    page_index = jnp.arange(page_limit)
    cached_hit = (page_table[0][None, :] == slot_all[:, None]) & (page_index[None, :] < page_count)
    is_cached = jnp.any(cached_hit, axis=1)
    cached_base = jnp.sum(jnp.where(cached_hit, page_index[None, :], 0), axis=1) * page_size
    fresh_hit = new_slots[0][None, :] == slot_all[:, None]
    is_fresh = jnp.any(fresh_hit, axis=1)
    fresh_base = (
        start_pos
        + jnp.sum(jnp.where(fresh_hit, jnp.arange(fresh_pages)[None, :], 0), axis=1) * page_size
    )
    key_pos = (
        jnp.where(is_fresh, fresh_base, cached_base)[:, None] + jnp.arange(page_size)[None, :]
    ).reshape(-1)
    key_live = jnp.repeat(is_cached | is_fresh, page_size)
    all_fresh = lax.all_gather(kv_rot, "req", axis=0, tiled=True)
    own_hit = lax.dynamic_slice_in_dim(fresh_hit, own_index * slots_dev, slots_dev, 0)
    own_fresh = lax.dynamic_slice_in_dim(is_fresh, own_index * slots_dev, slots_dev, 0)
    appended = jnp.dot(
        own_hit.astype(jnp.bfloat16),
        all_fresh.reshape(fresh_pages, page_size * 2 * kv_width),
        preferred_element_type=jnp.float32,
    )
    appended = appended.astype(jnp.bfloat16).reshape(slots_dev, page_size, 2 * kv_width)
    local_pages = jnp.where(own_fresh[:, None, None], appended, kv_pool[0])
    head_pool = lax.all_to_all(
        spread_heads(
            local_pages.reshape(slots_dev * page_size, 2 * kv_width), head_count, kv_heads, n_req
        ),
        "req",
        split_axis=1,
        concat_axis=0,
        tiled=True,
    )
    head_pool = head_pool.reshape(slot_total * page_size, head_width)
    q_here = lax.all_to_all(
        q_rot.reshape(tok_dev, n_req, heads_dev * HD),
        "req",
        split_axis=1,
        concat_axis=0,
        tiled=True,
    )
    q_here = q_here.reshape(fresh_count, heads_dev * HD)
    key_total = slot_total * page_size
    all_keys = head_pool[:, : kv_dev * HD].reshape(key_total, kv_dev, HD)
    all_values = head_pool[:, kv_dev * HD :].reshape(key_total, kv_dev, HD)
    sink_mine = lax.dynamic_slice_in_dim(sinks, own_index * heads_dev, heads_dev, 0).reshape(
        kv_dev, per_dev_group
    )
    scale = 1.0 / math.sqrt(HD)
    query_block = math.gcd(fresh_count, 128)
    contexts = []
    for block_start in range(0, fresh_count, query_block):
        block_queries = q_here[block_start : block_start + query_block].reshape(
            query_block, kv_dev, per_dev_group, HD
        )
        query_pos = start_pos + block_start + jnp.arange(query_block)
        visible = key_live[None, :] & (key_pos[None, :] <= query_pos[:, None])
        scores = (
            jnp.einsum(
                "tghd,kgd->tghk", block_queries, all_keys, preferred_element_type=jnp.float32
            )
            * scale
        )
        scores = jnp.where(visible[:, None, None, :], scores, NEGATIVE)
        top_score = jnp.maximum(jnp.max(scores, axis=-1), sink_mine[None])
        expo = jnp.where(visible[:, None, None, :], jnp.exp(scores - top_score[..., None]), 0.0)
        denominator = jnp.sum(expo, axis=-1) + jnp.exp(sink_mine[None] - top_score)
        weighted = jnp.einsum(
            "tghk,kgd->tghd",
            expo.astype(jnp.bfloat16),
            all_values,
            preferred_element_type=jnp.float32,
        )
        contexts.append(
            (weighted / denominator[..., None])
            .astype(jnp.bfloat16)
            .reshape(query_block, heads_dev * HD)
        )
    context = jnp.concatenate(contexts, axis=0)
    terms = jnp.dot(
        context,
        lax.all_gather(out_weight, "exp", axis=1, tiled=True),
        preferred_element_type=jnp.float32,
    ).astype(jnp.bfloat16)
    width = terms.shape[1]
    arrived = lax.all_to_all(
        terms.reshape(n_req, tok_dev, width), "req", split_axis=0, concat_axis=0, tiled=True
    )
    attn = jnp.sum(arrived.astype(jnp.float32), axis=0)
    layer_out = (hidden_in[0].astype(jnp.float32) + attn).astype(jnp.bfloat16)
    return (layer_out[None], local_pages[None])


def solution(mesh):
    return jax.shard_map(
        per_device,
        mesh=mesh,
        in_specs=(
            P("exp", "req", None),
            P("exp", "req", None),
            P("exp", "req", None),
            P("exp", "req", None, None),
            P("exp", None),
            P("exp", None),
            P("exp"),
            P(),
            P("req", "exp"),
        ),
        out_specs=(P("exp", "req", None), P("exp", "req", None, None)),
        check_vma=False,
    )
```

profile of v0, /device:TPU:0, one launch (start us, length us, event | category | flops | bytes accessed | tf_op | source)
XLA Modules:
  0.0 144.2 jit_solution(15059542093213412865)
XLA Ops:
  7.3 0.7 all-gather.2.cloned.1.call-update
  8.6 0.9 slice_convert_fusion
  10.3 8.6 %all_gather.6 = bf16[256,1024]{1,0:T(8,128)(2,1)S(1)} all-gather(bf16[64,1024]{1,0:T(8,128)(2,1)S(1)} %pad_maximum_fusion.2), channel_id=1, replica_groups=mesh['req'=4,'exp'=8] {'req'}, dimensions={0}, use_global_device_ids=true | all-gather | bytes 655360 | tf_op jit(solution)/shard_map/all_gather | solution.py:88
  20.5 0.9 copy.46
  21.4 3.4 %all-to-all-start = ((bf16[128,4,256]{0,2,1:T(8,128)(2,1)}), bf16[128,4,256]{0,2,1:T(8,128)(2,1)S(1)}, u32[]{:S(2)}, u32[]{:S(2)}) async-start(bf16[128,4,256]{0,2,1:T(8,128)(2,1)} %bitcast.4), calls=%async_computation | async-start | bytes 524288 | tf_op jit(solution)/shard_map/all_to_all | solution.py:98
  25.4 0.9 reshape.266
  26.3 0.9 subtract_convert_fusion
  28.5 0.9 copy.50
  29.6 1.2 all-to-all-done
  30.8 3.6 %all-to-all-start.1 = ((bf16[64,4,1024]{2,0,1:T(8,128)(2,1)}), bf16[64,4,1024]{2,0,1:T(8,128)(2,1)S(1)}, u32[]{:S(2)}, u32[]{:S(2)}) async-start(bf16[64,4,1024]{2,0,1:T(8,128)(2,1)} %copy.50), calls=%async_computation.1 | async-start | bytes 1048576 | tf_op jit(solution)/shard_map/all_to_all | solution.py:108
  35.1 8.0 %all-to-all-done.1 = bf16[64,4,1024]{2,0,1:T(8,128)(2,1)S(1)} async-done(((bf16[64,4,1024]{2,0,1:T(8,128)(2,1)}), bf16[64,4,1024]{2,0,1:T(8,128)(2,1)S(1)}, u32[]{:S(2)}, u32[]{:S(2)}) %all-to-all-start.1) | async-done | bytes 524320 | tf_op jit(solution)/shard_map/all_to_all | solution.py:108
  43.8 0.9 fusion
  44.8 0.9 fusion.1
  45.6 1.0 fusion.2
  46.7 1.0 fusion.4
  47.8 1.1 fusion.27
  48.8 1.1 fusion.21
  49.9 57.3 %all-gather.2.cloned.1.call-done = bf16[1024,2880]{0,1:T(8,128)(2,1)} async-done(((bf16[1024,360]{0,1:T(8,128)(2,1)}), bf16[1024,2880]{0,1:T(8,128)(2,1)}) %all-gather.2.cloned.1.call-update) | async-done | bytes 5898256 | tf_op jit(solution)/shard_map/all_gather | solution.py:155
  107.3 4.4 %convolution_convert_fusion.1 = bf16[256,2880]{0,1:T(8,128)(2,1)S(1)} fusion(bf16[1024,2880]{0,1:T(8,128)(2,1)} %all-gather.2.cloned.1.call-done, bf16[128,1024]{0,1:T(8,128)(2,1)S(1)} %bitcast.110, bf16[128,1024]{0,1:T(8,128)(2,1)S(1)} %bitcast.109), kind=kOutput, calls=%fused_computation.5 | convolution fusion | flops 1511735296 | bytes 7897088 | tf_op jit(solution)/shard_map/dot_general | solution.py:153
  111.6 1.7 %copy.55 = bf16[256,2880]{1,0:T(8,128)(2,1)} copy(bf16[256,2880]{0,1:T(8,128)(2,1)S(1)} %convolution_convert_fusion.1) | data formatting | bytes 2949120 | tf_op jit(solution)/shard_map/convert_element_type | solution.py:157
  113.4 3.6 %all-to-all-start.2 = ((bf16[4,64,2880]{2,1,0:T(8,128)(2,1)}), bf16[4,64,2880]{2,1,0:T(8,128)(2,1)S(1)}, u32[]{:S(2)}, u32[]{:S(2)}) async-start(bf16[4,64,2880]{2,1,0:T(8,128)(2,1)} %bitcast.28), calls=%async_computation.2 | async-start | bytes 3014656 | tf_op jit(solution)/shard_map/all_to_all | solution.py:159
  116.9 0.9 copy_select_fusion
  117.8 18.5 %all-to-all-done.2 = bf16[4,64,2880]{2,1,0:T(8,128)(2,1)S(1)} async-done(((bf16[4,64,2880]{2,1,0:T(8,128)(2,1)}), bf16[4,64,2880]{2,1,0:T(8,128)(2,1)S(1)}, u32[]{:S(2)}, u32[]{:S(2)}) %all-to-all-start.2) | async-done | bytes 1474592 | tf_op jit(solution)/shard_map/all_to_all | solution.py:159
  136.5 0.8 fusion.30
  (56 shorter events, 6.1 us)
Async XLA Ops:
  7.2 12.0 %copy-start.3 = (s32[1,16]{1,0:T(1,128)S(1)}, s32[1,16]{1,0:T(1,128)}, u32[]{:S(2)}) copy-start(s32[1,16]{1,0:T(1,128)} %param.14) | copy-start | bytes 196
  7.2 12.9 %copy-start = (bf16[1,8,16,1024]{3,2,1,0:T(8,128)(2,1)S(1)}, bf16[1,8,16,1024]{3,2,1,0:T(8,128)(2,1)}, u32[]{:S(2)}) copy-start(bf16[1,8,16,1024]{3,2,1,0:T(8,128)(2,1)} %param.12) | copy-start | bytes 786436
  7.2 17.6 %copy-start.4 = (s32[1,16]{1,0:T(1,128)S(1)}, s32[1,16]{1,0:T(1,128)}, u32[]{:S(2)}) copy-start(s32[1,16]{1,0:T(1,128)} %param.13) | copy-start | bytes 196
  7.2 18.2 %copy-start.1 = (bf16[1,64,4096]{2,1,0:T(8,128)(2,1)S(1)}, bf16[1,64,4096]{2,1,0:T(8,128)(2,1)}, u32[]{:S(2)}) copy-start(bf16[1,64,4096]{2,1,0:T(8,128)(2,1)} %param.10) | copy-start | bytes 1572868
  7.2 100.0 %all-gather.2.cloned.1.call-start = ((), (), s32[]{:S(2)}) async-start(), calls=%async_computation.3 | async-start | bytes 6635520 | tf_op jit(solution)/shard_map/all_gather | solution.py:155
  21.4 9.4 %all-to-all-start = ((bf16[128,4,256]{0,2,1:T(8,128)(2,1)}), bf16[128,4,256]{0,2,1:T(8,128)(2,1)S(1)}, u32[]{:S(2)}, u32[]{:S(2)}) async-start(bf16[128,4,256]{0,2,1:T(8,128)(2,1)} %bitcast.4), calls=%async_computation | async-start | bytes 524288 | tf_op jit(solution)/shard_map/all_to_all | solution.py:98
  27.2 2.2 %copy-start.5 = (f32[64]{0:T(128)S(1)}, f32[64]{0:T(128)}, u32[]{:S(2)}) copy-start(f32[64]{0:T(128)} %param.16) | copy-start | bytes 772
  30.8 12.3 %all-to-all-start.1 = ((bf16[64,4,1024]{2,0,1:T(8,128)(2,1)}), bf16[64,4,1024]{2,0,1:T(8,128)(2,1)S(1)}, u32[]{:S(2)}, u32[]{:S(2)}) async-start(bf16[64,4,1024]{2,0,1:T(8,128)(2,1)} %copy.50), calls=%async_computation.1 | async-start | bytes 1048576 | tf_op jit(solution)/shard_map/all_to_all | solution.py:108
  111.6 24.9 %copy-start.2 = (bf16[1,64,2880]{2,1,0:T(8,128)(2,1)S(1)}, bf16[1,64,2880]{2,1,0:T(8,128)(2,1)}, u32[]{:S(2)}) copy-start(bf16[1,64,2880]{2,1,0:T(8,128)(2,1)} %param.9) | copy-start | bytes 1105924
  113.4 22.9 %all-to-all-start.2 = ((bf16[4,64,2880]{2,1,0:T(8,128)(2,1)}), bf16[4,64,2880]{2,1,0:T(8,128)(2,1)S(1)}, u32[]{:S(2)}, u32[]{:S(2)}) async-start(bf16[4,64,2880]{2,1,0:T(8,128)(2,1)} %bitcast.28), calls=%async_computation.2 | async-start | bytes 3014656 | tf_op jit(solution)/shard_map/all_to_all | solution.py:159
Sparse Core Ops, SparseCore 0:
  10.2 96.9 all-gather.1
where the time goes:
time: 145 us; the launch traced here: 144 us
  waiting for transfers between devices  85.7 us (59%)
  between operations  15 us (10%)
  starting transfers between devices  10.7 us (7%)
  blocking collectives  8.65 us (6%)
  matrix products  8.57 us (6%)
  local copies, waits for them, and re-layouts  7.81 us (5%)
  other arithmetic  7.81 us (5%)
    all_gather x1, waiting for transfers between devices, per_device(): lax.all_gather(out_weight, 'exp', axis=1, tiled=True)  57.3 us
    all_to_all x1, waiting for transfers between devices, per_device(): lax.all_to_all(terms.reshape(n_req, tok_dev, width), 'req', split_axis=0,...  18.5 us
    all_gather x1, blocking collectives, per_device(): all_fresh = lax.all_gather(kv_rot, 'req', axis=0, tiled=True)  8.65 us
    all_to_all x1, waiting for transfers between devices, per_device(): lax.all_to_all(q_rot.reshape(tok_dev, n_req, heads_dev * HD), 'req', spli...  7.99 us
    dot_general x1, matrix products, per_device(): jnp.dot(context, lax.all_gather(out_weight, 'exp', axis=1, tiled=True), p...  4.37 us
    all_to_all x1, starting transfers between devices, per_device(): lax.all_to_all(q_rot.reshape(tok_dev, n_req, heads_dev * HD), 'req', spli...  3.65 us
    all_to_all x1, starting transfers between devices, per_device(): lax.all_to_all(terms.reshape(n_req, tok_dev, width), 'req', split_axis=0,...  3.56 us
    all_to_all x1, starting transfers between devices, per_device(): lax.all_to_all(spread_heads(local_pages.reshape(slots_dev * page_size, 2...  3.41 us
  transfers between devices with their start and end apart: 4, of which 4 were waited for; matrix products, arithmetic and copies ran while one was open for 12% of the time, Pallas kernels for 0%

commit v1 on v0

--- a/solution.py
+++ b/solution.py
@@ -1,8 +1,11 @@
+import functools
 import math
 
 import jax
 import jax.numpy as jnp
 from jax import lax
+from jax.experimental import pallas as pl
+from jax.experimental.pallas import tpu as pltpu
 from jax.sharding import PartitionSpec as P
 
 HD = 64
@@ -40,7 +43,7 @@
     return jnp.transpose(split, (0, 2, 1, 3)).reshape(count, dev_count, 2 * kv_dev * HD)
 
 
-def per_device(
+def general_plan(
     hidden_in, queries, new_kv, kv_pool, page_table, new_slots, cached_pages, sinks, out_weight
 ):
     tok_dev = hidden_in.shape[1]
@@ -164,9 +167,405 @@
     return (layer_out[None], local_pages[None])
 
 
+VMEM_LIMIT = 56 * 1024 * 1024
+F32 = jnp.float32
+BF16 = jnp.bfloat16
+
+PAIR_BIT, NEAR_BIT, FAR_BIT = 2, 1, 4
+
+
+def vmem():
+    return pl.BlockSpec(memory_space=pltpu.VMEM)
+
+
+def smem():
+    return pl.BlockSpec(memory_space=pltpu.SMEM)
+
+
+def anywhere():
+    return pl.BlockSpec(memory_space=pl.ANY)
+
+
+def params():
+    return pltpu.CompilerParams(vmem_limit_bytes=VMEM_LIMIT)
+
+
+def cost(flops, nbytes):
+    return pl.CostEstimate(flops=int(flops), bytes_accessed=int(nbytes), transcendentals=0)
+
+
+def swap(values, req_bits, exp_bits):
+    if not exp_bits:
+        return lax.ppermute(values, "req", [(i, i ^ req_bits) for i in range(lax.axis_size("req"))])
+    if not req_bits:
+        return lax.ppermute(values, "exp", [(i, i ^ exp_bits) for i in range(lax.axis_size("exp"))])
+    rows, cols = lax.axis_size("req"), lax.axis_size("exp")
+    pairs = [
+        (i * cols + j, (i ^ req_bits) * cols + (j ^ exp_bits)) for i in range(rows) for j in range(cols)
+    ]
+    return lax.ppermute(values, ("req", "exp"), pairs)
+
+
+def pack_kernel(q_ref, kv_ref, pool_ref, *rest):
+    outs, sems = rest[:-1], rest[-1]
+    n_req = len(outs)
+    own = lax.axis_index("req")
+    tok = q_ref.shape[0]
+    q_width = q_ref.shape[1] // n_req
+    kv_width = kv_ref.shape[1] // 2
+    head_width = kv_width // n_req
+    copies = []
+
+    def copy(source, target):
+        one = pltpu.make_async_copy(source, target, sems.at[len(copies)])
+        one.start()
+        copies.append(one)
+
+    for k in (2, 3, 1, 0):
+        dest = jnp.bitwise_xor(own, k)
+        out = outs[k]
+        q_col = pl.multiple_of(dest * q_width, 128)
+        copy(q_ref.at[:, pl.ds(q_col, q_width)], out.at[:, pl.ds(0, q_width)])
+        at = q_width
+        blocks = [kv_ref]
+        blocks += [pool_ref.at[pl.ds(i * tok, tok), :] for i in range(pool_ref.shape[0] // tok)]
+        for block in blocks:
+            for half in range(2):
+                col = pl.multiple_of(half * kv_width + dest * head_width, 128)
+                copy(block.at[:, pl.ds(col, head_width)], out.at[:, pl.ds(at, head_width)])
+                at += head_width
+    for one in copies:
+        one.wait()
+
+
+def pack(q, kv, pool, n_req):
+    tok = q.shape[0]
+    blocks = 1 + pool.shape[0] // tok
+    width = (q.shape[1] + blocks * kv.shape[1]) // n_req
+    return pl.pallas_call(
+        pack_kernel,
+        out_shape=[jax.ShapeDtypeStruct((tok, width), BF16)] * n_req,
+        in_specs=[anywhere()] * 3,
+        out_specs=[anywhere()] * n_req,
+        scratch_shapes=[pltpu.SemaphoreType.DMA((n_req * (1 + 2 * blocks),))],
+        compiler_params=params(),
+        cost_estimate=cost(0, 4 * tok * width * n_req),
+        name="pack",
+    )(q, kv, pool)
+
+
+def turn(values, cosine, sine):
+    lane = lax.broadcasted_iota(jnp.int32, values.shape, 1)
+    other = jnp.where(lane % HD < HD // 2, pltpu.roll(values, 128 - HD // 2, 1), pltpu.roll(values, HD // 2, 1))
+    return values * cosine + other * sine
+
+
+def attention_kernel(
+    pages_ref, table_ref, sink_ref, cos_ref, sin_ref, *rest, kv_dev, per_kv, page_size
+):
+    n_req = len(rest) - 6
+    pieces, out_ref = rest[:n_req], rest[n_req]
+    q_scr, pool_scr, key_scr, value_scr, flat_scr = rest[n_req + 1 :]
+    own = lax.axis_index("req")
+    tok = pieces[0].shape[0]
+    q_width = kv_dev * per_kv * HD
+    head_width = kv_dev * HD
+    page_limit = table_ref.shape[1]
+    cached = page_limit * page_size
+    fresh = tok * n_req
+    total = cached + fresh
+    pool_rows = pool_scr.shape[1]
+    page_count = pages_ref[0]
+    pairs = per_kv // 2
+    for k in range(n_req):
+        shard = jnp.bitwise_xor(own, k)
+        row = pl.multiple_of(shard * tok, tok)
+        cosine = cos_ref[pl.ds(row, tok), :]
+        sine = sin_ref[pl.ds(row, tok), :]
+        for g in range(kv_dev):
+            for p in range(pairs):
+                col = (g * pairs + p) * 2 * HD
+                turned = turn(pieces[k][:, col : col + 2 * HD].astype(F32), cosine, sine).astype(BF16)
+                q_scr[k, g, p * tok : (p + 1) * tok, :] = turned * jnp.asarray(1.0 / math.sqrt(HD), BF16)
+        at = q_width
+        key_row = pl.multiple_of(cached + row, tok)
+        flat_scr[pl.ds(key_row, tok), :head_width] = turn(
+            pieces[k][:, at : at + head_width].astype(F32), cosine, sine
+        )
+        flat_scr[pl.ds(key_row, tok), head_width:] = pieces[k][
+            :, at + head_width : at + 2 * head_width
+        ].astype(F32)
+        at += 2 * head_width
+        for i in range(pool_rows // tok):
+            pool_scr[shard, i * tok : (i + 1) * tok, :] = pieces[k][:, at : at + 2 * head_width].astype(F32)
+            at += 2 * head_width
+    per_dev = pool_rows // page_size
+    for j in range(page_limit):
+        slot = table_ref[0, j]
+        source = pl.multiple_of((slot % per_dev) * page_size, page_size)
+        flat_scr[j * page_size : (j + 1) * page_size, :] = pool_scr[
+            slot // per_dev, pl.ds(source, page_size), :
+        ]
+    for scr, at in ((key_scr, 0), (value_scr, head_width)):
+        flat = flat_scr[:, at : at + head_width]
+        rolled = pltpu.roll(flat, HD, 1)
+        low = lax.broadcasted_iota(jnp.int32, flat.shape, 1) < HD
+        zero = jnp.zeros_like(flat)
+        scr[0, :total, :] = jnp.where(low, flat, zero).astype(BF16)
+        scr[0, total:, :] = jnp.where(low, zero, rolled).astype(BF16)
+        scr[1, :total, :] = jnp.where(low, rolled, zero).astype(BF16)
+        scr[1, total:, :] = jnp.where(low, zero, flat).astype(BF16)
+    live = page_count * page_size
+
+    def one_shard(k, carry):
+        shard = jnp.bitwise_xor(own, k)
+        key = lax.broadcasted_iota(jnp.int32, (tok, total), 1)
+        query = lax.broadcasted_iota(jnp.int32, (tok, total), 0) + shard * tok
+        last = jnp.where(key < cached, live - 1, query + cached)
+        bias = jnp.where(key > last, NEGATIVE, 0.0)
+        bias = jnp.concatenate([bias] * pairs, axis=0)
+        for g in range(kv_dev):
+            scores = lax.dot_general(
+                q_scr[k, g], key_scr[g], (((1,), (1,)), ((), ())), preferred_element_type=F32
+            )
+            weights, dens = [], []
+            for a in range(2):
+                part = scores[:, a * total : (a + 1) * total] + bias
+                first = own * (kv_dev * per_kv) + g * per_kv + a
+                sink = jnp.concatenate(
+                    [jnp.full((tok, 1), sink_ref[first + 2 * p], F32) for p in range(pairs)], axis=0
+                )
+                top = jnp.maximum(jnp.max(part, axis=1, keepdims=True), sink)
+                expo = jnp.exp(part - top)
+                dens.append(jnp.sum(expo, axis=1, keepdims=True) + jnp.exp(sink - top))
+                weights.append(expo.astype(BF16))
+            summed = jnp.dot(weights[0], value_scr[g, :total, :], preferred_element_type=F32) + jnp.dot(
+                weights[1], value_scr[g, total:, :], preferred_element_type=F32
+            )
+            low = lax.broadcasted_iota(jnp.int32, summed.shape, 1) < HD
+            ctx = (summed / jnp.where(low, dens[0], dens[1])).astype(BF16)
+            for p in range(pairs):
+                col = (g * pairs + p) * 2 * HD
+                out_ref[k, :, col : col + 2 * HD] = ctx[p * tok : (p + 1) * tok, :]
+        return carry
+
+    lax.fori_loop(0, n_req, one_shard, 0)
+
+
+def attention(pages, table, sinks, cosine, sine, pieces, kv_dev, per_kv, pool_rows, page_size):
+    n_req = len(pieces)
+    tok = pieces[0].shape[0]
+    total = table.shape[1] * page_size + n_req * tok
+    q_width = kv_dev * per_kv * HD
+    return pl.pallas_call(
+        functools.partial(attention_kernel, kv_dev=kv_dev, per_kv=per_kv, page_size=page_size),
+        out_shape=jax.ShapeDtypeStruct((n_req, tok, q_width), BF16),
+        in_specs=[smem()] * 3 + [vmem()] * (2 + n_req),
+        out_specs=vmem(),
+        scratch_shapes=[
+            pltpu.VMEM((n_req, kv_dev, per_kv // 2 * tok, 2 * HD), BF16),
+            pltpu.VMEM((n_req, pool_rows, 2 * kv_dev * HD), F32),
+            pltpu.VMEM((kv_dev, 2 * total, 2 * HD), BF16),
+            pltpu.VMEM((kv_dev, 2 * total, 2 * HD), BF16),
+            pltpu.VMEM((total, 2 * kv_dev * HD), F32),
+        ],
+        compiler_params=params(),
+        cost_estimate=cost(3e9, 2**22),
+        name="attention",
+    )(pages, table, sinks, cosine, sine, *pieces)
+
+
+def pool_kernel(slots_ref, cos_ref, sin_ref, pool_ref, *rest, page_size):
+    pieces, out_ref, fresh_scr = rest[:-2], rest[-2], rest[-1]
+    own = lax.axis_index("req")
+    tok = pieces[0].shape[0]
+    kv_width = pieces[0].shape[1] // 2
+    for k, piece in enumerate(pieces):
+        row = pl.multiple_of(jnp.bitwise_xor(own, k) * tok, tok)
+        cosine = cos_ref[pl.ds(row, tok), :]
+        sine = sin_ref[pl.ds(row, tok), :]
+        for col in range(0, kv_width, 128):
+            turned = turn(piece[:, col : col + 128].astype(F32), cosine, sine).astype(BF16)
+            fresh_scr[pl.ds(row, tok), col : col + 128] = turned
+        fresh_scr[pl.ds(row, tok), kv_width:] = piece[:, kv_width:]
+    out_ref[...] = pool_ref[...]
+    slots_dev = out_ref.shape[0]
+    for n in range(slots_ref.shape[1]):
+        slot = slots_ref[0, n]
+
+        @pl.when(slot // slots_dev == own)
+        def _(slot=slot, n=n):
+            out_ref[slot % slots_dev] = fresh_scr[n * page_size : (n + 1) * page_size, :]
+
+
+def write_pool(slots, cosine, sine, pool, pieces):
+    tok, width = pieces[0].shape
+    return pl.pallas_call(
+        functools.partial(pool_kernel, page_size=pool.shape[1]),
+        out_shape=jax.ShapeDtypeStruct(pool.shape, BF16),
+        in_specs=[smem()] + [vmem()] * (3 + len(pieces)),
+        out_specs=vmem(),
+        scratch_shapes=[pltpu.VMEM((tok * len(pieces), width), BF16)],
+        compiler_params=params(),
+        cost_estimate=cost(1e8, 2**21),
+        name="write_pool",
+    )(slots, cosine, sine, pool, *pieces)
+
+
+def project_kernel(*refs, n_ctx, chunks):
+    contexts = refs[:n_ctx]
+    weights = refs[n_ctx:-2]
+    send_ref, keep_ref = refs[-2:]
+    n_req, tok, depth = contexts[0].shape
+    for i in range(n_ctx):
+        ctx = contexts[i][...].reshape(n_req * tok, depth)
+        at = 0
+        for b, count in enumerate(chunks):
+            total, row = None, 0
+            for j in range(count):
+                rows = weights[at].shape[0]
+                part = jnp.dot(ctx[:, row : row + rows], weights[at][...], preferred_element_type=F32)
+                total = part if total is None else total + part
+                row += rows
+                at += 1
+            terms = total.astype(BF16)
+            for k in range(n_req):
+                target = send_ref if k % 2 else keep_ref
+                target[i, b, k // 2] = terms[k * tok : (k + 1) * tok, :]
+
+
+def project(contexts, blocks):
+    n_req, tok, depth = contexts[0].shape
+    cols = blocks[0][0].shape[1]
+    shape = jax.ShapeDtypeStruct((len(contexts), len(blocks), n_req // 2, tok, cols), BF16)
+    flat = [chunk for block in blocks for chunk in block]
+    work = len(contexts) * len(blocks)
+    return pl.pallas_call(
+        functools.partial(project_kernel, n_ctx=len(contexts), chunks=tuple(len(b) for b in blocks)),
+        out_shape=[shape, shape],
+        in_specs=[vmem()] * (len(contexts) + len(flat)),
+        out_specs=[vmem()] * 2,
+        compiler_params=params(),
+        cost_estimate=cost(work * 2 * n_req * tok * depth * cols, 2 * depth * cols * len(blocks)),
+        name="project",
+    )(*contexts, *flat)
+
+
+def pair_kernel(keep_ref, got_ref, *out_refs):
+    half = len(out_refs) // keep_ref.shape[0]
+    for i in range(keep_ref.shape[0]):
+        for k in range(half):
+            out_refs[i * half + k][...] = (
+                keep_ref[i, :, k].astype(F32) + got_ref[i, :, k].astype(F32)
+            ).astype(BF16)
+
+
+def pair_sum(keep, got):
+    n_ctx, blocks, half, tok, cols = keep.shape
+    return pl.pallas_call(
+        pair_kernel,
+        out_shape=[jax.ShapeDtypeStruct((blocks, tok, cols), BF16)] * (n_ctx * half),
+        in_specs=[vmem()] * 2,
+        out_specs=[vmem()] * (n_ctx * half),
+        compiler_params=params(),
+        cost_estimate=cost(1e6, 6 * keep.size),
+        name="pair_sum",
+    )(keep, got)
+
+
+def final_kernel(hidden_ref, *rest, places):
+    parts, out_ref, scr = rest[:-2], rest[-2], rest[-1]
+    own = lax.axis_index("exp")
+    cols = parts[0].shape[-1]
+    for (first, second), bits in zip(zip(parts[0::2], parts[1::2]), places):
+        for b, bit in enumerate(bits):
+            scr[jnp.bitwise_xor(own, bit)] = first[b].astype(F32) + second[b].astype(F32)
+    for b in range(scr.shape[0]):
+        at = slice(b * cols, (b + 1) * cols)
+        out_ref[:, at] = (hidden_ref[:, at].astype(F32) + scr[b]).astype(BF16)
+
+
+def finish(hidden, parts, places):
+    tok, width = hidden.shape
+    n_exp = lax.axis_size("exp")
+    return pl.pallas_call(
+        functools.partial(final_kernel, places=places),
+        out_shape=jax.ShapeDtypeStruct(hidden.shape, BF16),
+        in_specs=[vmem()] * (1 + len(parts)),
+        out_specs=vmem(),
+        scratch_shapes=[pltpu.VMEM((n_exp, tok, width // n_exp), F32)],
+        compiler_params=params(),
+        cost_estimate=cost(1e6, 8 * hidden.size),
+        name="finish",
+    )(hidden, *parts)
+
+
+CHUNKS = 4
+
+
+def paired_plan(
+    hidden_in, queries, new_kv, kv_pool, page_table, new_slots, cached_pages, sinks, out_weight
+):
+    tok = hidden_in.shape[1]
+    n_req = lax.axis_size("req")
+    head_count = sinks.shape[0]
+    kv_width = new_kv.shape[2] // 2
+    kv_heads = kv_width // HD
+    slots_dev, page_size = kv_pool.shape[1:3]
+    pool_rows = slots_dev * page_size
+    depth = out_weight.shape[0]
+    pieces = pack(queries[0], new_kv[0], kv_pool[0].reshape(pool_rows, 2 * kv_width), n_req)
+    pieces = [pieces[0]] + [swap(pieces[k], k, 0) for k in range(1, n_req)]
+
+    near = swap(out_weight, 0, NEAR_BIT)
+    step = depth // CHUNKS
+    own_chunks = [out_weight[i * step : (i + 1) * step] for i in range(CHUNKS)]
+    far = [swap(chunk, 0, FAR_BIT) for chunk in own_chunks]
+    both = [swap(chunk, 0, NEAR_BIT) for chunk in far]
+
+    position = cached_pages[0] * page_size + jnp.arange(n_req * tok)
+    frequency = THETA ** (-2.0 * jnp.arange(HD // 2).astype(F32) / HD)
+    angles = position.astype(F32)[:, None] * frequency[None, :]
+    cosine, sine = jnp.cos(angles), jnp.sin(angles)
+    cosine = jnp.concatenate([cosine] * 4, axis=1)
+    sine = jnp.concatenate([-sine, sine, -sine, sine], axis=1)
+
+    ctx = attention(
+        cached_pages, page_table, sinks, cosine, sine, pieces, kv_heads // n_req,
+        head_count // kv_heads, pool_rows, page_size,
+    )
+    ctx_mate = swap(ctx, 0, PAIR_BIT)
+    fresh = [new_kv[0]] + [swap(new_kv[0], k, 0) for k in range(1, n_req)]
+    pool_out = write_pool(new_slots, cosine, sine, kv_pool[0], fresh)
+
+    early = [[out_weight], [near], far]
+    late = [both]
+    parts = []
+    send, keep = project([ctx], early)
+    own_a, over_y = pair_sum(keep, swap(send, 1, 0))
+    parts += [own_a, swap(over_y, 2, 0)]
+    send, keep = project([ctx_mate], early)
+    over_pair, over_both = pair_sum(keep, swap(send, 1, 0))
+    parts += [swap(over_pair, 0, PAIR_BIT), swap(over_both, 2, PAIR_BIT)]
+    send, keep = project([ctx, ctx_mate], late)
+    own_c, over_y, over_pair, over_both = pair_sum(keep, swap(send, 1, 0))
+    parts += [own_c, swap(over_y, 2, 0), swap(over_pair, 0, PAIR_BIT), swap(over_both, 2, PAIR_BIT)]
+    early_bits = (0, NEAR_BIT, FAR_BIT)
+    late_bits = (NEAR_BIT ^ FAR_BIT,)
+    places = (
+        early_bits,
+        tuple(PAIR_BIT ^ b for b in early_bits),
+        late_bits,
+        tuple(PAIR_BIT ^ b for b in late_bits),
+    )
+    layer_out = finish(hidden_in[0], parts, places)
+    return (layer_out[None], pool_out[None])
+
+
 def solution(mesh):
+    paired = mesh.shape["req"] == 4 and mesh.shape["exp"] == 8
     return jax.shard_map(
-        per_device,
+        paired_plan if paired else general_plan,
         mesh=mesh,
         in_specs=(
             P("exp", "req", None),

time: 145 us -> 141 us (0.972)
  Pallas kernels: 0 us -> 64 us
  waiting for transfers between devices: 85.7 us -> 38.9 us
  starting transfers between devices: 10.7 us -> 28.9 us
  between operations: 15 us -> 1.53 us
  blocking collectives: 8.65 us -> 0 us
  matrix products: 8.57 us -> 0 us
  other arithmetic: 7.81 us -> 1.53 us
  local copies, waits for them, and re-layouts: 7.81 us -> 5.55 us
    pallas_call x0 -> x10, Pallas kernels: none -> 64 us  [the longest x1 29.2 us: pack(): pl.pallas_call(pack_kernel, out_shape=[jax.ShapeDtypeStruct((tok, width),...]
    all_gather x1 -> x0, waiting for transfers between devices: 57.3 us -> none  [per_device(): lax.all_gather(out_weight, 'exp', axis=1, tiled=True)]
    ppermute x0 -> x25, waiting for transfers between devices: none -> 38.9 us  [the longest x12 25.7 us: swap(): lax.ppermute(values, 'exp', [(i, i ^ exp_bits) for i in range(lax.axis_si...]
    ppermute x0 -> x25, starting transfers between devices: none -> 28.9 us  [the longest x12 17.5 us: swap(): lax.ppermute(values, 'exp', [(i, i ^ exp_bits) for i in range(lax.axis_si...]
    all_to_all x3 -> x0, waiting for transfers between devices: 27.7 us -> none  [the longest x1 18.5 us: per_device(): lax.all_to_all(terms.reshape(n_req, tok_dev, width), 'req', split_axis=0,...]
    all_to_all x3 -> x0, starting transfers between devices: 10.6 us -> none  [the longest x1 3.65 us: per_device(): lax.all_to_all(q_rot.reshape(tok_dev, n_req, heads_dev * HD), 'req', spli...]
    all_gather x1 -> x0, blocking collectives: 8.65 us -> none  [per_device(): all_fresh = lax.all_gather(kv_rot, 'req', axis=0, tiled=True)]
    dot_general x6 -> x0, matrix products: 8.57 us -> none  [the longest x1 4.37 us: per_device(): jnp.dot(context, lax.all_gather(out_weight, 'exp', axis=1, tiled=True), p...]
  transfers between devices with their start and end apart: 4 -> 25, of which waited for: 4 -> 8; matrix products, arithmetic and copies ran while one was open for 12% -> 2% of each run, Pallas kernels for 0% -> 23%
where the time goes in v1:
time: 141 us; the launch traced here: 140 us
  Pallas kernels  64 us (45%)
  waiting for transfers between devices  38.9 us (28%)
  starting transfers between devices  28.9 us (20%)
  local copies, waits for them, and re-layouts  5.55 us (4%)
  other arithmetic  1.53 us (1%)
  between operations  1.53 us (1%)
    pallas_call x1, Pallas kernels, pack(): pl.pallas_call(pack_kernel, out_shape=[jax.ShapeDtypeStruct((tok, width),...  29.2 us
    ppermute x12, waiting for transfers between devices, swap(): lax.ppermute(values, 'exp', [(i, i ^ exp_bits) for i in range(lax.axis_si...  25.7 us
    ppermute x12, starting transfers between devices, swap(): lax.ppermute(values, 'exp', [(i, i ^ exp_bits) for i in range(lax.axis_si...  17.5 us
    pallas_call x1, Pallas kernels, attention(): pl.pallas_call(functools.partial(attention_kernel, kv_dev=kv_dev, per_kv=...  14.8 us
    ppermute x11, waiting for transfers between devices, swap(): lax.ppermute(values, 'req', [(i, i ^ req_bits) for i in range(lax.axis_si...  11.5 us
    pallas_call x3, Pallas kernels, project(): pl.pallas_call(functools.partial(project_kernel, n_ctx=len(contexts), chu...  9.91 us
    ppermute x11, starting transfers between devices, swap(): lax.ppermute(values, 'req', [(i, i ^ req_bits) for i in range(lax.axis_si...  7.95 us
    pallas_call x3, Pallas kernels, pair_sum(): pl.pallas_call(pair_kernel, out_shape=[jax.ShapeDtypeStruct((blocks, tok,...  5.32 us
  transfers between devices with their start and end apart: 25, of which 8 were waited for; matrix products, arithmetic and copies ran while one was open for 2% of the time, Pallas kernels for 23%

profile of v1, /device:TPU:0, one launch (start us, length us, event | category | flops | bytes accessed | tf_op | source)
XLA Modules:
  0.0 140.4 jit_solution(7655011215215614852)
XLA Ops:
  0.6 29.2 %pack.1 = (bf16[64,1792]{1,0:T(8,128)(2,1)}, bf16[64,1792]{1,0:T(8,128)(2,1)}, bf16[64,1792]{1,0:T(8,128)(2,1)}, bf16[64,1792]{1,0:T(8,128)(2,1)}) custom-call(bf16[64,4096]{1,0:T(8,128)(2,1)} %bitcast.15, bf16[64,1024]{1,0:T(8,128)(2,1)} %bitcast.10, bf16[128,1024]{1,0:T(8,128)(2,1)} %bitcast.8), custom_call_target="tpu_custom_call" | custom-call | bytes 1835008 | tf_op jit(solution)/shard_map/pack/pallas_call | solution.py:245
  30.3 2.6 %collective-permute-start.1 = (bf16[64,1792]{1,0:T(8,128)(2,1)}, bf16[64,1792]{1,0:T(8,128)(2,1)S(1)}, u32[]{:S(2)}, u32[]{:S(2)}) collective-permute-start(bf16[64,1792]{1,0:T(8,128)(2,1)} %get-tuple-element.22), channel_id=1, source_target_pairs={{0,16},{8,24},{16,0},{24,8},{1,17},{9,25},{17,1},{25,9},{2,18},{10... | collective-permute-start | bytes 688136 | tf_op jit(solution)/shard_map/ppermute | solution.py:199
  33.0 1.7 %collective-permute-start.3 = (bf16[1024,360]{0,1:T(8,128)(2,1)S(1)}, bf16[1024,360]{0,1:T(8,128)(2,1)S(1)}, u32[]{:S(2)}, u32[]{:S(2)}) collective-permute-start(bf16[1024,360]{0,1:T(8,128)(2,1)S(1)} %copy-done.6), channel_id=1, source_target_pairs={{0,1},{1,0},{2,3},{3,2},{4,5},{5,4},{6,7},{7,6},{8,9},{9,8},{10,11... | collective-permute-start | bytes 2211848 | tf_op jit(solution)/shard_map/ppermute | solution.py:201
  37.3 2.3 %collective-permute-done.1.rest_2_ = bf16[64,1792]{1,0:T(8,128)(2,1)S(1)} collective-permute-done((bf16[64,1792]{1,0:T(8,128)(2,1)}, bf16[64,1792]{1,0:T(8,128)(2,1)S(1)}, u32[]{:S(2)}, u32[]{:S(2)}) %collective-permute-start.1) | collective-permute-done | bytes 229408 | tf_op jit(solution)/shard_map/ppermute | solution.py:199
  39.6 4.4 %collective-permute-done.2.rest_3_ = bf16[64,1792]{1,0:T(8,128)(2,1)S(1)} collective-permute-done((bf16[64,1792]{1,0:T(8,128)(2,1)}, bf16[64,1792]{1,0:T(8,128)(2,1)S(1)}, u32[]{:S(2)}, u32[]{:S(2)}) %collective-permute-start.2) | collective-permute-done | bytes 229408 | tf_op jit(solution)/shard_map/ppermute | solution.py:199
  44.7 14.8 %attention.1.refs_0_ = bf16[4,64,1024]{2,1,0:T(8,128)(2,1)} custom-call(s32[1]{0:T(128)S(6)} %copy.35.pages_ref, s32[1,16]{1,0:T(1,128)} %table_ref.1, f32[64]{0:T(128)} %sink_ref.1, f32[256,128]{1,0:T(8,128)} %get-tuple-element.45.cos_ref, f32[256,128]{1,0:T(8,128)} %get-tuple-element.46.sin_ref, bf16[64,1792]{1,0:T(8,128)(2,1)} %get-tuple-element.20.rest_0_, ...), custom_call_target="tpu_custom_call" | custom-call | flops 3000000000 | bytes 4194304 | tf_op jit(solution)/shard_map/attention/pallas_call | solution.py:360
  59.5 1.6 %collective-permute-start.10 = (bf16[4,64,1024]{2,1,0:T(8,128)(2,1)}, bf16[4,64,1024]{2,1,0:T(8,128)(2,1)S(1)}, u32[]{:S(2)}, u32[]{:S(2)}) collective-permute-start(bf16[4,64,1024]{2,1,0:T(8,128)(2,1)} %attention.1.refs_0_), channel_id=1, source_target_pairs={{0,2},{1,3},{2,0},{3,1},{4,6},{5,7},{6,4},{7,5},{8,10},{9,11},{10,... | collective-permute-start | bytes 1572872 | tf_op jit(solution)/shard_map/ppermute | solution.py:201
  61.2 2.7 %collective-permute-start.4 = (bf16[256,360]{1,0:T(8,128)(2,1)S(1)}, bf16[256,360]{1,0:T(8,128)(2,1)S(1)}, u32[]{:S(2)}, u32[]{:S(2)}) collective-permute-start(bf16[256,360]{1,0:T(8,128)(2,1)S(1)} %get-tuple-element.41), channel_id=1, source_target_pairs={{0,4},{1,5},{2,6},{3,7},{4,0},{5,1},{6,2},{7,3},{8,12},{9,13},{10,... | collective-permute-start | bytes 552968 | tf_op jit(solution)/shard_map/ppermute | solution.py:201
  64.2 2.6 %collective-permute-start.6 = (bf16[256,360]{1,0:T(8,128)(2,1)S(1)}, bf16[256,360]{1,0:T(8,128)(2,1)S(1)}, u32[]{:S(2)}, u32[]{:S(2)}) collective-permute-start(bf16[256,360]{1,0:T(8,128)(2,1)S(1)} %get-tuple-element.39), channel_id=1, source_target_pairs={{0,4},{1,5},{2,6},{3,7},{4,0},{5,1},{6,2},{7,3},{8,12},{9,13},{10,... | collective-permute-start | bytes 552968 | tf_op jit(solution)/shard_map/ppermute | solution.py:201
  66.8 11.0 %collective-permute-done.4.refs_3_ = bf16[256,360]{1,0:T(8,128)(2,1)S(1)} collective-permute-done((bf16[256,360]{1,0:T(8,128)(2,1)S(1)}, bf16[256,360]{1,0:T(8,128)(2,1)S(1)}, u32[]{:S(2)}, u32[]{:S(2)}) %collective-permute-start.4) | collective-permute-done | bytes 184352 | tf_op jit(solution)/shard_map/ppermute | solution.py:201
  77.8 3.4 %collective-permute-start.7 = (bf16[256,360]{1,0:T(8,128)(2,1)S(1)}, bf16[256,360]{1,0:T(8,128)(2,1)S(1)}, u32[]{:S(2)}, u32[]{:S(2)}) collective-permute-start(bf16[256,360]{1,0:T(8,128)(2,1)S(1)} %get-tuple-element.38), channel_id=1, source_target_pairs={{0,4},{1,5},{2,6},{3,7},{4,0},{5,1},{6,2},{7,3},{8,12},{9,13},{10,... | collective-permute-start | bytes 552968 | tf_op jit(solution)/shard_map/ppermute | solution.py:201
  83.5 11.7 %collective-permute-done.6.refs_5_ = bf16[256,360]{1,0:T(8,128)(2,1)S(1)} collective-permute-done((bf16[256,360]{1,0:T(8,128)(2,1)S(1)}, bf16[256,360]{1,0:T(8,128)(2,1)S(1)}, u32[]{:S(2)}, u32[]{:S(2)}) %collective-permute-start.6) | collective-permute-done | bytes 184352 | tf_op jit(solution)/shard_map/ppermute | solution.py:201
  96.7 2.1 %collective-permute-done.7.refs_6_ = bf16[256,360]{1,0:T(8,128)(2,1)S(1)} collective-permute-done((bf16[256,360]{1,0:T(8,128)(2,1)S(1)}, bf16[256,360]{1,0:T(8,128)(2,1)S(1)}, u32[]{:S(2)}, u32[]{:S(2)}) %collective-permute-start.7) | collective-permute-done | bytes 184352 | tf_op jit(solution)/shard_map/ppermute | solution.py:201
  102.0 3.5 %project.3 = (bf16[1,3,2,64,360]{4,3,2,1,0:T(8,128)(2,1)}, bf16[1,3,2,64,360]{4,3,2,1,0:T(8,128)(2,1)}) custom-call(bf16[4,64,1024]{2,1,0:T(8,128)(2,1)} %attention.1.refs_0_, bf16[1024,360]{1,0:T(8,128)(2,1)} %copy-done, bf16[1024,360]{1,0:T(8,128)(2,1)} %copy.32.refs_2_, bf16[256,360]{1,0:T(8,128)(2,1)} %copy-done.4, bf16[256,360]{1,0:T(8,128)(2,1)} %copy-done.2, ...), custom_call_target="tpu_custom_call" | custom-call | flops 566231040 | bytes 2211840 | tf_op jit(solution)/shard_map/project/pallas_call | solution.py:443
  106.3 3.5 %project.4 = (bf16[1,3,2,64,360]{4,3,2,1,0:T(8,128)(2,1)}, bf16[1,3,2,64,360]{4,3,2,1,0:T(8,128)(2,1)}) custom-call(bf16[4,64,1024]{2,1,0:T(8,128)(2,1)} %copy-done.1, bf16[1024,360]{1,0:T(8,128)(2,1)} %copy-done, bf16[1024,360]{1,0:T(8,128)(2,1)} %copy.32.refs_2_, bf16[256,360]{1,0:T(8,128)(2,1)} %copy-done.4, bf16[256,360]{1,0:T(8,128)(2,1)} %copy-done.2, ...), custom_call_target="tpu_custom_call" | custom-call | flops 566231040 | bytes 2211840 | tf_op jit(solution)/shard_map/project/pallas_call | solution.py:443
  111.4 2.9 %project.5 = (bf16[2,1,2,64,360]{4,3,2,1,0:T(8,128)(2,1)}, bf16[2,1,2,64,360]{4,3,2,1,0:T(8,128)(2,1)}) custom-call(bf16[4,64,1024]{2,1,0:T(8,128)(2,1)} %attention.1.refs_0_, bf16[4,64,1024]{2,1,0:T(8,128)(2,1)} %copy-done.1, bf16[256,360]{1,0:T(8,128)(2,1)} %copy-done.10, bf16[256,360]{1,0:T(8,128)(2,1)} %copy-done.11, bf16[256,360]{1,0:T(8,128)(2,1)} %copy-done.12, ...), custom_call_target="tpu_custom_call" | custom-call | flops 377487360 | bytes 737280 | tf_op jit(solution)/shard_map/project/pallas_call | solution.py:443
  117.0 1.8 %pair_sum.3 = (bf16[3,64,360]{2,1,0:T(8,128)(2,1)}, bf16[3,64,360]{2,1,0:T(8,128)(2,1)}) custom-call(bf16[1,3,2,64,360]{4,3,2,1,0:T(8,128)(2,1)} %get-tuple-element.24.keep_ref, bf16[1,3,2,64,360]{4,3,2,1,0:T(8,128)(2,1)} %copy-done.9), custom_call_target="tpu_custom_call" | custom-call | flops 1000000 | bytes 829440 | tf_op jit(solution)/shard_map/pair_sum/pallas_call | solution.py:465
  120.0 1.8 %pair_sum.4 = (bf16[3,64,360]{2,1,0:T(8,128)(2,1)}, bf16[3,64,360]{2,1,0:T(8,128)(2,1)}) custom-call(bf16[1,3,2,64,360]{4,3,2,1,0:T(8,128)(2,1)} %get-tuple-element.28.keep_ref, bf16[1,3,2,64,360]{4,3,2,1,0:T(8,128)(2,1)} %copy-done.8), custom_call_target="tpu_custom_call" | custom-call | flops 1000000 | bytes 829440 | tf_op jit(solution)/shard_map/pair_sum/pallas_call | solution.py:465
  121.8 2.4 %collective-permute-start.13 = (bf16[3,64,360]{2,1,0:T(8,128)(2,1)}, bf16[3,64,360]{2,1,0:T(8,128)(2,1)S(1)}, u32[]{:S(2)}, u32[]{:S(2)}) collective-permute-start(bf16[3,64,360]{2,1,0:T(8,128)(2,1)} %get-tuple-element.31), channel_id=1, source_target_pairs={{0,18},{1,19},{2,16},{3,17},{4,22},{5,23},{6,20},{7,21},{8,26},{9,... | collective-permute-start | bytes 414728 | tf_op jit(solution)/shard_map/ppermute | solution.py:206
  124.2 1.7 %pair_sum.5 = (bf16[1,64,360]{2,1,0:T(8,128)(2,1)}, bf16[1,64,360]{2,1,0:T(8,128)(2,1)}, bf16[1,64,360]{2,1,0:T(8,128)(2,1)}, bf16[1,64,360]{2,1,0:T(8,128)(2,1)}) custom-call(bf16[2,1,2,64,360]{4,3,2,1,0:T(8,128)(2,1)} %get-tuple-element.32.keep_ref, bf16[2,1,2,64,360]{4,3,2,1,0:T(8,128)(2,1)} %copy-done.14), custom_call_target="tpu_custom_call" | custom-call | flops 1000000 | bytes 552960 | tf_op jit(solution)/shard_map/pair_sum/pallas_call | solution.py:465
  127.2 4.8 %collective-permute-done.19.rest_5_ = bf16[1,64,360]{2,1,0:T(8,128)(2,1)S(1)} collective-permute-done((bf16[1,64,360]{2,1,0:T(8,128)(2,1)}, bf16[1,64,360]{2,1,0:T(8,128)(2,1)S(1)}, u32[]{:S(2)}, u32[]{:S(2)}) %collective-permute-start.19) | collective-permute-done | bytes 46112 | tf_op jit(solution)/shard_map/ppermute | solution.py:199
  133.1 2.4 %write_pool.1 = bf16[8,16,1024]{2,1,0:T(8,128)(2,1)} custom-call(s32[1,16]{1,0:T(1,128)} %slots_ref.1, f32[256,128]{1,0:T(8,128)} %get-tuple-element.45.cos_ref, f32[256,128]{1,0:T(8,128)} %get-tuple-element.46.sin_ref, bf16[8,16,1024]{2,1,0:T(8,128)(2,1)} %bitcast.9, bf16[64,1024]{1,0:T(8,128)(2,1)} %bitcast.11, bf16[64,1024]{1,0:T(8,128)(2,1)} %copy-done.18, ...), custom_call_target="tpu_custom_call" | custom-call | flops 100000000 | bytes 2097152 | tf_op jit(solution)/shard_map/write_pool/pallas_call | solution.py:403
  135.6 1.7 %collective-permute-done.21.rest_7_ = bf16[1,64,360]{2,1,0:T(8,128)(2,1)S(1)} collective-permute-done((bf16[1,64,360]{2,1,0:T(8,128)(2,1)}, bf16[1,64,360]{2,1,0:T(8,128)(2,1)S(1)}, u32[]{:S(2)}, u32[]{:S(2)}) %collective-permute-start.21) | collective-permute-done | bytes 46112 | tf_op jit(solution)/shard_map/ppermute | solution.py:206
  138.0 2.3 %finish.1 = bf16[64,2880]{1,0:T(8,128)(2,1)} custom-call(bf16[64,2880]{1,0:T(8,128)(2,1)} %bitcast.16, bf16[3,64,360]{2,1,0:T(8,128)(2,1)} %get-tuple-element.26.rest_0_, bf16[3,64,360]{2,1,0:T(8,128)(2,1)} %copy-done.15, bf16[3,64,360]{2,1,0:T(8,128)(2,1)} %copy-done.16, bf16[3,64,360]{2,1,0:T(8,128)(2,1)} %copy-done.17, ...), custom_call_target="tpu_custom_call" | custom-call | flops 1000000 | bytes 1474560 | tf_op jit(solution)/shard_map/finish/pallas_call | solution.py:491
  (97 shorter events, 19.8 us)
Async XLA Ops:
  29.8 7.5 %collective-permute-start = (bf16[64,1792]{1,0:T(8,128)(2,1)}, bf16[64,1792]{1,0:T(8,128)(2,1)S(1)}, u32[]{:S(2)}, u32[]{:S(2)}) collective-permute-start(bf16[64,1792]{1,0:T(8,128)(2,1)} %get-tuple-element.21), channel_id=1, source_target_pairs={{0,8},{8,0},{16,24},{24,16},{1,9},{9,1},{17,25},{25,17},{2,10},{10... | collective-permute-start | bytes 688136 | tf_op jit(solution)/shard_map/ppermute | solution.py:199
  30.3 9.3 %collective-permute-start.1 = (bf16[64,1792]{1,0:T(8,128)(2,1)}, bf16[64,1792]{1,0:T(8,128)(2,1)S(1)}, u32[]{:S(2)}, u32[]{:S(2)}) collective-permute-start(bf16[64,1792]{1,0:T(8,128)(2,1)} %get-tuple-element.22), channel_id=1, source_target_pairs={{0,16},{8,24},{16,0},{24,8},{1,17},{9,25},{17,1},{25,9},{2,18},{10... | collective-permute-start | bytes 688136 | tf_op jit(solution)/shard_map/ppermute | solution.py:199
  32.9 11.1 %collective-permute-start.2 = (bf16[64,1792]{1,0:T(8,128)(2,1)}, bf16[64,1792]{1,0:T(8,128)(2,1)S(1)}, u32[]{:S(2)}, u32[]{:S(2)}) collective-permute-start(bf16[64,1792]{1,0:T(8,128)(2,1)} %get-tuple-element.23), channel_id=1, source_target_pairs={{0,24},{8,16},{16,8},{24,0},{1,25},{9,17},{17,9},{25,1},{2,26},{10... | collective-permute-start | bytes 688136 | tf_op jit(solution)/shard_map/ppermute | solution.py:199
  33.0 67.3 %collective-permute-start.3 = (bf16[1024,360]{0,1:T(8,128)(2,1)S(1)}, bf16[1024,360]{0,1:T(8,128)(2,1)S(1)}, u32[]{:S(2)}, u32[]{:S(2)}) collective-permute-start(bf16[1024,360]{0,1:T(8,128)(2,1)S(1)} %copy-done.6), channel_id=1, source_target_pairs={{0,1},{1,0},{2,3},{3,2},{4,5},{5,4},{6,7},{7,6},{8,9},{9,8},{10,11... | collective-permute-start | bytes 2211848 | tf_op jit(solution)/shard_map/ppermute | solution.py:201
  59.5 46.0 %collective-permute-start.10 = (bf16[4,64,1024]{2,1,0:T(8,128)(2,1)}, bf16[4,64,1024]{2,1,0:T(8,128)(2,1)S(1)}, u32[]{:S(2)}, u32[]{:S(2)}) collective-permute-start(bf16[4,64,1024]{2,1,0:T(8,128)(2,1)} %attention.1.refs_0_), channel_id=1, source_target_pairs={{0,2},{1,3},{2,0},{3,1},{4,6},{5,7},{6,4},{7,5},{8,10},{9,11},{10,... | collective-permute-start | bytes 1572872 | tf_op jit(solution)/shard_map/ppermute | solution.py:201
  61.2 16.6 %collective-permute-start.4 = (bf16[256,360]{1,0:T(8,128)(2,1)S(1)}, bf16[256,360]{1,0:T(8,128)(2,1)S(1)}, u32[]{:S(2)}, u32[]{:S(2)}) collective-permute-start(bf16[256,360]{1,0:T(8,128)(2,1)S(1)} %get-tuple-element.41), channel_id=1, source_target_pairs={{0,4},{1,5},{2,6},{3,7},{4,0},{5,1},{6,2},{7,3},{8,12},{9,13},{10,... | collective-permute-start | bytes 552968 | tf_op jit(solution)/shard_map/ppermute | solution.py:201
  63.9 18.2 %collective-permute-start.5 = (bf16[256,360]{1,0:T(8,128)(2,1)S(1)}, bf16[256,360]{1,0:T(8,128)(2,1)S(1)}, u32[]{:S(2)}, u32[]{:S(2)}) collective-permute-start(bf16[256,360]{1,0:T(8,128)(2,1)S(1)} %get-tuple-element.40), channel_id=1, source_target_pairs={{0,4},{1,5},{2,6},{3,7},{4,0},{5,1},{6,2},{7,3},{8,12},{9,13},{10,... | collective-permute-start | bytes 552968 | tf_op jit(solution)/shard_map/ppermute | solution.py:201
  64.2 31.0 %collective-permute-start.6 = (bf16[256,360]{1,0:T(8,128)(2,1)S(1)}, bf16[256,360]{1,0:T(8,128)(2,1)S(1)}, u32[]{:S(2)}, u32[]{:S(2)}) collective-permute-start(bf16[256,360]{1,0:T(8,128)(2,1)S(1)} %get-tuple-element.39), channel_id=1, source_target_pairs={{0,4},{1,5},{2,6},{3,7},{4,0},{5,1},{6,2},{7,3},{8,12},{9,13},{10,... | collective-permute-start | bytes 552968 | tf_op jit(solution)/shard_map/ppermute | solution.py:201
  77.8 21.0 %collective-permute-start.7 = (bf16[256,360]{1,0:T(8,128)(2,1)S(1)}, bf16[256,360]{1,0:T(8,128)(2,1)S(1)}, u32[]{:S(2)}, u32[]{:S(2)}) collective-permute-start(bf16[256,360]{1,0:T(8,128)(2,1)S(1)} %get-tuple-element.38), channel_id=1, source_target_pairs={{0,4},{1,5},{2,6},{3,7},{4,0},{5,1},{6,2},{7,3},{8,12},{9,13},{10,... | collective-permute-start | bytes 552968 | tf_op jit(solution)/shard_map/ppermute | solution.py:201
  82.1 27.8 %collective-permute-start.14 = (bf16[256,360]{1,0:T(8,128)(2,1)S(1)}, bf16[256,360]{1,0:T(8,128)(2,1)S(1)}, u32[]{:S(2)}, u32[]{:S(2)}) collective-permute-start(bf16[256,360]{1,0:T(8,128)(2,1)S(1)} %collective-permute-done.4.refs_3_), channel_id=1, source_target_pairs={{0,1},{1,0},{2,3},{3,2},{4,5},{5,4},{6,7},{7,6},{8,9},{9,8},{10,11... | collective-permute-start | bytes 552968 | tf_op jit(solution)/shard_map/ppermute | solution.py:201
  95.3 14.7 %collective-permute-start.15 = (bf16[256,360]{1,0:T(8,128)(2,1)S(1)}, bf16[256,360]{1,0:T(8,128)(2,1)S(1)}, u32[]{:S(2)}, u32[]{:S(2)}) collective-permute-start(bf16[256,360]{1,0:T(8,128)(2,1)S(1)} %collective-permute-done.5.refs_4_), channel_id=1, source_target_pairs={{0,1},{1,0},{2,3},{3,2},{4,5},{5,4},{6,7},{7,6},{8,9},{9,8},{10,11... | collective-permute-start | bytes 552968 | tf_op jit(solution)/shard_map/ppermute | solution.py:201
  98.8 11.2 %collective-permute-start.16 = (bf16[256,360]{1,0:T(8,128)(2,1)S(1)}, bf16[256,360]{1,0:T(8,128)(2,1)S(1)}, u32[]{:S(2)}, u32[]{:S(2)}) collective-permute-start(bf16[256,360]{1,0:T(8,128)(2,1)S(1)} %collective-permute-done.6.refs_5_), channel_id=1, source_target_pairs={{0,1},{1,0},{2,3},{3,2},{4,5},{5,4},{6,7},{7,6},{8,9},{9,8},{10,11... | collective-permute-start | bytes 552968 | tf_op jit(solution)/shard_map/ppermute | solution.py:201
  100.3 9.7 %collective-permute-start.17 = (bf16[256,360]{1,0:T(8,128)(2,1)S(1)}, bf16[256,360]{1,0:T(8,128)(2,1)S(1)}, u32[]{:S(2)}, u32[]{:S(2)}) collective-permute-start(bf16[256,360]{1,0:T(8,128)(2,1)S(1)} %collective-permute-done.7.refs_6_), channel_id=1, source_target_pairs={{0,1},{1,0},{2,3},{3,2},{4,5},{5,4},{6,7},{7,6},{8,9},{9,8},{10,11... | collective-permute-start | bytes 552968 | tf_op jit(solution)/shard_map/ppermute | solution.py:201
  105.6 10.8 %collective-permute-start.8 = (bf16[1,3,2,64,360]{4,3,2,1,0:T(8,128)(2,1)}, bf16[1,3,2,64,360]{4,3,2,1,0:T(8,128)(2,1)S(1)}, u32[]{:S(2)}, u32[]{:S(2)}) collective-permute-start(bf16[1,3,2,64,360]{4,3,2,1,0:T(8,128)(2,1)} %get-tuple-element.25), channel_id=1, source_target_pairs={{0,8},{8,0},{16,24},{24,16},{1,9},{9,1},{17,25},{25,17},{2,10},{10... | collective-permute-start | bytes 829448 | tf_op jit(solution)/shard_map/ppermute | solution.py:199
  109.9 9.0 %collective-permute-start.11 = (bf16[1,3,2,64,360]{4,3,2,1,0:T(8,128)(2,1)}, bf16[1,3,2,64,360]{4,3,2,1,0:T(8,128)(2,1)S(1)}, u32[]{:S(2)}, u32[]{:S(2)}) collective-permute-start(bf16[1,3,2,64,360]{4,3,2,1,0:T(8,128)(2,1)} %get-tuple-element.29), channel_id=1, source_target_pairs={{0,8},{8,0},{16,24},{24,16},{1,9},{9,1},{17,25},{25,17},{2,10},{10... | collective-permute-start | bytes 829448 | tf_op jit(solution)/shard_map/ppermute | solution.py:199
  114.3 7.6 %collective-permute-start.18 = (bf16[2,1,2,64,360]{4,3,2,1,0:T(8,128)(2,1)}, bf16[2,1,2,64,360]{4,3,2,1,0:T(8,128)(2,1)S(1)}, u32[]{:S(2)}, u32[]{:S(2)}) collective-permute-start(bf16[2,1,2,64,360]{4,3,2,1,0:T(8,128)(2,1)} %get-tuple-element.33), channel_id=1, source_target_pairs={{0,8},{8,0},{16,24},{24,16},{1,9},{9,1},{17,25},{25,17},{2,10},{10... | collective-permute-start | bytes 552968 | tf_op jit(solution)/shard_map/ppermute | solution.py:199
  114.8 7.0 %collective-permute-start.22 = (bf16[64,1024]{1,0:T(8,128)(2,1)S(1)}, bf16[64,1024]{1,0:T(8,128)(2,1)S(1)}, u32[]{:S(2)}, u32[]{:S(2)}) collective-permute-start(bf16[64,1024]{1,0:T(8,128)(2,1)S(1)} %bitcast.12), channel_id=1, source_target_pairs={{0,8},{8,0},{16,24},{24,16},{1,9},{9,1},{17,25},{25,17},{2,10},{10... | collective-permute-start | bytes 393224 | tf_op jit(solution)/shard_map/ppermute | solution.py:199
  114.8 11.1 %collective-permute-start.23 = (bf16[64,1024]{1,0:T(8,128)(2,1)S(1)}, bf16[64,1024]{1,0:T(8,128)(2,1)S(1)}, u32[]{:S(2)}, u32[]{:S(2)}) collective-permute-start(bf16[64,1024]{1,0:T(8,128)(2,1)S(1)} %bitcast.13), channel_id=1, source_target_pairs={{0,16},{8,24},{16,0},{24,8},{1,17},{9,25},{17,1},{25,9},{2,18},{10... | collective-permute-start | bytes 393224 | tf_op jit(solution)/shard_map/ppermute | solution.py:199
  116.3 10.8 %collective-permute-start.24 = (bf16[64,1024]{1,0:T(8,128)(2,1)S(1)}, bf16[64,1024]{1,0:T(8,128)(2,1)S(1)}, u32[]{:S(2)}, u32[]{:S(2)}) collective-permute-start(bf16[64,1024]{1,0:T(8,128)(2,1)S(1)} %bitcast.14), channel_id=1, source_target_pairs={{0,24},{8,16},{16,8},{24,0},{1,25},{9,17},{17,9},{25,1},{2,26},{10... | collective-permute-start | bytes 393224 | tf_op jit(solution)/shard_map/ppermute | solution.py:199
  118.8 18.4 %collective-permute-start.9 = (bf16[3,64,360]{2,1,0:T(8,128)(2,1)}, bf16[3,64,360]{2,1,0:T(8,128)(2,1)S(1)}, u32[]{:S(2)}, u32[]{:S(2)}) collective-permute-start(bf16[3,64,360]{2,1,0:T(8,128)(2,1)} %get-tuple-element.27), channel_id=1, source_target_pairs={{0,16},{8,24},{16,0},{24,8},{1,17},{9,25},{17,1},{25,9},{2,18},{10... | collective-permute-start | bytes 414728 | tf_op jit(solution)/shard_map/ppermute | solution.py:199
  121.8 15.5 %collective-permute-start.12 = (bf16[3,64,360]{2,1,0:T(8,128)(2,1)}, bf16[3,64,360]{2,1,0:T(8,128)(2,1)S(1)}, u32[]{:S(2)}, u32[]{:S(2)}) collective-permute-start(bf16[3,64,360]{2,1,0:T(8,128)(2,1)} %get-tuple-element.30), channel_id=1, source_target_pairs={{0,2},{1,3},{2,0},{3,1},{4,6},{5,7},{6,4},{7,5},{8,10},{9,11},{10,... | collective-permute-start | bytes 414728 | tf_op jit(solution)/shard_map/ppermute | solution.py:201
  121.8 15.4 %collective-permute-start.13 = (bf16[3,64,360]{2,1,0:T(8,128)(2,1)}, bf16[3,64,360]{2,1,0:T(8,128)(2,1)S(1)}, u32[]{:S(2)}, u32[]{:S(2)}) collective-permute-start(bf16[3,64,360]{2,1,0:T(8,128)(2,1)} %get-tuple-element.31), channel_id=1, source_target_pairs={{0,18},{1,19},{2,16},{3,17},{4,22},{5,23},{6,20},{7,21},{8,26},{9,... | collective-permute-start | bytes 414728 | tf_op jit(solution)/shard_map/ppermute | solution.py:206
  125.9 6.1 %collective-permute-start.19 = (bf16[1,64,360]{2,1,0:T(8,128)(2,1)}, bf16[1,64,360]{2,1,0:T(8,128)(2,1)S(1)}, u32[]{:S(2)}, u32[]{:S(2)}) collective-permute-start(bf16[1,64,360]{2,1,0:T(8,128)(2,1)} %get-tuple-element.35), channel_id=1, source_target_pairs={{0,16},{8,24},{16,0},{24,8},{1,17},{9,25},{17,1},{25,9},{2,18},{10... | collective-permute-start | bytes 138248 | tf_op jit(solution)/shard_map/ppermute | solution.py:199
  127.1 8.5 %collective-permute-start.20 = (bf16[1,64,360]{2,1,0:T(8,128)(2,1)}, bf16[1,64,360]{2,1,0:T(8,128)(2,1)S(1)}, u32[]{:S(2)}, u32[]{:S(2)}) collective-permute-start(bf16[1,64,360]{2,1,0:T(8,128)(2,1)} %get-tuple-element.36), channel_id=1, source_target_pairs={{0,2},{1,3},{2,0},{3,1},{4,6},{5,7},{6,4},{7,5},{8,10},{9,11},{10,... | collective-permute-start | bytes 138248 | tf_op jit(solution)/shard_map/ppermute | solution.py:201
  (28 other events, 173.5 us)

commit v2 on v1

--- a/solution.py
+++ b/solution.py
@@ -167,11 +167,12 @@
     return (layer_out[None], local_pages[None])
 
 
-VMEM_LIMIT = 56 * 1024 * 1024
+VMEM_LIMIT = 24 * 1024 * 1024
 F32 = jnp.float32
 BF16 = jnp.bfloat16
 
 PAIR_BIT, NEAR_BIT, FAR_BIT = 2, 1, 4
+ORDER = (0, 2, 1, 3)
 
 
 def vmem():
@@ -180,10 +181,6 @@
 
 def smem():
     return pl.BlockSpec(memory_space=pltpu.SMEM)
-
-
-def anywhere():
-    return pl.BlockSpec(memory_space=pl.ANY)
 
 
 def params():
@@ -206,36 +203,24 @@
     return lax.ppermute(values, ("req", "exp"), pairs)
 
 
-def pack_kernel(q_ref, kv_ref, pool_ref, *rest):
-    outs, sems = rest[:-1], rest[-1]
+def pack_kernel(q_ref, kv_ref, pool_ref, *outs):
     n_req = len(outs)
     own = lax.axis_index("req")
     tok = q_ref.shape[0]
     q_width = q_ref.shape[1] // n_req
     kv_width = kv_ref.shape[1] // 2
     head_width = kv_width // n_req
-    copies = []
-
-    def copy(source, target):
-        one = pltpu.make_async_copy(source, target, sems.at[len(copies)])
-        one.start()
-        copies.append(one)
-
-    for k in (2, 3, 1, 0):
+    for k, out in enumerate(outs):
         dest = jnp.bitwise_xor(own, k)
-        out = outs[k]
-        q_col = pl.multiple_of(dest * q_width, 128)
-        copy(q_ref.at[:, pl.ds(q_col, q_width)], out.at[:, pl.ds(0, q_width)])
+        out[:, :q_width] = q_ref[:, pl.ds(pl.multiple_of(dest * q_width, 128), q_width)]
         at = q_width
-        blocks = [kv_ref]
-        blocks += [pool_ref.at[pl.ds(i * tok, tok), :] for i in range(pool_ref.shape[0] // tok)]
-        for block in blocks:
+        blocks = [(kv_ref, 0)]
+        blocks += [(pool_ref, i * tok) for i in range(pool_ref.shape[0] // tok)]
+        for block, row in blocks:
             for half in range(2):
                 col = pl.multiple_of(half * kv_width + dest * head_width, 128)
-                copy(block.at[:, pl.ds(col, head_width)], out.at[:, pl.ds(at, head_width)])
+                out[:, at : at + head_width] = block[row : row + tok, pl.ds(col, head_width)]
                 at += head_width
-    for one in copies:
-        one.wait()
 
 
 def pack(q, kv, pool, n_req):
@@ -245,9 +230,8 @@
     return pl.pallas_call(
         pack_kernel,
         out_shape=[jax.ShapeDtypeStruct((tok, width), BF16)] * n_req,
-        in_specs=[anywhere()] * 3,
-        out_specs=[anywhere()] * n_req,
-        scratch_shapes=[pltpu.SemaphoreType.DMA((n_req * (1 + 2 * blocks),))],
+        in_specs=[vmem()] * 3,
+        out_specs=[vmem()] * n_req,
         compiler_params=params(),
         cost_estimate=cost(0, 4 * tok * width * n_req),
         name="pack",
@@ -263,9 +247,9 @@
 def attention_kernel(
     pages_ref, table_ref, sink_ref, cos_ref, sin_ref, *rest, kv_dev, per_kv, page_size
 ):
-    n_req = len(rest) - 6
+    n_req = len(rest) - 7
     pieces, out_ref = rest[:n_req], rest[n_req]
-    q_scr, pool_scr, key_scr, value_scr, flat_scr = rest[n_req + 1 :]
+    q_scr, pool_scr, flat_scr, key_scr, value_scr, bias_scr = rest[n_req + 1 :]
     own = lax.axis_index("req")
     tok = pieces[0].shape[0]
     q_width = kv_dev * per_kv * HD
@@ -275,18 +259,17 @@
     fresh = tok * n_req
     total = cached + fresh
     pool_rows = pool_scr.shape[1]
-    page_count = pages_ref[0]
+    live = pages_ref[0] * page_size
     pairs = per_kv // 2
-    for k in range(n_req):
+    for place, k in enumerate(ORDER):
         shard = jnp.bitwise_xor(own, k)
         row = pl.multiple_of(shard * tok, tok)
         cosine = cos_ref[pl.ds(row, tok), :]
         sine = sin_ref[pl.ds(row, tok), :]
-        for g in range(kv_dev):
-            for p in range(pairs):
-                col = (g * pairs + p) * 2 * HD
-                turned = turn(pieces[k][:, col : col + 2 * HD].astype(F32), cosine, sine).astype(BF16)
-                q_scr[k, g, p * tok : (p + 1) * tok, :] = turned * jnp.asarray(1.0 / math.sqrt(HD), BF16)
+        for p in range(kv_dev * pairs):
+            col = p * 2 * HD
+            turned = turn(pieces[k][:, col : col + 2 * HD].astype(F32), cosine, sine).astype(BF16)
+            q_scr[p, place * tok : (place + 1) * tok, :] = turned * jnp.asarray(1.0 / math.sqrt(HD), BF16)
         at = q_width
         key_row = pl.multiple_of(cached + row, tok)
         flat_scr[pl.ds(key_row, tok), :head_width] = turn(
@@ -299,6 +282,10 @@
         for i in range(pool_rows // tok):
             pool_scr[shard, i * tok : (i + 1) * tok, :] = pieces[k][:, at : at + 2 * head_width].astype(F32)
             at += 2 * head_width
+        key = lax.broadcasted_iota(jnp.int32, (total, tok), 0)
+        query = lax.broadcasted_iota(jnp.int32, (total, tok), 1) + (cached + shard * tok)
+        last = jnp.where(key < cached, live - 1, query)
+        bias_scr[:, place * tok : (place + 1) * tok] = jnp.where(key > last, NEGATIVE, 0.0)
     per_dev = pool_rows // page_size
     for j in range(page_limit):
         slot = table_ref[0, j]
@@ -306,71 +293,55 @@
         flat_scr[j * page_size : (j + 1) * page_size, :] = pool_scr[
             slot // per_dev, pl.ds(source, page_size), :
         ]
-    for scr, at in ((key_scr, 0), (value_scr, head_width)):
-        flat = flat_scr[:, at : at + head_width]
-        rolled = pltpu.roll(flat, HD, 1)
-        low = lax.broadcasted_iota(jnp.int32, flat.shape, 1) < HD
-        zero = jnp.zeros_like(flat)
-        scr[0, :total, :] = jnp.where(low, flat, zero).astype(BF16)
-        scr[0, total:, :] = jnp.where(low, zero, rolled).astype(BF16)
-        scr[1, :total, :] = jnp.where(low, rolled, zero).astype(BF16)
-        scr[1, total:, :] = jnp.where(low, zero, flat).astype(BF16)
-    live = page_count * page_size
-
-    def one_shard(k, carry):
-        shard = jnp.bitwise_xor(own, k)
-        key = lax.broadcasted_iota(jnp.int32, (tok, total), 1)
-        query = lax.broadcasted_iota(jnp.int32, (tok, total), 0) + shard * tok
-        last = jnp.where(key < cached, live - 1, query + cached)
-        bias = jnp.where(key > last, NEGATIVE, 0.0)
-        bias = jnp.concatenate([bias] * pairs, axis=0)
-        for g in range(kv_dev):
+    flat = flat_scr[:, :head_width]
+    rolled = pltpu.roll(flat, HD, 1)
+    low = lax.broadcasted_iota(jnp.int32, flat.shape, 1) < HD
+    zero = jnp.zeros_like(flat)
+    key_scr[0] = jnp.where(low, flat, zero).astype(BF16)
+    key_scr[1] = jnp.where(low, zero, rolled).astype(BF16)
+    key_scr[2] = jnp.where(low, rolled, zero).astype(BF16)
+    key_scr[3] = jnp.where(low, zero, flat).astype(BF16)
+    value_scr[...] = flat_scr[:, head_width:].T.astype(BF16)
+
+    def one_pair(i, carry):
+        g = i // pairs
+        for a in range(2):
             scores = lax.dot_general(
-                q_scr[k, g], key_scr[g], (((1,), (1,)), ((), ())), preferred_element_type=F32
+                key_scr[g * 2 + a], q_scr[i], (((1,), (1,)), ((), ())), preferred_element_type=F32
             )
-            weights, dens = [], []
-            for a in range(2):
-                part = scores[:, a * total : (a + 1) * total] + bias
-                first = own * (kv_dev * per_kv) + g * per_kv + a
-                sink = jnp.concatenate(
-                    [jnp.full((tok, 1), sink_ref[first + 2 * p], F32) for p in range(pairs)], axis=0
-                )
-                top = jnp.maximum(jnp.max(part, axis=1, keepdims=True), sink)
-                expo = jnp.exp(part - top)
-                dens.append(jnp.sum(expo, axis=1, keepdims=True) + jnp.exp(sink - top))
-                weights.append(expo.astype(BF16))
-            summed = jnp.dot(weights[0], value_scr[g, :total, :], preferred_element_type=F32) + jnp.dot(
-                weights[1], value_scr[g, total:, :], preferred_element_type=F32
-            )
-            low = lax.broadcasted_iota(jnp.int32, summed.shape, 1) < HD
-            ctx = (summed / jnp.where(low, dens[0], dens[1])).astype(BF16)
-            for p in range(pairs):
-                col = (g * pairs + p) * 2 * HD
-                out_ref[k, :, col : col + 2 * HD] = ctx[p * tok : (p + 1) * tok, :]
+            scores = scores + bias_scr[...]
+            sink = sink_ref[own * (kv_dev * per_kv) + i * 2 + a]
+            top = jnp.maximum(jnp.max(scores, axis=0, keepdims=True), sink)
+            expo = jnp.exp(scores - top)
+            den = jnp.sum(expo, axis=0, keepdims=True) + jnp.exp(sink - top)
+            values = value_scr[pl.ds(pl.multiple_of(g * HD, HD), HD), :]
+            summed = jnp.dot(values, expo.astype(BF16), preferred_element_type=F32)
+            out_ref[pl.ds(pl.multiple_of((i * 2 + a) * HD, HD), HD), :] = (summed / den).astype(BF16)
         return carry
 
-    lax.fori_loop(0, n_req, one_shard, 0)
+    lax.fori_loop(0, kv_dev * pairs, one_pair, 0)
 
 
 def attention(pages, table, sinks, cosine, sine, pieces, kv_dev, per_kv, pool_rows, page_size):
     n_req = len(pieces)
     tok = pieces[0].shape[0]
     total = table.shape[1] * page_size + n_req * tok
-    q_width = kv_dev * per_kv * HD
+    head_width = kv_dev * HD
     return pl.pallas_call(
         functools.partial(attention_kernel, kv_dev=kv_dev, per_kv=per_kv, page_size=page_size),
-        out_shape=jax.ShapeDtypeStruct((n_req, tok, q_width), BF16),
+        out_shape=jax.ShapeDtypeStruct((per_kv * head_width, n_req * tok), BF16),
         in_specs=[smem()] * 3 + [vmem()] * (2 + n_req),
         out_specs=vmem(),
         scratch_shapes=[
-            pltpu.VMEM((n_req, kv_dev, per_kv // 2 * tok, 2 * HD), BF16),
-            pltpu.VMEM((n_req, pool_rows, 2 * kv_dev * HD), F32),
-            pltpu.VMEM((kv_dev, 2 * total, 2 * HD), BF16),
-            pltpu.VMEM((kv_dev, 2 * total, 2 * HD), BF16),
-            pltpu.VMEM((total, 2 * kv_dev * HD), F32),
+            pltpu.VMEM((kv_dev * per_kv // 2, n_req * tok, 2 * HD), BF16),
+            pltpu.VMEM((n_req, pool_rows, 2 * head_width), F32),
+            pltpu.VMEM((total, 2 * head_width), F32),
+            pltpu.VMEM((2 * kv_dev, total, head_width), BF16),
+            pltpu.VMEM((head_width, total), BF16),
+            pltpu.VMEM((total, n_req * tok), F32),
         ],
         compiler_params=params(),
-        cost_estimate=cost(3e9, 2**22),
+        cost_estimate=cost(4e9, 2**22),
         name="attention",
     )(pages, table, sinks, cosine, sine, *pieces)
 
@@ -416,28 +387,24 @@
     contexts = refs[:n_ctx]
     weights = refs[n_ctx:-2]
     send_ref, keep_ref = refs[-2:]
-    n_req, tok, depth = contexts[0].shape
+    half = contexts[0].shape[1] // 2
     for i in range(n_ctx):
-        ctx = contexts[i][...].reshape(n_req * tok, depth)
         at = 0
         for b, count in enumerate(chunks):
-            total, row = None, 0
-            for j in range(count):
+            row = 0
+            for _ in range(count):
                 rows = weights[at].shape[0]
-                part = jnp.dot(ctx[:, row : row + rows], weights[at][...], preferred_element_type=F32)
-                total = part if total is None else total + part
+                terms = jnp.dot(weights[at][...], contexts[i][...], preferred_element_type=F32).astype(BF16)
+                keep_ref[i, b, row : row + rows, :] = terms[:, :half]
+                send_ref[i, b, row : row + rows, :] = terms[:, half:]
                 row += rows
                 at += 1
-            terms = total.astype(BF16)
-            for k in range(n_req):
-                target = send_ref if k % 2 else keep_ref
-                target[i, b, k // 2] = terms[k * tok : (k + 1) * tok, :]
 
 
 def project(contexts, blocks):
-    n_req, tok, depth = contexts[0].shape
-    cols = blocks[0][0].shape[1]
-    shape = jax.ShapeDtypeStruct((len(contexts), len(blocks), n_req // 2, tok, cols), BF16)
+    depth, tokens = contexts[0].shape
+    cols = sum(chunk.shape[0] for chunk in blocks[0])
+    shape = jax.ShapeDtypeStruct((len(contexts), len(blocks), cols, tokens // 2), BF16)
     flat = [chunk for block in blocks for chunk in block]
     work = len(contexts) * len(blocks)
     return pl.pallas_call(
@@ -446,27 +413,36 @@
         in_specs=[vmem()] * (len(contexts) + len(flat)),
         out_specs=[vmem()] * 2,
         compiler_params=params(),
-        cost_estimate=cost(work * 2 * n_req * tok * depth * cols, 2 * depth * cols * len(blocks)),
+        cost_estimate=cost(work * 2 * tokens * depth * cols, 2 * depth * cols * len(blocks)),
         name="project",
     )(*contexts, *flat)
 
 
+def fold_rows(cols):
+    return -(-cols // 32) * 16
+
+
 def pair_kernel(keep_ref, got_ref, *out_refs):
-    half = len(out_refs) // keep_ref.shape[0]
-    for i in range(keep_ref.shape[0]):
-        for k in range(half):
-            out_refs[i * half + k][...] = (
-                keep_ref[i, :, k].astype(F32) + got_ref[i, :, k].astype(F32)
-            ).astype(BF16)
+    n_ctx, blocks, cols, width = keep_ref.shape
+    rows = out_refs[0].shape[1]
+    tok = width // 2
+    low = lax.broadcasted_iota(jnp.int32, (rows, width), 1) < tok
+    for i in range(n_ctx):
+        for b in range(blocks):
+            both = keep_ref[i, b].astype(F32) + got_ref[i, b].astype(F32)
+            top = both[:rows]
+            rest = jnp.concatenate([both[rows:], jnp.zeros((2 * rows - cols, width), F32)], axis=0)
+            out_refs[2 * i][b] = jnp.where(low, top, pltpu.roll(rest, tok, 1)).astype(BF16)
+            out_refs[2 * i + 1][b] = jnp.where(low, pltpu.roll(top, tok, 1), rest).astype(BF16)
 
 
 def pair_sum(keep, got):
-    n_ctx, blocks, half, tok, cols = keep.shape
+    n_ctx, blocks, cols, width = keep.shape
     return pl.pallas_call(
         pair_kernel,
-        out_shape=[jax.ShapeDtypeStruct((blocks, tok, cols), BF16)] * (n_ctx * half),
+        out_shape=[jax.ShapeDtypeStruct((blocks, fold_rows(cols), width), BF16)] * (2 * n_ctx),
         in_specs=[vmem()] * 2,
-        out_specs=[vmem()] * (n_ctx * half),
+        out_specs=[vmem()] * (2 * n_ctx),
         compiler_params=params(),
         cost_estimate=cost(1e6, 6 * keep.size),
         name="pair_sum",
@@ -476,31 +452,30 @@
 def final_kernel(hidden_ref, *rest, places):
     parts, out_ref, scr = rest[:-2], rest[-2], rest[-1]
     own = lax.axis_index("exp")
-    cols = parts[0].shape[-1]
+    tok, width = hidden_ref.shape
+    rows = parts[0].shape[1]
+    cols = width // lax.axis_size("exp")
     for (first, second), bits in zip(zip(parts[0::2], parts[1::2]), places):
         for b, bit in enumerate(bits):
-            scr[jnp.bitwise_xor(own, bit)] = first[b].astype(F32) + second[b].astype(F32)
-    for b in range(scr.shape[0]):
-        at = slice(b * cols, (b + 1) * cols)
-        out_ref[:, at] = (hidden_ref[:, at].astype(F32) + scr[b]).astype(BF16)
+            both = first[b].astype(F32) + second[b].astype(F32)
+            row = pl.multiple_of(jnp.bitwise_xor(own, bit) * cols, 8)
+            scr[pl.ds(row, rows), :] = both
+            scr[pl.ds(row + rows, cols - rows), :] = pltpu.roll(both, tok, 1)[: cols - rows]
+    attn = scr[...].T[:tok]
+    out_ref[...] = (hidden_ref[...].astype(F32) + attn).astype(BF16)
 
 
 def finish(hidden, parts, places):
-    tok, width = hidden.shape
-    n_exp = lax.axis_size("exp")
     return pl.pallas_call(
         functools.partial(final_kernel, places=places),
         out_shape=jax.ShapeDtypeStruct(hidden.shape, BF16),
         in_specs=[vmem()] * (1 + len(parts)),
         out_specs=vmem(),
-        scratch_shapes=[pltpu.VMEM((n_exp, tok, width // n_exp), F32)],
+        scratch_shapes=[pltpu.VMEM((hidden.shape[1], parts[0].shape[2]), F32)],
         compiler_params=params(),
         cost_estimate=cost(1e6, 8 * hidden.size),
         name="finish",
     )(hidden, *parts)
-
-
-CHUNKS = 4
 
 
 def paired_plan(
@@ -513,15 +488,15 @@
     kv_heads = kv_width // HD
     slots_dev, page_size = kv_pool.shape[1:3]
     pool_rows = slots_dev * page_size
-    depth = out_weight.shape[0]
+    weight = out_weight.T
+    cols = weight.shape[0]
+    cut = fold_rows(cols)
+    far = [swap(chunk, 0, FAR_BIT) for chunk in (weight[:cut], weight[cut:])]
+    near = swap(weight, 0, NEAR_BIT)
+    both = [swap(chunk, 0, NEAR_BIT) for chunk in far]
+
     pieces = pack(queries[0], new_kv[0], kv_pool[0].reshape(pool_rows, 2 * kv_width), n_req)
     pieces = [pieces[0]] + [swap(pieces[k], k, 0) for k in range(1, n_req)]
-
-    near = swap(out_weight, 0, NEAR_BIT)
-    step = depth // CHUNKS
-    own_chunks = [out_weight[i * step : (i + 1) * step] for i in range(CHUNKS)]
-    far = [swap(chunk, 0, FAR_BIT) for chunk in own_chunks]
-    both = [swap(chunk, 0, NEAR_BIT) for chunk in far]
 
     position = cached_pages[0] * page_size + jnp.arange(n_req * tok)
     frequency = THETA ** (-2.0 * jnp.arange(HD // 2).astype(F32) / HD)
@@ -538,7 +513,7 @@
     fresh = [new_kv[0]] + [swap(new_kv[0], k, 0) for k in range(1, n_req)]
     pool_out = write_pool(new_slots, cosine, sine, kv_pool[0], fresh)
 
-    early = [[out_weight], [near], far]
+    early = [[weight], [near], far]
     late = [both]
     parts = []
     send, keep = project([ctx], early)

time: 141 us -> 79.9 us (0.57)
  Pallas kernels: 64 us -> 14.7 us
  starting transfers between devices: 28.9 us -> 18.7 us
  local copies, waits for them, and re-layouts: 5.55 us -> 3.8 us
    pallas_call x1, Pallas kernels: 29.2 us -> 0.13 us  [pack(): pl.pallas_call(pack_kernel, out_shape=[jax.ShapeDtypeStruct((tok, width),...]
    ppermute x12 -> x8, starting transfers between devices: 17.5 us -> 7.3 us  [swap(): lax.ppermute(values, 'exp', [(i, i ^ exp_bits) for i in range(lax.axis_si...]
    pallas_call x3, Pallas kernels: 9.91 us -> 2.08 us  [project(): pl.pallas_call(functools.partial(project_kernel, n_ctx=len(contexts), chu...]
    pallas_call x1, Pallas kernels: 14.8 us -> 8.92 us  [attention(): pl.pallas_call(functools.partial(attention_kernel, kv_dev=kv_dev, per_kv=...]
    pallas_call x3, Pallas kernels: 5.32 us -> 0.4 us  [pair_sum(): pl.pallas_call(pair_kernel, out_shape=[jax.ShapeDtypeStruct((blocks, fold...]
    ppermute x11, waiting for transfers between devices: 11.5 us -> 13.1 us  [swap(): lax.ppermute(values, 'req', [(i, i ^ req_bits) for i in range(lax.axis_si...]
    ppermute x12 -> x8, waiting for transfers between devices: 25.7 us -> 24.5 us  [swap(): lax.ppermute(values, 'exp', [(i, i ^ exp_bits) for i in range(lax.axis_si...]
    unnamed x55 -> x20, local copies, waits for them, and re-layouts: 4.32 us -> 3.75 us
  transfers between devices with their start and end apart: 25 -> 21, of which waited for: 8 -> 9; matrix products, arithmetic and copies ran while one was open for 2% -> 1% of each run, Pallas kernels for 23% -> 16%
where the time goes in v2:
time: 79.9 us; the launch traced here: 79.7 us
  waiting for transfers between devices  40.2 us (50%)
  starting transfers between devices  18.7 us (23%)
  Pallas kernels  14.7 us (18%)
  local copies, waits for them, and re-layouts  3.8 us (5%)
  between operations  1.49 us (2%)
  other arithmetic  0.82 us (1%)
    ppermute x8, waiting for transfers between devices, swap(): lax.ppermute(values, 'exp', [(i, i ^ exp_bits) for i in range(lax.axis_si...  24.5 us
    ppermute x11, waiting for transfers between devices, swap(): lax.ppermute(values, 'req', [(i, i ^ req_bits) for i in range(lax.axis_si...  13.1 us
    pallas_call x1, Pallas kernels, attention(): pl.pallas_call(functools.partial(attention_kernel, kv_dev=kv_dev, per_kv=...  8.92 us
    ppermute x11, starting transfers between devices, swap(): lax.ppermute(values, 'req', [(i, i ^ req_bits) for i in range(lax.axis_si...  8.88 us
    ppermute x8, starting transfers between devices, swap(): lax.ppermute(values, 'exp', [(i, i ^ exp_bits) for i in range(lax.axis_si...  7.3 us
    unnamed x20, local copies, waits for them, and re-layouts  3.75 us
    ppermute x2, waiting for transfers between devices, swap(): return lax.ppermute(values, ('req', 'exp'), pairs)  2.64 us
    ppermute x2, starting transfers between devices, swap(): return lax.ppermute(values, ('req', 'exp'), pairs)  2.5 us
  transfers between devices with their start and end apart: 21, of which 9 were waited for; matrix products, arithmetic and copies ran while one was open for 1% of the time, Pallas kernels for 16%

profile of v2, /device:TPU:0, one launch (start us, length us, event | category | flops | bytes accessed | tf_op | source)
XLA Modules:
  0.0 79.7 jit_solution(2594747150653240438)
XLA Ops:
  0.7 1.0 %copy-done.1 = bf16[1,8,16,1024]{3,2,1,0:T(8,128)(2,1)S(1)} copy-done((bf16[1,8,16,1024]{3,2,1,0:T(8,128)(2,1)S(1)}, bf16[1,8,16,1024]{3,2,1,0:T(8,128)(2,1)}, u32[]{:S(2)}) %copy-start.1) | copy-done | bytes 262168
  1.7 0.9 %copy-done.3 = bf16[1,64,1024]{2,1,0:T(8,128)(2,1)S(1)} copy-done((bf16[1,64,1024]{2,1,0:T(8,128)(2,1)S(1)}, bf16[1,64,1024]{2,1,0:T(8,128)(2,1)}, u32[]{:S(2)}) %copy-start.3) | copy-done | bytes 131096
  2.6 1.0 %copy-done.5 = bf16[1,64,4096]{2,1,0:T(8,128)(2,1)S(1)} copy-done((bf16[1,64,4096]{2,1,0:T(8,128)(2,1)S(1)}, bf16[1,64,4096]{2,1,0:T(8,128)(2,1)}, u32[]{:S(2)}) %copy-start.5) | copy-done | bytes 524312
  4.3 2.6 %collective-permute-start.1 = (bf16[64,1792]{1,0:T(8,128)(2,1)S(1)}, bf16[64,1792]{1,0:T(8,128)(2,1)S(1)}, u32[]{:S(2)}, u32[]{:S(2)}) collective-permute-start(bf16[64,1792]{1,0:T(8,128)(2,1)S(1)} %get-tuple-element.22), channel_id=1, source_target_pairs={{0,16},{8,24},{16,0},{24,8},{1,17},{9,25},{17,1},{25,9},{2,18},{10... | collective-permute-start | bytes 688136 | tf_op jit(solution)/shard_map/ppermute | solution.py:196
  6.9 1.7 %collective-permute-start.3 = (bf16[360,1024]{1,0:T(8,128)(2,1)S(1)}, bf16[360,1024]{1,0:T(8,128)(2,1)S(1)}, u32[]{:S(2)}, u32[]{:S(2)}) collective-permute-start(bf16[360,1024]{1,0:T(8,128)(2,1)S(1)} %bitcast.9), channel_id=1, source_target_pairs={{0,1},{1,0},{2,3},{3,2},{4,5},{5,4},{6,7},{7,6},{8,9},{9,8},{10,11... | collective-permute-start | bytes 2211848 | tf_op jit(solution)/shard_map/ppermute | solution.py:198
  8.7 2.7 %collective-permute-start.4 = (bf16[192,1024]{1,0:T(8,128)(2,1)S(1)}, bf16[192,1024]{1,0:T(8,128)(2,1)S(1)}, u32[]{:S(2)}, u32[]{:S(2)}) collective-permute-start(bf16[192,1024]{1,0:T(8,128)(2,1)S(1)} %slice.8), channel_id=1, source_target_pairs={{0,4},{1,5},{2,6},{3,7},{4,0},{5,1},{6,2},{7,3},{8,12},{9,13},{10,... | collective-permute-start | bytes 1179656 | tf_op jit(solution)/shard_map/ppermute | solution.py:198
  13.3 4.4 %collective-permute-done.2.rest_3_ = bf16[64,1792]{1,0:T(8,128)(2,1)S(1)} collective-permute-done((bf16[64,1792]{1,0:T(8,128)(2,1)S(1)}, bf16[64,1792]{1,0:T(8,128)(2,1)S(1)}, u32[]{:S(2)}, u32[]{:S(2)}) %collective-permute-start.2) | collective-permute-done | bytes 229408 | tf_op jit(solution)/shard_map/ppermute | solution.py:196
  17.7 0.7 copy-done.8
  18.4 8.9 %attention.1.refs_0_ = bf16[1024,256]{1,0:T(8,128)(2,1)S(1)} custom-call(s32[1]{0:T(128)S(6)} %copy.12.pages_ref, s32[1,16]{1,0:T(1,128)S(1)} %copy-done.8, f32[64]{0:T(128)S(1)} %copy-done.9, f32[256,128]{1,0:T(8,128)S(1)} %get-tuple-element.41.cos_ref, f32[256,128]{1,0:T(8,128)S(1)} %get-tuple-element.42.sin_ref, ...), custom_call_target="tpu_custom_call" | custom-call | flops 4000000000 | bytes 4194304 | tf_op jit(solution)/shard_map/attention/pallas_call | solution.py:330
  27.3 1.7 %collective-permute-start.8 = (bf16[1024,256]{1,0:T(8,128)(2,1)S(1)}, bf16[1024,256]{1,0:T(8,128)(2,1)S(1)}, u32[]{:S(2)}, u32[]{:S(2)}) collective-permute-start(bf16[1024,256]{1,0:T(8,128)(2,1)S(1)} %attention.1.refs_0_), channel_id=1, source_target_pairs={{0,2},{1,3},{2,0},{3,1},{4,6},{5,7},{6,4},{7,5},{8,10},{9,11},{10,... | collective-permute-start | bytes 1572872 | tf_op jit(solution)/shard_map/ppermute | solution.py:198
  29.0 8.5 %collective-permute-done.4.refs_3_ = bf16[192,1024]{1,0:T(8,128)(2,1)S(1)} collective-permute-done((bf16[192,1024]{1,0:T(8,128)(2,1)S(1)}, bf16[192,1024]{1,0:T(8,128)(2,1)S(1)}, u32[]{:S(2)}, u32[]{:S(2)}) %collective-permute-start.4) | collective-permute-done | bytes 393248 | tf_op jit(solution)/shard_map/ppermute | solution.py:198
  37.8 6.2 %collective-permute-done.5.refs_4_ = bf16[168,1024]{1,0:T(8,128)(2,1)S(1)} collective-permute-done((bf16[168,1024]{1,0:T(8,128)(2,1)S(1)}, bf16[168,1024]{1,0:T(8,128)(2,1)S(1)}, u32[]{:S(2)}, u32[]{:S(2)}) %collective-permute-start.5) | collective-permute-done | bytes 344096 | tf_op jit(solution)/shard_map/ppermute | solution.py:198
  44.5 0.8 project.3
  45.3 9.8 %collective-permute-done.8.refs_0_.refs_1_ = bf16[1024,256]{1,0:T(8,128)(2,1)S(1)} collective-permute-done((bf16[1024,256]{1,0:T(8,128)(2,1)S(1)}, bf16[1024,256]{1,0:T(8,128)(2,1)S(1)}, u32[]{:S(2)}, u32[]{:S(2)}) %collective-permute-start.8) | collective-permute-done | bytes 524320 | tf_op jit(solution)/shard_map/ppermute | solution.py:198
  55.1 0.8 project.4
  56.0 0.6 project.5
  57.2 1.5 %collective-permute-start.19 = (bf16[64,1024]{1,0:T(8,128)(2,1)S(1)}, bf16[64,1024]{1,0:T(8,128)(2,1)S(1)}, u32[]{:S(2)}, u32[]{:S(2)}) collective-permute-start(bf16[64,1024]{1,0:T(8,128)(2,1)S(1)} %bitcast.18), channel_id=1, source_target_pairs={{0,16},{8,24},{16,0},{24,8},{1,17},{9,25},{17,1},{25,9},{2,18},{10... | collective-permute-start | bytes 393224 | tf_op jit(solution)/shard_map/ppermute | solution.py:196
  59.2 1.6 %collective-permute-start.7 = (bf16[3,192,128]{2,1,0:T(8,128)(2,1)S(1)}, bf16[3,192,128]{2,1,0:T(8,128)(2,1)S(1)}, u32[]{:S(2)}, u32[]{:S(2)}) collective-permute-start(bf16[3,192,128]{2,1,0:T(8,128)(2,1)S(1)} %get-tuple-element.27), channel_id=1, source_target_pairs={{0,16},{8,24},{16,0},{24,8},{1,17},{9,25},{17,1},{25,9},{2,18},{10... | collective-permute-start | bytes 442376 | tf_op jit(solution)/shard_map/ppermute | solution.py:196
  61.0 1.9 %collective-permute-start.11 = (bf16[3,192,128]{2,1,0:T(8,128)(2,1)S(1)}, bf16[3,192,128]{2,1,0:T(8,128)(2,1)S(1)}, u32[]{:S(2)}, u32[]{:S(2)}) collective-permute-start(bf16[3,192,128]{2,1,0:T(8,128)(2,1)S(1)} %get-tuple-element.31), channel_id=1, source_target_pairs={{0,18},{1,19},{2,16},{3,17},{4,22},{5,23},{6,20},{7,21},{8,26},{9,... | collective-permute-start | bytes 442376 | tf_op jit(solution)/shard_map/ppermute | solution.py:203
  63.5 1.5 %collective-permute-start.15 = (bf16[1,192,128]{2,1,0:T(8,128)(2,1)S(1)}, bf16[1,192,128]{2,1,0:T(8,128)(2,1)S(1)}, u32[]{:S(2)}, u32[]{:S(2)}) collective-permute-start(bf16[1,192,128]{2,1,0:T(8,128)(2,1)S(1)} %get-tuple-element.35), channel_id=1, source_target_pairs={{0,16},{8,24},{16,0},{24,8},{1,17},{9,25},{17,1},{25,9},{2,18},{10... | collective-permute-start | bytes 147464 | tf_op jit(solution)/shard_map/ppermute | solution.py:196
  65.4 7.8 %collective-permute-done.15.rest_5_ = bf16[1,192,128]{2,1,0:T(8,128)(2,1)S(1)} collective-permute-done((bf16[1,192,128]{2,1,0:T(8,128)(2,1)S(1)}, bf16[1,192,128]{2,1,0:T(8,128)(2,1)S(1)}, u32[]{:S(2)}, u32[]{:S(2)}) %collective-permute-start.15) | collective-permute-done | bytes 49184 | tf_op jit(solution)/shard_map/ppermute | solution.py:196
  73.9 1.7 %write_pool.1 = bf16[8,16,1024]{2,1,0:T(8,128)(2,1)} custom-call(s32[1,16]{1,0:T(1,128)S(1)} %copy-done.7, f32[256,128]{1,0:T(8,128)S(1)} %get-tuple-element.41.cos_ref, f32[256,128]{1,0:T(8,128)S(1)} %get-tuple-element.42.sin_ref, bf16[8,16,1024]{2,1,0:T(8,128)(2,1)S(1)} %bitcast.15, bf16[64,1024]{1,0:T(8,128)(2,1)S(1)} %bitcast.20, ...), custom_call_target="tpu_custom_call" | custom-call | flops 100000000 | bytes 2097152 | tf_op jit(solution)/shard_map/write_pool/pallas_call | solution.py:374
  75.6 2.6 %collective-permute-done.17.rest_7_ = bf16[1,192,128]{2,1,0:T(8,128)(2,1)S(1)} collective-permute-done((bf16[1,192,128]{2,1,0:T(8,128)(2,1)S(1)}, bf16[1,192,128]{2,1,0:T(8,128)(2,1)S(1)}, u32[]{:S(2)}, u32[]{:S(2)}) %collective-permute-start.17) | collective-permute-done | bytes 49184 | tf_op jit(solution)/shard_map/ppermute | solution.py:203
  78.2 1.5 %finish.1 = bf16[64,2880]{1,0:T(8,128)(2,1)} custom-call(bf16[64,2880]{1,0:T(8,128)(2,1)S(1)} %bitcast.22, bf16[3,192,128]{2,1,0:T(8,128)(2,1)S(1)} %get-tuple-element.26.rest_0_, bf16[3,192,128]{2,1,0:T(8,128)(2,1)S(1)} %collective-permute-done.7.rest_1_, bf16[3,192,128]{2,1,0:T(8,128)(2,1)S(1)} %collective-permute-done.10.rest_2_, ...), custom_call_target="tpu_custom_call" | custom-call | flops 1000000 | bytes 1474560 | tf_op jit(solution)/shard_map/finish/pallas_call | solution.py:469
  (54 shorter events, 5.9 us)
Async XLA Ops:
  0.6 6.3 %copy-start = (bf16[1024,360]{0,1:T(8,128)(2,1)S(1)}, bf16[1024,360]{0,1:T(8,128)(2,1)}, u32[]{:S(2)}) copy-start(bf16[1024,360]{0,1:T(8,128)(2,1)} %param.17) | copy-start | bytes 2211844
  3.7 9.1 %collective-permute-start = (bf16[64,1792]{1,0:T(8,128)(2,1)S(1)}, bf16[64,1792]{1,0:T(8,128)(2,1)S(1)}, u32[]{:S(2)}, u32[]{:S(2)}) collective-permute-start(bf16[64,1792]{1,0:T(8,128)(2,1)S(1)} %get-tuple-element.21), channel_id=1, source_target_pairs={{0,8},{8,0},{16,24},{24,16},{1,9},{9,1},{17,25},{25,17},{2,10},{10... | collective-permute-start | bytes 688136 | tf_op jit(solution)/shard_map/ppermute | solution.py:196
  4.3 9.1 %collective-permute-start.1 = (bf16[64,1792]{1,0:T(8,128)(2,1)S(1)}, bf16[64,1792]{1,0:T(8,128)(2,1)S(1)}, u32[]{:S(2)}, u32[]{:S(2)}) collective-permute-start(bf16[64,1792]{1,0:T(8,128)(2,1)S(1)} %get-tuple-element.22), channel_id=1, source_target_pairs={{0,16},{8,24},{16,0},{24,8},{1,17},{9,25},{17,1},{25,9},{2,18},{10... | collective-permute-start | bytes 688136 | tf_op jit(solution)/shard_map/ppermute | solution.py:196
  6.9 10.8 %collective-permute-start.2 = (bf16[64,1792]{1,0:T(8,128)(2,1)S(1)}, bf16[64,1792]{1,0:T(8,128)(2,1)S(1)}, u32[]{:S(2)}, u32[]{:S(2)}) collective-permute-start(bf16[64,1792]{1,0:T(8,128)(2,1)S(1)} %get-tuple-element.23), channel_id=1, source_target_pairs={{0,24},{8,16},{16,8},{24,0},{1,25},{9,17},{17,9},{25,1},{2,26},{10... | collective-permute-start | bytes 688136 | tf_op jit(solution)/shard_map/ppermute | solution.py:196
  6.9 37.5 %collective-permute-start.3 = (bf16[360,1024]{1,0:T(8,128)(2,1)S(1)}, bf16[360,1024]{1,0:T(8,128)(2,1)S(1)}, u32[]{:S(2)}, u32[]{:S(2)}) collective-permute-start(bf16[360,1024]{1,0:T(8,128)(2,1)S(1)} %bitcast.9), channel_id=1, source_target_pairs={{0,1},{1,0},{2,3},{3,2},{4,5},{5,4},{6,7},{7,6},{8,9},{9,8},{10,11... | collective-permute-start | bytes 2211848 | tf_op jit(solution)/shard_map/ppermute | solution.py:198
  8.7 28.8 %collective-permute-start.4 = (bf16[192,1024]{1,0:T(8,128)(2,1)S(1)}, bf16[192,1024]{1,0:T(8,128)(2,1)S(1)}, u32[]{:S(2)}, u32[]{:S(2)}) collective-permute-start(bf16[192,1024]{1,0:T(8,128)(2,1)S(1)} %slice.8), channel_id=1, source_target_pairs={{0,4},{1,5},{2,6},{3,7},{4,0},{5,1},{6,2},{7,3},{8,12},{9,13},{10,... | collective-permute-start | bytes 1179656 | tf_op jit(solution)/shard_map/ppermute | solution.py:198
  12.8 31.1 %collective-permute-start.5 = (bf16[168,1024]{1,0:T(8,128)(2,1)S(1)}, bf16[168,1024]{1,0:T(8,128)(2,1)S(1)}, u32[]{:S(2)}, u32[]{:S(2)}) collective-permute-start(bf16[168,1024]{1,0:T(8,128)(2,1)S(1)} %slice.9), channel_id=1, source_target_pairs={{0,4},{1,5},{2,6},{3,7},{4,0},{5,1},{6,2},{7,3},{8,12},{9,13},{10,... | collective-permute-start | bytes 1032200 | tf_op jit(solution)/shard_map/ppermute | solution.py:198
  27.3 27.8 %collective-permute-start.8 = (bf16[1024,256]{1,0:T(8,128)(2,1)S(1)}, bf16[1024,256]{1,0:T(8,128)(2,1)S(1)}, u32[]{:S(2)}, u32[]{:S(2)}) collective-permute-start(bf16[1024,256]{1,0:T(8,128)(2,1)S(1)} %attention.1.refs_0_), channel_id=1, source_target_pairs={{0,2},{1,3},{2,0},{3,1},{4,6},{5,7},{6,4},{7,5},{8,10},{9,11},{10,... | collective-permute-start | bytes 1572872 | tf_op jit(solution)/shard_map/ppermute | solution.py:198
  37.5 18.5 %collective-permute-start.12 = (bf16[192,1024]{1,0:T(8,128)(2,1)S(1)}, bf16[192,1024]{1,0:T(8,128)(2,1)S(1)}, u32[]{:S(2)}, u32[]{:S(2)}) collective-permute-start(bf16[192,1024]{1,0:T(8,128)(2,1)S(1)} %collective-permute-done.4.refs_3_), channel_id=1, source_target_pairs={{0,1},{1,0},{2,3},{3,2},{4,5},{5,4},{6,7},{7,6},{8,9},{9,8},{10,11... | collective-permute-start | bytes 1179656 | tf_op jit(solution)/shard_map/ppermute | solution.py:198
  44.0 12.0 %collective-permute-start.13 = (bf16[168,1024]{1,0:T(8,128)(2,1)S(1)}, bf16[168,1024]{1,0:T(8,128)(2,1)S(1)}, u32[]{:S(2)}, u32[]{:S(2)}) collective-permute-start(bf16[168,1024]{1,0:T(8,128)(2,1)S(1)} %collective-permute-done.5.refs_4_), channel_id=1, source_target_pairs={{0,1},{1,0},{2,3},{3,2},{4,5},{5,4},{6,7},{7,6},{8,9},{9,8},{10,11... | collective-permute-start | bytes 1032200 | tf_op jit(solution)/shard_map/ppermute | solution.py:198
  45.2 13.5 %collective-permute-start.6 = (bf16[1,3,360,128]{3,2,1,0:T(8,128)(2,1)S(1)}, bf16[1,3,360,128]{3,2,1,0:T(8,128)(2,1)S(1)}, u32[]{:S(2)}, u32[]{:S(2)}) collective-permute-start(bf16[1,3,360,128]{3,2,1,0:T(8,128)(2,1)S(1)} %get-tuple-element.25), channel_id=1, source_target_pairs={{0,8},{8,0},{16,24},{24,16},{1,9},{9,1},{17,25},{25,17},{2,10},{10... | collective-permute-start | bytes 829448 | tf_op jit(solution)/shard_map/ppermute | solution.py:196
  55.9 3.3 %collective-permute-start.9 = (bf16[1,3,360,128]{3,2,1,0:T(8,128)(2,1)S(1)}, bf16[1,3,360,128]{3,2,1,0:T(8,128)(2,1)S(1)}, u32[]{:S(2)}, u32[]{:S(2)}) collective-permute-start(bf16[1,3,360,128]{3,2,1,0:T(8,128)(2,1)S(1)} %get-tuple-element.29), channel_id=1, source_target_pairs={{0,8},{8,0},{16,24},{24,16},{1,9},{9,1},{17,25},{25,17},{2,10},{10... | collective-permute-start | bytes 829448 | tf_op jit(solution)/shard_map/ppermute | solution.py:196
  56.6 4.4 %collective-permute-start.14 = (bf16[2,1,360,128]{3,2,1,0:T(8,128)(2,1)S(1)}, bf16[2,1,360,128]{3,2,1,0:T(8,128)(2,1)S(1)}, u32[]{:S(2)}, u32[]{:S(2)}) collective-permute-start(bf16[2,1,360,128]{3,2,1,0:T(8,128)(2,1)S(1)} %get-tuple-element.33), channel_id=1, source_target_pairs={{0,8},{8,0},{16,24},{24,16},{1,9},{9,1},{17,25},{25,17},{2,10},{10... | collective-permute-start | bytes 552968 | tf_op jit(solution)/shard_map/ppermute | solution.py:196
  57.1 3.8 %collective-permute-start.18 = (bf16[64,1024]{1,0:T(8,128)(2,1)S(1)}, bf16[64,1024]{1,0:T(8,128)(2,1)S(1)}, u32[]{:S(2)}, u32[]{:S(2)}) collective-permute-start(bf16[64,1024]{1,0:T(8,128)(2,1)S(1)} %bitcast.17), channel_id=1, source_target_pairs={{0,8},{8,0},{16,24},{24,16},{1,9},{9,1},{17,25},{25,17},{2,10},{10... | collective-permute-start | bytes 393224 | tf_op jit(solution)/shard_map/ppermute | solution.py:196
  57.2 6.3 %collective-permute-start.19 = (bf16[64,1024]{1,0:T(8,128)(2,1)S(1)}, bf16[64,1024]{1,0:T(8,128)(2,1)S(1)}, u32[]{:S(2)}, u32[]{:S(2)}) collective-permute-start(bf16[64,1024]{1,0:T(8,128)(2,1)S(1)} %bitcast.18), channel_id=1, source_target_pairs={{0,16},{8,24},{16,0},{24,8},{1,17},{9,25},{17,1},{25,9},{2,18},{10... | collective-permute-start | bytes 393224 | tf_op jit(solution)/shard_map/ppermute | solution.py:196
  58.7 6.7 %collective-permute-start.20 = (bf16[64,1024]{1,0:T(8,128)(2,1)S(1)}, bf16[64,1024]{1,0:T(8,128)(2,1)S(1)}, u32[]{:S(2)}, u32[]{:S(2)}) collective-permute-start(bf16[64,1024]{1,0:T(8,128)(2,1)S(1)} %bitcast.19), channel_id=1, source_target_pairs={{0,24},{8,16},{16,8},{24,0},{1,25},{9,17},{17,9},{25,1},{2,26},{10... | collective-permute-start | bytes 393224 | tf_op jit(solution)/shard_map/ppermute | solution.py:196
  59.2 19.1 %collective-permute-start.7 = (bf16[3,192,128]{2,1,0:T(8,128)(2,1)S(1)}, bf16[3,192,128]{2,1,0:T(8,128)(2,1)S(1)}, u32[]{:S(2)}, u32[]{:S(2)}) collective-permute-start(bf16[3,192,128]{2,1,0:T(8,128)(2,1)S(1)} %get-tuple-element.27), channel_id=1, source_target_pairs={{0,16},{8,24},{16,0},{24,8},{1,17},{9,25},{17,1},{25,9},{2,18},{10... | collective-permute-start | bytes 442376 | tf_op jit(solution)/shard_map/ppermute | solution.py:196
  60.9 12.9 %copy-start.2 = (bf16[1,8,16,1024]{3,2,1,0:T(8,128)(2,1)S(1)}, bf16[1,8,16,1024]{3,2,1,0:T(8,128)(2,1)}, u32[]{:S(2)}) copy-start(bf16[1,8,16,1024]{3,2,1,0:T(8,128)(2,1)} %param.12) | copy-start | bytes 786436
  60.9 17.3 %collective-permute-start.10 = (bf16[3,192,128]{2,1,0:T(8,128)(2,1)S(1)}, bf16[3,192,128]{2,1,0:T(8,128)(2,1)S(1)}, u32[]{:S(2)}, u32[]{:S(2)}) collective-permute-start(bf16[3,192,128]{2,1,0:T(8,128)(2,1)S(1)} %get-tuple-element.30), channel_id=1, source_target_pairs={{0,2},{1,3},{2,0},{3,1},{4,6},{5,7},{6,4},{7,5},{8,10},{9,11},{10,... | collective-permute-start | bytes 442376 | tf_op jit(solution)/shard_map/ppermute | solution.py:198
  61.0 17.2 %collective-permute-start.11 = (bf16[3,192,128]{2,1,0:T(8,128)(2,1)S(1)}, bf16[3,192,128]{2,1,0:T(8,128)(2,1)S(1)}, u32[]{:S(2)}, u32[]{:S(2)}) collective-permute-start(bf16[3,192,128]{2,1,0:T(8,128)(2,1)S(1)} %get-tuple-element.31), channel_id=1, source_target_pairs={{0,18},{1,19},{2,16},{3,17},{4,22},{5,23},{6,20},{7,21},{8,26},{9,... | collective-permute-start | bytes 442376 | tf_op jit(solution)/shard_map/ppermute | solution.py:203
  63.5 9.7 %collective-permute-start.15 = (bf16[1,192,128]{2,1,0:T(8,128)(2,1)S(1)}, bf16[1,192,128]{2,1,0:T(8,128)(2,1)S(1)}, u32[]{:S(2)}, u32[]{:S(2)}) collective-permute-start(bf16[1,192,128]{2,1,0:T(8,128)(2,1)S(1)} %get-tuple-element.35), channel_id=1, source_target_pairs={{0,16},{8,24},{16,0},{24,8},{1,17},{9,25},{17,1},{25,9},{2,18},{10... | collective-permute-start | bytes 147464 | tf_op jit(solution)/shard_map/ppermute | solution.py:196
  65.4 10.2 %collective-permute-start.16 = (bf16[1,192,128]{2,1,0:T(8,128)(2,1)S(1)}, bf16[1,192,128]{2,1,0:T(8,128)(2,1)S(1)}, u32[]{:S(2)}, u32[]{:S(2)}) collective-permute-start(bf16[1,192,128]{2,1,0:T(8,128)(2,1)S(1)} %get-tuple-element.36), channel_id=1, source_target_pairs={{0,2},{1,3},{2,0},{3,1},{4,6},{5,7},{6,4},{7,5},{8,10},{9,11},{10,... | collective-permute-start | bytes 147464 | tf_op jit(solution)/shard_map/ppermute | solution.py:198
  73.2 5.0 %collective-permute-start.17 = (bf16[1,192,128]{2,1,0:T(8,128)(2,1)S(1)}, bf16[1,192,128]{2,1,0:T(8,128)(2,1)S(1)}, u32[]{:S(2)}, u32[]{:S(2)}) collective-permute-start(bf16[1,192,128]{2,1,0:T(8,128)(2,1)S(1)} %get-tuple-element.37), channel_id=1, source_target_pairs={{0,18},{1,19},{2,16},{3,17},{4,22},{5,23},{6,20},{7,21},{8,26},{9,... | collective-permute-start | bytes 147464 | tf_op jit(solution)/shard_map/ppermute | solution.py:203
  73.9 4.3 %copy-start.6 = (bf16[1,64,2880]{2,1,0:T(8,128)(2,1)S(1)}, bf16[1,64,2880]{2,1,0:T(8,128)(2,1)}, u32[]{:S(2)}) copy-start(bf16[1,64,2880]{2,1,0:T(8,128)(2,1)} %param.9) | copy-start | bytes 1105924
  (7 other events, 6.2 us)

commit v3 on v2

--- a/solution.py
+++ b/solution.py
@@ -171,7 +171,8 @@
 F32 = jnp.float32
 BF16 = jnp.bfloat16
 
-PAIR_BIT, NEAR_BIT, FAR_BIT = 2, 1, 4
+PAIR_BIT, NEAR_BIT, FAR_BIT = 2, 1, 6
+OUTER, INNER = (0, 1, 6, 7), (2, 3, 4, 5)
 ORDER = (0, 2, 1, 3)
 
 
@@ -191,11 +192,12 @@
     return pl.CostEstimate(flops=int(flops), bytes_accessed=int(nbytes), transcendentals=0)
 
 
-def swap(values, req_bits, exp_bits):
+def swap(values, req_bits, exp_bits, among=None):
     if not exp_bits:
         return lax.ppermute(values, "req", [(i, i ^ req_bits) for i in range(lax.axis_size("req"))])
     if not req_bits:
-        return lax.ppermute(values, "exp", [(i, i ^ exp_bits) for i in range(lax.axis_size("exp"))])
+        among = range(lax.axis_size("exp")) if among is None else among
+        return lax.ppermute(values, "exp", [(i, i ^ exp_bits) for i in among])
     rows, cols = lax.axis_size("req"), lax.axis_size("exp")
     pairs = [
         (i * cols + j, (i ^ req_bits) * cols + (j ^ exp_bits)) for i in range(rows) for j in range(cols)
@@ -203,35 +205,53 @@
     return lax.ppermute(values, ("req", "exp"), pairs)
 
 
-def pack_kernel(q_ref, kv_ref, pool_ref, *outs):
+def pack_kernel(q_ref, kv_ref, pool_ref, *rest):
+    outs, sems = rest[:-1], rest[-1]
     n_req = len(outs)
     own = lax.axis_index("req")
     tok = q_ref.shape[0]
     q_width = q_ref.shape[1] // n_req
     kv_width = kv_ref.shape[1] // 2
     head_width = kv_width // n_req
-    for k, out in enumerate(outs):
+    copies = []
+
+    def copy(source, target):
+        copies.append(pltpu.make_async_copy(source, target, sems.at[len(copies)]))
+        copies[-1].start()
+
+    for k in (3, 2, 1, 0):
+        out = outs[k]
         dest = jnp.bitwise_xor(own, k)
-        out[:, :q_width] = q_ref[:, pl.ds(pl.multiple_of(dest * q_width, 128), q_width)]
+        col = pl.multiple_of(dest * q_width, 128)
+        copy(q_ref.at[:, pl.ds(col, q_width)], out.at[:, pl.ds(0, q_width)])
         at = q_width
         blocks = [(kv_ref, 0)]
         blocks += [(pool_ref, i * tok) for i in range(pool_ref.shape[0] // tok)]
         for block, row in blocks:
             for half in range(2):
                 col = pl.multiple_of(half * kv_width + dest * head_width, 128)
-                out[:, at : at + head_width] = block[row : row + tok, pl.ds(col, head_width)]
+                copy(
+                    block.at[pl.ds(row, tok), pl.ds(col, head_width)],
+                    out.at[:, pl.ds(at, head_width)],
+                )
                 at += head_width
+        if k == 1:
+            copy(kv_ref, out.at[:, pl.ds(at, 2 * kv_width)])
+    for one in copies:
+        one.wait()
 
 
 def pack(q, kv, pool, n_req):
     tok = q.shape[0]
     blocks = 1 + pool.shape[0] // tok
     width = (q.shape[1] + blocks * kv.shape[1]) // n_req
+    widths = [width + (kv.shape[1] if k == 1 else 0) for k in range(n_req)]
     return pl.pallas_call(
         pack_kernel,
-        out_shape=[jax.ShapeDtypeStruct((tok, width), BF16)] * n_req,
-        in_specs=[vmem()] * 3,
+        out_shape=[jax.ShapeDtypeStruct((tok, w), BF16) for w in widths],
+        in_specs=[pl.BlockSpec(memory_space=pltpu.MemorySpace.HBM)] * 3,
         out_specs=[vmem()] * n_req,
+        scratch_shapes=[pltpu.SemaphoreType.DMA((n_req * (1 + 2 * blocks) + 1,))],
         compiler_params=params(),
         cost_estimate=cost(0, 4 * tok * width * n_req),
         name="pack",
@@ -347,11 +367,12 @@
 
 
 def pool_kernel(slots_ref, cos_ref, sin_ref, pool_ref, *rest, page_size):
-    pieces, out_ref, fresh_scr = rest[:-2], rest[-2], rest[-1]
+    pairs, out_ref, fresh_scr = rest[:-2], rest[-2], rest[-1]
     own = lax.axis_index("req")
-    tok = pieces[0].shape[0]
-    kv_width = pieces[0].shape[1] // 2
-    for k, piece in enumerate(pieces):
+    tok = pairs[0].shape[0] // 2
+    kv_width = pairs[0].shape[1] // 2
+    for k in range(2 * len(pairs)):
+        piece = pairs[k // 2][k % 2 * tok : (k % 2 + 1) * tok, :]
         row = pl.multiple_of(jnp.bitwise_xor(own, k) * tok, tok)
         cosine = cos_ref[pl.ds(row, tok), :]
         sine = sin_ref[pl.ds(row, tok), :]
@@ -369,46 +390,48 @@
             out_ref[slot % slots_dev] = fresh_scr[n * page_size : (n + 1) * page_size, :]
 
 
-def write_pool(slots, cosine, sine, pool, pieces):
-    tok, width = pieces[0].shape
+def write_pool(slots, cosine, sine, pool, pairs):
+    rows, width = pairs[0].shape
     return pl.pallas_call(
         functools.partial(pool_kernel, page_size=pool.shape[1]),
         out_shape=jax.ShapeDtypeStruct(pool.shape, BF16),
-        in_specs=[smem()] + [vmem()] * (3 + len(pieces)),
+        in_specs=[smem()] + [vmem()] * (3 + len(pairs)),
         out_specs=vmem(),
-        scratch_shapes=[pltpu.VMEM((tok * len(pieces), width), BF16)],
+        scratch_shapes=[pltpu.VMEM((rows * len(pairs), width), BF16)],
         compiler_params=params(),
         cost_estimate=cost(1e8, 2**21),
         name="write_pool",
-    )(slots, cosine, sine, pool, *pieces)
-
-
-def project_kernel(*refs, n_ctx, chunks):
+    )(slots, cosine, sine, pool, *pairs)
+
+
+def project_kernel(*refs, n_ctx, counts):
     contexts = refs[:n_ctx]
     weights = refs[n_ctx:-2]
     send_ref, keep_ref = refs[-2:]
     half = contexts[0].shape[1] // 2
-    for i in range(n_ctx):
-        at = 0
-        for b, count in enumerate(chunks):
-            row = 0
-            for _ in range(count):
-                rows = weights[at].shape[0]
-                terms = jnp.dot(weights[at][...], contexts[i][...], preferred_element_type=F32).astype(BF16)
-                keep_ref[i, b, row : row + rows, :] = terms[:, :half]
-                send_ref[i, b, row : row + rows, :] = terms[:, half:]
-                row += rows
-                at += 1
+    at = 0
+    for b, count in enumerate(counts):
+        whole, pieces = weights[at], weights[at + 1 : at + count]
+        at += count
+        row = 0
+        for piece in pieces or (whole,):
+            rows = slice(row, row + piece.shape[0])
+            block = whole[rows, :] + piece[...] if pieces else whole[...]
+            for i in range(n_ctx):
+                terms = jnp.dot(block, contexts[i][...], preferred_element_type=F32).astype(BF16)
+                keep_ref[i, b, rows, :] = terms[:, :half]
+                send_ref[i, b, rows, :] = terms[:, half:]
+            row += piece.shape[0]
 
 
 def project(contexts, blocks):
     depth, tokens = contexts[0].shape
-    cols = sum(chunk.shape[0] for chunk in blocks[0])
+    cols = blocks[0][0].shape[0]
     shape = jax.ShapeDtypeStruct((len(contexts), len(blocks), cols, tokens // 2), BF16)
     flat = [chunk for block in blocks for chunk in block]
     work = len(contexts) * len(blocks)
     return pl.pallas_call(
-        functools.partial(project_kernel, n_ctx=len(contexts), chunks=tuple(len(b) for b in blocks)),
+        functools.partial(project_kernel, n_ctx=len(contexts), counts=tuple(len(b) for b in blocks)),
         out_shape=[shape, shape],
         in_specs=[vmem()] * (len(contexts) + len(flat)),
         out_specs=[vmem()] * 2,
@@ -491,12 +514,13 @@
     weight = out_weight.T
     cols = weight.shape[0]
     cut = fold_rows(cols)
-    far = [swap(chunk, 0, FAR_BIT) for chunk in (weight[:cut], weight[cut:])]
+    outer = swap(weight, 0, FAR_BIT, OUTER)
     near = swap(weight, 0, NEAR_BIT)
-    both = [swap(chunk, 0, NEAR_BIT) for chunk in far]
 
     pieces = pack(queries[0], new_kv[0], kv_pool[0].reshape(pool_rows, 2 * kv_width), n_req)
     pieces = [pieces[0]] + [swap(pieces[k], k, 0) for k in range(1, n_req)]
+    pieces, weight_late = lax.optimization_barrier((pieces, weight))
+    inner = [swap(chunk, 0, FAR_BIT, INNER) for chunk in (weight_late[:cut], weight_late[cut:])]
 
     position = cached_pages[0] * page_size + jnp.arange(n_req * tok)
     frequency = THETA ** (-2.0 * jnp.arange(HD // 2).astype(F32) / HD)
@@ -509,10 +533,16 @@
         cached_pages, page_table, sinks, cosine, sine, pieces, kv_heads // n_req,
         head_count // kv_heads, pool_rows, page_size,
     )
+    chip_rows = jnp.concatenate([new_kv[0], pieces[1][:, -2 * kv_width :]], axis=0)
+    ctx, outer, near, chip_rows = lax.optimization_barrier((ctx, outer, near, chip_rows))
     ctx_mate = swap(ctx, 0, PAIR_BIT)
-    fresh = [new_kv[0]] + [swap(new_kv[0], k, 0) for k in range(1, n_req)]
-    pool_out = write_pool(new_slots, cosine, sine, kv_pool[0], fresh)
-
+    outer_both = swap(outer, 0, NEAR_BIT, OUTER)
+    inner_both = [swap(chunk, 0, NEAR_BIT, INNER) for chunk in inner]
+    far = [outer, *inner]
+    both = [outer_both, *inner_both]
+    pool_out = write_pool(new_slots, cosine, sine, kv_pool[0], [chip_rows, swap(chip_rows, 2, 0)])
+
+    ctx, pool_out = lax.optimization_barrier((ctx, pool_out))
     early = [[weight], [near], far]
     late = [both]
     parts = []

time: 79.9 us -> 77.8 us (0.974)
  waiting for transfers between devices: 40.2 us -> 25 us
  starting transfers between devices: 18.7 us -> 31.2 us
    ppermute x8 -> x10, waiting for transfers between devices: 24.5 us -> 6.06 us  [swap(): return lax.ppermute(values, 'exp', [(i, i ^ exp_bits) for i in among])]
    ppermute x8 -> x10, starting transfers between devices: 7.3 us -> 22.5 us  [swap(): return lax.ppermute(values, 'exp', [(i, i ^ exp_bits) for i in among])]
    ppermute x11 -> x9, starting transfers between devices: 8.88 us -> 6.25 us  [swap(): lax.ppermute(values, 'req', [(i, i ^ req_bits) for i in range(lax.axis_si...]
    ppermute x11 -> x9, waiting for transfers between devices: 13.1 us -> 14.7 us  [swap(): lax.ppermute(values, 'req', [(i, i ^ req_bits) for i in range(lax.axis_si...]
    ppermute x2, waiting for transfers between devices: 2.64 us -> 4.19 us  [swap(): return lax.ppermute(values, ('req', 'exp'), pairs)]
  transfers between devices with their start and end apart: 21 -> 21, of which waited for: 9 -> 8; matrix products, arithmetic and copies ran while one was open for 1% -> 1% of each run, Pallas kernels for 16% -> 18%
where the time goes in v3:
time: 77.8 us; the launch traced here: 77.4 us
  starting transfers between devices  31.2 us (40%)
  waiting for transfers between devices  25 us (32%)
  Pallas kernels  15.1 us (19%)
  local copies, waits for them, and re-layouts  3.64 us (5%)
  between operations  1.6 us (2%)
  other arithmetic  0.84 us (1%)
    ppermute x10, starting transfers between devices, swap(): return lax.ppermute(values, 'exp', [(i, i ^ exp_bits) for i in among])  22.5 us
    ppermute x9, waiting for transfers between devices, swap(): lax.ppermute(values, 'req', [(i, i ^ req_bits) for i in range(lax.axis_si...  14.7 us
    pallas_call x1, Pallas kernels, attention(): pl.pallas_call(functools.partial(attention_kernel, kv_dev=kv_dev, per_kv=...  8.92 us
    ppermute x9, starting transfers between devices, swap(): lax.ppermute(values, 'req', [(i, i ^ req_bits) for i in range(lax.axis_si...  6.25 us
    ppermute x10, waiting for transfers between devices, swap(): return lax.ppermute(values, 'exp', [(i, i ^ exp_bits) for i in among])  6.06 us
    ppermute x2, waiting for transfers between devices, swap(): return lax.ppermute(values, ('req', 'exp'), pairs)  4.19 us
    unnamed x20, local copies, waits for them, and re-layouts  3.58 us
    ppermute x2, starting transfers between devices, swap(): return lax.ppermute(values, ('req', 'exp'), pairs)  2.47 us
  transfers between devices with their start and end apart: 21, of which 8 were waited for; matrix products, arithmetic and copies ran while one was open for 1% of the time, Pallas kernels for 18%

profile of v3, /device:TPU:0, one launch (start us, length us, event | category | flops | bytes accessed | tf_op | source)
XLA Modules:
  0.0 77.4 jit_solution(1279683278612518567)
XLA Ops:
  0.6 7.0 %collective-permute-start.3 = (bf16[360,1024]{1,0:T(8,128)(2,1)}, bf16[360,1024]{1,0:T(8,128)(2,1)S(1)}, u32[]{:S(2)}, u32[]{:S(2)}) collective-permute-start(bf16[360,1024]{1,0:T(8,128)(2,1)} %bitcast.9), channel_id=1, source_target_pairs={{0,6},{1,7},{6,0},{7,1},{8,14},{9,15},{14,8},{15,9},{16,22},{17,23... | collective-permute-start | bytes 2211848 | tf_op jit(solution)/shard_map/ppermute | solution.py:200
  7.6 1.6 %collective-permute-start.4 = (bf16[360,1024]{1,0:T(8,128)(2,1)}, bf16[360,1024]{1,0:T(8,128)(2,1)S(1)}, u32[]{:S(2)}, u32[]{:S(2)}) collective-permute-start(bf16[360,1024]{1,0:T(8,128)(2,1)} %bitcast.10), channel_id=1, source_target_pairs={{0,1},{1,0},{2,3},{3,2},{4,5},{5,4},{6,7},{7,6},{8,9},{9,8},{10,11... | collective-permute-start | bytes 2211848 | tf_op jit(solution)/shard_map/ppermute | solution.py:200
  9.2 0.9 %copy-done.1 = bf16[1,8,16,1024]{3,2,1,0:T(8,128)(2,1)S(1)} copy-done((bf16[1,8,16,1024]{3,2,1,0:T(8,128)(2,1)S(1)}, bf16[1,8,16,1024]{3,2,1,0:T(8,128)(2,1)}, u32[]{:S(2)}) %copy-start.1) | copy-done | bytes 262168
  10.1 1.0 %copy-done.3 = bf16[1,64,4096]{2,1,0:T(8,128)(2,1)S(1)} copy-done((bf16[1,64,4096]{2,1,0:T(8,128)(2,1)S(1)}, bf16[1,64,4096]{2,1,0:T(8,128)(2,1)}, u32[]{:S(2)}) %copy-start.3) | copy-done | bytes 524312
  11.1 0.9 %copy-done.4 = bf16[1,64,1024]{2,1,0:T(8,128)(2,1)S(1)} copy-done((bf16[1,64,1024]{2,1,0:T(8,128)(2,1)S(1)}, bf16[1,64,1024]{2,1,0:T(8,128)(2,1)}, u32[]{:S(2)}) %copy-start.4) | copy-done | bytes 131096
  12.7 1.6 %collective-permute-start.1 = (bf16[64,1792]{1,0:T(8,128)(2,1)S(1)}, bf16[64,1792]{1,0:T(8,128)(2,1)S(1)}, u32[]{:S(2)}, u32[]{:S(2)}) collective-permute-start(bf16[64,1792]{1,0:T(8,128)(2,1)S(1)} %get-tuple-element.33), channel_id=1, source_target_pairs={{0,16},{8,24},{16,0},{24,8},{1,17},{9,25},{17,1},{25,9},{2,18},{10... | collective-permute-start | bytes 688136 | tf_op jit(solution)/shard_map/ppermute | solution.py:197
  16.1 5.1 %collective-permute-done.1.rest_2_ = bf16[64,1792]{1,0:T(8,128)(2,1)S(1)} collective-permute-done((bf16[64,1792]{1,0:T(8,128)(2,1)S(1)}, bf16[64,1792]{1,0:T(8,128)(2,1)S(1)}, u32[]{:S(2)}, u32[]{:S(2)}) %collective-permute-start.1) | collective-permute-done | bytes 229408 | tf_op jit(solution)/shard_map/ppermute | solution.py:197
  21.2 4.0 %collective-permute-done.2.rest_3_ = bf16[64,1792]{1,0:T(8,128)(2,1)S(1)} collective-permute-done((bf16[64,1792]{1,0:T(8,128)(2,1)S(1)}, bf16[64,1792]{1,0:T(8,128)(2,1)S(1)}, u32[]{:S(2)}, u32[]{:S(2)}) %collective-permute-start.2) | collective-permute-done | bytes 229408 | tf_op jit(solution)/shard_map/ppermute | solution.py:197
  26.6 8.9 %attention.1.refs_0_ = bf16[1024,256]{1,0:T(8,128)(2,1)S(1)} custom-call(s32[1]{0:T(128)S(6)} %copy.12.pages_ref, s32[1,16]{1,0:T(1,128)S(1)} %copy-done.8, f32[64]{0:T(128)S(1)} %copy-done.9, f32[256,128]{1,0:T(8,128)S(1)} %get-tuple-element.63.cos_ref, f32[256,128]{1,0:T(8,128)S(1)} %get-tuple-element.64.sin_ref, ...), custom_call_target="tpu_custom_call" | custom-call | flops 4000000000 | bytes 4194304 | tf_op jit(solution)/shard_map/attention/pallas_call | solution.py:350
  35.6 2.6 %collective-permute-start.14 = (bf16[360,1024]{1,0:T(8,128)(2,1)S(1)}, bf16[360,1024]{1,0:T(8,128)(2,1)S(1)}, u32[]{:S(2)}, u32[]{:S(2)}) collective-permute-start(bf16[360,1024]{1,0:T(8,128)(2,1)S(1)} %collective-permute-done.3.refs_3_), channel_id=1, source_target_pairs={{0,1},{1,0},{6,7},{7,6},{8,9},{9,8},{14,15},{15,14},{16,17},{17,16... | collective-permute-start | bytes 2211848 | tf_op jit(solution)/shard_map/ppermute | solution.py:200
  39.0 1.6 %collective-permute-start.5 = (bf16[128,1024]{1,0:T(8,128)(2,1)S(1)}, bf16[128,1024]{1,0:T(8,128)(2,1)S(1)}, u32[]{:S(2)}, u32[]{:S(2)}) collective-permute-start(bf16[128,1024]{1,0:T(8,128)(2,1)S(1)} %pad_maximum_fusion.rest_0_), channel_id=1, source_target_pairs={{0,16},{8,24},{16,0},{24,8},{1,17},{9,25},{17,1},{25,9},{2,18},{10... | collective-permute-start | bytes 786440 | tf_op jit(solution)/shard_map/ppermute | solution.py:197
  42.0 5.6 %collective-permute-done.5.rest_1_ = bf16[128,1024]{1,0:T(8,128)(2,1)S(1)} collective-permute-done((bf16[128,1024]{1,0:T(8,128)(2,1)S(1)}, bf16[128,1024]{1,0:T(8,128)(2,1)S(1)}, u32[]{:S(2)}, u32[]{:S(2)}) %collective-permute-start.5) | collective-permute-done | bytes 262176 | tf_op jit(solution)/shard_map/ppermute | solution.py:197
  47.6 1.7 %write_pool.1 = bf16[8,16,1024]{2,1,0:T(8,128)(2,1)} custom-call(s32[1,16]{1,0:T(1,128)S(1)} %copy-done.7, f32[256,128]{1,0:T(8,128)S(1)} %get-tuple-element.63.cos_ref, f32[256,128]{1,0:T(8,128)S(1)} %get-tuple-element.64.sin_ref, bf16[8,16,1024]{2,1,0:T(8,128)(2,1)S(1)} %bitcast.16, bf16[128,1024]{1,0:T(8,128)(2,1)S(1)} %pad_maximum_fusion.rest_0_, ...), custom_call_target="tpu_custom_call" | custom-call | flops 100000000 | bytes 2097152 | tf_op jit(solution)/shard_map/write_pool/pallas_call | solution.py:395
  50.1 2.2 %collective-permute-done.10.refs_0_.refs_1_ = bf16[1024,256]{1,0:T(8,128)(2,1)S(1)} collective-permute-done((bf16[1024,256]{1,0:T(8,128)(2,1)S(1)}, bf16[1024,256]{1,0:T(8,128)(2,1)S(1)}, u32[]{:S(2)}, u32[]{:S(2)}) %collective-permute-start.10) | collective-permute-done | bytes 524320 | tf_op jit(solution)/shard_map/ppermute | solution.py:200
  52.4 0.8 project.4
  53.3 3.3 %collective-permute-done.14.refs_2_ = bf16[360,1024]{1,0:T(8,128)(2,1)S(1)} collective-permute-done((bf16[360,1024]{1,0:T(8,128)(2,1)S(1)}, bf16[360,1024]{1,0:T(8,128)(2,1)S(1)}, u32[]{:S(2)}, u32[]{:S(2)}) %collective-permute-start.14) | collective-permute-done | bytes 737312 | tf_op jit(solution)/shard_map/ppermute | solution.py:200
  57.4 1.6 %collective-permute-start.9 = (bf16[3,192,128]{2,1,0:T(8,128)(2,1)S(1)}, bf16[3,192,128]{2,1,0:T(8,128)(2,1)S(1)}, u32[]{:S(2)}, u32[]{:S(2)}) collective-permute-start(bf16[3,192,128]{2,1,0:T(8,128)(2,1)S(1)} %get-tuple-element.48), channel_id=1, source_target_pairs={{0,16},{8,24},{16,0},{24,8},{1,17},{9,25},{17,1},{25,9},{2,18},{10... | collective-permute-start | bytes 442376 | tf_op jit(solution)/shard_map/ppermute | solution.py:197
  59.2 6.7 %collective-permute-start.12 = (bf16[3,192,128]{2,1,0:T(8,128)(2,1)S(1)}, bf16[3,192,128]{2,1,0:T(8,128)(2,1)S(1)}, u32[]{:S(2)}, u32[]{:S(2)}) collective-permute-start(bf16[3,192,128]{2,1,0:T(8,128)(2,1)S(1)} %get-tuple-element.51), channel_id=1, source_target_pairs={{0,2},{1,3},{2,0},{3,1},{4,6},{5,7},{6,4},{7,5},{8,10},{9,11},{10,... | collective-permute-start | bytes 442376 | tf_op jit(solution)/shard_map/ppermute | solution.py:200
  66.6 0.9 %collective-permute-start.18 = (bf16[1,192,128]{2,1,0:T(8,128)(2,1)S(1)}, bf16[1,192,128]{2,1,0:T(8,128)(2,1)S(1)}, u32[]{:S(2)}, u32[]{:S(2)}) collective-permute-start(bf16[1,192,128]{2,1,0:T(8,128)(2,1)S(1)} %get-tuple-element.56), channel_id=1, source_target_pairs={{0,16},{8,24},{16,0},{24,8},{1,17},{9,25},{17,1},{25,9},{2,18},{10... | collective-permute-start | bytes 147464 | tf_op jit(solution)/shard_map/ppermute | solution.py:197
  67.6 1.9 %collective-permute-start.19 = (bf16[1,192,128]{2,1,0:T(8,128)(2,1)S(1)}, bf16[1,192,128]{2,1,0:T(8,128)(2,1)S(1)}, u32[]{:S(2)}, u32[]{:S(2)}) collective-permute-start(bf16[1,192,128]{2,1,0:T(8,128)(2,1)S(1)} %get-tuple-element.57), channel_id=1, source_target_pairs={{0,2},{1,3},{2,0},{3,1},{4,6},{5,7},{6,4},{7,5},{8,10},{9,11},{10,... | collective-permute-start | bytes 147464 | tf_op jit(solution)/shard_map/ppermute | solution.py:200
  69.5 1.8 %collective-permute-start.20 = (bf16[1,192,128]{2,1,0:T(8,128)(2,1)S(1)}, bf16[1,192,128]{2,1,0:T(8,128)(2,1)S(1)}, u32[]{:S(2)}, u32[]{:S(2)}) collective-permute-start(bf16[1,192,128]{2,1,0:T(8,128)(2,1)S(1)} %get-tuple-element.58), channel_id=1, source_target_pairs={{0,18},{1,19},{2,16},{3,17},{4,22},{5,23},{6,20},{7,21},{8,26},{9,... | collective-permute-start | bytes 147464 | tf_op jit(solution)/shard_map/ppermute | solution.py:205
  71.3 2.9 %collective-permute-done.13.rest_3_ = bf16[3,192,128]{2,1,0:T(8,128)(2,1)S(1)} collective-permute-done((bf16[3,192,128]{2,1,0:T(8,128)(2,1)S(1)}, bf16[3,192,128]{2,1,0:T(8,128)(2,1)S(1)}, u32[]{:S(2)}, u32[]{:S(2)}) %collective-permute-start.13) | collective-permute-done | bytes 147488 | tf_op jit(solution)/shard_map/ppermute | solution.py:205
  74.7 1.3 %collective-permute-done.20.rest_7_ = bf16[1,192,128]{2,1,0:T(8,128)(2,1)S(1)} collective-permute-done((bf16[1,192,128]{2,1,0:T(8,128)(2,1)S(1)}, bf16[1,192,128]{2,1,0:T(8,128)(2,1)S(1)}, u32[]{:S(2)}, u32[]{:S(2)}) %collective-permute-start.20) | collective-permute-done | bytes 49184 | tf_op jit(solution)/shard_map/ppermute | solution.py:205
  76.0 1.5 %finish.1 = bf16[64,2880]{1,0:T(8,128)(2,1)} custom-call(bf16[64,2880]{1,0:T(8,128)(2,1)S(1)} %bitcast.20, bf16[3,192,128]{2,1,0:T(8,128)(2,1)S(1)} %get-tuple-element.47.rest_0_, bf16[3,192,128]{2,1,0:T(8,128)(2,1)S(1)} %collective-permute-done.9.rest_1_, bf16[3,192,128]{2,1,0:T(8,128)(2,1)S(1)} %collective-permute-done.12.rest_2_, ...), custom_call_target="tpu_custom_call" | custom-call | flops 1000000 | bytes 1474560 | tf_op jit(solution)/shard_map/finish/pallas_call | solution.py:492
  (56 shorter events, 8.4 us)
Async XLA Ops:
  0.6 35.0 %collective-permute-start.3 = (bf16[360,1024]{1,0:T(8,128)(2,1)}, bf16[360,1024]{1,0:T(8,128)(2,1)S(1)}, u32[]{:S(2)}, u32[]{:S(2)}) collective-permute-start(bf16[360,1024]{1,0:T(8,128)(2,1)} %bitcast.9), channel_id=1, source_target_pairs={{0,6},{1,7},{6,0},{7,1},{8,14},{9,15},{14,8},{15,9},{16,22},{17,23... | collective-permute-start | bytes 2211848 | tf_op jit(solution)/shard_map/ppermute | solution.py:200
  7.6 28.0 %collective-permute-start.4 = (bf16[360,1024]{1,0:T(8,128)(2,1)}, bf16[360,1024]{1,0:T(8,128)(2,1)S(1)}, u32[]{:S(2)}, u32[]{:S(2)}) collective-permute-start(bf16[360,1024]{1,0:T(8,128)(2,1)} %bitcast.10), channel_id=1, source_target_pairs={{0,1},{1,0},{2,3},{3,2},{4,5},{5,4},{6,7},{7,6},{8,9},{9,8},{10,11... | collective-permute-start | bytes 2211848 | tf_op jit(solution)/shard_map/ppermute | solution.py:200
  12.6 12.6 %copy-start = (bf16[1024,360]{0,1:T(8,128)(2,1)S(1)}, bf16[1024,360]{0,1:T(8,128)(2,1)}, u32[]{:S(2)}) copy-start(bf16[1024,360]{0,1:T(8,128)(2,1)} %param.17) | copy-start | bytes 2211844
  12.6 12.6 %collective-permute-start = (bf16[64,2816]{1,0:T(8,128)(2,1)S(1)}, bf16[64,2816]{1,0:T(8,128)(2,1)S(1)}, u32[]{:S(2)}, u32[]{:S(2)}) collective-permute-start(bf16[64,2816]{1,0:T(8,128)(2,1)S(1)} %get-tuple-element.32), channel_id=1, source_target_pairs={{0,8},{8,0},{16,24},{24,16},{1,9},{9,1},{17,25},{25,17},{2,10},{10... | collective-permute-start | bytes 1081352 | tf_op jit(solution)/shard_map/ppermute | solution.py:197
  12.7 8.5 %collective-permute-start.1 = (bf16[64,1792]{1,0:T(8,128)(2,1)S(1)}, bf16[64,1792]{1,0:T(8,128)(2,1)S(1)}, u32[]{:S(2)}, u32[]{:S(2)}) collective-permute-start(bf16[64,1792]{1,0:T(8,128)(2,1)S(1)} %get-tuple-element.33), channel_id=1, source_target_pairs={{0,16},{8,24},{16,0},{24,8},{1,17},{9,25},{17,1},{25,9},{2,18},{10... | collective-permute-start | bytes 688136 | tf_op jit(solution)/shard_map/ppermute | solution.py:197
  14.3 10.9 %collective-permute-start.2 = (bf16[64,1792]{1,0:T(8,128)(2,1)S(1)}, bf16[64,1792]{1,0:T(8,128)(2,1)S(1)}, u32[]{:S(2)}, u32[]{:S(2)}) collective-permute-start(bf16[64,1792]{1,0:T(8,128)(2,1)S(1)} %get-tuple-element.34), channel_id=1, source_target_pairs={{0,24},{8,16},{16,8},{24,0},{1,25},{9,17},{17,9},{25,1},{2,26},{10... | collective-permute-start | bytes 688136 | tf_op jit(solution)/shard_map/ppermute | solution.py:197
  25.2 15.4 %collective-permute-start.6 = (bf16[192,1024]{1,0:T(8,128)(2,1)S(1)}, bf16[192,1024]{1,0:T(8,128)(2,1)S(1)}, u32[]{:S(2)}, u32[]{:S(2)}) collective-permute-start(bf16[192,1024]{1,0:T(8,128)(2,1)S(1)} %slice.10), channel_id=1, source_target_pairs={{2,4},{3,5},{4,2},{5,3},{10,12},{11,13},{12,10},{13,11},{18,20},{1... | collective-permute-start | bytes 1179656 | tf_op jit(solution)/shard_map/ppermute | solution.py:200
  35.6 12.0 %copy-start.2 = (bf16[1,8,16,1024]{3,2,1,0:T(8,128)(2,1)S(1)}, bf16[1,8,16,1024]{3,2,1,0:T(8,128)(2,1)}, u32[]{:S(2)}) copy-start(bf16[1,8,16,1024]{3,2,1,0:T(8,128)(2,1)} %param.12) | copy-start | bytes 786436
  35.6 21.0 %collective-permute-start.14 = (bf16[360,1024]{1,0:T(8,128)(2,1)S(1)}, bf16[360,1024]{1,0:T(8,128)(2,1)S(1)}, u32[]{:S(2)}, u32[]{:S(2)}) collective-permute-start(bf16[360,1024]{1,0:T(8,128)(2,1)S(1)} %collective-permute-done.3.refs_3_), channel_id=1, source_target_pairs={{0,1},{1,0},{6,7},{7,6},{8,9},{9,8},{14,15},{15,14},{16,17},{17,16... | collective-permute-start | bytes 2211848 | tf_op jit(solution)/shard_map/ppermute | solution.py:200
  38.2 14.2 %collective-permute-start.10 = (bf16[1024,256]{1,0:T(8,128)(2,1)S(1)}, bf16[1024,256]{1,0:T(8,128)(2,1)S(1)}, u32[]{:S(2)}, u32[]{:S(2)}) collective-permute-start(bf16[1024,256]{1,0:T(8,128)(2,1)S(1)} %attention.1.refs_0_), channel_id=1, source_target_pairs={{0,2},{1,3},{2,0},{3,1},{4,6},{5,7},{6,4},{7,5},{8,10},{9,11},{10,... | collective-permute-start | bytes 1572872 | tf_op jit(solution)/shard_map/ppermute | solution.py:200
  38.3 3.0 %collective-permute-start.7 = (bf16[168,1024]{1,0:T(8,128)(2,1)S(1)}, bf16[168,1024]{1,0:T(8,128)(2,1)S(1)}, u32[]{:S(2)}, u32[]{:S(2)}) collective-permute-start(bf16[168,1024]{1,0:T(8,128)(2,1)S(1)} %slice.11), channel_id=1, source_target_pairs={{2,4},{3,5},{4,2},{5,3},{10,12},{11,13},{12,10},{13,11},{18,20},{1... | collective-permute-start | bytes 1032200 | tf_op jit(solution)/shard_map/ppermute | solution.py:200
  39.0 8.6 %collective-permute-start.5 = (bf16[128,1024]{1,0:T(8,128)(2,1)S(1)}, bf16[128,1024]{1,0:T(8,128)(2,1)S(1)}, u32[]{:S(2)}, u32[]{:S(2)}) collective-permute-start(bf16[128,1024]{1,0:T(8,128)(2,1)S(1)} %pad_maximum_fusion.rest_0_), channel_id=1, source_target_pairs={{0,16},{8,24},{16,0},{24,8},{1,17},{9,25},{17,1},{25,9},{2,18},{10... | collective-permute-start | bytes 786440 | tf_op jit(solution)/shard_map/ppermute | solution.py:197
  40.6 12.6 %collective-permute-start.15 = (bf16[192,1024]{1,0:T(8,128)(2,1)S(1)}, bf16[192,1024]{1,0:T(8,128)(2,1)S(1)}, u32[]{:S(2)}, u32[]{:S(2)}) collective-permute-start(bf16[192,1024]{1,0:T(8,128)(2,1)S(1)} %collective-permute-done.6.refs_4_), channel_id=1, source_target_pairs={{2,3},{3,2},{4,5},{5,4},{10,11},{11,10},{12,13},{13,12},{18,19},{1... | collective-permute-start | bytes 1179656 | tf_op jit(solution)/shard_map/ppermute | solution.py:200
  41.3 11.9 %collective-permute-start.16 = (bf16[168,1024]{1,0:T(8,128)(2,1)S(1)}, bf16[168,1024]{1,0:T(8,128)(2,1)S(1)}, u32[]{:S(2)}, u32[]{:S(2)}) collective-permute-start(bf16[168,1024]{1,0:T(8,128)(2,1)S(1)} %collective-permute-done.7.refs_5_), channel_id=1, source_target_pairs={{2,3},{3,2},{4,5},{5,4},{10,11},{11,10},{12,13},{13,12},{18,19},{1... | collective-permute-start | bytes 1032200 | tf_op jit(solution)/shard_map/ppermute | solution.py:200
  50.1 7.2 %collective-permute-start.8 = (bf16[1,3,360,128]{3,2,1,0:T(8,128)(2,1)S(1)}, bf16[1,3,360,128]{3,2,1,0:T(8,128)(2,1)S(1)}, u32[]{:S(2)}, u32[]{:S(2)}) collective-permute-start(bf16[1,3,360,128]{3,2,1,0:T(8,128)(2,1)S(1)} %get-tuple-element.46), channel_id=1, source_target_pairs={{0,8},{8,0},{16,24},{24,16},{1,9},{9,1},{17,25},{25,17},{2,10},{10... | collective-permute-start | bytes 829448 | tf_op jit(solution)/shard_map/ppermute | solution.py:197
  53.2 5.9 %collective-permute-start.11 = (bf16[1,3,360,128]{3,2,1,0:T(8,128)(2,1)S(1)}, bf16[1,3,360,128]{3,2,1,0:T(8,128)(2,1)S(1)}, u32[]{:S(2)}, u32[]{:S(2)}) collective-permute-start(bf16[1,3,360,128]{3,2,1,0:T(8,128)(2,1)S(1)} %get-tuple-element.50), channel_id=1, source_target_pairs={{0,8},{8,0},{16,24},{24,16},{1,9},{9,1},{17,25},{25,17},{2,10},{10... | collective-permute-start | bytes 829448 | tf_op jit(solution)/shard_map/ppermute | solution.py:197
  57.2 9.3 %collective-permute-start.17 = (bf16[2,1,360,128]{3,2,1,0:T(8,128)(2,1)S(1)}, bf16[2,1,360,128]{3,2,1,0:T(8,128)(2,1)S(1)}, u32[]{:S(2)}, u32[]{:S(2)}) collective-permute-start(bf16[2,1,360,128]{3,2,1,0:T(8,128)(2,1)S(1)} %get-tuple-element.54), channel_id=1, source_target_pairs={{0,8},{8,0},{16,24},{24,16},{1,9},{9,1},{17,25},{25,17},{2,10},{10... | collective-permute-start | bytes 552968 | tf_op jit(solution)/shard_map/ppermute | solution.py:197
  57.4 12.1 %collective-permute-start.9 = (bf16[3,192,128]{2,1,0:T(8,128)(2,1)S(1)}, bf16[3,192,128]{2,1,0:T(8,128)(2,1)S(1)}, u32[]{:S(2)}, u32[]{:S(2)}) collective-permute-start(bf16[3,192,128]{2,1,0:T(8,128)(2,1)S(1)} %get-tuple-element.48), channel_id=1, source_target_pairs={{0,16},{8,24},{16,0},{24,8},{1,17},{9,25},{17,1},{25,9},{2,18},{10... | collective-permute-start | bytes 442376 | tf_op jit(solution)/shard_map/ppermute | solution.py:197
  59.0 16.9 %copy-start.6 = (bf16[1,64,2880]{2,1,0:T(8,128)(2,1)S(1)}, bf16[1,64,2880]{2,1,0:T(8,128)(2,1)}, u32[]{:S(2)}) copy-start(bf16[1,64,2880]{2,1,0:T(8,128)(2,1)} %param.9) | copy-start | bytes 1105924
  59.2 12.1 %collective-permute-start.12 = (bf16[3,192,128]{2,1,0:T(8,128)(2,1)S(1)}, bf16[3,192,128]{2,1,0:T(8,128)(2,1)S(1)}, u32[]{:S(2)}, u32[]{:S(2)}) collective-permute-start(bf16[3,192,128]{2,1,0:T(8,128)(2,1)S(1)} %get-tuple-element.51), channel_id=1, source_target_pairs={{0,2},{1,3},{2,0},{3,1},{4,6},{5,7},{6,4},{7,5},{8,10},{9,11},{10,... | collective-permute-start | bytes 442376 | tf_op jit(solution)/shard_map/ppermute | solution.py:200
  65.8 8.4 %collective-permute-start.13 = (bf16[3,192,128]{2,1,0:T(8,128)(2,1)S(1)}, bf16[3,192,128]{2,1,0:T(8,128)(2,1)S(1)}, u32[]{:S(2)}, u32[]{:S(2)}) collective-permute-start(bf16[3,192,128]{2,1,0:T(8,128)(2,1)S(1)} %get-tuple-element.52), channel_id=1, source_target_pairs={{0,18},{1,19},{2,16},{3,17},{4,22},{5,23},{6,20},{7,21},{8,26},{9,... | collective-permute-start | bytes 442376 | tf_op jit(solution)/shard_map/ppermute | solution.py:205
  66.6 7.6 %collective-permute-start.18 = (bf16[1,192,128]{2,1,0:T(8,128)(2,1)S(1)}, bf16[1,192,128]{2,1,0:T(8,128)(2,1)S(1)}, u32[]{:S(2)}, u32[]{:S(2)}) collective-permute-start(bf16[1,192,128]{2,1,0:T(8,128)(2,1)S(1)} %get-tuple-element.56), channel_id=1, source_target_pairs={{0,16},{8,24},{16,0},{24,8},{1,17},{9,25},{17,1},{25,9},{2,18},{10... | collective-permute-start | bytes 147464 | tf_op jit(solution)/shard_map/ppermute | solution.py:197
  67.6 7.1 %collective-permute-start.19 = (bf16[1,192,128]{2,1,0:T(8,128)(2,1)S(1)}, bf16[1,192,128]{2,1,0:T(8,128)(2,1)S(1)}, u32[]{:S(2)}, u32[]{:S(2)}) collective-permute-start(bf16[1,192,128]{2,1,0:T(8,128)(2,1)S(1)} %get-tuple-element.57), channel_id=1, source_target_pairs={{0,2},{1,3},{2,0},{3,1},{4,6},{5,7},{6,4},{7,5},{8,10},{9,11},{10,... | collective-permute-start | bytes 147464 | tf_op jit(solution)/shard_map/ppermute | solution.py:200
  69.5 6.4 %collective-permute-start.20 = (bf16[1,192,128]{2,1,0:T(8,128)(2,1)S(1)}, bf16[1,192,128]{2,1,0:T(8,128)(2,1)S(1)}, u32[]{:S(2)}, u32[]{:S(2)}) collective-permute-start(bf16[1,192,128]{2,1,0:T(8,128)(2,1)S(1)} %get-tuple-element.58), channel_id=1, source_target_pairs={{0,18},{1,19},{2,16},{3,17},{4,22},{5,23},{6,20},{7,21},{8,26},{9,... | collective-permute-start | bytes 147464 | tf_op jit(solution)/shard_map/ppermute | solution.py:205
  (7 other events, 22.4 us)

commit v4 on v3

--- a/solution.py
+++ b/solution.py
@@ -168,11 +168,11 @@
 
 
 VMEM_LIMIT = 24 * 1024 * 1024
+FREE = pl.CostEstimate(flops=0, bytes_accessed=0, transcendentals=0)
 F32 = jnp.float32
 BF16 = jnp.bfloat16
 
 PAIR_BIT, NEAR_BIT, FAR_BIT = 2, 1, 6
-OUTER, INNER = (0, 1, 6, 7), (2, 3, 4, 5)
 ORDER = (0, 2, 1, 3)
 
 
@@ -188,21 +188,25 @@
     return pltpu.CompilerParams(vmem_limit_bytes=VMEM_LIMIT)
 
 
-def cost(flops, nbytes):
-    return pl.CostEstimate(flops=int(flops), bytes_accessed=int(nbytes), transcendentals=0)
-
-
-def swap(values, req_bits, exp_bits, among=None):
+def swap(values, req_bits, exp_bits):
     if not exp_bits:
         return lax.ppermute(values, "req", [(i, i ^ req_bits) for i in range(lax.axis_size("req"))])
     if not req_bits:
-        among = range(lax.axis_size("exp")) if among is None else among
-        return lax.ppermute(values, "exp", [(i, i ^ exp_bits) for i in among])
+        return lax.ppermute(values, "exp", [(i, i ^ exp_bits) for i in range(lax.axis_size("exp"))])
     rows, cols = lax.axis_size("req"), lax.axis_size("exp")
     pairs = [
         (i * cols + j, (i ^ req_bits) * cols + (j ^ exp_bits)) for i in range(rows) for j in range(cols)
     ]
     return lax.ppermute(values, ("req", "exp"), pairs)
+
+
+def is_inner(index):
+    return (index & 2) * 2 != (index & 4)
+
+
+def swap_blocks(values, inner_bits, outer_bits):
+    pairs = [(i, i ^ (inner_bits if is_inner(i) else outer_bits)) for i in range(lax.axis_size("exp"))]
+    return lax.ppermute(values, "exp", pairs)
 
 
 def pack_kernel(q_ref, kv_ref, pool_ref, *rest):
@@ -253,7 +257,7 @@
         out_specs=[vmem()] * n_req,
         scratch_shapes=[pltpu.SemaphoreType.DMA((n_req * (1 + 2 * blocks) + 1,))],
         compiler_params=params(),
-        cost_estimate=cost(0, 4 * tok * width * n_req),
+        cost_estimate=FREE,
         name="pack",
     )(q, kv, pool)
 
@@ -267,9 +271,9 @@
 def attention_kernel(
     pages_ref, table_ref, sink_ref, cos_ref, sin_ref, *rest, kv_dev, per_kv, page_size
 ):
-    n_req = len(rest) - 7
+    n_req = len(rest) - 8
     pieces, out_ref = rest[:n_req], rest[n_req]
-    q_scr, pool_scr, flat_scr, key_scr, value_scr, bias_scr = rest[n_req + 1 :]
+    q_scr, qt_scr, pool_scr, flat_scr, key_scr, value_scr, bias_scr = rest[n_req + 1 :]
     own = lax.axis_index("req")
     tok = pieces[0].shape[0]
     q_width = kv_dev * per_kv * HD
@@ -289,7 +293,7 @@
         for p in range(kv_dev * pairs):
             col = p * 2 * HD
             turned = turn(pieces[k][:, col : col + 2 * HD].astype(F32), cosine, sine).astype(BF16)
-            q_scr[p, place * tok : (place + 1) * tok, :] = turned * jnp.asarray(1.0 / math.sqrt(HD), BF16)
+            q_scr[p, place // 2, place % 2 * tok : (place % 2 + 1) * tok, :] = turned.astype(F32) * (1.0 / math.sqrt(HD))
         at = q_width
         key_row = pl.multiple_of(cached + row, tok)
         flat_scr[pl.ds(key_row, tok), :head_width] = turn(
@@ -306,6 +310,10 @@
         query = lax.broadcasted_iota(jnp.int32, (total, tok), 1) + (cached + shard * tok)
         last = jnp.where(key < cached, live - 1, query)
         bias_scr[:, place * tok : (place + 1) * tok] = jnp.where(key > last, NEGATIVE, 0.0)
+    for p in range(kv_dev * pairs):
+        for h in range(2):
+            at = (p % pairs * 2 + h) * 2 * tok
+            qt_scr[p // pairs, :, at : at + 2 * tok] = q_scr[p, h].T.astype(BF16)
     per_dev = pool_rows // page_size
     for j in range(page_limit):
         slot = table_ref[0, j]
@@ -323,23 +331,26 @@
     key_scr[3] = jnp.where(low, zero, flat).astype(BF16)
     value_scr[...] = flat_scr[:, head_width:].T.astype(BF16)
 
-    def one_pair(i, carry):
-        g = i // pairs
-        for a in range(2):
-            scores = lax.dot_general(
-                key_scr[g * 2 + a], q_scr[i], (((1,), (1,)), ((), ())), preferred_element_type=F32
-            )
-            scores = scores + bias_scr[...]
-            sink = sink_ref[own * (kv_dev * per_kv) + i * 2 + a]
-            top = jnp.maximum(jnp.max(scores, axis=0, keepdims=True), sink)
-            expo = jnp.exp(scores - top)
-            den = jnp.sum(expo, axis=0, keepdims=True) + jnp.exp(sink - top)
-            values = value_scr[pl.ds(pl.multiple_of(g * HD, HD), HD), :]
-            summed = jnp.dot(values, expo.astype(BF16), preferred_element_type=F32)
-            out_ref[pl.ds(pl.multiple_of((i * 2 + a) * HD, HD), HD), :] = (summed / den).astype(BF16)
+    def one_set(i, carry):
+        g, a = i // 2, i % 2
+        wide = n_req * tok
+        scores = jnp.dot(key_scr[i], qt_scr[g], preferred_element_type=F32)
+        weights, dens = [], []
+        for p in range(pairs):
+            part = scores[:, p * wide : (p + 1) * wide] + bias_scr[...]
+            sink = sink_ref[own * (kv_dev * per_kv) + g * per_kv + 2 * p + a]
+            top = jnp.maximum(jnp.max(part, axis=0, keepdims=True), sink)
+            expo = jnp.exp(part - top)
+            dens.append(jnp.sum(expo, axis=0, keepdims=True) + jnp.exp(sink - top))
+            weights.append(expo.astype(BF16))
+        values = value_scr[pl.ds(pl.multiple_of(g * HD, HD), HD), :]
+        summed = jnp.dot(values, jnp.concatenate(weights, axis=1), preferred_element_type=F32)
+        for p in range(pairs):
+            row = pl.multiple_of((g * per_kv + 2 * p + a) * HD, HD)
+            out_ref[pl.ds(row, HD), :] = (summed[:, p * wide : (p + 1) * wide] / dens[p]).astype(BF16)
         return carry
 
-    lax.fori_loop(0, kv_dev * pairs, one_pair, 0)
+    lax.fori_loop(0, 2 * kv_dev, one_set, 0, unroll=False)
 
 
 def attention(pages, table, sinks, cosine, sine, pieces, kv_dev, per_kv, pool_rows, page_size):
@@ -353,7 +364,8 @@
         in_specs=[smem()] * 3 + [vmem()] * (2 + n_req),
         out_specs=vmem(),
         scratch_shapes=[
-            pltpu.VMEM((kv_dev * per_kv // 2, n_req * tok, 2 * HD), BF16),
+            pltpu.VMEM((kv_dev * per_kv // 2, 2, 2 * tok, 2 * HD), F32),
+            pltpu.VMEM((kv_dev, 2 * HD, per_kv // 2 * n_req * tok), BF16),
             pltpu.VMEM((n_req, pool_rows, 2 * head_width), F32),
             pltpu.VMEM((total, 2 * head_width), F32),
             pltpu.VMEM((2 * kv_dev, total, head_width), BF16),
@@ -361,7 +373,7 @@
             pltpu.VMEM((total, n_req * tok), F32),
         ],
         compiler_params=params(),
-        cost_estimate=cost(4e9, 2**22),
+        cost_estimate=FREE,
         name="attention",
     )(pages, table, sinks, cosine, sine, *pieces)
 
@@ -399,44 +411,40 @@
         out_specs=vmem(),
         scratch_shapes=[pltpu.VMEM((rows * len(pairs), width), BF16)],
         compiler_params=params(),
-        cost_estimate=cost(1e8, 2**21),
+        cost_estimate=FREE,
         name="write_pool",
     )(slots, cosine, sine, pool, *pairs)
 
 
-def project_kernel(*refs, n_ctx, counts):
+def project_kernel(*refs, n_ctx, counts, pairs):
     contexts = refs[:n_ctx]
     weights = refs[n_ctx:-2]
     send_ref, keep_ref = refs[-2:]
     half = contexts[0].shape[1] // 2
-    at = 0
-    for b, count in enumerate(counts):
-        whole, pieces = weights[at], weights[at + 1 : at + count]
-        at += count
+    for n, (i, b) in enumerate(pairs):
+        at = sum(counts[:b])
         row = 0
-        for piece in pieces or (whole,):
+        for piece in weights[at : at + counts[b]]:
             rows = slice(row, row + piece.shape[0])
-            block = whole[rows, :] + piece[...] if pieces else whole[...]
-            for i in range(n_ctx):
-                terms = jnp.dot(block, contexts[i][...], preferred_element_type=F32).astype(BF16)
-                keep_ref[i, b, rows, :] = terms[:, :half]
-                send_ref[i, b, rows, :] = terms[:, half:]
+            terms = jnp.dot(piece[...], contexts[i][...], preferred_element_type=F32).astype(BF16)
+            keep_ref[n, rows, :] = terms[:, :half]
+            send_ref[n, rows, :] = terms[:, half:]
             row += piece.shape[0]
 
 
-def project(contexts, blocks):
-    depth, tokens = contexts[0].shape
-    cols = blocks[0][0].shape[0]
-    shape = jax.ShapeDtypeStruct((len(contexts), len(blocks), cols, tokens // 2), BF16)
-    flat = [chunk for block in blocks for chunk in block]
-    work = len(contexts) * len(blocks)
+def project(contexts, blocks, pairs):
+    tokens = contexts[0].shape[1]
+    cols = sum(piece.shape[0] for piece in blocks[0])
+    shape = jax.ShapeDtypeStruct((len(pairs), cols, tokens // 2), BF16)
+    flat = [piece for block in blocks for piece in block]
+    counts = tuple(len(block) for block in blocks)
     return pl.pallas_call(
-        functools.partial(project_kernel, n_ctx=len(contexts), counts=tuple(len(b) for b in blocks)),
+        functools.partial(project_kernel, n_ctx=len(contexts), counts=counts, pairs=pairs),
         out_shape=[shape, shape],
         in_specs=[vmem()] * (len(contexts) + len(flat)),
         out_specs=[vmem()] * 2,
         compiler_params=params(),
-        cost_estimate=cost(work * 2 * tokens * depth * cols, 2 * depth * cols * len(blocks)),
+        cost_estimate=FREE,
         name="project",
     )(*contexts, *flat)
 
@@ -445,29 +453,32 @@
     return -(-cols // 32) * 16
 
 
-def pair_kernel(keep_ref, got_ref, *out_refs):
-    n_ctx, blocks, cols, width = keep_ref.shape
+def pair_kernel(keep_ref, got_ref, *out_refs, counts):
+    cols, width = keep_ref.shape[1:]
     rows = out_refs[0].shape[1]
     tok = width // 2
     low = lax.broadcasted_iota(jnp.int32, (rows, width), 1) < tok
-    for i in range(n_ctx):
-        for b in range(blocks):
-            both = keep_ref[i, b].astype(F32) + got_ref[i, b].astype(F32)
+    at = 0
+    for i, count in enumerate(counts):
+        for b in range(count):
+            both = keep_ref[at].astype(F32) + got_ref[at].astype(F32)
             top = both[:rows]
             rest = jnp.concatenate([both[rows:], jnp.zeros((2 * rows - cols, width), F32)], axis=0)
             out_refs[2 * i][b] = jnp.where(low, top, pltpu.roll(rest, tok, 1)).astype(BF16)
             out_refs[2 * i + 1][b] = jnp.where(low, pltpu.roll(top, tok, 1), rest).astype(BF16)
-
-
-def pair_sum(keep, got):
-    n_ctx, blocks, cols, width = keep.shape
+            at += 1
+
+
+def pair_sum(keep, got, counts):
+    cols, width = keep.shape[1:]
+    shapes = [jax.ShapeDtypeStruct((c, fold_rows(cols), width), BF16) for c in counts for _ in range(2)]
     return pl.pallas_call(
-        pair_kernel,
-        out_shape=[jax.ShapeDtypeStruct((blocks, fold_rows(cols), width), BF16)] * (2 * n_ctx),
+        functools.partial(pair_kernel, counts=counts),
+        out_shape=shapes,
         in_specs=[vmem()] * 2,
-        out_specs=[vmem()] * (2 * n_ctx),
+        out_specs=[vmem()] * len(shapes),
         compiler_params=params(),
-        cost_estimate=cost(1e6, 6 * keep.size),
+        cost_estimate=FREE,
         name="pair_sum",
     )(keep, got)
 
@@ -475,11 +486,13 @@
 def final_kernel(hidden_ref, *rest, places):
     parts, out_ref, scr = rest[:-2], rest[-2], rest[-1]
     own = lax.axis_index("exp")
+    inner = is_inner(own)
     tok, width = hidden_ref.shape
     rows = parts[0].shape[1]
     cols = width // lax.axis_size("exp")
     for (first, second), bits in zip(zip(parts[0::2], parts[1::2]), places):
-        for b, bit in enumerate(bits):
+        for b, (inner_bits, outer_bits) in enumerate(bits):
+            bit = jnp.where(inner, inner_bits, outer_bits)
             both = first[b].astype(F32) + second[b].astype(F32)
             row = pl.multiple_of(jnp.bitwise_xor(own, bit) * cols, 8)
             scr[pl.ds(row, rows), :] = both
@@ -496,7 +509,7 @@
         out_specs=vmem(),
         scratch_shapes=[pltpu.VMEM((hidden.shape[1], parts[0].shape[2]), F32)],
         compiler_params=params(),
-        cost_estimate=cost(1e6, 8 * hidden.size),
+        cost_estimate=FREE,
         name="finish",
     )(hidden, *parts)
 
@@ -514,13 +527,11 @@
     weight = out_weight.T
     cols = weight.shape[0]
     cut = fold_rows(cols)
-    outer = swap(weight, 0, FAR_BIT, OUTER)
-    near = swap(weight, 0, NEAR_BIT)
+    first = swap_blocks(weight, FAR_BIT, NEAR_BIT)
 
     pieces = pack(queries[0], new_kv[0], kv_pool[0].reshape(pool_rows, 2 * kv_width), n_req)
     pieces = [pieces[0]] + [swap(pieces[k], k, 0) for k in range(1, n_req)]
-    pieces, weight_late = lax.optimization_barrier((pieces, weight))
-    inner = [swap(chunk, 0, FAR_BIT, INNER) for chunk in (weight_late[:cut], weight_late[cut:])]
+    second = [swap_blocks(chunk, NEAR_BIT, FAR_BIT) for chunk in (weight[:cut], weight[cut:])]
 
     position = cached_pages[0] * page_size + jnp.arange(n_req * tok)
     frequency = THETA ** (-2.0 * jnp.arange(HD // 2).astype(F32) / HD)
@@ -534,34 +545,40 @@
         head_count // kv_heads, pool_rows, page_size,
     )
     chip_rows = jnp.concatenate([new_kv[0], pieces[1][:, -2 * kv_width :]], axis=0)
-    ctx, outer, near, chip_rows = lax.optimization_barrier((ctx, outer, near, chip_rows))
+    ctx, first, chip_rows = lax.optimization_barrier((ctx, first, chip_rows))
     ctx_mate = swap(ctx, 0, PAIR_BIT)
-    outer_both = swap(outer, 0, NEAR_BIT, OUTER)
-    inner_both = [swap(chunk, 0, NEAR_BIT, INNER) for chunk in inner]
-    far = [outer, *inner]
-    both = [outer_both, *inner_both]
+    inner = is_inner(lax.axis_index("exp"))
+    far = [jnp.where(inner, first[:cut], second[0]), jnp.where(inner, first[cut:], second[1])]
+    both = [swap(chunk, 0, NEAR_BIT) for chunk in far]
     pool_out = write_pool(new_slots, cosine, sine, kv_pool[0], [chip_rows, swap(chip_rows, 2, 0)])
 
+    def both_sides(contexts, blocks, pairs):
+        send, keep = project(contexts, blocks, pairs)
+        counts = tuple(n for n in (sum(i == c for c, _ in pairs) for i in range(len(contexts))) if n)
+        return pair_sum(keep, swap(send, 1, 0), counts)
+
+    parts = []
     ctx, pool_out = lax.optimization_barrier((ctx, pool_out))
-    early = [[weight], [near], far]
-    late = [both]
-    parts = []
-    send, keep = project([ctx], early)
-    own_a, over_y = pair_sum(keep, swap(send, 1, 0))
-    parts += [own_a, swap(over_y, 2, 0)]
-    send, keep = project([ctx_mate], early)
-    over_pair, over_both = pair_sum(keep, swap(send, 1, 0))
+    own_part, over_y = both_sides([ctx], [[weight], [first]], ((0, 0), (0, 1)))
+    parts += [own_part, swap(over_y, 2, 0)]
+    ctx_mate, parts[1] = lax.optimization_barrier((ctx_mate, parts[1]))
+    over_pair, over_both = both_sides([ctx_mate], [[weight], [first], second], ((0, 0), (0, 1), (0, 2)))
     parts += [swap(over_pair, 0, PAIR_BIT), swap(over_both, 2, PAIR_BIT)]
-    send, keep = project([ctx, ctx_mate], late)
-    own_c, over_y, over_pair, over_both = pair_sum(keep, swap(send, 1, 0))
-    parts += [own_c, swap(over_y, 2, 0), swap(over_pair, 0, PAIR_BIT), swap(over_both, 2, PAIR_BIT)]
-    early_bits = (0, NEAR_BIT, FAR_BIT)
-    late_bits = (NEAR_BIT ^ FAR_BIT,)
+    own_part, over_y, over_pair, over_both = both_sides([ctx, ctx_mate], [second, both], ((0, 0), (0, 1), (1, 1)))
+    parts += [own_part, swap(over_y, 2, 0)]
+    parts += [swap(over_pair, 0, PAIR_BIT), swap(over_both, 2, PAIR_BIT)]
+    own_bits, first_bits, second_bits, both_bits = (
+        (0, 0), (FAR_BIT, NEAR_BIT), (NEAR_BIT, FAR_BIT), (FAR_BIT ^ NEAR_BIT,) * 2
+    )
+
+    def of_mate(bits):
+        return PAIR_BIT ^ bits[1], PAIR_BIT ^ bits[0]
+
     places = (
-        early_bits,
-        tuple(PAIR_BIT ^ b for b in early_bits),
-        late_bits,
-        tuple(PAIR_BIT ^ b for b in late_bits),
+        (own_bits, first_bits),
+        (of_mate(own_bits), of_mate(first_bits), of_mate(second_bits)),
+        (second_bits, both_bits),
+        (of_mate(both_bits),),
     )
     layer_out = finish(hidden_in[0], parts, places)
     return (layer_out[None], pool_out[None])

time: 77.8 us -> 70.7 us (0.909)
  waiting for transfers between devices: 25 us -> 18.4 us
  Pallas kernels: 15.1 us -> 12 us
  other arithmetic: 0.84 us -> 2.99 us
  local copies, waits for them, and re-layouts: 3.64 us -> 5.18 us
  starting transfers between devices: 31.2 us -> 30.4 us
    ppermute x9, waiting for transfers between devices: 14.7 us -> 3.54 us  [swap(): lax.ppermute(values, 'req', [(i, i ^ req_bits) for i in range(lax.axis_si...]
    ppermute x10 -> x8, waiting for transfers between devices: 6.06 us -> 14.2 us  [the longest x5 14.2 us: swap(): lax.ppermute(values, 'exp', [(i, i ^ exp_bits) for i in range(lax.axis_si...]
    pallas_call x1, Pallas kernels: 8.92 us -> 5.12 us  [attention(): pl.pallas_call(functools.partial(attention_kernel, kv_dev=kv_dev, per_kv=...]
    ppermute x2, waiting for transfers between devices: 4.19 us -> 0.6 us  [swap(): return lax.ppermute(values, ('req', 'exp'), pairs)]
    slice x2, local copies, waits for them, and re-layouts: 0.05 us -> 1.54 us  [the longest x1 0.79 us: paired_plan(): weight[:cut]]
    concatenate x1, other arithmetic: 0.27 us -> 1.59 us  [paired_plan(): cosine = jnp.concatenate([cosine] * 4, axis=1)]
    ppermute x10 -> x8, starting transfers between devices: 22.5 us -> 21.2 us  [the longest x5 14.3 us: swap(): lax.ppermute(values, 'exp', [(i, i ^ exp_bits) for i in range(lax.axis_si...]
    ppermute x2, starting transfers between devices: 2.47 us -> 3.37 us  [swap(): return lax.ppermute(values, ('req', 'exp'), pairs)]
  transfers between devices with their start and end apart: 21 -> 19, of which waited for: 8 -> 7; matrix products, arithmetic and copies ran while one was open for 1% -> 6% of each run, Pallas kernels for 18% -> 15%
where the time goes in v4:
time: 70.7 us; the launch traced here: 70.5 us
  starting transfers between devices  30.4 us (43%)
  waiting for transfers between devices  18.4 us (26%)
  Pallas kernels  12 us (17%)
  local copies, waits for them, and re-layouts  5.18 us (7%)
  other arithmetic  2.99 us (4%)
  between operations  1.53 us (2%)
    ppermute x5, starting transfers between devices, swap(): lax.ppermute(values, 'exp', [(i, i ^ exp_bits) for i in range(lax.axis_si...  14.3 us
    ppermute x5, waiting for transfers between devices, swap(): lax.ppermute(values, 'exp', [(i, i ^ exp_bits) for i in range(lax.axis_si...  14.2 us
    ppermute x3, starting transfers between devices, swap_blocks(): return lax.ppermute(values, 'exp', pairs)  6.89 us
    ppermute x9, starting transfers between devices, swap(): lax.ppermute(values, 'req', [(i, i ^ req_bits) for i in range(lax.axis_si...  5.88 us
    pallas_call x1, Pallas kernels, attention(): pl.pallas_call(functools.partial(attention_kernel, kv_dev=kv_dev, per_kv=...  5.12 us
    unnamed x22, local copies, waits for them, and re-layouts  3.63 us
    ppermute x9, waiting for transfers between devices, swap(): lax.ppermute(values, 'req', [(i, i ^ req_bits) for i in range(lax.axis_si...  3.54 us
    ppermute x2, starting transfers between devices, swap(): return lax.ppermute(values, ('req', 'exp'), pairs)  3.37 us
  transfers between devices with their start and end apart: 19, of which 7 were waited for; matrix products, arithmetic and copies ran while one was open for 6% of the time, Pallas kernels for 15%

profile of v4, /device:TPU:0, one launch (start us, length us, event | category | flops | bytes accessed | tf_op | source)
XLA Modules:
  0.0 70.5 jit_solution(16069228691293598479)
XLA Ops:
  0.6 3.0 %collective-permute-start.3 = (bf16[360,1024]{1,0:T(8,128)(2,1)}, bf16[360,1024]{1,0:T(8,128)(2,1)S(1)}, u32[]{:S(2)}, u32[]{:S(2)}) collective-permute-start(bf16[360,1024]{1,0:T(8,128)(2,1)} %bitcast.9), channel_id=1, source_target_pairs={{0,1},{1,0},{2,4},{3,5},{4,2},{5,3},{6,7},{7,6},{8,9},{9,8},{10,12... | collective-permute-start | bytes 2211848 | tf_op jit(solution)/shard_map/ppermute | solution.py:209
  3.6 0.9 %copy-done.1 = bf16[1,8,16,1024]{3,2,1,0:T(8,128)(2,1)S(1)} copy-done((bf16[1,8,16,1024]{3,2,1,0:T(8,128)(2,1)S(1)}, bf16[1,8,16,1024]{3,2,1,0:T(8,128)(2,1)}, u32[]{:S(2)}) %copy-start.1) | copy-done | bytes 262168
  4.6 1.0 %copy-done.3 = bf16[1,64,4096]{2,1,0:T(8,128)(2,1)S(1)} copy-done((bf16[1,64,4096]{2,1,0:T(8,128)(2,1)S(1)}, bf16[1,64,4096]{2,1,0:T(8,128)(2,1)}, u32[]{:S(2)}) %copy-start.3) | copy-done | bytes 524312
  5.6 0.9 %copy-done.4 = bf16[1,64,1024]{2,1,0:T(8,128)(2,1)S(1)} copy-done((bf16[1,64,1024]{2,1,0:T(8,128)(2,1)S(1)}, bf16[1,64,1024]{2,1,0:T(8,128)(2,1)}, u32[]{:S(2)}) %copy-start.4) | copy-done | bytes 131096
  6.5 1.2 %pack.1 = (bf16[64,1792]{1,0:T(8,128)(2,1)S(1)}, bf16[64,2816]{1,0:T(8,128)(2,1)S(1)}, bf16[64,1792]{1,0:T(8,128)(2,1)}, bf16[64,1792]{1,0:T(8,128)(2,1)S(1)}) custom-call(bf16[64,4096]{1,0:T(8,128)(2,1)S(1)} %bitcast.16, bf16[64,1024]{1,0:T(8,128)(2,1)S(1)} %bitcast.17, bf16[128,1024]{1,0:T(8,128)(2,1)S(1)} %bitcast.14), custom_call_target="tpu_custom_call" | custom-call | tf_op jit(solution)/shard_map/pack/pallas_call | solution.py:253
  7.9 1.6 %collective-permute-start.1 = (bf16[64,1792]{1,0:T(8,128)(2,1)}, bf16[64,1792]{1,0:T(8,128)(2,1)S(1)}, u32[]{:S(2)}, u32[]{:S(2)}) collective-permute-start(bf16[64,1792]{1,0:T(8,128)(2,1)} %get-tuple-element.29), channel_id=1, source_target_pairs={{0,16},{8,24},{16,0},{24,8},{1,17},{9,25},{17,1},{25,9},{2,18},{10... | collective-permute-start | bytes 688136 | tf_op jit(solution)/shard_map/ppermute | solution.py:193
  9.7 0.8 %slice.21 = bf16[192,1024]{1,0:T(8,128)(2,1)} slice(bf16[360,1024]{1,0:T(8,128)(2,1)S(1)} %bitcast.10), slice={[0:192], [0:1024]} | slice | bytes 786432 | tf_op jit(solution)/shard_map/slice | solution.py:534
  10.5 3.6 %collective-permute-start.8 = (bf16[192,1024]{1,0:T(8,128)(2,1)}, bf16[192,1024]{1,0:T(8,128)(2,1)S(1)}, u32[]{:S(2)}, u32[]{:S(2)}) collective-permute-start(bf16[192,1024]{1,0:T(8,128)(2,1)} %slice.21), channel_id=1, source_target_pairs={{0,6},{1,7},{2,3},{3,2},{4,5},{5,4},{6,0},{7,1},{8,14},{9,15},{10,... | collective-permute-start | bytes 1179656 | tf_op jit(solution)/shard_map/ppermute | solution.py:209
  14.8 1.3 %fusion = (f32[256,32]{1,0:T(8,128)}, f32[256,32]{1,0:T(8,128)}, f32[256,32]{1,0:T(8,128)}) fusion(f32[32]{0:T(128)S(1)} %multiply_power_fusion, f32[256]{0:T(256)S(1)} %add_convert_fusion), kind=kLoop, calls=%fused_computation.7 | loop fusion | flops 16384 | bytes 99456 | tf_op jit(solution)/shard_map/neg | solution.py:541
  16.8 1.6 %pad_maximum_fusion.1 = (f32[256,128]{1,0:T(8,128)S(1)}, f32[256,128]{1,0:T(8,128)S(1)}) fusion(f32[256,32]{1,0:T(8,128)} %get-tuple-element.54, f32[256,32]{1,0:T(8,128)} %get-tuple-element.53, f32[256,32]{1,0:T(8,128)} %get-tuple-element.52), kind=kLoop, calls=%fused_computation.5 | loop fusion | flops 196608 | bytes 360448 | tf_op jit(solution)/shard_map/concatenate | solution.py:540
  18.8 1.8 %collective-permute-done.2.rest_3_ = bf16[64,1792]{1,0:T(8,128)(2,1)S(1)} collective-permute-done((bf16[64,1792]{1,0:T(8,128)(2,1)S(1)}, bf16[64,1792]{1,0:T(8,128)(2,1)S(1)}, u32[]{:S(2)}, u32[]{:S(2)}) %collective-permute-start.2) | collective-permute-done | bytes 229408 | tf_op jit(solution)/shard_map/ppermute | solution.py:193
  21.2 5.1 %attention.1.refs_0_ = bf16[1024,256]{1,0:T(8,128)(2,1)S(1)} custom-call(s32[1]{0:T(128)S(6)} %copy.12.pages_ref, s32[1,16]{1,0:T(1,128)S(1)} %copy-done.8, f32[64]{0:T(128)S(1)} %copy-done.9, f32[256,128]{1,0:T(8,128)S(1)} %get-tuple-element.55.cos_ref, f32[256,128]{1,0:T(8,128)S(1)} %get-tuple-element.56.sin_ref, ...), custom_call_target="tpu_custom_call" | custom-call | tf_op jit(solution)/shard_map/attention/pallas_call | solution.py:361
  26.4 1.6 %collective-permute-start.4 = (bf16[128,1024]{1,0:T(8,128)(2,1)S(1)}, bf16[128,1024]{1,0:T(8,128)(2,1)S(1)}, u32[]{:S(2)}, u32[]{:S(2)}) collective-permute-start(bf16[128,1024]{1,0:T(8,128)(2,1)S(1)} %pad_maximum_fusion.rest_0_), channel_id=1, source_target_pairs={{0,16},{8,24},{16,0},{24,8},{1,17},{9,25},{17,1},{25,9},{2,18},{10... | collective-permute-start | bytes 786440 | tf_op jit(solution)/shard_map/ppermute | solution.py:193
  28.0 11.5 %collective-permute-start.6 = (bf16[1024,256]{1,0:T(8,128)(2,1)S(1)}, bf16[1024,256]{1,0:T(8,128)(2,1)S(1)}, u32[]{:S(2)}, u32[]{:S(2)}) collective-permute-start(bf16[1024,256]{1,0:T(8,128)(2,1)S(1)} %attention.1.refs_0_), channel_id=1, source_target_pairs={{0,2},{1,3},{2,0},{3,1},{4,6},{5,7},{6,4},{7,5},{8,10},{9,11},{10,... | collective-permute-start | bytes 1572872 | tf_op jit(solution)/shard_map/ppermute | solution.py:195
  39.5 1.6 %collective-permute-start.13 = (bf16[192,1024]{1,0:T(8,128)(2,1)S(1)}, bf16[192,1024]{1,0:T(8,128)(2,1)S(1)}, u32[]{:S(2)}, u32[]{:S(2)}) collective-permute-start(bf16[192,1024]{1,0:T(8,128)(2,1)S(1)} %slice_select_fusion), channel_id=1, source_target_pairs={{0,1},{1,0},{2,3},{3,2},{4,5},{5,4},{6,7},{7,6},{8,9},{9,8},{10,11... | collective-permute-start | bytes 1179656 | tf_op jit(solution)/shard_map/ppermute | solution.py:195
  41.8 1.7 %write_pool.1 = bf16[8,16,1024]{2,1,0:T(8,128)(2,1)} custom-call(s32[1,16]{1,0:T(1,128)S(1)} %copy-done.7, f32[256,128]{1,0:T(8,128)S(1)} %get-tuple-element.55.cos_ref, f32[256,128]{1,0:T(8,128)S(1)} %get-tuple-element.56.sin_ref, bf16[8,16,1024]{2,1,0:T(8,128)(2,1)S(1)} %bitcast.15, bf16[128,1024]{1,0:T(8,128)(2,1)S(1)} %pad_maximum_fusion.rest_0_, ...), custom_call_target="tpu_custom_call" | custom-call | tf_op jit(solution)/shard_map/write_pool/pallas_call | solution.py:407
  44.1 1.4 %collective-permute-done.5.got_ref = bf16[2,360,128]{2,1,0:T(8,128)(2,1)S(1)} collective-permute-done((bf16[2,360,128]{2,1,0:T(8,128)(2,1)S(1)}, bf16[2,360,128]{2,1,0:T(8,128)(2,1)S(1)}, u32[]{:S(2)}, u32[]{:S(2)}) %collective-permute-start.5) | collective-permute-done | bytes 184352 | tf_op jit(solution)/shard_map/ppermute | solution.py:193
  46.2 4.0 %collective-permute-done.6.refs_0_.refs_1_ = bf16[1024,256]{1,0:T(8,128)(2,1)S(1)} collective-permute-done((bf16[1024,256]{1,0:T(8,128)(2,1)S(1)}, bf16[1024,256]{1,0:T(8,128)(2,1)S(1)}, u32[]{:S(2)}, u32[]{:S(2)}) %collective-permute-start.6) | collective-permute-done | bytes 524320 | tf_op jit(solution)/shard_map/ppermute | solution.py:195
  51.4 5.0 %collective-permute-done.14.refs_5_ = bf16[168,1024]{1,0:T(8,128)(2,1)S(1)} collective-permute-done((bf16[168,1024]{1,0:T(8,128)(2,1)S(1)}, bf16[168,1024]{1,0:T(8,128)(2,1)S(1)}, u32[]{:S(2)}, u32[]{:S(2)}) %collective-permute-start.14) | collective-permute-done | bytes 344096 | tf_op jit(solution)/shard_map/ppermute | solution.py:195
  57.8 1.7 %collective-permute-start.12 = (bf16[3,192,128]{2,1,0:T(8,128)(2,1)S(1)}, bf16[3,192,128]{2,1,0:T(8,128)(2,1)S(1)}, u32[]{:S(2)}, u32[]{:S(2)}) collective-permute-start(bf16[3,192,128]{2,1,0:T(8,128)(2,1)S(1)} %get-tuple-element.44), channel_id=1, source_target_pairs={{0,18},{1,19},{2,16},{3,17},{4,22},{5,23},{6,20},{7,21},{8,26},{9,... | collective-permute-start | bytes 442376 | tf_op jit(solution)/shard_map/ppermute | solution.py:200
  59.6 1.6 %collective-permute-start.16 = (bf16[2,192,128]{2,1,0:T(8,128)(2,1)S(1)}, bf16[2,192,128]{2,1,0:T(8,128)(2,1)S(1)}, u32[]{:S(2)}, u32[]{:S(2)}) collective-permute-start(bf16[2,192,128]{2,1,0:T(8,128)(2,1)S(1)} %get-tuple-element.48), channel_id=1, source_target_pairs={{0,16},{8,24},{16,0},{24,8},{1,17},{9,25},{17,1},{25,9},{2,18},{10... | collective-permute-start | bytes 294920 | tf_op jit(solution)/shard_map/ppermute | solution.py:193
  61.5 1.7 %collective-permute-start.18 = (bf16[1,192,128]{2,1,0:T(8,128)(2,1)S(1)}, bf16[1,192,128]{2,1,0:T(8,128)(2,1)S(1)}, u32[]{:S(2)}, u32[]{:S(2)}) collective-permute-start(bf16[1,192,128]{2,1,0:T(8,128)(2,1)S(1)} %get-tuple-element.50), channel_id=1, source_target_pairs={{0,18},{1,19},{2,16},{3,17},{4,22},{5,23},{6,20},{7,21},{8,26},{9,... | collective-permute-start | bytes 147464 | tf_op jit(solution)/shard_map/ppermute | solution.py:200
  63.2 5.2 %collective-permute-done.17.rest_6_ = bf16[1,192,128]{2,1,0:T(8,128)(2,1)S(1)} collective-permute-done((bf16[1,192,128]{2,1,0:T(8,128)(2,1)S(1)}, bf16[1,192,128]{2,1,0:T(8,128)(2,1)S(1)}, u32[]{:S(2)}, u32[]{:S(2)}) %collective-permute-start.17) | collective-permute-done | bytes 49184 | tf_op jit(solution)/shard_map/ppermute | solution.py:195
  69.0 1.4 %finish.1 = bf16[64,2880]{1,0:T(8,128)(2,1)} custom-call(bf16[64,2880]{1,0:T(8,128)(2,1)S(1)} %bitcast.19, bf16[2,192,128]{2,1,0:T(8,128)(2,1)S(1)} %get-tuple-element.37.rest_0_, bf16[2,192,128]{2,1,0:T(8,128)(2,1)S(1)} %collective-permute-done.7.rest_1_, bf16[3,192,128]{2,1,0:T(8,128)(2,1)S(1)} %collective-permute-done.11.rest_2_, ...), custom_call_target="tpu_custom_call" | custom-call | tf_op jit(solution)/shard_map/finish/pallas_call | solution.py:505
  (56 shorter events, 7.7 us)
Async XLA Ops:
  0.6 9.1 %copy-start = (bf16[1024,360]{0,1:T(8,128)(2,1)S(1)}, bf16[1024,360]{0,1:T(8,128)(2,1)}, u32[]{:S(2)}) copy-start(bf16[1024,360]{0,1:T(8,128)(2,1)} %param.17) | copy-start | bytes 2211844
  0.6 25.8 %collective-permute-start.3 = (bf16[360,1024]{1,0:T(8,128)(2,1)}, bf16[360,1024]{1,0:T(8,128)(2,1)S(1)}, u32[]{:S(2)}, u32[]{:S(2)}) collective-permute-start(bf16[360,1024]{1,0:T(8,128)(2,1)} %bitcast.9), channel_id=1, source_target_pairs={{0,1},{1,0},{2,4},{3,5},{4,2},{5,3},{6,7},{7,6},{8,9},{9,8},{10,12... | collective-permute-start | bytes 2211848 | tf_op jit(solution)/shard_map/ppermute | solution.py:209
  7.8 10.7 %collective-permute-start = (bf16[64,2816]{1,0:T(8,128)(2,1)S(1)}, bf16[64,2816]{1,0:T(8,128)(2,1)S(1)}, u32[]{:S(2)}, u32[]{:S(2)}) collective-permute-start(bf16[64,2816]{1,0:T(8,128)(2,1)S(1)} %get-tuple-element.28), channel_id=1, source_target_pairs={{0,8},{8,0},{16,24},{24,16},{1,9},{9,1},{17,25},{25,17},{2,10},{10... | collective-permute-start | bytes 1081352 | tf_op jit(solution)/shard_map/ppermute | solution.py:193
  7.9 10.9 %collective-permute-start.1 = (bf16[64,1792]{1,0:T(8,128)(2,1)}, bf16[64,1792]{1,0:T(8,128)(2,1)S(1)}, u32[]{:S(2)}, u32[]{:S(2)}) collective-permute-start(bf16[64,1792]{1,0:T(8,128)(2,1)} %get-tuple-element.29), channel_id=1, source_target_pairs={{0,16},{8,24},{16,0},{24,8},{1,17},{9,25},{17,1},{25,9},{2,18},{10... | collective-permute-start | bytes 688136 | tf_op jit(solution)/shard_map/ppermute | solution.py:193
  9.5 11.1 %collective-permute-start.2 = (bf16[64,1792]{1,0:T(8,128)(2,1)S(1)}, bf16[64,1792]{1,0:T(8,128)(2,1)S(1)}, u32[]{:S(2)}, u32[]{:S(2)}) collective-permute-start(bf16[64,1792]{1,0:T(8,128)(2,1)S(1)} %get-tuple-element.30), channel_id=1, source_target_pairs={{0,24},{8,16},{16,8},{24,0},{1,25},{9,17},{17,9},{25,1},{2,26},{10... | collective-permute-start | bytes 688136 | tf_op jit(solution)/shard_map/ppermute | solution.py:193
  10.5 29.0 %collective-permute-start.8 = (bf16[192,1024]{1,0:T(8,128)(2,1)}, bf16[192,1024]{1,0:T(8,128)(2,1)S(1)}, u32[]{:S(2)}, u32[]{:S(2)}) collective-permute-start(bf16[192,1024]{1,0:T(8,128)(2,1)} %slice.21), channel_id=1, source_target_pairs={{0,6},{1,7},{2,3},{3,2},{4,5},{5,4},{6,0},{7,1},{8,14},{9,15},{10,... | collective-permute-start | bytes 1179656 | tf_op jit(solution)/shard_map/ppermute | solution.py:209
  16.8 1.6 %copy-start.10 = (bf16[168,1024]{1,0:T(8,128)(2,1)S(1)}, bf16[168,1024]{1,0:T(8,128)(2,1)}, u32[]{:S(2)}) copy-start(bf16[168,1024]{1,0:T(8,128)(2,1)} %slice.22) | copy-start | bytes 1032196
  18.5 22.6 %collective-permute-start.9 = (bf16[168,1024]{1,0:T(8,128)(2,1)S(1)}, bf16[168,1024]{1,0:T(8,128)(2,1)S(1)}, u32[]{:S(2)}, u32[]{:S(2)}) collective-permute-start(bf16[168,1024]{1,0:T(8,128)(2,1)S(1)} %copy-done.10), channel_id=1, source_target_pairs={{0,6},{1,7},{2,3},{3,2},{4,5},{5,4},{6,0},{7,1},{8,14},{9,15},{10,... | collective-permute-start | bytes 1032200 | tf_op jit(solution)/shard_map/ppermute | solution.py:209
  21.2 5.1 %copy-start.5 = (bf16[1,64,1024]{2,1,0:T(8,128)(2,1)S(1)}, bf16[1,64,1024]{2,1,0:T(8,128)(2,1)}, u32[]{:S(2)}) copy-start(bf16[1,64,1024]{2,1,0:T(8,128)(2,1)} %param.11) | copy-start | bytes 393220
  26.4 15.4 %collective-permute-start.4 = (bf16[128,1024]{1,0:T(8,128)(2,1)S(1)}, bf16[128,1024]{1,0:T(8,128)(2,1)S(1)}, u32[]{:S(2)}, u32[]{:S(2)}) collective-permute-start(bf16[128,1024]{1,0:T(8,128)(2,1)S(1)} %pad_maximum_fusion.rest_0_), channel_id=1, source_target_pairs={{0,16},{8,24},{16,0},{24,8},{1,17},{9,25},{17,1},{25,9},{2,18},{10... | collective-permute-start | bytes 786440 | tf_op jit(solution)/shard_map/ppermute | solution.py:193
  28.0 22.3 %collective-permute-start.6 = (bf16[1024,256]{1,0:T(8,128)(2,1)S(1)}, bf16[1024,256]{1,0:T(8,128)(2,1)S(1)}, u32[]{:S(2)}, u32[]{:S(2)}) collective-permute-start(bf16[1024,256]{1,0:T(8,128)(2,1)S(1)} %attention.1.refs_0_), channel_id=1, source_target_pairs={{0,2},{1,3},{2,0},{3,1},{4,6},{5,7},{6,4},{7,5},{8,10},{9,11},{10,... | collective-permute-start | bytes 1572872 | tf_op jit(solution)/shard_map/ppermute | solution.py:195
  39.5 2.2 %copy-start.2 = (bf16[1,8,16,1024]{3,2,1,0:T(8,128)(2,1)S(1)}, bf16[1,8,16,1024]{3,2,1,0:T(8,128)(2,1)}, u32[]{:S(2)}) copy-start(bf16[1,8,16,1024]{3,2,1,0:T(8,128)(2,1)} %param.12) | copy-start | bytes 786436
  39.5 16.9 %collective-permute-start.13 = (bf16[192,1024]{1,0:T(8,128)(2,1)S(1)}, bf16[192,1024]{1,0:T(8,128)(2,1)S(1)}, u32[]{:S(2)}, u32[]{:S(2)}) collective-permute-start(bf16[192,1024]{1,0:T(8,128)(2,1)S(1)} %slice_select_fusion), channel_id=1, source_target_pairs={{0,1},{1,0},{2,3},{3,2},{4,5},{5,4},{6,7},{7,6},{8,9},{9,8},{10,11... | collective-permute-start | bytes 1179656 | tf_op jit(solution)/shard_map/ppermute | solution.py:195
  41.2 15.2 %collective-permute-start.14 = (bf16[168,1024]{1,0:T(8,128)(2,1)S(1)}, bf16[168,1024]{1,0:T(8,128)(2,1)S(1)}, u32[]{:S(2)}, u32[]{:S(2)}) collective-permute-start(bf16[168,1024]{1,0:T(8,128)(2,1)S(1)} %slice_select_fusion.1), channel_id=1, source_target_pairs={{0,1},{1,0},{2,3},{3,2},{4,5},{5,4},{6,7},{7,6},{8,9},{9,8},{10,11... | collective-permute-start | bytes 1032200 | tf_op jit(solution)/shard_map/ppermute | solution.py:195
  44.1 1.5 %collective-permute-start.5 = (bf16[2,360,128]{2,1,0:T(8,128)(2,1)S(1)}, bf16[2,360,128]{2,1,0:T(8,128)(2,1)S(1)}, u32[]{:S(2)}, u32[]{:S(2)}) collective-permute-start(bf16[2,360,128]{2,1,0:T(8,128)(2,1)S(1)} %get-tuple-element.36), channel_id=1, source_target_pairs={{0,8},{8,0},{16,24},{24,16},{1,9},{9,1},{17,25},{25,17},{2,10},{10... | collective-permute-start | bytes 552968 | tf_op jit(solution)/shard_map/ppermute | solution.py:193
  45.7 4.9 %collective-permute-start.7 = (bf16[2,192,128]{2,1,0:T(8,128)(2,1)S(1)}, bf16[2,192,128]{2,1,0:T(8,128)(2,1)S(1)}, u32[]{:S(2)}, u32[]{:S(2)}) collective-permute-start(bf16[2,192,128]{2,1,0:T(8,128)(2,1)S(1)} %get-tuple-element.38), channel_id=1, source_target_pairs={{0,16},{8,24},{16,0},{24,8},{1,17},{9,25},{17,1},{25,9},{2,18},{10... | collective-permute-start | bytes 294920 | tf_op jit(solution)/shard_map/ppermute | solution.py:193
  51.3 5.9 %collective-permute-start.10 = (bf16[3,360,128]{2,1,0:T(8,128)(2,1)S(1)}, bf16[3,360,128]{2,1,0:T(8,128)(2,1)S(1)}, u32[]{:S(2)}, u32[]{:S(2)}) collective-permute-start(bf16[3,360,128]{2,1,0:T(8,128)(2,1)S(1)} %get-tuple-element.42), channel_id=1, source_target_pairs={{0,8},{8,0},{16,24},{24,16},{1,9},{9,1},{17,25},{25,17},{2,10},{10... | collective-permute-start | bytes 829448 | tf_op jit(solution)/shard_map/ppermute | solution.py:193
  57.2 2.3 %collective-permute-start.15 = (bf16[3,360,128]{2,1,0:T(8,128)(2,1)S(1)}, bf16[3,360,128]{2,1,0:T(8,128)(2,1)S(1)}, u32[]{:S(2)}, u32[]{:S(2)}) collective-permute-start(bf16[3,360,128]{2,1,0:T(8,128)(2,1)S(1)} %get-tuple-element.46), channel_id=1, source_target_pairs={{0,8},{8,0},{16,24},{24,16},{1,9},{9,1},{17,25},{25,17},{2,10},{10... | collective-permute-start | bytes 829448 | tf_op jit(solution)/shard_map/ppermute | solution.py:193
  57.4 11.6 %copy-start.6 = (bf16[1,64,2880]{2,1,0:T(8,128)(2,1)S(1)}, bf16[1,64,2880]{2,1,0:T(8,128)(2,1)}, u32[]{:S(2)}) copy-start(bf16[1,64,2880]{2,1,0:T(8,128)(2,1)} %param.9) | copy-start | bytes 1105924
  57.4 11.6 %collective-permute-start.11 = (bf16[3,192,128]{2,1,0:T(8,128)(2,1)S(1)}, bf16[3,192,128]{2,1,0:T(8,128)(2,1)S(1)}, u32[]{:S(2)}, u32[]{:S(2)}) collective-permute-start(bf16[3,192,128]{2,1,0:T(8,128)(2,1)S(1)} %get-tuple-element.43), channel_id=1, source_target_pairs={{0,2},{1,3},{2,0},{3,1},{4,6},{5,7},{6,4},{7,5},{8,10},{9,11},{10,... | collective-permute-start | bytes 442376 | tf_op jit(solution)/shard_map/ppermute | solution.py:195
  57.8 11.2 %collective-permute-start.12 = (bf16[3,192,128]{2,1,0:T(8,128)(2,1)S(1)}, bf16[3,192,128]{2,1,0:T(8,128)(2,1)S(1)}, u32[]{:S(2)}, u32[]{:S(2)}) collective-permute-start(bf16[3,192,128]{2,1,0:T(8,128)(2,1)S(1)} %get-tuple-element.44), channel_id=1, source_target_pairs={{0,18},{1,19},{2,16},{3,17},{4,22},{5,23},{6,20},{7,21},{8,26},{9,... | collective-permute-start | bytes 442376 | tf_op jit(solution)/shard_map/ppermute | solution.py:200
  59.6 9.4 %collective-permute-start.16 = (bf16[2,192,128]{2,1,0:T(8,128)(2,1)S(1)}, bf16[2,192,128]{2,1,0:T(8,128)(2,1)S(1)}, u32[]{:S(2)}, u32[]{:S(2)}) collective-permute-start(bf16[2,192,128]{2,1,0:T(8,128)(2,1)S(1)} %get-tuple-element.48), channel_id=1, source_target_pairs={{0,16},{8,24},{16,0},{24,8},{1,17},{9,25},{17,1},{25,9},{2,18},{10... | collective-permute-start | bytes 294920 | tf_op jit(solution)/shard_map/ppermute | solution.py:193
  61.2 7.2 %collective-permute-start.17 = (bf16[1,192,128]{2,1,0:T(8,128)(2,1)S(1)}, bf16[1,192,128]{2,1,0:T(8,128)(2,1)S(1)}, u32[]{:S(2)}, u32[]{:S(2)}) collective-permute-start(bf16[1,192,128]{2,1,0:T(8,128)(2,1)S(1)} %get-tuple-element.49), channel_id=1, source_target_pairs={{0,2},{1,3},{2,0},{3,1},{4,6},{5,7},{6,4},{7,5},{8,10},{9,11},{10,... | collective-permute-start | bytes 147464 | tf_op jit(solution)/shard_map/ppermute | solution.py:195
  61.5 7.5 %collective-permute-start.18 = (bf16[1,192,128]{2,1,0:T(8,128)(2,1)S(1)}, bf16[1,192,128]{2,1,0:T(8,128)(2,1)S(1)}, u32[]{:S(2)}, u32[]{:S(2)}) collective-permute-start(bf16[1,192,128]{2,1,0:T(8,128)(2,1)S(1)} %get-tuple-element.50), channel_id=1, source_target_pairs={{0,18},{1,19},{2,16},{3,17},{4,22},{5,23},{6,20},{7,21},{8,26},{9,... | collective-permute-start | bytes 147464 | tf_op jit(solution)/shard_map/ppermute | solution.py:200
  (6 other events, 4.9 us)

commit v5 on v4

--- a/solution.py
+++ b/solution.py
@@ -526,12 +526,12 @@
     pool_rows = slots_dev * page_size
     weight = out_weight.T
     cols = weight.shape[0]
-    cut = fold_rows(cols)
+    cuts = [slice(cols * i // 360, cols * j // 360) for i, j in zip((0, 200), (200, 360))]
     first = swap_blocks(weight, FAR_BIT, NEAR_BIT)
 
     pieces = pack(queries[0], new_kv[0], kv_pool[0].reshape(pool_rows, 2 * kv_width), n_req)
     pieces = [pieces[0]] + [swap(pieces[k], k, 0) for k in range(1, n_req)]
-    second = [swap_blocks(chunk, NEAR_BIT, FAR_BIT) for chunk in (weight[:cut], weight[cut:])]
+    second = [swap_blocks(weight[cuts[0]], NEAR_BIT, FAR_BIT)]
 
     position = cached_pages[0] * page_size + jnp.arange(n_req * tok)
     frequency = THETA ** (-2.0 * jnp.arange(HD // 2).astype(F32) / HD)
@@ -545,10 +545,12 @@
         head_count // kv_heads, pool_rows, page_size,
     )
     chip_rows = jnp.concatenate([new_kv[0], pieces[1][:, -2 * kv_width :]], axis=0)
+    ctx, later = lax.optimization_barrier((ctx, weight))
+    second += [swap_blocks(later[cuts[1]], NEAR_BIT, FAR_BIT)]
     ctx, first, chip_rows = lax.optimization_barrier((ctx, first, chip_rows))
     ctx_mate = swap(ctx, 0, PAIR_BIT)
     inner = is_inner(lax.axis_index("exp"))
-    far = [jnp.where(inner, first[:cut], second[0]), jnp.where(inner, first[cut:], second[1])]
+    far = [jnp.where(inner, first[rows], piece) for rows, piece in zip(cuts, second)]
     both = [swap(chunk, 0, NEAR_BIT) for chunk in far]
     pool_out = write_pool(new_slots, cosine, sine, kv_pool[0], [chip_rows, swap(chip_rows, 2, 0)])
 

time: 70.7 us -> 67.7 us (0.958)
  starting transfers between devices: 30.4 us -> 26.3 us
  waiting for transfers between devices: 18.4 us -> 22.3 us
  other arithmetic: 2.99 us -> 0.92 us
    ppermute x9, waiting for transfers between devices: 3.54 us -> 10.1 us  [swap(): lax.ppermute(values, 'req', [(i, i ^ req_bits) for i in range(lax.axis_si...]
    ppermute x5, starting transfers between devices: 14.3 us -> 8.02 us  [swap(): lax.ppermute(values, 'exp', [(i, i ^ exp_bits) for i in range(lax.axis_si...]
    ppermute x5, waiting for transfers between devices: 14.2 us -> 10.4 us  [swap(): lax.ppermute(values, 'exp', [(i, i ^ exp_bits) for i in range(lax.axis_si...]
    ppermute x3, starting transfers between devices: 6.89 us -> 10.2 us  [swap_blocks(): return lax.ppermute(values, 'exp', pairs)]
    concatenate x1, other arithmetic: 1.59 us -> 0.27 us  [paired_plan(): cosine = jnp.concatenate([cosine] * 4, axis=1)]
    ppermute x2, starting transfers between devices: 3.37 us -> 2.07 us  [swap(): return lax.ppermute(values, ('req', 'exp'), pairs)]
    ppermute x2, waiting for transfers between devices: 0.6 us -> 1.81 us  [swap(): return lax.ppermute(values, ('req', 'exp'), pairs)]
    neg x1, other arithmetic: 1.29 us -> 0.54 us  [paired_plan(): sine = jnp.concatenate([-sine, sine, -sine, sine], axis=1)]
  transfers between devices with their start and end apart: 19 -> 19, of which waited for: 7 -> 9; matrix products, arithmetic and copies ran while one was open for 6% -> 4% of each run, Pallas kernels for 15% -> 15%
where the time goes in v5:
time: 67.7 us; the launch traced here: 67.4 us
  starting transfers between devices  26.3 us (39%)
  waiting for transfers between devices  22.3 us (33%)
  Pallas kernels  11.3 us (17%)
  local copies, waits for them, and re-layouts  5.12 us (8%)
  between operations  1.48 us (2%)
  other arithmetic  0.92 us (1%)
    ppermute x5, waiting for transfers between devices, swap(): lax.ppermute(values, 'exp', [(i, i ^ exp_bits) for i in range(lax.axis_si...  10.4 us
    ppermute x3, starting transfers between devices, swap_blocks(): return lax.ppermute(values, 'exp', pairs)  10.2 us
    ppermute x9, waiting for transfers between devices, swap(): lax.ppermute(values, 'req', [(i, i ^ req_bits) for i in range(lax.axis_si...  10.1 us
    ppermute x5, starting transfers between devices, swap(): lax.ppermute(values, 'exp', [(i, i ^ exp_bits) for i in range(lax.axis_si...  8.02 us
    ppermute x9, starting transfers between devices, swap(): lax.ppermute(values, 'req', [(i, i ^ req_bits) for i in range(lax.axis_si...  5.98 us
    pallas_call x1, Pallas kernels, attention(): pl.pallas_call(functools.partial(attention_kernel, kv_dev=kv_dev, per_kv=...  5.13 us
    unnamed x18, local copies, waits for them, and re-layouts  3.59 us
    pallas_call x3, Pallas kernels, project(): pl.pallas_call(functools.partial(project_kernel, n_ctx=len(contexts), cou...  2.08 us
  transfers between devices with their start and end apart: 19, of which 9 were waited for; matrix products, arithmetic and copies ran while one was open for 4% of the time, Pallas kernels for 15%

profile of v5, /device:TPU:0, one launch (start us, length us, event | category | flops | bytes accessed | tf_op | source)
XLA Modules:
  0.0 67.4 jit_solution(787646197656670093)
XLA Ops:
  0.6 3.0 %collective-permute-start.3 = (bf16[360,1024]{1,0:T(8,128)(2,1)}, bf16[360,1024]{1,0:T(8,128)(2,1)S(1)}, u32[]{:S(2)}, u32[]{:S(2)}) collective-permute-start(bf16[360,1024]{1,0:T(8,128)(2,1)} %bitcast.9), channel_id=1, source_target_pairs={{0,1},{1,0},{2,4},{3,5},{4,2},{5,3},{6,7},{7,6},{8,9},{9,8},{10,12... | collective-permute-start | bytes 2211848 | tf_op jit(solution)/shard_map/ppermute | solution.py:209
  3.6 0.9 %copy-done.1 = bf16[1,8,16,1024]{3,2,1,0:T(8,128)(2,1)S(1)} copy-done((bf16[1,8,16,1024]{3,2,1,0:T(8,128)(2,1)S(1)}, bf16[1,8,16,1024]{3,2,1,0:T(8,128)(2,1)}, u32[]{:S(2)}) %copy-start.1) | copy-done | bytes 262168
  4.6 1.0 %copy-done.3 = bf16[1,64,4096]{2,1,0:T(8,128)(2,1)S(1)} copy-done((bf16[1,64,4096]{2,1,0:T(8,128)(2,1)S(1)}, bf16[1,64,4096]{2,1,0:T(8,128)(2,1)}, u32[]{:S(2)}) %copy-start.3) | copy-done | bytes 524312
  5.6 0.9 %copy-done.4 = bf16[1,64,1024]{2,1,0:T(8,128)(2,1)S(1)} copy-done((bf16[1,64,1024]{2,1,0:T(8,128)(2,1)S(1)}, bf16[1,64,1024]{2,1,0:T(8,128)(2,1)}, u32[]{:S(2)}) %copy-start.4) | copy-done | bytes 131096
  7.2 1.6 %collective-permute-start.1 = (bf16[64,1792]{1,0:T(8,128)(2,1)S(1)}, bf16[64,1792]{1,0:T(8,128)(2,1)S(1)}, u32[]{:S(2)}, u32[]{:S(2)}) collective-permute-start(bf16[64,1792]{1,0:T(8,128)(2,1)S(1)} %get-tuple-element.31), channel_id=1, source_target_pairs={{0,16},{8,24},{16,0},{24,8},{1,17},{9,25},{17,1},{25,9},{2,18},{10... | collective-permute-start | bytes 688136 | tf_op jit(solution)/shard_map/ppermute | solution.py:193
  9.0 0.8 %slice.21 = bf16[200,1024]{1,0:T(8,128)(2,1)} slice(bf16[360,1024]{1,0:T(8,128)(2,1)S(1)} %bitcast.10), slice={[0:200], [0:1024]} | slice | bytes 819200 | tf_op jit(solution)/shard_map/slice | solution.py:534
  9.8 3.6 %collective-permute-start.8 = (bf16[200,1024]{1,0:T(8,128)(2,1)}, bf16[200,1024]{1,0:T(8,128)(2,1)S(1)}, u32[]{:S(2)}, u32[]{:S(2)}) collective-permute-start(bf16[200,1024]{1,0:T(8,128)(2,1)} %slice.21), channel_id=1, source_target_pairs={{0,6},{1,7},{2,3},{3,2},{4,5},{5,4},{6,0},{7,1},{8,14},{9,15},{10,... | collective-permute-start | bytes 1228808 | tf_op jit(solution)/shard_map/ppermute | solution.py:209
  15.7 4.0 %collective-permute-done.2.rest_3_ = bf16[64,1792]{1,0:T(8,128)(2,1)S(1)} collective-permute-done((bf16[64,1792]{1,0:T(8,128)(2,1)S(1)}, bf16[64,1792]{1,0:T(8,128)(2,1)S(1)}, u32[]{:S(2)}, u32[]{:S(2)}) %collective-permute-start.2) | collective-permute-done | bytes 229408 | tf_op jit(solution)/shard_map/ppermute | solution.py:193
  20.3 5.1 %attention.1.refs_0_ = bf16[1024,256]{1,0:T(8,128)(2,1)S(1)} custom-call(s32[1]{0:T(128)S(6)} %copy.12.pages_ref, s32[1,16]{1,0:T(1,128)S(1)} %copy-done.7, f32[64]{0:T(128)S(1)} %copy-done.8, f32[256,128]{1,0:T(8,128)S(1)} %get-tuple-element.59.cos_ref, f32[256,128]{1,0:T(8,128)S(1)} %get-tuple-element.60.sin_ref, ...), custom_call_target="tpu_custom_call" | custom-call | tf_op jit(solution)/shard_map/attention/pallas_call | solution.py:361
  26.2 3.6 %collective-permute-start.9 = (bf16[160,1024]{1,0:T(8,128)(2,1)}, bf16[160,1024]{1,0:T(8,128)(2,1)S(1)}, u32[]{:S(2)}, u32[]{:S(2)}) collective-permute-start(bf16[160,1024]{1,0:T(8,128)(2,1)} %slice.17), channel_id=1, source_target_pairs={{0,6},{1,7},{2,3},{3,2},{4,5},{5,4},{6,0},{7,1},{8,14},{9,15},{10,... | collective-permute-start | bytes 983048 | tf_op jit(solution)/shard_map/ppermute | solution.py:209
  29.9 1.6 %collective-permute-start.4 = (bf16[128,1024]{1,0:T(8,128)(2,1)S(1)}, bf16[128,1024]{1,0:T(8,128)(2,1)S(1)}, u32[]{:S(2)}, u32[]{:S(2)}) collective-permute-start(bf16[128,1024]{1,0:T(8,128)(2,1)S(1)} %pad_maximum_fusion.rest_0_), channel_id=1, source_target_pairs={{0,16},{8,24},{16,0},{24,8},{1,17},{9,25},{17,1},{25,9},{2,18},{10... | collective-permute-start | bytes 786440 | tf_op jit(solution)/shard_map/ppermute | solution.py:193
  31.5 1.0 %collective-permute-start.6 = (bf16[1024,256]{1,0:T(8,128)(2,1)S(1)}, bf16[1024,256]{1,0:T(8,128)(2,1)S(1)}, u32[]{:S(2)}, u32[]{:S(2)}) collective-permute-start(bf16[1024,256]{1,0:T(8,128)(2,1)S(1)} %attention.1.refs_0_), channel_id=1, source_target_pairs={{0,2},{1,3},{2,0},{3,1},{4,6},{5,7},{6,4},{7,5},{8,10},{9,11},{10,... | collective-permute-start | bytes 1572872 | tf_op jit(solution)/shard_map/ppermute | solution.py:195
  32.5 1.6 %collective-permute-start.13 = (bf16[200,1024]{1,0:T(8,128)(2,1)S(1)}, bf16[200,1024]{1,0:T(8,128)(2,1)S(1)}, u32[]{:S(2)}, u32[]{:S(2)}) collective-permute-start(bf16[200,1024]{1,0:T(8,128)(2,1)S(1)} %slice_select_fusion), channel_id=1, source_target_pairs={{0,1},{1,0},{2,3},{3,2},{4,5},{5,4},{6,7},{7,6},{8,9},{9,8},{10,11... | collective-permute-start | bytes 1228808 | tf_op jit(solution)/shard_map/ppermute | solution.py:195
  34.1 4.4 %collective-permute-done.4.rest_1_ = bf16[128,1024]{1,0:T(8,128)(2,1)S(1)} collective-permute-done((bf16[128,1024]{1,0:T(8,128)(2,1)S(1)}, bf16[128,1024]{1,0:T(8,128)(2,1)S(1)}, u32[]{:S(2)}, u32[]{:S(2)}) %collective-permute-start.4) | collective-permute-done | bytes 262176 | tf_op jit(solution)/shard_map/ppermute | solution.py:193
  38.5 1.7 %write_pool.1 = bf16[8,16,1024]{2,1,0:T(8,128)(2,1)} custom-call(s32[1,16]{1,0:T(1,128)S(1)} %copy-done.6, f32[256,128]{1,0:T(8,128)S(1)} %get-tuple-element.59.cos_ref, f32[256,128]{1,0:T(8,128)S(1)} %get-tuple-element.60.sin_ref, bf16[8,16,1024]{2,1,0:T(8,128)(2,1)S(1)} %bitcast.15, bf16[128,1024]{1,0:T(8,128)(2,1)S(1)} %pad_maximum_fusion.rest_0_, ...), custom_call_target="tpu_custom_call" | custom-call | tf_op jit(solution)/shard_map/write_pool/pallas_call | solution.py:407
  42.3 1.6 %collective-permute-start.7 = (bf16[2,192,128]{2,1,0:T(8,128)(2,1)S(1)}, bf16[2,192,128]{2,1,0:T(8,128)(2,1)S(1)}, u32[]{:S(2)}, u32[]{:S(2)}) collective-permute-start(bf16[2,192,128]{2,1,0:T(8,128)(2,1)S(1)} %get-tuple-element.41), channel_id=1, source_target_pairs={{0,16},{8,24},{16,0},{24,8},{1,17},{9,25},{17,1},{25,9},{2,18},{10... | collective-permute-start | bytes 294920 | tf_op jit(solution)/shard_map/ppermute | solution.py:193
  43.9 5.8 %collective-permute-done.6.refs_0_.refs_1_ = bf16[1024,256]{1,0:T(8,128)(2,1)S(1)} collective-permute-done((bf16[1024,256]{1,0:T(8,128)(2,1)S(1)}, bf16[1024,256]{1,0:T(8,128)(2,1)S(1)}, u32[]{:S(2)}, u32[]{:S(2)}) %collective-permute-start.6) | collective-permute-done | bytes 524320 | tf_op jit(solution)/shard_map/ppermute | solution.py:195
  52.3 2.9 %collective-permute-start.11 = (bf16[3,192,128]{2,1,0:T(8,128)(2,1)S(1)}, bf16[3,192,128]{2,1,0:T(8,128)(2,1)S(1)}, u32[]{:S(2)}, u32[]{:S(2)}) collective-permute-start(bf16[3,192,128]{2,1,0:T(8,128)(2,1)S(1)} %get-tuple-element.47), channel_id=1, source_target_pairs={{0,2},{1,3},{2,0},{3,1},{4,6},{5,7},{6,4},{7,5},{8,10},{9,11},{10,... | collective-permute-start | bytes 442376 | tf_op jit(solution)/shard_map/ppermute | solution.py:195
  55.2 1.0 %collective-permute-start.12 = (bf16[3,192,128]{2,1,0:T(8,128)(2,1)S(1)}, bf16[3,192,128]{2,1,0:T(8,128)(2,1)S(1)}, u32[]{:S(2)}, u32[]{:S(2)}) collective-permute-start(bf16[3,192,128]{2,1,0:T(8,128)(2,1)S(1)} %get-tuple-element.48), channel_id=1, source_target_pairs={{0,18},{1,19},{2,16},{3,17},{4,22},{5,23},{6,20},{7,21},{8,26},{9,... | collective-permute-start | bytes 442376 | tf_op jit(solution)/shard_map/ppermute | solution.py:200
  56.9 1.9 %collective-permute-start.17 = (bf16[1,192,128]{2,1,0:T(8,128)(2,1)S(1)}, bf16[1,192,128]{2,1,0:T(8,128)(2,1)S(1)}, u32[]{:S(2)}, u32[]{:S(2)}) collective-permute-start(bf16[1,192,128]{2,1,0:T(8,128)(2,1)S(1)} %get-tuple-element.53), channel_id=1, source_target_pairs={{0,2},{1,3},{2,0},{3,1},{4,6},{5,7},{6,4},{7,5},{8,10},{9,11},{10,... | collective-permute-start | bytes 147464 | tf_op jit(solution)/shard_map/ppermute | solution.py:195
  58.9 1.0 %collective-permute-start.18 = (bf16[1,192,128]{2,1,0:T(8,128)(2,1)S(1)}, bf16[1,192,128]{2,1,0:T(8,128)(2,1)S(1)}, u32[]{:S(2)}, u32[]{:S(2)}) collective-permute-start(bf16[1,192,128]{2,1,0:T(8,128)(2,1)S(1)} %get-tuple-element.54), channel_id=1, source_target_pairs={{0,18},{1,19},{2,16},{3,17},{4,22},{5,23},{6,20},{7,21},{8,26},{9,... | collective-permute-start | bytes 147464 | tf_op jit(solution)/shard_map/ppermute | solution.py:200
  59.9 4.2 %collective-permute-done.17.rest_6_ = bf16[1,192,128]{2,1,0:T(8,128)(2,1)S(1)} collective-permute-done((bf16[1,192,128]{2,1,0:T(8,128)(2,1)S(1)}, bf16[1,192,128]{2,1,0:T(8,128)(2,1)S(1)}, u32[]{:S(2)}, u32[]{:S(2)}) %collective-permute-start.17) | collective-permute-done | bytes 49184 | tf_op jit(solution)/shard_map/ppermute | solution.py:195
  64.1 1.8 %collective-permute-done.18.rest_7_ = bf16[1,192,128]{2,1,0:T(8,128)(2,1)S(1)} collective-permute-done((bf16[1,192,128]{2,1,0:T(8,128)(2,1)S(1)}, bf16[1,192,128]{2,1,0:T(8,128)(2,1)S(1)}, u32[]{:S(2)}, u32[]{:S(2)}) %collective-permute-start.18) | collective-permute-done | bytes 49184 | tf_op jit(solution)/shard_map/ppermute | solution.py:200
  66.0 1.4 %finish.1 = bf16[64,2880]{1,0:T(8,128)(2,1)} custom-call(bf16[64,2880]{1,0:T(8,128)(2,1)S(1)} %bitcast.19, bf16[2,192,128]{2,1,0:T(8,128)(2,1)S(1)} %get-tuple-element.40.rest_0_, bf16[2,192,128]{2,1,0:T(8,128)(2,1)S(1)} %collective-permute-done.7.rest_1_, bf16[3,192,128]{2,1,0:T(8,128)(2,1)S(1)} %collective-permute-done.11.rest_2_, ...), custom_call_target="tpu_custom_call" | custom-call | tf_op jit(solution)/shard_map/finish/pallas_call | solution.py:505
  (52 shorter events, 9.4 us)
Async XLA Ops:
  0.6 8.4 %copy-start = (bf16[1024,360]{0,1:T(8,128)(2,1)S(1)}, bf16[1024,360]{0,1:T(8,128)(2,1)}, u32[]{:S(2)}) copy-start(bf16[1024,360]{0,1:T(8,128)(2,1)} %param.17) | copy-start | bytes 2211844
  0.6 29.2 %collective-permute-start.3 = (bf16[360,1024]{1,0:T(8,128)(2,1)}, bf16[360,1024]{1,0:T(8,128)(2,1)S(1)}, u32[]{:S(2)}, u32[]{:S(2)}) collective-permute-start(bf16[360,1024]{1,0:T(8,128)(2,1)} %bitcast.9), channel_id=1, source_target_pairs={{0,1},{1,0},{2,4},{3,5},{4,2},{5,3},{6,7},{7,6},{8,9},{9,8},{10,12... | collective-permute-start | bytes 2211848 | tf_op jit(solution)/shard_map/ppermute | solution.py:209
  4.6 1.0 %copy-start.3 = (bf16[1,64,4096]{2,1,0:T(8,128)(2,1)S(1)}, bf16[1,64,4096]{2,1,0:T(8,128)(2,1)}, u32[]{:S(2)}) copy-start(bf16[1,64,4096]{2,1,0:T(8,128)(2,1)} %param.10) | copy-start | bytes 1572868
  7.1 12.6 %collective-permute-start = (bf16[64,2816]{1,0:T(8,128)(2,1)S(1)}, bf16[64,2816]{1,0:T(8,128)(2,1)S(1)}, u32[]{:S(2)}, u32[]{:S(2)}) collective-permute-start(bf16[64,2816]{1,0:T(8,128)(2,1)S(1)} %get-tuple-element.30), channel_id=1, source_target_pairs={{0,8},{8,0},{16,24},{24,16},{1,9},{9,1},{17,25},{25,17},{2,10},{10... | collective-permute-start | bytes 1081352 | tf_op jit(solution)/shard_map/ppermute | solution.py:193
  7.2 8.5 %collective-permute-start.1 = (bf16[64,1792]{1,0:T(8,128)(2,1)S(1)}, bf16[64,1792]{1,0:T(8,128)(2,1)S(1)}, u32[]{:S(2)}, u32[]{:S(2)}) collective-permute-start(bf16[64,1792]{1,0:T(8,128)(2,1)S(1)} %get-tuple-element.31), channel_id=1, source_target_pairs={{0,16},{8,24},{16,0},{24,8},{1,17},{9,25},{17,1},{25,9},{2,18},{10... | collective-permute-start | bytes 688136 | tf_op jit(solution)/shard_map/ppermute | solution.py:193
  8.8 10.9 %collective-permute-start.2 = (bf16[64,1792]{1,0:T(8,128)(2,1)S(1)}, bf16[64,1792]{1,0:T(8,128)(2,1)S(1)}, u32[]{:S(2)}, u32[]{:S(2)}) collective-permute-start(bf16[64,1792]{1,0:T(8,128)(2,1)S(1)} %get-tuple-element.32), channel_id=1, source_target_pairs={{0,24},{8,16},{16,8},{24,0},{1,25},{9,17},{17,9},{25,1},{2,26},{10... | collective-permute-start | bytes 688136 | tf_op jit(solution)/shard_map/ppermute | solution.py:193
  9.8 22.6 %collective-permute-start.8 = (bf16[200,1024]{1,0:T(8,128)(2,1)}, bf16[200,1024]{1,0:T(8,128)(2,1)S(1)}, u32[]{:S(2)}, u32[]{:S(2)}) collective-permute-start(bf16[200,1024]{1,0:T(8,128)(2,1)} %slice.21), channel_id=1, source_target_pairs={{0,6},{1,7},{2,3},{3,2},{4,5},{5,4},{6,0},{7,1},{8,14},{9,15},{10,... | collective-permute-start | bytes 1228808 | tf_op jit(solution)/shard_map/ppermute | solution.py:209
  26.2 14.6 %collective-permute-start.9 = (bf16[160,1024]{1,0:T(8,128)(2,1)}, bf16[160,1024]{1,0:T(8,128)(2,1)S(1)}, u32[]{:S(2)}, u32[]{:S(2)}) collective-permute-start(bf16[160,1024]{1,0:T(8,128)(2,1)} %slice.17), channel_id=1, source_target_pairs={{0,6},{1,7},{2,3},{3,2},{4,5},{5,4},{6,0},{7,1},{8,14},{9,15},{10,... | collective-permute-start | bytes 983048 | tf_op jit(solution)/shard_map/ppermute | solution.py:209
  29.9 8.6 %collective-permute-start.4 = (bf16[128,1024]{1,0:T(8,128)(2,1)S(1)}, bf16[128,1024]{1,0:T(8,128)(2,1)S(1)}, u32[]{:S(2)}, u32[]{:S(2)}) collective-permute-start(bf16[128,1024]{1,0:T(8,128)(2,1)S(1)} %pad_maximum_fusion.rest_0_), channel_id=1, source_target_pairs={{0,16},{8,24},{16,0},{24,8},{1,17},{9,25},{17,1},{25,9},{2,18},{10... | collective-permute-start | bytes 786440 | tf_op jit(solution)/shard_map/ppermute | solution.py:193
  31.5 7.0 %copy-start.2 = (bf16[1,8,16,1024]{3,2,1,0:T(8,128)(2,1)S(1)}, bf16[1,8,16,1024]{3,2,1,0:T(8,128)(2,1)}, u32[]{:S(2)}) copy-start(bf16[1,8,16,1024]{3,2,1,0:T(8,128)(2,1)} %param.12) | copy-start | bytes 786436
  31.5 18.2 %collective-permute-start.6 = (bf16[1024,256]{1,0:T(8,128)(2,1)S(1)}, bf16[1024,256]{1,0:T(8,128)(2,1)S(1)}, u32[]{:S(2)}, u32[]{:S(2)}) collective-permute-start(bf16[1024,256]{1,0:T(8,128)(2,1)S(1)} %attention.1.refs_0_), channel_id=1, source_target_pairs={{0,2},{1,3},{2,0},{3,1},{4,6},{5,7},{6,4},{7,5},{8,10},{9,11},{10,... | collective-permute-start | bytes 1572872 | tf_op jit(solution)/shard_map/ppermute | solution.py:195
  32.5 5.9 %copy-start.6 = (s32[1,16]{1,0:T(1,128)S(1)}, s32[1,16]{1,0:T(1,128)}, u32[]{:S(2)}) copy-start(s32[1,16]{1,0:T(1,128)} %slots_ref.1) | copy-start | bytes 196
  32.5 18.5 %collective-permute-start.13 = (bf16[200,1024]{1,0:T(8,128)(2,1)S(1)}, bf16[200,1024]{1,0:T(8,128)(2,1)S(1)}, u32[]{:S(2)}, u32[]{:S(2)}) collective-permute-start(bf16[200,1024]{1,0:T(8,128)(2,1)S(1)} %slice_select_fusion), channel_id=1, source_target_pairs={{0,1},{1,0},{2,3},{3,2},{4,5},{5,4},{6,7},{7,6},{8,9},{9,8},{10,11... | collective-permute-start | bytes 1228808 | tf_op jit(solution)/shard_map/ppermute | solution.py:195
  40.7 1.5 %collective-permute-start.5 = (bf16[2,360,128]{2,1,0:T(8,128)(2,1)S(1)}, bf16[2,360,128]{2,1,0:T(8,128)(2,1)S(1)}, u32[]{:S(2)}, u32[]{:S(2)}) collective-permute-start(bf16[2,360,128]{2,1,0:T(8,128)(2,1)S(1)} %get-tuple-element.39), channel_id=1, source_target_pairs={{0,8},{8,0},{16,24},{24,16},{1,9},{9,1},{17,25},{25,17},{2,10},{10... | collective-permute-start | bytes 552968 | tf_op jit(solution)/shard_map/ppermute | solution.py:193
  40.8 10.2 %collective-permute-start.14 = (bf16[160,1024]{1,0:T(8,128)(2,1)S(1)}, bf16[160,1024]{1,0:T(8,128)(2,1)S(1)}, u32[]{:S(2)}, u32[]{:S(2)}) collective-permute-start(bf16[160,1024]{1,0:T(8,128)(2,1)S(1)} %slice_select_fusion.1), channel_id=1, source_target_pairs={{0,1},{1,0},{2,3},{3,2},{4,5},{5,4},{6,7},{7,6},{8,9},{9,8},{10,11... | collective-permute-start | bytes 983048 | tf_op jit(solution)/shard_map/ppermute | solution.py:195
  42.3 7.4 %collective-permute-start.7 = (bf16[2,192,128]{2,1,0:T(8,128)(2,1)S(1)}, bf16[2,192,128]{2,1,0:T(8,128)(2,1)S(1)}, u32[]{:S(2)}, u32[]{:S(2)}) collective-permute-start(bf16[2,192,128]{2,1,0:T(8,128)(2,1)S(1)} %get-tuple-element.41), channel_id=1, source_target_pairs={{0,16},{8,24},{16,0},{24,8},{1,17},{9,25},{17,1},{25,9},{2,18},{10... | collective-permute-start | bytes 294920 | tf_op jit(solution)/shard_map/ppermute | solution.py:193
  50.5 1.6 %collective-permute-start.10 = (bf16[3,360,128]{2,1,0:T(8,128)(2,1)S(1)}, bf16[3,360,128]{2,1,0:T(8,128)(2,1)S(1)}, u32[]{:S(2)}, u32[]{:S(2)}) collective-permute-start(bf16[3,360,128]{2,1,0:T(8,128)(2,1)S(1)} %get-tuple-element.46), channel_id=1, source_target_pairs={{0,8},{8,0},{16,24},{24,16},{1,9},{9,1},{17,25},{25,17},{2,10},{10... | collective-permute-start | bytes 829448 | tf_op jit(solution)/shard_map/ppermute | solution.py:193
  51.8 4.4 %collective-permute-start.15 = (bf16[3,360,128]{2,1,0:T(8,128)(2,1)S(1)}, bf16[3,360,128]{2,1,0:T(8,128)(2,1)S(1)}, u32[]{:S(2)}, u32[]{:S(2)}) collective-permute-start(bf16[3,360,128]{2,1,0:T(8,128)(2,1)S(1)} %get-tuple-element.50), channel_id=1, source_target_pairs={{0,8},{8,0},{16,24},{24,16},{1,9},{9,1},{17,25},{25,17},{2,10},{10... | collective-permute-start | bytes 829448 | tf_op jit(solution)/shard_map/ppermute | solution.py:193
  52.3 13.7 %copy-start.5 = (bf16[1,64,2880]{2,1,0:T(8,128)(2,1)S(1)}, bf16[1,64,2880]{2,1,0:T(8,128)(2,1)}, u32[]{:S(2)}) copy-start(bf16[1,64,2880]{2,1,0:T(8,128)(2,1)} %param.9) | copy-start | bytes 1105924
  52.3 13.7 %collective-permute-start.11 = (bf16[3,192,128]{2,1,0:T(8,128)(2,1)S(1)}, bf16[3,192,128]{2,1,0:T(8,128)(2,1)S(1)}, u32[]{:S(2)}, u32[]{:S(2)}) collective-permute-start(bf16[3,192,128]{2,1,0:T(8,128)(2,1)S(1)} %get-tuple-element.47), channel_id=1, source_target_pairs={{0,2},{1,3},{2,0},{3,1},{4,6},{5,7},{6,4},{7,5},{8,10},{9,11},{10,... | collective-permute-start | bytes 442376 | tf_op jit(solution)/shard_map/ppermute | solution.py:195
  55.2 10.8 %collective-permute-start.12 = (bf16[3,192,128]{2,1,0:T(8,128)(2,1)S(1)}, bf16[3,192,128]{2,1,0:T(8,128)(2,1)S(1)}, u32[]{:S(2)}, u32[]{:S(2)}) collective-permute-start(bf16[3,192,128]{2,1,0:T(8,128)(2,1)S(1)} %get-tuple-element.48), channel_id=1, source_target_pairs={{0,18},{1,19},{2,16},{3,17},{4,22},{5,23},{6,20},{7,21},{8,26},{9,... | collective-permute-start | bytes 442376 | tf_op jit(solution)/shard_map/ppermute | solution.py:200
  56.4 9.6 %collective-permute-start.16 = (bf16[2,192,128]{2,1,0:T(8,128)(2,1)S(1)}, bf16[2,192,128]{2,1,0:T(8,128)(2,1)S(1)}, u32[]{:S(2)}, u32[]{:S(2)}) collective-permute-start(bf16[2,192,128]{2,1,0:T(8,128)(2,1)S(1)} %get-tuple-element.52), channel_id=1, source_target_pairs={{0,16},{8,24},{16,0},{24,8},{1,17},{9,25},{17,1},{25,9},{2,18},{10... | collective-permute-start | bytes 294920 | tf_op jit(solution)/shard_map/ppermute | solution.py:193
  56.9 7.2 %collective-permute-start.17 = (bf16[1,192,128]{2,1,0:T(8,128)(2,1)S(1)}, bf16[1,192,128]{2,1,0:T(8,128)(2,1)S(1)}, u32[]{:S(2)}, u32[]{:S(2)}) collective-permute-start(bf16[1,192,128]{2,1,0:T(8,128)(2,1)S(1)} %get-tuple-element.53), channel_id=1, source_target_pairs={{0,2},{1,3},{2,0},{3,1},{4,6},{5,7},{6,4},{7,5},{8,10},{9,11},{10,... | collective-permute-start | bytes 147464 | tf_op jit(solution)/shard_map/ppermute | solution.py:195
  58.9 7.1 %collective-permute-start.18 = (bf16[1,192,128]{2,1,0:T(8,128)(2,1)S(1)}, bf16[1,192,128]{2,1,0:T(8,128)(2,1)S(1)}, u32[]{:S(2)}, u32[]{:S(2)}) collective-permute-start(bf16[1,192,128]{2,1,0:T(8,128)(2,1)S(1)} %get-tuple-element.54), channel_id=1, source_target_pairs={{0,18},{1,19},{2,16},{3,17},{4,22},{5,23},{6,20},{7,21},{8,26},{9,... | collective-permute-start | bytes 147464 | tf_op jit(solution)/shard_map/ppermute | solution.py:200
  (4 other events, 3.2 us)

commit v6 on v5

--- a/solution.py
+++ b/solution.py
@@ -527,11 +527,12 @@
     weight = out_weight.T
     cols = weight.shape[0]
     cuts = [slice(cols * i // 360, cols * j // 360) for i, j in zip((0, 200), (200, 360))]
-    first = swap_blocks(weight, FAR_BIT, NEAR_BIT)
+    first = swap_blocks(weight, NEAR_BIT, FAR_BIT)
 
     pieces = pack(queries[0], new_kv[0], kv_pool[0].reshape(pool_rows, 2 * kv_width), n_req)
     pieces = [pieces[0]] + [swap(pieces[k], k, 0) for k in range(1, n_req)]
-    second = [swap_blocks(weight[cuts[0]], NEAR_BIT, FAR_BIT)]
+    second = [swap_blocks(weight[cuts[0]], FAR_BIT, NEAR_BIT)]
+    second += [swap_blocks(weight[cuts[1]], FAR_BIT, NEAR_BIT)]
 
     position = cached_pages[0] * page_size + jnp.arange(n_req * tok)
     frequency = THETA ** (-2.0 * jnp.arange(HD // 2).astype(F32) / HD)
@@ -545,14 +546,13 @@
         head_count // kv_heads, pool_rows, page_size,
     )
     chip_rows = jnp.concatenate([new_kv[0], pieces[1][:, -2 * kv_width :]], axis=0)
-    ctx, later = lax.optimization_barrier((ctx, weight))
-    second += [swap_blocks(later[cuts[1]], NEAR_BIT, FAR_BIT)]
     ctx, first, chip_rows = lax.optimization_barrier((ctx, first, chip_rows))
     ctx_mate = swap(ctx, 0, PAIR_BIT)
     inner = is_inner(lax.axis_index("exp"))
-    far = [jnp.where(inner, first[rows], piece) for rows, piece in zip(cuts, second)]
+    far = [jnp.where(inner, piece, first[rows]) for rows, piece in zip(cuts, second)]
     both = [swap(chunk, 0, NEAR_BIT) for chunk in far]
-    pool_out = write_pool(new_slots, cosine, sine, kv_pool[0], [chip_rows, swap(chip_rows, 2, 0)])
+    fresh = swap(chip_rows, 2, 0)
+    pool_out = write_pool(new_slots, cosine, sine, kv_pool[0], [chip_rows, fresh])
 
     def both_sides(contexts, blocks, pairs):
         send, keep = project(contexts, blocks, pairs)
@@ -570,7 +570,7 @@
     parts += [own_part, swap(over_y, 2, 0)]
     parts += [swap(over_pair, 0, PAIR_BIT), swap(over_both, 2, PAIR_BIT)]
     own_bits, first_bits, second_bits, both_bits = (
-        (0, 0), (FAR_BIT, NEAR_BIT), (NEAR_BIT, FAR_BIT), (FAR_BIT ^ NEAR_BIT,) * 2
+        (0, 0), (NEAR_BIT, FAR_BIT), (FAR_BIT, NEAR_BIT), (FAR_BIT ^ NEAR_BIT,) * 2
     )
 
     def of_mate(bits):

time: 67.7 us -> 64.3 us (0.950)
  starting transfers between devices: 26.3 us -> 22.2 us
  waiting for transfers between devices: 22.3 us -> 23 us
    ppermute x9, waiting for transfers between devices: 10.1 us -> 13.3 us  [swap(): lax.ppermute(values, 'req', [(i, i ^ req_bits) for i in range(lax.axis_si...]
    ppermute x3, starting transfers between devices: 10.2 us -> 7.21 us  [swap_blocks(): return lax.ppermute(values, 'exp', pairs)]
    ppermute x5, waiting for transfers between devices: 10.4 us -> 8.1 us  [swap(): lax.ppermute(values, 'exp', [(i, i ^ exp_bits) for i in range(lax.axis_si...]
    ppermute x5, starting transfers between devices: 8.02 us -> 6.37 us  [swap(): lax.ppermute(values, 'exp', [(i, i ^ exp_bits) for i in range(lax.axis_si...]
  transfers between devices with their start and end apart: 19 -> 19, of which waited for: 9 -> 8; matrix products, arithmetic and copies ran while one was open for 4% -> 4% of each run, Pallas kernels for 15% -> 15%
where the time goes in v6:
time: 64.3 us; the launch traced here: 64.1 us
  waiting for transfers between devices  23 us (36%)
  starting transfers between devices  22.2 us (35%)
  Pallas kernels  11.3 us (18%)
  local copies, waits for them, and re-layouts  5.12 us (8%)
  between operations  1.52 us (2%)
  other arithmetic  0.92 us (1%)
    ppermute x9, waiting for transfers between devices, swap(): lax.ppermute(values, 'req', [(i, i ^ req_bits) for i in range(lax.axis_si...  13.3 us
    ppermute x5, waiting for transfers between devices, swap(): lax.ppermute(values, 'exp', [(i, i ^ exp_bits) for i in range(lax.axis_si...  8.1 us
    ppermute x3, starting transfers between devices, swap_blocks(): return lax.ppermute(values, 'exp', pairs)  7.21 us
    ppermute x5, starting transfers between devices, swap(): lax.ppermute(values, 'exp', [(i, i ^ exp_bits) for i in range(lax.axis_si...  6.37 us
    ppermute x9, starting transfers between devices, swap(): lax.ppermute(values, 'req', [(i, i ^ req_bits) for i in range(lax.axis_si...  5.89 us
    pallas_call x1, Pallas kernels, attention(): pl.pallas_call(functools.partial(attention_kernel, kv_dev=kv_dev, per_kv=...  5.13 us
    unnamed x18, local copies, waits for them, and re-layouts  3.58 us
    ppermute x2, starting transfers between devices, swap(): return lax.ppermute(values, ('req', 'exp'), pairs)  2.74 us
  transfers between devices with their start and end apart: 19, of which 8 were waited for; matrix products, arithmetic and copies ran while one was open for 4% of the time, Pallas kernels for 15%

profile of v6, /device:TPU:0, one launch (start us, length us, event | category | flops | bytes accessed | tf_op | source)
XLA Modules:
  0.0 64.1 jit_solution(11900655838368909637)
XLA Ops:
  0.6 5.1 %collective-permute-start.3 = (bf16[360,1024]{1,0:T(8,128)(2,1)}, bf16[360,1024]{1,0:T(8,128)(2,1)S(1)}, u32[]{:S(2)}, u32[]{:S(2)}) collective-permute-start(bf16[360,1024]{1,0:T(8,128)(2,1)} %bitcast.9), channel_id=1, source_target_pairs={{0,6},{1,7},{2,3},{3,2},{4,5},{5,4},{6,0},{7,1},{8,14},{9,15},{10,... | collective-permute-start | bytes 2211848 | tf_op jit(solution)/shard_map/ppermute | solution.py:209
  5.8 0.9 %copy-done.1 = bf16[1,8,16,1024]{3,2,1,0:T(8,128)(2,1)S(1)} copy-done((bf16[1,8,16,1024]{3,2,1,0:T(8,128)(2,1)S(1)}, bf16[1,8,16,1024]{3,2,1,0:T(8,128)(2,1)}, u32[]{:S(2)}) %copy-start.1) | copy-done | bytes 262168
  6.7 1.0 %copy-done.3 = bf16[1,64,4096]{2,1,0:T(8,128)(2,1)S(1)} copy-done((bf16[1,64,4096]{2,1,0:T(8,128)(2,1)S(1)}, bf16[1,64,4096]{2,1,0:T(8,128)(2,1)}, u32[]{:S(2)}) %copy-start.3) | copy-done | bytes 524312
  9.3 1.6 %collective-permute-start.1 = (bf16[64,1792]{1,0:T(8,128)(2,1)S(1)}, bf16[64,1792]{1,0:T(8,128)(2,1)S(1)}, u32[]{:S(2)}, u32[]{:S(2)}) collective-permute-start(bf16[64,1792]{1,0:T(8,128)(2,1)S(1)} %get-tuple-element.29), channel_id=1, source_target_pairs={{0,16},{8,24},{16,0},{24,8},{1,17},{9,25},{17,1},{25,9},{2,18},{10... | collective-permute-start | bytes 688136 | tf_op jit(solution)/shard_map/ppermute | solution.py:193
  11.9 1.5 %collective-permute-start.8 = (bf16[200,1024]{1,0:T(8,128)(2,1)}, bf16[200,1024]{1,0:T(8,128)(2,1)S(1)}, u32[]{:S(2)}, u32[]{:S(2)}) collective-permute-start(bf16[200,1024]{1,0:T(8,128)(2,1)} %slice.21), channel_id=1, source_target_pairs={{0,1},{1,0},{2,4},{3,5},{4,2},{5,3},{6,7},{7,6},{8,9},{9,8},{10,12... | collective-permute-start | bytes 1228808 | tf_op jit(solution)/shard_map/ppermute | solution.py:209
  16.3 1.5 %collective-permute-done.1.rest_2_ = bf16[64,1792]{1,0:T(8,128)(2,1)S(1)} collective-permute-done((bf16[64,1792]{1,0:T(8,128)(2,1)S(1)}, bf16[64,1792]{1,0:T(8,128)(2,1)S(1)}, u32[]{:S(2)}, u32[]{:S(2)}) %collective-permute-start.1) | collective-permute-done | bytes 229408 | tf_op jit(solution)/shard_map/ppermute | solution.py:193
  17.8 4.0 %collective-permute-done.2.rest_3_ = bf16[64,1792]{1,0:T(8,128)(2,1)S(1)} collective-permute-done((bf16[64,1792]{1,0:T(8,128)(2,1)S(1)}, bf16[64,1792]{1,0:T(8,128)(2,1)S(1)}, u32[]{:S(2)}, u32[]{:S(2)}) %collective-permute-start.2) | collective-permute-done | bytes 229408 | tf_op jit(solution)/shard_map/ppermute | solution.py:193
  22.4 5.1 %attention.1.refs_0_ = bf16[1024,256]{1,0:T(8,128)(2,1)S(1)} custom-call(s32[1]{0:T(128)S(6)} %copy.12.pages_ref, s32[1,16]{1,0:T(1,128)S(1)} %copy-done.7, f32[64]{0:T(128)S(1)} %copy-done.8, f32[256,128]{1,0:T(8,128)S(1)} %get-tuple-element.55.cos_ref, f32[256,128]{1,0:T(8,128)S(1)} %get-tuple-element.56.sin_ref, ...), custom_call_target="tpu_custom_call" | custom-call | tf_op jit(solution)/shard_map/attention/pallas_call | solution.py:361
  27.6 1.6 %collective-permute-start.4 = (bf16[128,1024]{1,0:T(8,128)(2,1)S(1)}, bf16[128,1024]{1,0:T(8,128)(2,1)S(1)}, u32[]{:S(2)}, u32[]{:S(2)}) collective-permute-start(bf16[128,1024]{1,0:T(8,128)(2,1)S(1)} %pad_maximum_fusion.rest_0_), channel_id=1, source_target_pairs={{0,16},{8,24},{16,0},{24,8},{1,17},{9,25},{17,1},{25,9},{2,18},{10... | collective-permute-start | bytes 786440 | tf_op jit(solution)/shard_map/ppermute | solution.py:193
  29.3 1.6 %collective-permute-start.13 = (bf16[200,1024]{1,0:T(8,128)(2,1)S(1)}, bf16[200,1024]{1,0:T(8,128)(2,1)S(1)}, u32[]{:S(2)}, u32[]{:S(2)}) collective-permute-start(bf16[200,1024]{1,0:T(8,128)(2,1)S(1)} %slice_select_fusion), channel_id=1, source_target_pairs={{0,1},{1,0},{2,3},{3,2},{4,5},{5,4},{6,7},{7,6},{8,9},{9,8},{10,11... | collective-permute-start | bytes 1228808 | tf_op jit(solution)/shard_map/ppermute | solution.py:195
  30.8 5.6 %collective-permute-done.4.rest_1_ = bf16[128,1024]{1,0:T(8,128)(2,1)S(1)} collective-permute-done((bf16[128,1024]{1,0:T(8,128)(2,1)S(1)}, bf16[128,1024]{1,0:T(8,128)(2,1)S(1)}, u32[]{:S(2)}, u32[]{:S(2)}) %collective-permute-start.4) | collective-permute-done | bytes 262176 | tf_op jit(solution)/shard_map/ppermute | solution.py:193
  36.5 1.7 %write_pool.1 = bf16[8,16,1024]{2,1,0:T(8,128)(2,1)} custom-call(s32[1,16]{1,0:T(1,128)S(1)} %copy-done.6, f32[256,128]{1,0:T(8,128)S(1)} %get-tuple-element.55.cos_ref, f32[256,128]{1,0:T(8,128)S(1)} %get-tuple-element.56.sin_ref, bf16[8,16,1024]{2,1,0:T(8,128)(2,1)S(1)} %bitcast.15, bf16[128,1024]{1,0:T(8,128)(2,1)S(1)} %pad_maximum_fusion.rest_0_, ...), custom_call_target="tpu_custom_call" | custom-call | tf_op jit(solution)/shard_map/write_pool/pallas_call | solution.py:407
  38.9 1.6 %collective-permute-start.14 = (bf16[160,1024]{1,0:T(8,128)(2,1)S(1)}, bf16[160,1024]{1,0:T(8,128)(2,1)S(1)}, u32[]{:S(2)}, u32[]{:S(2)}) collective-permute-start(bf16[160,1024]{1,0:T(8,128)(2,1)S(1)} %slice_select_fusion.1), channel_id=1, source_target_pairs={{0,1},{1,0},{2,3},{3,2},{4,5},{5,4},{6,7},{7,6},{8,9},{9,8},{10,11... | collective-permute-start | bytes 983048 | tf_op jit(solution)/shard_map/ppermute | solution.py:195
  40.6 1.6 %collective-permute-start.7 = (bf16[2,192,128]{2,1,0:T(8,128)(2,1)S(1)}, bf16[2,192,128]{2,1,0:T(8,128)(2,1)S(1)}, u32[]{:S(2)}, u32[]{:S(2)}) collective-permute-start(bf16[2,192,128]{2,1,0:T(8,128)(2,1)S(1)} %get-tuple-element.38), channel_id=1, source_target_pairs={{0,16},{8,24},{16,0},{24,8},{1,17},{9,25},{17,1},{25,9},{2,18},{10... | collective-permute-start | bytes 294920 | tf_op jit(solution)/shard_map/ppermute | solution.py:193
  42.1 1.2 %collective-permute-done.6.refs_0_.refs_1_ = bf16[1024,256]{1,0:T(8,128)(2,1)S(1)} collective-permute-done((bf16[1024,256]{1,0:T(8,128)(2,1)S(1)}, bf16[1024,256]{1,0:T(8,128)(2,1)S(1)}, u32[]{:S(2)}, u32[]{:S(2)}) %collective-permute-start.6) | collective-permute-done | bytes 524320 | tf_op jit(solution)/shard_map/ppermute | solution.py:195
  43.3 2.2 %collective-permute-done.7.rest_1_ = bf16[2,192,128]{2,1,0:T(8,128)(2,1)S(1)} collective-permute-done((bf16[2,192,128]{2,1,0:T(8,128)(2,1)S(1)}, bf16[2,192,128]{2,1,0:T(8,128)(2,1)S(1)}, u32[]{:S(2)}, u32[]{:S(2)}) %collective-permute-start.7) | collective-permute-done | bytes 98336 | tf_op jit(solution)/shard_map/ppermute | solution.py:193
  46.4 2.7 %collective-permute-done.14.refs_5_ = bf16[160,1024]{1,0:T(8,128)(2,1)S(1)} collective-permute-done((bf16[160,1024]{1,0:T(8,128)(2,1)S(1)}, bf16[160,1024]{1,0:T(8,128)(2,1)S(1)}, u32[]{:S(2)}, u32[]{:S(2)}) %collective-permute-start.14) | collective-permute-done | bytes 327712 | tf_op jit(solution)/shard_map/ppermute | solution.py:195
  50.1 1.7 %collective-permute-start.11 = (bf16[3,192,128]{2,1,0:T(8,128)(2,1)S(1)}, bf16[3,192,128]{2,1,0:T(8,128)(2,1)S(1)}, u32[]{:S(2)}, u32[]{:S(2)}) collective-permute-start(bf16[3,192,128]{2,1,0:T(8,128)(2,1)S(1)} %get-tuple-element.43), channel_id=1, source_target_pairs={{0,2},{1,3},{2,0},{3,1},{4,6},{5,7},{6,4},{7,5},{8,10},{9,11},{10,... | collective-permute-start | bytes 442376 | tf_op jit(solution)/shard_map/ppermute | solution.py:195
  51.7 1.4 %collective-permute-start.12 = (bf16[3,192,128]{2,1,0:T(8,128)(2,1)S(1)}, bf16[3,192,128]{2,1,0:T(8,128)(2,1)S(1)}, u32[]{:S(2)}, u32[]{:S(2)}) collective-permute-start(bf16[3,192,128]{2,1,0:T(8,128)(2,1)S(1)} %get-tuple-element.44), channel_id=1, source_target_pairs={{0,18},{1,19},{2,16},{3,17},{4,22},{5,23},{6,20},{7,21},{8,26},{9,... | collective-permute-start | bytes 442376 | tf_op jit(solution)/shard_map/ppermute | solution.py:200
  53.8 1.6 %collective-permute-start.17 = (bf16[1,192,128]{2,1,0:T(8,128)(2,1)S(1)}, bf16[1,192,128]{2,1,0:T(8,128)(2,1)S(1)}, u32[]{:S(2)}, u32[]{:S(2)}) collective-permute-start(bf16[1,192,128]{2,1,0:T(8,128)(2,1)S(1)} %get-tuple-element.49), channel_id=1, source_target_pairs={{0,2},{1,3},{2,0},{3,1},{4,6},{5,7},{6,4},{7,5},{8,10},{9,11},{10,... | collective-permute-start | bytes 147464 | tf_op jit(solution)/shard_map/ppermute | solution.py:195
  55.4 1.4 %collective-permute-start.18 = (bf16[1,192,128]{2,1,0:T(8,128)(2,1)S(1)}, bf16[1,192,128]{2,1,0:T(8,128)(2,1)S(1)}, u32[]{:S(2)}, u32[]{:S(2)}) collective-permute-start(bf16[1,192,128]{2,1,0:T(8,128)(2,1)S(1)} %get-tuple-element.50), channel_id=1, source_target_pairs={{0,18},{1,19},{2,16},{3,17},{4,22},{5,23},{6,20},{7,21},{8,26},{9,... | collective-permute-start | bytes 147464 | tf_op jit(solution)/shard_map/ppermute | solution.py:200
  56.8 4.2 %collective-permute-done.17.rest_6_ = bf16[1,192,128]{2,1,0:T(8,128)(2,1)S(1)} collective-permute-done((bf16[1,192,128]{2,1,0:T(8,128)(2,1)S(1)}, bf16[1,192,128]{2,1,0:T(8,128)(2,1)S(1)}, u32[]{:S(2)}, u32[]{:S(2)}) %collective-permute-start.17) | collective-permute-done | bytes 49184 | tf_op jit(solution)/shard_map/ppermute | solution.py:195
  61.0 1.6 %collective-permute-done.18.rest_7_ = bf16[1,192,128]{2,1,0:T(8,128)(2,1)S(1)} collective-permute-done((bf16[1,192,128]{2,1,0:T(8,128)(2,1)S(1)}, bf16[1,192,128]{2,1,0:T(8,128)(2,1)S(1)}, u32[]{:S(2)}, u32[]{:S(2)}) %collective-permute-start.18) | collective-permute-done | bytes 49184 | tf_op jit(solution)/shard_map/ppermute | solution.py:200
  62.7 1.4 %finish.1 = bf16[64,2880]{1,0:T(8,128)(2,1)} custom-call(bf16[64,2880]{1,0:T(8,128)(2,1)S(1)} %bitcast.19, bf16[2,192,128]{2,1,0:T(8,128)(2,1)S(1)} %get-tuple-element.37.rest_0_, bf16[2,192,128]{2,1,0:T(8,128)(2,1)S(1)} %collective-permute-done.7.rest_1_, bf16[3,192,128]{2,1,0:T(8,128)(2,1)S(1)} %collective-permute-done.11.rest_2_, ...), custom_call_target="tpu_custom_call" | custom-call | tf_op jit(solution)/shard_map/finish/pallas_call | solution.py:505
  (52 shorter events, 8.9 us)
Async XLA Ops:
  0.6 10.5 %copy-start = (bf16[1024,360]{0,1:T(8,128)(2,1)S(1)}, bf16[1024,360]{0,1:T(8,128)(2,1)}, u32[]{:S(2)}) copy-start(bf16[1024,360]{0,1:T(8,128)(2,1)} %param.17) | copy-start | bytes 2211844
  0.6 27.0 %collective-permute-start.3 = (bf16[360,1024]{1,0:T(8,128)(2,1)}, bf16[360,1024]{1,0:T(8,128)(2,1)S(1)}, u32[]{:S(2)}, u32[]{:S(2)}) collective-permute-start(bf16[360,1024]{1,0:T(8,128)(2,1)} %bitcast.9), channel_id=1, source_target_pairs={{0,6},{1,7},{2,3},{3,2},{4,5},{5,4},{6,0},{7,1},{8,14},{9,15},{10,... | collective-permute-start | bytes 2211848 | tf_op jit(solution)/shard_map/ppermute | solution.py:209
  6.7 1.0 %copy-start.3 = (bf16[1,64,4096]{2,1,0:T(8,128)(2,1)S(1)}, bf16[1,64,4096]{2,1,0:T(8,128)(2,1)}, u32[]{:S(2)}) copy-start(bf16[1,64,4096]{2,1,0:T(8,128)(2,1)} %param.10) | copy-start | bytes 1572868
  9.2 6.5 %collective-permute-start = (bf16[64,2816]{1,0:T(8,128)(2,1)S(1)}, bf16[64,2816]{1,0:T(8,128)(2,1)S(1)}, u32[]{:S(2)}, u32[]{:S(2)}) collective-permute-start(bf16[64,2816]{1,0:T(8,128)(2,1)S(1)} %get-tuple-element.28), channel_id=1, source_target_pairs={{0,8},{8,0},{16,24},{24,16},{1,9},{9,1},{17,25},{25,17},{2,10},{10... | collective-permute-start | bytes 1081352 | tf_op jit(solution)/shard_map/ppermute | solution.py:193
  9.3 8.5 %collective-permute-start.1 = (bf16[64,1792]{1,0:T(8,128)(2,1)S(1)}, bf16[64,1792]{1,0:T(8,128)(2,1)S(1)}, u32[]{:S(2)}, u32[]{:S(2)}) collective-permute-start(bf16[64,1792]{1,0:T(8,128)(2,1)S(1)} %get-tuple-element.29), channel_id=1, source_target_pairs={{0,16},{8,24},{16,0},{24,8},{1,17},{9,25},{17,1},{25,9},{2,18},{10... | collective-permute-start | bytes 688136 | tf_op jit(solution)/shard_map/ppermute | solution.py:193
  10.9 10.9 %collective-permute-start.2 = (bf16[64,1792]{1,0:T(8,128)(2,1)S(1)}, bf16[64,1792]{1,0:T(8,128)(2,1)S(1)}, u32[]{:S(2)}, u32[]{:S(2)}) collective-permute-start(bf16[64,1792]{1,0:T(8,128)(2,1)S(1)} %get-tuple-element.30), channel_id=1, source_target_pairs={{0,24},{8,16},{16,8},{24,0},{1,25},{9,17},{17,9},{25,1},{2,26},{10... | collective-permute-start | bytes 688136 | tf_op jit(solution)/shard_map/ppermute | solution.py:193
  11.9 17.3 %collective-permute-start.8 = (bf16[200,1024]{1,0:T(8,128)(2,1)}, bf16[200,1024]{1,0:T(8,128)(2,1)S(1)}, u32[]{:S(2)}, u32[]{:S(2)}) collective-permute-start(bf16[200,1024]{1,0:T(8,128)(2,1)} %slice.21), channel_id=1, source_target_pairs={{0,1},{1,0},{2,4},{3,5},{4,2},{5,3},{6,7},{7,6},{8,9},{9,8},{10,12... | collective-permute-start | bytes 1228808 | tf_op jit(solution)/shard_map/ppermute | solution.py:209
  15.7 23.1 %collective-permute-start.9 = (bf16[160,1024]{1,0:T(8,128)(2,1)}, bf16[160,1024]{1,0:T(8,128)(2,1)S(1)}, u32[]{:S(2)}, u32[]{:S(2)}) collective-permute-start(bf16[160,1024]{1,0:T(8,128)(2,1)} %slice.22), channel_id=1, source_target_pairs={{0,1},{1,0},{2,4},{3,5},{4,2},{5,3},{6,7},{7,6},{8,9},{9,8},{10,12... | collective-permute-start | bytes 983048 | tf_op jit(solution)/shard_map/ppermute | solution.py:209
  27.6 8.8 %collective-permute-start.4 = (bf16[128,1024]{1,0:T(8,128)(2,1)S(1)}, bf16[128,1024]{1,0:T(8,128)(2,1)S(1)}, u32[]{:S(2)}, u32[]{:S(2)}) collective-permute-start(bf16[128,1024]{1,0:T(8,128)(2,1)S(1)} %pad_maximum_fusion.rest_0_), channel_id=1, source_target_pairs={{0,16},{8,24},{16,0},{24,8},{1,17},{9,25},{17,1},{25,9},{2,18},{10... | collective-permute-start | bytes 786440 | tf_op jit(solution)/shard_map/ppermute | solution.py:193
  29.2 7.3 %copy-start.2 = (bf16[1,8,16,1024]{3,2,1,0:T(8,128)(2,1)S(1)}, bf16[1,8,16,1024]{3,2,1,0:T(8,128)(2,1)}, u32[]{:S(2)}) copy-start(bf16[1,8,16,1024]{3,2,1,0:T(8,128)(2,1)} %param.12) | copy-start | bytes 786436
  29.2 14.1 %collective-permute-start.6 = (bf16[1024,256]{1,0:T(8,128)(2,1)S(1)}, bf16[1024,256]{1,0:T(8,128)(2,1)S(1)}, u32[]{:S(2)}, u32[]{:S(2)}) collective-permute-start(bf16[1024,256]{1,0:T(8,128)(2,1)S(1)} %attention.1.refs_0_), channel_id=1, source_target_pairs={{0,2},{1,3},{2,0},{3,1},{4,6},{5,7},{6,4},{7,5},{8,10},{9,11},{10,... | collective-permute-start | bytes 1572872 | tf_op jit(solution)/shard_map/ppermute | solution.py:195
  29.3 7.2 %copy-start.6 = (s32[1,16]{1,0:T(1,128)S(1)}, s32[1,16]{1,0:T(1,128)}, u32[]{:S(2)}) copy-start(s32[1,16]{1,0:T(1,128)} %slots_ref.1) | copy-start | bytes 196
  29.3 19.8 %collective-permute-start.13 = (bf16[200,1024]{1,0:T(8,128)(2,1)S(1)}, bf16[200,1024]{1,0:T(8,128)(2,1)S(1)}, u32[]{:S(2)}, u32[]{:S(2)}) collective-permute-start(bf16[200,1024]{1,0:T(8,128)(2,1)S(1)} %slice_select_fusion), channel_id=1, source_target_pairs={{0,1},{1,0},{2,3},{3,2},{4,5},{5,4},{6,7},{7,6},{8,9},{9,8},{10,11... | collective-permute-start | bytes 1228808 | tf_op jit(solution)/shard_map/ppermute | solution.py:195
  38.7 1.7 %collective-permute-start.5 = (bf16[2,360,128]{2,1,0:T(8,128)(2,1)S(1)}, bf16[2,360,128]{2,1,0:T(8,128)(2,1)S(1)}, u32[]{:S(2)}, u32[]{:S(2)}) collective-permute-start(bf16[2,360,128]{2,1,0:T(8,128)(2,1)S(1)} %get-tuple-element.36), channel_id=1, source_target_pairs={{0,8},{8,0},{16,24},{24,16},{1,9},{9,1},{17,25},{25,17},{2,10},{10... | collective-permute-start | bytes 552968 | tf_op jit(solution)/shard_map/ppermute | solution.py:193
  38.9 10.2 %collective-permute-start.14 = (bf16[160,1024]{1,0:T(8,128)(2,1)S(1)}, bf16[160,1024]{1,0:T(8,128)(2,1)S(1)}, u32[]{:S(2)}, u32[]{:S(2)}) collective-permute-start(bf16[160,1024]{1,0:T(8,128)(2,1)S(1)} %slice_select_fusion.1), channel_id=1, source_target_pairs={{0,1},{1,0},{2,3},{3,2},{4,5},{5,4},{6,7},{7,6},{8,9},{9,8},{10,11... | collective-permute-start | bytes 983048 | tf_op jit(solution)/shard_map/ppermute | solution.py:195
  40.6 5.0 %collective-permute-start.7 = (bf16[2,192,128]{2,1,0:T(8,128)(2,1)S(1)}, bf16[2,192,128]{2,1,0:T(8,128)(2,1)S(1)}, u32[]{:S(2)}, u32[]{:S(2)}) collective-permute-start(bf16[2,192,128]{2,1,0:T(8,128)(2,1)S(1)} %get-tuple-element.38), channel_id=1, source_target_pairs={{0,16},{8,24},{16,0},{24,8},{1,17},{9,25},{17,1},{25,9},{2,18},{10... | collective-permute-start | bytes 294920 | tf_op jit(solution)/shard_map/ppermute | solution.py:193
  46.3 3.6 %collective-permute-start.10 = (bf16[3,360,128]{2,1,0:T(8,128)(2,1)S(1)}, bf16[3,360,128]{2,1,0:T(8,128)(2,1)S(1)}, u32[]{:S(2)}, u32[]{:S(2)}) collective-permute-start(bf16[3,360,128]{2,1,0:T(8,128)(2,1)S(1)} %get-tuple-element.42), channel_id=1, source_target_pairs={{0,8},{8,0},{16,24},{24,16},{1,9},{9,1},{17,25},{25,17},{2,10},{10... | collective-permute-start | bytes 829448 | tf_op jit(solution)/shard_map/ppermute | solution.py:193
  49.8 3.3 %collective-permute-start.15 = (bf16[3,360,128]{2,1,0:T(8,128)(2,1)S(1)}, bf16[3,360,128]{2,1,0:T(8,128)(2,1)S(1)}, u32[]{:S(2)}, u32[]{:S(2)}) collective-permute-start(bf16[3,360,128]{2,1,0:T(8,128)(2,1)S(1)} %get-tuple-element.46), channel_id=1, source_target_pairs={{0,8},{8,0},{16,24},{24,16},{1,9},{9,1},{17,25},{25,17},{2,10},{10... | collective-permute-start | bytes 829448 | tf_op jit(solution)/shard_map/ppermute | solution.py:193
  50.1 12.6 %copy-start.5 = (bf16[1,64,2880]{2,1,0:T(8,128)(2,1)S(1)}, bf16[1,64,2880]{2,1,0:T(8,128)(2,1)}, u32[]{:S(2)}) copy-start(bf16[1,64,2880]{2,1,0:T(8,128)(2,1)} %param.9) | copy-start | bytes 1105924
  50.1 12.6 %collective-permute-start.11 = (bf16[3,192,128]{2,1,0:T(8,128)(2,1)S(1)}, bf16[3,192,128]{2,1,0:T(8,128)(2,1)S(1)}, u32[]{:S(2)}, u32[]{:S(2)}) collective-permute-start(bf16[3,192,128]{2,1,0:T(8,128)(2,1)S(1)} %get-tuple-element.43), channel_id=1, source_target_pairs={{0,2},{1,3},{2,0},{3,1},{4,6},{5,7},{6,4},{7,5},{8,10},{9,11},{10,... | collective-permute-start | bytes 442376 | tf_op jit(solution)/shard_map/ppermute | solution.py:195
  51.7 10.9 %collective-permute-start.12 = (bf16[3,192,128]{2,1,0:T(8,128)(2,1)S(1)}, bf16[3,192,128]{2,1,0:T(8,128)(2,1)S(1)}, u32[]{:S(2)}, u32[]{:S(2)}) collective-permute-start(bf16[3,192,128]{2,1,0:T(8,128)(2,1)S(1)} %get-tuple-element.44), channel_id=1, source_target_pairs={{0,18},{1,19},{2,16},{3,17},{4,22},{5,23},{6,20},{7,21},{8,26},{9,... | collective-permute-start | bytes 442376 | tf_op jit(solution)/shard_map/ppermute | solution.py:200
  53.3 9.4 %collective-permute-start.16 = (bf16[2,192,128]{2,1,0:T(8,128)(2,1)S(1)}, bf16[2,192,128]{2,1,0:T(8,128)(2,1)S(1)}, u32[]{:S(2)}, u32[]{:S(2)}) collective-permute-start(bf16[2,192,128]{2,1,0:T(8,128)(2,1)S(1)} %get-tuple-element.48), channel_id=1, source_target_pairs={{0,16},{8,24},{16,0},{24,8},{1,17},{9,25},{17,1},{25,9},{2,18},{10... | collective-permute-start | bytes 294920 | tf_op jit(solution)/shard_map/ppermute | solution.py:193
  53.8 7.2 %collective-permute-start.17 = (bf16[1,192,128]{2,1,0:T(8,128)(2,1)S(1)}, bf16[1,192,128]{2,1,0:T(8,128)(2,1)S(1)}, u32[]{:S(2)}, u32[]{:S(2)}) collective-permute-start(bf16[1,192,128]{2,1,0:T(8,128)(2,1)S(1)} %get-tuple-element.49), channel_id=1, source_target_pairs={{0,2},{1,3},{2,0},{3,1},{4,6},{5,7},{6,4},{7,5},{8,10},{9,11},{10,... | collective-permute-start | bytes 147464 | tf_op jit(solution)/shard_map/ppermute | solution.py:195
  55.4 7.2 %collective-permute-start.18 = (bf16[1,192,128]{2,1,0:T(8,128)(2,1)S(1)}, bf16[1,192,128]{2,1,0:T(8,128)(2,1)S(1)}, u32[]{:S(2)}, u32[]{:S(2)}) collective-permute-start(bf16[1,192,128]{2,1,0:T(8,128)(2,1)S(1)} %get-tuple-element.50), channel_id=1, source_target_pairs={{0,18},{1,19},{2,16},{3,17},{4,22},{5,23},{6,20},{7,21},{8,26},{9,... | collective-permute-start | bytes 147464 | tf_op jit(solution)/shard_map/ppermute | solution.py:200
  (4 other events, 3.2 us)

commit v7 on v6

--- a/solution.py
+++ b/solution.py
@@ -350,7 +350,7 @@
             out_ref[pl.ds(row, HD), :] = (summed[:, p * wide : (p + 1) * wide] / dens[p]).astype(BF16)
         return carry
 
-    lax.fori_loop(0, 2 * kv_dev, one_set, 0, unroll=False)
+    lax.fori_loop(0, 2 * kv_dev, one_set, 0, unroll=True)
 
 
 def attention(pages, table, sinks, cosine, sine, pieces, kv_dev, per_kv, pool_rows, page_size):
@@ -464,14 +464,16 @@
             both = keep_ref[at].astype(F32) + got_ref[at].astype(F32)
             top = both[:rows]
             rest = jnp.concatenate([both[rows:], jnp.zeros((2 * rows - cols, width), F32)], axis=0)
-            out_refs[2 * i][b] = jnp.where(low, top, pltpu.roll(rest, tok, 1)).astype(BF16)
+            out_refs[2 * i][b] = jnp.where(low, top, pltpu.roll(rest, tok, 1)).astype(out_refs[2 * i].dtype)
             out_refs[2 * i + 1][b] = jnp.where(low, pltpu.roll(top, tok, 1), rest).astype(BF16)
             at += 1
 
 
-def pair_sum(keep, got, counts):
+def pair_sum(keep, got, counts, own_first):
     cols, width = keep.shape[1:]
     shapes = [jax.ShapeDtypeStruct((c, fold_rows(cols), width), BF16) for c in counts for _ in range(2)]
+    if own_first:
+        shapes[0] = jax.ShapeDtypeStruct(shapes[0].shape, F32)
     return pl.pallas_call(
         functools.partial(pair_kernel, counts=counts),
         out_shape=shapes,
@@ -526,7 +528,8 @@
     pool_rows = slots_dev * page_size
     weight = out_weight.T
     cols = weight.shape[0]
-    cuts = [slice(cols * i // 360, cols * j // 360) for i, j in zip((0, 200), (200, 360))]
+    cut = cols * 5 // 9
+    cuts = (slice(0, cut), slice(cut, cols))
     first = swap_blocks(weight, NEAR_BIT, FAR_BIT)
 
     pieces = pack(queries[0], new_kv[0], kv_pool[0].reshape(pool_rows, 2 * kv_width), n_req)
@@ -552,21 +555,22 @@
     far = [jnp.where(inner, piece, first[rows]) for rows, piece in zip(cuts, second)]
     both = [swap(chunk, 0, NEAR_BIT) for chunk in far]
     fresh = swap(chip_rows, 2, 0)
-    pool_out = write_pool(new_slots, cosine, sine, kv_pool[0], [chip_rows, fresh])
-
-    def both_sides(contexts, blocks, pairs):
+
+    def both_sides(contexts, blocks, pairs, own_first):
         send, keep = project(contexts, blocks, pairs)
         counts = tuple(n for n in (sum(i == c for c, _ in pairs) for i in range(len(contexts))) if n)
-        return pair_sum(keep, swap(send, 1, 0), counts)
+        return pair_sum(keep, swap(send, 1, 0), counts, own_first)
 
     parts = []
-    ctx, pool_out = lax.optimization_barrier((ctx, pool_out))
-    own_part, over_y = both_sides([ctx], [[weight], [first]], ((0, 0), (0, 1)))
+    ctx, fresh = lax.optimization_barrier((ctx, fresh))
+    own_part, over_y = both_sides([ctx], [[weight], [first]], ((0, 0), (0, 1)), True)
     parts += [own_part, swap(over_y, 2, 0)]
+    pool_out = write_pool(new_slots, cosine, sine, kv_pool[0], [chip_rows, fresh])
+    ctx_mate, pool_out = lax.optimization_barrier((ctx_mate, pool_out))
     ctx_mate, parts[1] = lax.optimization_barrier((ctx_mate, parts[1]))
-    over_pair, over_both = both_sides([ctx_mate], [[weight], [first], second], ((0, 0), (0, 1), (0, 2)))
+    over_pair, over_both = both_sides([ctx_mate], [[weight], [first], second], ((0, 0), (0, 1), (0, 2)), False)
     parts += [swap(over_pair, 0, PAIR_BIT), swap(over_both, 2, PAIR_BIT)]
-    own_part, over_y, over_pair, over_both = both_sides([ctx, ctx_mate], [second, both], ((0, 0), (0, 1), (1, 1)))
+    own_part, over_y, over_pair, over_both = both_sides([ctx, ctx_mate], [second, both], ((0, 0), (0, 1), (1, 1)), True)
     parts += [own_part, swap(over_y, 2, 0)]
     parts += [swap(over_pair, 0, PAIR_BIT), swap(over_both, 2, PAIR_BIT)]
     own_bits, first_bits, second_bits, both_bits = (

time: 64.3 us -> 64.2 us (level)
  starting transfers between devices: 22.2 us -> 23.5 us
  waiting for transfers between devices: 23 us -> 22.1 us
    ppermute x5, starting transfers between devices: 6.37 us -> 8.36 us  [swap(): lax.ppermute(values, 'exp', [(i, i ^ exp_bits) for i in range(lax.axis_si...]
    ppermute x9, waiting for transfers between devices: 13.3 us -> 11.7 us  [swap(): lax.ppermute(values, 'req', [(i, i ^ req_bits) for i in range(lax.axis_si...]
    ppermute x2, starting transfers between devices: 2.74 us -> 2.06 us  [swap(): return lax.ppermute(values, ('req', 'exp'), pairs)]
where the time goes in v7:
time: 64.2 us; the launch traced here: 64 us
  starting transfers between devices  23.5 us (37%)
  waiting for transfers between devices  22.1 us (34%)
  Pallas kernels  10.7 us (17%)
  local copies, waits for them, and re-layouts  5.12 us (8%)
  between operations  1.52 us (2%)
  other arithmetic  0.92 us (1%)
    ppermute x9, waiting for transfers between devices, swap(): lax.ppermute(values, 'req', [(i, i ^ req_bits) for i in range(lax.axis_si...  11.7 us
    ppermute x5, waiting for transfers between devices, swap(): lax.ppermute(values, 'exp', [(i, i ^ exp_bits) for i in range(lax.axis_si...  8.65 us
    ppermute x5, starting transfers between devices, swap(): lax.ppermute(values, 'exp', [(i, i ^ exp_bits) for i in range(lax.axis_si...  8.36 us
    ppermute x3, starting transfers between devices, swap_blocks(): return lax.ppermute(values, 'exp', pairs)  7.21 us
    ppermute x9, starting transfers between devices, swap(): lax.ppermute(values, 'req', [(i, i ^ req_bits) for i in range(lax.axis_si...  5.89 us
    pallas_call x1, Pallas kernels, attention(): pl.pallas_call(functools.partial(attention_kernel, kv_dev=kv_dev, per_kv=...  4.52 us
    unnamed x18, local copies, waits for them, and re-layouts  3.59 us
    pallas_call x3, Pallas kernels, project(): pl.pallas_call(functools.partial(project_kernel, n_ctx=len(contexts), cou...  2.08 us
  transfers between devices with their start and end apart: 19, of which 8 were waited for; matrix products, arithmetic and copies ran while one was open for 4% of the time, Pallas kernels for 15%

profile of v7, /device:TPU:0, one launch (start us, length us, event | category | flops | bytes accessed | tf_op | source)
XLA Modules:
  0.0 64.0 jit_solution(3086098877926096145)
XLA Ops:
  0.6 5.1 %collective-permute-start.3 = (bf16[360,1024]{1,0:T(8,128)(2,1)}, bf16[360,1024]{1,0:T(8,128)(2,1)S(1)}, u32[]{:S(2)}, u32[]{:S(2)}) collective-permute-start(bf16[360,1024]{1,0:T(8,128)(2,1)} %bitcast.9), channel_id=1, source_target_pairs={{0,6},{1,7},{2,3},{3,2},{4,5},{5,4},{6,0},{7,1},{8,14},{9,15},{10,... | collective-permute-start | bytes 2211848 | tf_op jit(solution)/shard_map/ppermute | solution.py:209
  5.8 0.9 %copy-done.1 = bf16[1,8,16,1024]{3,2,1,0:T(8,128)(2,1)S(1)} copy-done((bf16[1,8,16,1024]{3,2,1,0:T(8,128)(2,1)S(1)}, bf16[1,8,16,1024]{3,2,1,0:T(8,128)(2,1)}, u32[]{:S(2)}) %copy-start.1) | copy-done | bytes 262168
  6.7 1.0 %copy-done.3 = bf16[1,64,4096]{2,1,0:T(8,128)(2,1)S(1)} copy-done((bf16[1,64,4096]{2,1,0:T(8,128)(2,1)S(1)}, bf16[1,64,4096]{2,1,0:T(8,128)(2,1)}, u32[]{:S(2)}) %copy-start.3) | copy-done | bytes 524312
  7.7 0.9 %copy-done.4 = bf16[1,64,1024]{2,1,0:T(8,128)(2,1)S(1)} copy-done((bf16[1,64,1024]{2,1,0:T(8,128)(2,1)S(1)}, bf16[1,64,1024]{2,1,0:T(8,128)(2,1)}, u32[]{:S(2)}) %copy-start.4) | copy-done | bytes 131096
  9.3 1.6 %collective-permute-start.1 = (bf16[64,1792]{1,0:T(8,128)(2,1)S(1)}, bf16[64,1792]{1,0:T(8,128)(2,1)S(1)}, u32[]{:S(2)}, u32[]{:S(2)}) collective-permute-start(bf16[64,1792]{1,0:T(8,128)(2,1)S(1)} %get-tuple-element.31), channel_id=1, source_target_pairs={{0,16},{8,24},{16,0},{24,8},{1,17},{9,25},{17,1},{25,9},{2,18},{10... | collective-permute-start | bytes 688136 | tf_op jit(solution)/shard_map/ppermute | solution.py:193
  11.9 1.5 %collective-permute-start.8 = (bf16[200,1024]{1,0:T(8,128)(2,1)}, bf16[200,1024]{1,0:T(8,128)(2,1)S(1)}, u32[]{:S(2)}, u32[]{:S(2)}) collective-permute-start(bf16[200,1024]{1,0:T(8,128)(2,1)} %slice.21), channel_id=1, source_target_pairs={{0,1},{1,0},{2,4},{3,5},{4,2},{5,3},{6,7},{7,6},{8,9},{9,8},{10,12... | collective-permute-start | bytes 1228808 | tf_op jit(solution)/shard_map/ppermute | solution.py:209
  16.3 1.5 %collective-permute-done.1.rest_2_ = bf16[64,1792]{1,0:T(8,128)(2,1)S(1)} collective-permute-done((bf16[64,1792]{1,0:T(8,128)(2,1)S(1)}, bf16[64,1792]{1,0:T(8,128)(2,1)S(1)}, u32[]{:S(2)}, u32[]{:S(2)}) %collective-permute-start.1) | collective-permute-done | bytes 229408 | tf_op jit(solution)/shard_map/ppermute | solution.py:193
  17.8 4.0 %collective-permute-done.2.rest_3_ = bf16[64,1792]{1,0:T(8,128)(2,1)S(1)} collective-permute-done((bf16[64,1792]{1,0:T(8,128)(2,1)S(1)}, bf16[64,1792]{1,0:T(8,128)(2,1)S(1)}, u32[]{:S(2)}, u32[]{:S(2)}) %collective-permute-start.2) | collective-permute-done | bytes 229408 | tf_op jit(solution)/shard_map/ppermute | solution.py:193
  22.4 4.5 %attention.1.refs_0_ = bf16[1024,256]{1,0:T(8,128)(2,1)S(1)} custom-call(s32[1]{0:T(128)S(6)} %copy.12.pages_ref, s32[1,16]{1,0:T(1,128)S(1)} %copy-done.7, f32[64]{0:T(128)S(1)} %copy-done.8, f32[256,128]{1,0:T(8,128)S(1)} %get-tuple-element.59.cos_ref, f32[256,128]{1,0:T(8,128)S(1)} %get-tuple-element.60.sin_ref, ...), custom_call_target="tpu_custom_call" | custom-call | tf_op jit(solution)/shard_map/attention/pallas_call | solution.py:361
  27.0 1.6 %collective-permute-start.4 = (bf16[128,1024]{1,0:T(8,128)(2,1)S(1)}, bf16[128,1024]{1,0:T(8,128)(2,1)S(1)}, u32[]{:S(2)}, u32[]{:S(2)}) collective-permute-start(bf16[128,1024]{1,0:T(8,128)(2,1)S(1)} %pad_maximum_fusion.rest_0_), channel_id=1, source_target_pairs={{0,16},{8,24},{16,0},{24,8},{1,17},{9,25},{17,1},{25,9},{2,18},{10... | collective-permute-start | bytes 786440 | tf_op jit(solution)/shard_map/ppermute | solution.py:193
  28.6 1.6 %collective-permute-start.13 = (bf16[200,1024]{1,0:T(8,128)(2,1)S(1)}, bf16[200,1024]{1,0:T(8,128)(2,1)S(1)}, u32[]{:S(2)}, u32[]{:S(2)}) collective-permute-start(bf16[200,1024]{1,0:T(8,128)(2,1)S(1)} %slice_select_fusion), channel_id=1, source_target_pairs={{0,1},{1,0},{2,3},{3,2},{4,5},{5,4},{6,7},{7,6},{8,9},{9,8},{10,11... | collective-permute-start | bytes 1228808 | tf_op jit(solution)/shard_map/ppermute | solution.py:195
  30.2 5.7 %collective-permute-done.4.rest_1_ = bf16[128,1024]{1,0:T(8,128)(2,1)S(1)} collective-permute-done((bf16[128,1024]{1,0:T(8,128)(2,1)S(1)}, bf16[128,1024]{1,0:T(8,128)(2,1)S(1)}, u32[]{:S(2)}, u32[]{:S(2)}) %collective-permute-start.4) | collective-permute-done | bytes 262176 | tf_op jit(solution)/shard_map/ppermute | solution.py:193
  36.6 1.6 %collective-permute-start.14 = (bf16[160,1024]{1,0:T(8,128)(2,1)S(1)}, bf16[160,1024]{1,0:T(8,128)(2,1)S(1)}, u32[]{:S(2)}, u32[]{:S(2)}) collective-permute-start(bf16[160,1024]{1,0:T(8,128)(2,1)S(1)} %slice_select_fusion.1), channel_id=1, source_target_pairs={{0,1},{1,0},{2,3},{3,2},{4,5},{5,4},{6,7},{7,6},{8,9},{9,8},{10,11... | collective-permute-start | bytes 983048 | tf_op jit(solution)/shard_map/ppermute | solution.py:195
  38.3 1.6 %collective-permute-start.7 = (bf16[2,192,128]{2,1,0:T(8,128)(2,1)S(1)}, bf16[2,192,128]{2,1,0:T(8,128)(2,1)S(1)}, u32[]{:S(2)}, u32[]{:S(2)}) collective-permute-start(bf16[2,192,128]{2,1,0:T(8,128)(2,1)S(1)} %get-tuple-element.42), channel_id=1, source_target_pairs={{0,16},{8,24},{16,0},{24,8},{1,17},{9,25},{17,1},{25,9},{2,18},{10... | collective-permute-start | bytes 294920 | tf_op jit(solution)/shard_map/ppermute | solution.py:193
  39.9 1.7 %write_pool.1 = bf16[8,16,1024]{2,1,0:T(8,128)(2,1)} custom-call(s32[1,16]{1,0:T(1,128)S(1)} %copy-done.6, f32[256,128]{1,0:T(8,128)S(1)} %get-tuple-element.59.cos_ref, f32[256,128]{1,0:T(8,128)S(1)} %get-tuple-element.60.sin_ref, bf16[8,16,1024]{2,1,0:T(8,128)(2,1)S(1)} %bitcast.15, bf16[128,1024]{1,0:T(8,128)(2,1)S(1)} %pad_maximum_fusion.rest_0_, ...), custom_call_target="tpu_custom_call" | custom-call | tf_op jit(solution)/shard_map/write_pool/pallas_call | solution.py:407
  41.6 1.1 %collective-permute-done.6.refs_0_.refs_1_ = bf16[1024,256]{1,0:T(8,128)(2,1)S(1)} collective-permute-done((bf16[1024,256]{1,0:T(8,128)(2,1)S(1)}, bf16[1024,256]{1,0:T(8,128)(2,1)S(1)}, u32[]{:S(2)}, u32[]{:S(2)}) %collective-permute-start.6) | collective-permute-done | bytes 524320 | tf_op jit(solution)/shard_map/ppermute | solution.py:195
  44.1 3.3 %collective-permute-done.14.refs_5_ = bf16[160,1024]{1,0:T(8,128)(2,1)S(1)} collective-permute-done((bf16[160,1024]{1,0:T(8,128)(2,1)S(1)}, bf16[160,1024]{1,0:T(8,128)(2,1)S(1)}, u32[]{:S(2)}, u32[]{:S(2)}) %collective-permute-start.14) | collective-permute-done | bytes 327712 | tf_op jit(solution)/shard_map/ppermute | solution.py:195
  48.4 3.3 %collective-permute-start.11 = (bf16[3,192,128]{2,1,0:T(8,128)(2,1)S(1)}, bf16[3,192,128]{2,1,0:T(8,128)(2,1)S(1)}, u32[]{:S(2)}, u32[]{:S(2)}) collective-permute-start(bf16[3,192,128]{2,1,0:T(8,128)(2,1)S(1)} %get-tuple-element.47), channel_id=1, source_target_pairs={{0,2},{1,3},{2,0},{3,1},{4,6},{5,7},{6,4},{7,5},{8,10},{9,11},{10,... | collective-permute-start | bytes 442376 | tf_op jit(solution)/shard_map/ppermute | solution.py:195
  51.7 1.0 %collective-permute-start.12 = (bf16[3,192,128]{2,1,0:T(8,128)(2,1)S(1)}, bf16[3,192,128]{2,1,0:T(8,128)(2,1)S(1)}, u32[]{:S(2)}, u32[]{:S(2)}) collective-permute-start(bf16[3,192,128]{2,1,0:T(8,128)(2,1)S(1)} %get-tuple-element.48), channel_id=1, source_target_pairs={{0,18},{1,19},{2,16},{3,17},{4,22},{5,23},{6,20},{7,21},{8,26},{9,... | collective-permute-start | bytes 442376 | tf_op jit(solution)/shard_map/ppermute | solution.py:200
  53.5 1.9 %collective-permute-start.17 = (bf16[1,192,128]{2,1,0:T(8,128)(2,1)S(1)}, bf16[1,192,128]{2,1,0:T(8,128)(2,1)S(1)}, u32[]{:S(2)}, u32[]{:S(2)}) collective-permute-start(bf16[1,192,128]{2,1,0:T(8,128)(2,1)S(1)} %get-tuple-element.53), channel_id=1, source_target_pairs={{0,2},{1,3},{2,0},{3,1},{4,6},{5,7},{6,4},{7,5},{8,10},{9,11},{10,... | collective-permute-start | bytes 147464 | tf_op jit(solution)/shard_map/ppermute | solution.py:195
  55.4 1.0 %collective-permute-start.18 = (bf16[1,192,128]{2,1,0:T(8,128)(2,1)S(1)}, bf16[1,192,128]{2,1,0:T(8,128)(2,1)S(1)}, u32[]{:S(2)}, u32[]{:S(2)}) collective-permute-start(bf16[1,192,128]{2,1,0:T(8,128)(2,1)S(1)} %get-tuple-element.54), channel_id=1, source_target_pairs={{0,18},{1,19},{2,16},{3,17},{4,22},{5,23},{6,20},{7,21},{8,26},{9,... | collective-permute-start | bytes 147464 | tf_op jit(solution)/shard_map/ppermute | solution.py:200
  56.5 4.2 %collective-permute-done.17.rest_6_ = bf16[1,192,128]{2,1,0:T(8,128)(2,1)S(1)} collective-permute-done((bf16[1,192,128]{2,1,0:T(8,128)(2,1)S(1)}, bf16[1,192,128]{2,1,0:T(8,128)(2,1)S(1)}, u32[]{:S(2)}, u32[]{:S(2)}) %collective-permute-start.17) | collective-permute-done | bytes 49184 | tf_op jit(solution)/shard_map/ppermute | solution.py:195
  60.7 1.8 %collective-permute-done.18.rest_7_ = bf16[1,192,128]{2,1,0:T(8,128)(2,1)S(1)} collective-permute-done((bf16[1,192,128]{2,1,0:T(8,128)(2,1)S(1)}, bf16[1,192,128]{2,1,0:T(8,128)(2,1)S(1)}, u32[]{:S(2)}, u32[]{:S(2)}) %collective-permute-start.18) | collective-permute-done | bytes 49184 | tf_op jit(solution)/shard_map/ppermute | solution.py:200
  62.5 1.5 %finish.1 = bf16[64,2880]{1,0:T(8,128)(2,1)} custom-call(bf16[64,2880]{1,0:T(8,128)(2,1)S(1)} %bitcast.19, f32[2,192,128]{2,1,0:T(8,128)S(1)} %get-tuple-element.39.rest_0_, bf16[2,192,128]{2,1,0:T(8,128)(2,1)S(1)} %collective-permute-done.7.rest_1_, bf16[3,192,128]{2,1,0:T(8,128)(2,1)S(1)} %collective-permute-done.11.rest_2_, ...), custom_call_target="tpu_custom_call" | custom-call | tf_op jit(solution)/shard_map/finish/pallas_call | solution.py:507
  (52 shorter events, 8.5 us)
Async XLA Ops:
  0.6 10.5 %copy-start = (bf16[1024,360]{0,1:T(8,128)(2,1)S(1)}, bf16[1024,360]{0,1:T(8,128)(2,1)}, u32[]{:S(2)}) copy-start(bf16[1024,360]{0,1:T(8,128)(2,1)} %param.17) | copy-start | bytes 2211844
  0.6 26.4 %collective-permute-start.3 = (bf16[360,1024]{1,0:T(8,128)(2,1)}, bf16[360,1024]{1,0:T(8,128)(2,1)S(1)}, u32[]{:S(2)}, u32[]{:S(2)}) collective-permute-start(bf16[360,1024]{1,0:T(8,128)(2,1)} %bitcast.9), channel_id=1, source_target_pairs={{0,6},{1,7},{2,3},{3,2},{4,5},{5,4},{6,0},{7,1},{8,14},{9,15},{10,... | collective-permute-start | bytes 2211848 | tf_op jit(solution)/shard_map/ppermute | solution.py:209
  6.7 1.0 %copy-start.3 = (bf16[1,64,4096]{2,1,0:T(8,128)(2,1)S(1)}, bf16[1,64,4096]{2,1,0:T(8,128)(2,1)}, u32[]{:S(2)}) copy-start(bf16[1,64,4096]{2,1,0:T(8,128)(2,1)} %param.10) | copy-start | bytes 1572868
  9.2 6.5 %collective-permute-start = (bf16[64,2816]{1,0:T(8,128)(2,1)S(1)}, bf16[64,2816]{1,0:T(8,128)(2,1)S(1)}, u32[]{:S(2)}, u32[]{:S(2)}) collective-permute-start(bf16[64,2816]{1,0:T(8,128)(2,1)S(1)} %get-tuple-element.30), channel_id=1, source_target_pairs={{0,8},{8,0},{16,24},{24,16},{1,9},{9,1},{17,25},{25,17},{2,10},{10... | collective-permute-start | bytes 1081352 | tf_op jit(solution)/shard_map/ppermute | solution.py:193
  9.3 8.5 %collective-permute-start.1 = (bf16[64,1792]{1,0:T(8,128)(2,1)S(1)}, bf16[64,1792]{1,0:T(8,128)(2,1)S(1)}, u32[]{:S(2)}, u32[]{:S(2)}) collective-permute-start(bf16[64,1792]{1,0:T(8,128)(2,1)S(1)} %get-tuple-element.31), channel_id=1, source_target_pairs={{0,16},{8,24},{16,0},{24,8},{1,17},{9,25},{17,1},{25,9},{2,18},{10... | collective-permute-start | bytes 688136 | tf_op jit(solution)/shard_map/ppermute | solution.py:193
  10.9 10.9 %collective-permute-start.2 = (bf16[64,1792]{1,0:T(8,128)(2,1)S(1)}, bf16[64,1792]{1,0:T(8,128)(2,1)S(1)}, u32[]{:S(2)}, u32[]{:S(2)}) collective-permute-start(bf16[64,1792]{1,0:T(8,128)(2,1)S(1)} %get-tuple-element.32), channel_id=1, source_target_pairs={{0,24},{8,16},{16,8},{24,0},{1,25},{9,17},{17,9},{25,1},{2,26},{10... | collective-permute-start | bytes 688136 | tf_op jit(solution)/shard_map/ppermute | solution.py:193
  11.9 16.7 %collective-permute-start.8 = (bf16[200,1024]{1,0:T(8,128)(2,1)}, bf16[200,1024]{1,0:T(8,128)(2,1)S(1)}, u32[]{:S(2)}, u32[]{:S(2)}) collective-permute-start(bf16[200,1024]{1,0:T(8,128)(2,1)} %slice.21), channel_id=1, source_target_pairs={{0,1},{1,0},{2,4},{3,5},{4,2},{5,3},{6,7},{7,6},{8,9},{9,8},{10,12... | collective-permute-start | bytes 1228808 | tf_op jit(solution)/shard_map/ppermute | solution.py:209
  15.7 20.8 %collective-permute-start.9 = (bf16[160,1024]{1,0:T(8,128)(2,1)}, bf16[160,1024]{1,0:T(8,128)(2,1)S(1)}, u32[]{:S(2)}, u32[]{:S(2)}) collective-permute-start(bf16[160,1024]{1,0:T(8,128)(2,1)} %slice.22), channel_id=1, source_target_pairs={{0,1},{1,0},{2,4},{3,5},{4,2},{5,3},{6,7},{7,6},{8,9},{9,8},{10,12... | collective-permute-start | bytes 983048 | tf_op jit(solution)/shard_map/ppermute | solution.py:209
  27.0 8.8 %collective-permute-start.4 = (bf16[128,1024]{1,0:T(8,128)(2,1)S(1)}, bf16[128,1024]{1,0:T(8,128)(2,1)S(1)}, u32[]{:S(2)}, u32[]{:S(2)}) collective-permute-start(bf16[128,1024]{1,0:T(8,128)(2,1)S(1)} %pad_maximum_fusion.rest_0_), channel_id=1, source_target_pairs={{0,16},{8,24},{16,0},{24,8},{1,17},{9,25},{17,1},{25,9},{2,18},{10... | collective-permute-start | bytes 786440 | tf_op jit(solution)/shard_map/ppermute | solution.py:193
  28.6 14.1 %collective-permute-start.6 = (bf16[1024,256]{1,0:T(8,128)(2,1)S(1)}, bf16[1024,256]{1,0:T(8,128)(2,1)S(1)}, u32[]{:S(2)}, u32[]{:S(2)}) collective-permute-start(bf16[1024,256]{1,0:T(8,128)(2,1)S(1)} %attention.1.refs_0_), channel_id=1, source_target_pairs={{0,2},{1,3},{2,0},{3,1},{4,6},{5,7},{6,4},{7,5},{8,10},{9,11},{10,... | collective-permute-start | bytes 1572872 | tf_op jit(solution)/shard_map/ppermute | solution.py:195
  28.6 18.8 %collective-permute-start.13 = (bf16[200,1024]{1,0:T(8,128)(2,1)S(1)}, bf16[200,1024]{1,0:T(8,128)(2,1)S(1)}, u32[]{:S(2)}, u32[]{:S(2)}) collective-permute-start(bf16[200,1024]{1,0:T(8,128)(2,1)S(1)} %slice_select_fusion), channel_id=1, source_target_pairs={{0,1},{1,0},{2,3},{3,2},{4,5},{5,4},{6,7},{7,6},{8,9},{9,8},{10,11... | collective-permute-start | bytes 1228808 | tf_op jit(solution)/shard_map/ppermute | solution.py:195
  36.4 1.7 %collective-permute-start.5 = (bf16[2,360,128]{2,1,0:T(8,128)(2,1)S(1)}, bf16[2,360,128]{2,1,0:T(8,128)(2,1)S(1)}, u32[]{:S(2)}, u32[]{:S(2)}) collective-permute-start(bf16[2,360,128]{2,1,0:T(8,128)(2,1)S(1)} %get-tuple-element.38), channel_id=1, source_target_pairs={{0,8},{8,0},{16,24},{24,16},{1,9},{9,1},{17,25},{25,17},{2,10},{10... | collective-permute-start | bytes 552968 | tf_op jit(solution)/shard_map/ppermute | solution.py:193
  36.5 3.3 %copy-start.2 = (bf16[1,8,16,1024]{3,2,1,0:T(8,128)(2,1)S(1)}, bf16[1,8,16,1024]{3,2,1,0:T(8,128)(2,1)}, u32[]{:S(2)}) copy-start(bf16[1,8,16,1024]{3,2,1,0:T(8,128)(2,1)} %param.12) | copy-start | bytes 786436
  36.6 10.8 %collective-permute-start.14 = (bf16[160,1024]{1,0:T(8,128)(2,1)S(1)}, bf16[160,1024]{1,0:T(8,128)(2,1)S(1)}, u32[]{:S(2)}, u32[]{:S(2)}) collective-permute-start(bf16[160,1024]{1,0:T(8,128)(2,1)S(1)} %slice_select_fusion.1), channel_id=1, source_target_pairs={{0,1},{1,0},{2,3},{3,2},{4,5},{5,4},{6,7},{7,6},{8,9},{9,8},{10,11... | collective-permute-start | bytes 983048 | tf_op jit(solution)/shard_map/ppermute | solution.py:195
  38.3 1.6 %copy-start.6 = (s32[1,16]{1,0:T(1,128)S(1)}, s32[1,16]{1,0:T(1,128)}, u32[]{:S(2)}) copy-start(s32[1,16]{1,0:T(1,128)} %slots_ref.1) | copy-start | bytes 196
  38.3 5.0 %collective-permute-start.7 = (bf16[2,192,128]{2,1,0:T(8,128)(2,1)S(1)}, bf16[2,192,128]{2,1,0:T(8,128)(2,1)S(1)}, u32[]{:S(2)}, u32[]{:S(2)}) collective-permute-start(bf16[2,192,128]{2,1,0:T(8,128)(2,1)S(1)} %get-tuple-element.42), channel_id=1, source_target_pairs={{0,16},{8,24},{16,0},{24,8},{1,17},{9,25},{17,1},{25,9},{2,18},{10... | collective-permute-start | bytes 294920 | tf_op jit(solution)/shard_map/ppermute | solution.py:193
  44.0 4.2 %collective-permute-start.10 = (bf16[3,360,128]{2,1,0:T(8,128)(2,1)S(1)}, bf16[3,360,128]{2,1,0:T(8,128)(2,1)S(1)}, u32[]{:S(2)}, u32[]{:S(2)}) collective-permute-start(bf16[3,360,128]{2,1,0:T(8,128)(2,1)S(1)} %get-tuple-element.46), channel_id=1, source_target_pairs={{0,8},{8,0},{16,24},{24,16},{1,9},{9,1},{17,25},{25,17},{2,10},{10... | collective-permute-start | bytes 829448 | tf_op jit(solution)/shard_map/ppermute | solution.py:193
  48.2 4.6 %collective-permute-start.15 = (bf16[3,360,128]{2,1,0:T(8,128)(2,1)S(1)}, bf16[3,360,128]{2,1,0:T(8,128)(2,1)S(1)}, u32[]{:S(2)}, u32[]{:S(2)}) collective-permute-start(bf16[3,360,128]{2,1,0:T(8,128)(2,1)S(1)} %get-tuple-element.50), channel_id=1, source_target_pairs={{0,8},{8,0},{16,24},{24,16},{1,9},{9,1},{17,25},{25,17},{2,10},{10... | collective-permute-start | bytes 829448 | tf_op jit(solution)/shard_map/ppermute | solution.py:193
  48.4 14.1 %copy-start.5 = (bf16[1,64,2880]{2,1,0:T(8,128)(2,1)S(1)}, bf16[1,64,2880]{2,1,0:T(8,128)(2,1)}, u32[]{:S(2)}) copy-start(bf16[1,64,2880]{2,1,0:T(8,128)(2,1)} %param.9) | copy-start | bytes 1105924
  48.4 14.1 %collective-permute-start.11 = (bf16[3,192,128]{2,1,0:T(8,128)(2,1)S(1)}, bf16[3,192,128]{2,1,0:T(8,128)(2,1)S(1)}, u32[]{:S(2)}, u32[]{:S(2)}) collective-permute-start(bf16[3,192,128]{2,1,0:T(8,128)(2,1)S(1)} %get-tuple-element.47), channel_id=1, source_target_pairs={{0,2},{1,3},{2,0},{3,1},{4,6},{5,7},{6,4},{7,5},{8,10},{9,11},{10,... | collective-permute-start | bytes 442376 | tf_op jit(solution)/shard_map/ppermute | solution.py:195
  51.7 10.8 %collective-permute-start.12 = (bf16[3,192,128]{2,1,0:T(8,128)(2,1)S(1)}, bf16[3,192,128]{2,1,0:T(8,128)(2,1)S(1)}, u32[]{:S(2)}, u32[]{:S(2)}) collective-permute-start(bf16[3,192,128]{2,1,0:T(8,128)(2,1)S(1)} %get-tuple-element.48), channel_id=1, source_target_pairs={{0,18},{1,19},{2,16},{3,17},{4,22},{5,23},{6,20},{7,21},{8,26},{9,... | collective-permute-start | bytes 442376 | tf_op jit(solution)/shard_map/ppermute | solution.py:200
  52.9 9.6 %collective-permute-start.16 = (bf16[2,192,128]{2,1,0:T(8,128)(2,1)S(1)}, bf16[2,192,128]{2,1,0:T(8,128)(2,1)S(1)}, u32[]{:S(2)}, u32[]{:S(2)}) collective-permute-start(bf16[2,192,128]{2,1,0:T(8,128)(2,1)S(1)} %get-tuple-element.52), channel_id=1, source_target_pairs={{0,16},{8,24},{16,0},{24,8},{1,17},{9,25},{17,1},{25,9},{2,18},{10... | collective-permute-start | bytes 294920 | tf_op jit(solution)/shard_map/ppermute | solution.py:193
  53.5 7.2 %collective-permute-start.17 = (bf16[1,192,128]{2,1,0:T(8,128)(2,1)S(1)}, bf16[1,192,128]{2,1,0:T(8,128)(2,1)S(1)}, u32[]{:S(2)}, u32[]{:S(2)}) collective-permute-start(bf16[1,192,128]{2,1,0:T(8,128)(2,1)S(1)} %get-tuple-element.53), channel_id=1, source_target_pairs={{0,2},{1,3},{2,0},{3,1},{4,6},{5,7},{6,4},{7,5},{8,10},{9,11},{10,... | collective-permute-start | bytes 147464 | tf_op jit(solution)/shard_map/ppermute | solution.py:195
  55.4 7.0 %collective-permute-start.18 = (bf16[1,192,128]{2,1,0:T(8,128)(2,1)S(1)}, bf16[1,192,128]{2,1,0:T(8,128)(2,1)S(1)}, u32[]{:S(2)}, u32[]{:S(2)}) collective-permute-start(bf16[1,192,128]{2,1,0:T(8,128)(2,1)S(1)} %get-tuple-element.54), channel_id=1, source_target_pairs={{0,18},{1,19},{2,16},{3,17},{4,22},{5,23},{6,20},{7,21},{8,26},{9,... | collective-permute-start | bytes 147464 | tf_op jit(solution)/shard_map/ppermute | solution.py:200
  (4 other events, 3.2 us)

commit v8 on v7

--- a/solution.py
+++ b/solution.py
@@ -528,7 +528,7 @@
     pool_rows = slots_dev * page_size
     weight = out_weight.T
     cols = weight.shape[0]
-    cut = cols * 5 // 9
+    cut = cols // 32 * 16
     cuts = (slice(0, cut), slice(cut, cols))
     first = swap_blocks(weight, NEAR_BIT, FAR_BIT)
 

time: 64.2 us -> 63.5 us (0.989)
  other arithmetic: 0.92 us -> 2.99 us
  waiting for transfers between devices: 22.1 us -> 20.3 us
  starting transfers between devices: 23.5 us -> 21.9 us
  Pallas kernels: 10.7 us -> 11.4 us
    ppermute x9, waiting for transfers between devices: 11.7 us -> 8.87 us  [swap(): lax.ppermute(values, 'req', [(i, i ^ req_bits) for i in range(lax.axis_si...]
    ppermute x5, starting transfers between devices: 8.36 us -> 6.66 us  [swap(): lax.ppermute(values, 'exp', [(i, i ^ exp_bits) for i in range(lax.axis_si...]
    concatenate x1, other arithmetic: 0.27 us -> 1.59 us  [paired_plan(): cosine = jnp.concatenate([cosine] * 4, axis=1)]
    ppermute x5, waiting for transfers between devices: 8.65 us -> 9.46 us  [swap(): lax.ppermute(values, 'exp', [(i, i ^ exp_bits) for i in range(lax.axis_si...]
    neg x1, other arithmetic: 0.54 us -> 1.29 us  [paired_plan(): sine = jnp.concatenate([-sine, sine, -sine, sine], axis=1)]
    pallas_call x1, Pallas kernels: 0.55 us -> 1.24 us  [pack(): pl.pallas_call(pack_kernel, out_shape=[jax.ShapeDtypeStruct((tok, w), BF1...]
    unnamed x18 -> x22, local copies, waits for them, and re-layouts: 3.59 us -> 3.59 us
  transfers between devices with their start and end apart: 19 -> 19, of which waited for: 8 -> 9; matrix products, arithmetic and copies ran while one was open for 4% -> 7% of each run, Pallas kernels for 15% -> 16%
where the time goes in v8:
time: 63.5 us; the launch traced here: 63.2 us
  starting transfers between devices  21.9 us (34%)
  waiting for transfers between devices  20.3 us (32%)
  Pallas kernels  11.4 us (18%)
  local copies, waits for them, and re-layouts  5.13 us (8%)
  other arithmetic  2.99 us (5%)
  between operations  1.52 us (2%)
    ppermute x5, waiting for transfers between devices, swap(): lax.ppermute(values, 'exp', [(i, i ^ exp_bits) for i in range(lax.axis_si...  9.46 us
    ppermute x9, waiting for transfers between devices, swap(): lax.ppermute(values, 'req', [(i, i ^ req_bits) for i in range(lax.axis_si...  8.87 us
    ppermute x3, starting transfers between devices, swap_blocks(): return lax.ppermute(values, 'exp', pairs)  7.21 us
    ppermute x5, starting transfers between devices, swap(): lax.ppermute(values, 'exp', [(i, i ^ exp_bits) for i in range(lax.axis_si...  6.66 us
    ppermute x9, starting transfers between devices, swap(): lax.ppermute(values, 'req', [(i, i ^ req_bits) for i in range(lax.axis_si...  6.22 us
    pallas_call x1, Pallas kernels, attention(): pl.pallas_call(functools.partial(attention_kernel, kv_dev=kv_dev, per_kv=...  4.5 us
    unnamed x22, local copies, waits for them, and re-layouts  3.59 us
    pallas_call x3, Pallas kernels, project(): pl.pallas_call(functools.partial(project_kernel, n_ctx=len(contexts), cou...  2.06 us
  transfers between devices with their start and end apart: 19, of which 9 were waited for; matrix products, arithmetic and copies ran while one was open for 7% of the time, Pallas kernels for 16%

profile of v8, /device:TPU:0, one launch (start us, length us, event | category | flops | bytes accessed | tf_op | source)
XLA Modules:
  0.0 63.2 jit_solution(174477035640328157)
XLA Ops:
  0.6 5.1 %collective-permute-start.3 = (bf16[360,1024]{1,0:T(8,128)(2,1)}, bf16[360,1024]{1,0:T(8,128)(2,1)S(1)}, u32[]{:S(2)}, u32[]{:S(2)}) collective-permute-start(bf16[360,1024]{1,0:T(8,128)(2,1)} %bitcast.9), channel_id=1, source_target_pairs={{0,6},{1,7},{2,3},{3,2},{4,5},{5,4},{6,0},{7,1},{8,14},{9,15},{10,... | collective-permute-start | bytes 2211848 | tf_op jit(solution)/shard_map/ppermute | solution.py:209
  5.8 0.9 %copy-done.1 = bf16[1,8,16,1024]{3,2,1,0:T(8,128)(2,1)S(1)} copy-done((bf16[1,8,16,1024]{3,2,1,0:T(8,128)(2,1)S(1)}, bf16[1,8,16,1024]{3,2,1,0:T(8,128)(2,1)}, u32[]{:S(2)}) %copy-start.1) | copy-done | bytes 262168
  6.7 1.0 %copy-done.3 = bf16[1,64,4096]{2,1,0:T(8,128)(2,1)S(1)} copy-done((bf16[1,64,4096]{2,1,0:T(8,128)(2,1)S(1)}, bf16[1,64,4096]{2,1,0:T(8,128)(2,1)}, u32[]{:S(2)}) %copy-start.3) | copy-done | bytes 524312
  8.7 1.2 %pack.1 = (bf16[64,1792]{1,0:T(8,128)(2,1)S(1)}, bf16[64,2816]{1,0:T(8,128)(2,1)S(1)}, bf16[64,1792]{1,0:T(8,128)(2,1)}, bf16[64,1792]{1,0:T(8,128)(2,1)S(1)}) custom-call(bf16[64,4096]{1,0:T(8,128)(2,1)S(1)} %bitcast.16, bf16[64,1024]{1,0:T(8,128)(2,1)S(1)} %bitcast.17, bf16[128,1024]{1,0:T(8,128)(2,1)S(1)} %bitcast.14), custom_call_target="tpu_custom_call" | custom-call | tf_op jit(solution)/shard_map/pack/pallas_call | solution.py:253
  10.0 1.6 %collective-permute-start.1 = (bf16[64,1792]{1,0:T(8,128)(2,1)}, bf16[64,1792]{1,0:T(8,128)(2,1)S(1)}, u32[]{:S(2)}, u32[]{:S(2)}) collective-permute-start(bf16[64,1792]{1,0:T(8,128)(2,1)} %get-tuple-element.31), channel_id=1, source_target_pairs={{0,16},{8,24},{16,0},{24,8},{1,17},{9,25},{17,1},{25,9},{2,18},{10... | collective-permute-start | bytes 688136 | tf_op jit(solution)/shard_map/ppermute | solution.py:193
  12.6 1.5 %collective-permute-start.9 = (bf16[184,1024]{1,0:T(8,128)(2,1)}, bf16[184,1024]{1,0:T(8,128)(2,1)S(1)}, u32[]{:S(2)}, u32[]{:S(2)}) collective-permute-start(bf16[184,1024]{1,0:T(8,128)(2,1)} %slice.22), channel_id=1, source_target_pairs={{0,1},{1,0},{2,4},{3,5},{4,2},{5,3},{6,7},{7,6},{8,9},{9,8},{10,12... | collective-permute-start | bytes 1130504 | tf_op jit(solution)/shard_map/ppermute | solution.py:209
  14.8 1.3 %fusion = (f32[256,32]{1,0:T(8,128)}, f32[256,32]{1,0:T(8,128)}, f32[256,32]{1,0:T(8,128)}) fusion(f32[32]{0:T(128)S(1)} %multiply_power_fusion, f32[256]{0:T(256)S(1)} %add_convert_fusion), kind=kLoop, calls=%fused_computation.7 | loop fusion | flops 16384 | bytes 99456 | tf_op jit(solution)/shard_map/neg | solution.py:545
  16.8 1.6 %pad_maximum_fusion.1 = (f32[256,128]{1,0:T(8,128)S(1)}, f32[256,128]{1,0:T(8,128)S(1)}) fusion(f32[256,32]{1,0:T(8,128)} %get-tuple-element.58, f32[256,32]{1,0:T(8,128)} %get-tuple-element.57, f32[256,32]{1,0:T(8,128)} %get-tuple-element.56), kind=kLoop, calls=%fused_computation.5 | loop fusion | flops 196608 | bytes 360448 | tf_op jit(solution)/shard_map/concatenate | solution.py:544
  19.1 3.6 %collective-permute-done.2.rest_3_ = bf16[64,1792]{1,0:T(8,128)(2,1)S(1)} collective-permute-done((bf16[64,1792]{1,0:T(8,128)(2,1)S(1)}, bf16[64,1792]{1,0:T(8,128)(2,1)S(1)}, u32[]{:S(2)}, u32[]{:S(2)}) %collective-permute-start.2) | collective-permute-done | bytes 229408 | tf_op jit(solution)/shard_map/ppermute | solution.py:193
  23.3 4.5 %attention.1.refs_0_ = bf16[1024,256]{1,0:T(8,128)(2,1)S(1)} custom-call(s32[1]{0:T(128)S(6)} %copy.12.pages_ref, s32[1,16]{1,0:T(1,128)S(1)} %copy-done.8, f32[64]{0:T(128)S(1)} %copy-done.9, f32[256,128]{1,0:T(8,128)S(1)} %get-tuple-element.59.cos_ref, f32[256,128]{1,0:T(8,128)S(1)} %get-tuple-element.60.sin_ref, ...), custom_call_target="tpu_custom_call" | custom-call | tf_op jit(solution)/shard_map/attention/pallas_call | solution.py:361
  27.9 1.6 %collective-permute-start.4 = (bf16[128,1024]{1,0:T(8,128)(2,1)S(1)}, bf16[128,1024]{1,0:T(8,128)(2,1)S(1)}, u32[]{:S(2)}, u32[]{:S(2)}) collective-permute-start(bf16[128,1024]{1,0:T(8,128)(2,1)S(1)} %pad_maximum_fusion.rest_0_), channel_id=1, source_target_pairs={{0,16},{8,24},{16,0},{24,8},{1,17},{9,25},{17,1},{25,9},{2,18},{10... | collective-permute-start | bytes 786440 | tf_op jit(solution)/shard_map/ppermute | solution.py:193
  29.5 1.6 %collective-permute-start.14 = (bf16[184,1024]{1,0:T(8,128)(2,1)S(1)}, bf16[184,1024]{1,0:T(8,128)(2,1)S(1)}, u32[]{:S(2)}, u32[]{:S(2)}) collective-permute-start(bf16[184,1024]{1,0:T(8,128)(2,1)S(1)} %slice_select_fusion), channel_id=1, source_target_pairs={{0,1},{1,0},{2,3},{3,2},{4,5},{5,4},{6,7},{7,6},{8,9},{9,8},{10,11... | collective-permute-start | bytes 1130504 | tf_op jit(solution)/shard_map/ppermute | solution.py:195
  31.6 1.6 %collective-permute-start.13 = (bf16[176,1024]{1,0:T(8,128)(2,1)S(1)}, bf16[176,1024]{1,0:T(8,128)(2,1)S(1)}, u32[]{:S(2)}, u32[]{:S(2)}) collective-permute-start(bf16[176,1024]{1,0:T(8,128)(2,1)S(1)} %slice_select_fusion.1), channel_id=1, source_target_pairs={{0,1},{1,0},{2,3},{3,2},{4,5},{5,4},{6,7},{7,6},{8,9},{9,8},{10,11... | collective-permute-start | bytes 1081352 | tf_op jit(solution)/shard_map/ppermute | solution.py:195
  33.2 3.6 %collective-permute-done.4.rest_1_ = bf16[128,1024]{1,0:T(8,128)(2,1)S(1)} collective-permute-done((bf16[128,1024]{1,0:T(8,128)(2,1)S(1)}, bf16[128,1024]{1,0:T(8,128)(2,1)S(1)}, u32[]{:S(2)}, u32[]{:S(2)}) %collective-permute-start.4) | collective-permute-done | bytes 262176 | tf_op jit(solution)/shard_map/ppermute | solution.py:193
  37.4 1.4 %collective-permute-done.5.got_ref = bf16[2,360,128]{2,1,0:T(8,128)(2,1)S(1)} collective-permute-done((bf16[2,360,128]{2,1,0:T(8,128)(2,1)S(1)}, bf16[2,360,128]{2,1,0:T(8,128)(2,1)S(1)}, u32[]{:S(2)}, u32[]{:S(2)}) %collective-permute-start.5) | collective-permute-done | bytes 184352 | tf_op jit(solution)/shard_map/ppermute | solution.py:193
  39.0 1.6 %collective-permute-start.7 = (bf16[2,192,128]{2,1,0:T(8,128)(2,1)S(1)}, bf16[2,192,128]{2,1,0:T(8,128)(2,1)S(1)}, u32[]{:S(2)}, u32[]{:S(2)}) collective-permute-start(bf16[2,192,128]{2,1,0:T(8,128)(2,1)S(1)} %get-tuple-element.42), channel_id=1, source_target_pairs={{0,16},{8,24},{16,0},{24,8},{1,17},{9,25},{17,1},{25,9},{2,18},{10... | collective-permute-start | bytes 294920 | tf_op jit(solution)/shard_map/ppermute | solution.py:193
  40.6 1.7 %write_pool.1 = bf16[8,16,1024]{2,1,0:T(8,128)(2,1)} custom-call(s32[1,16]{1,0:T(1,128)S(1)} %copy-done.7, f32[256,128]{1,0:T(8,128)S(1)} %get-tuple-element.59.cos_ref, f32[256,128]{1,0:T(8,128)S(1)} %get-tuple-element.60.sin_ref, bf16[8,16,1024]{2,1,0:T(8,128)(2,1)S(1)} %bitcast.15, bf16[128,1024]{1,0:T(8,128)(2,1)S(1)} %pad_maximum_fusion.rest_0_, ...), custom_call_target="tpu_custom_call" | custom-call | tf_op jit(solution)/shard_map/write_pool/pallas_call | solution.py:407
  42.3 1.4 %collective-permute-done.6.refs_0_.refs_1_ = bf16[1024,256]{1,0:T(8,128)(2,1)S(1)} collective-permute-done((bf16[1024,256]{1,0:T(8,128)(2,1)S(1)}, bf16[1024,256]{1,0:T(8,128)(2,1)S(1)}, u32[]{:S(2)}, u32[]{:S(2)}) %collective-permute-start.6) | collective-permute-done | bytes 524320 | tf_op jit(solution)/shard_map/ppermute | solution.py:195
  44.7 3.6 %collective-permute-done.13.refs_4_ = bf16[176,1024]{1,0:T(8,128)(2,1)S(1)} collective-permute-done((bf16[176,1024]{1,0:T(8,128)(2,1)S(1)}, bf16[176,1024]{1,0:T(8,128)(2,1)S(1)}, u32[]{:S(2)}, u32[]{:S(2)}) %collective-permute-start.13) | collective-permute-done | bytes 360480 | tf_op jit(solution)/shard_map/ppermute | solution.py:195
  49.3 1.8 %collective-permute-start.11 = (bf16[3,192,128]{2,1,0:T(8,128)(2,1)S(1)}, bf16[3,192,128]{2,1,0:T(8,128)(2,1)S(1)}, u32[]{:S(2)}, u32[]{:S(2)}) collective-permute-start(bf16[3,192,128]{2,1,0:T(8,128)(2,1)S(1)} %get-tuple-element.47), channel_id=1, source_target_pairs={{0,2},{1,3},{2,0},{3,1},{4,6},{5,7},{6,4},{7,5},{8,10},{9,11},{10,... | collective-permute-start | bytes 442376 | tf_op jit(solution)/shard_map/ppermute | solution.py:195
  53.1 1.7 %collective-permute-start.17 = (bf16[1,192,128]{2,1,0:T(8,128)(2,1)S(1)}, bf16[1,192,128]{2,1,0:T(8,128)(2,1)S(1)}, u32[]{:S(2)}, u32[]{:S(2)}) collective-permute-start(bf16[1,192,128]{2,1,0:T(8,128)(2,1)S(1)} %get-tuple-element.53), channel_id=1, source_target_pairs={{0,2},{1,3},{2,0},{3,1},{4,6},{5,7},{6,4},{7,5},{8,10},{9,11},{10,... | collective-permute-start | bytes 147464 | tf_op jit(solution)/shard_map/ppermute | solution.py:195
  55.8 4.5 %collective-permute-done.17.rest_6_ = bf16[1,192,128]{2,1,0:T(8,128)(2,1)S(1)} collective-permute-done((bf16[1,192,128]{2,1,0:T(8,128)(2,1)S(1)}, bf16[1,192,128]{2,1,0:T(8,128)(2,1)S(1)}, u32[]{:S(2)}, u32[]{:S(2)}) %collective-permute-start.17) | collective-permute-done | bytes 49184 | tf_op jit(solution)/shard_map/ppermute | solution.py:195
  60.3 1.5 %collective-permute-done.18.rest_7_ = bf16[1,192,128]{2,1,0:T(8,128)(2,1)S(1)} collective-permute-done((bf16[1,192,128]{2,1,0:T(8,128)(2,1)S(1)}, bf16[1,192,128]{2,1,0:T(8,128)(2,1)S(1)}, u32[]{:S(2)}, u32[]{:S(2)}) %collective-permute-start.18) | collective-permute-done | bytes 49184 | tf_op jit(solution)/shard_map/ppermute | solution.py:200
  61.8 1.4 %finish.1 = bf16[64,2880]{1,0:T(8,128)(2,1)} custom-call(bf16[64,2880]{1,0:T(8,128)(2,1)S(1)} %bitcast.19, f32[2,192,128]{2,1,0:T(8,128)S(1)} %get-tuple-element.39.rest_0_, bf16[2,192,128]{2,1,0:T(8,128)(2,1)S(1)} %collective-permute-done.7.rest_1_, bf16[3,192,128]{2,1,0:T(8,128)(2,1)S(1)} %collective-permute-done.11.rest_2_, ...), custom_call_target="tpu_custom_call" | custom-call | tf_op jit(solution)/shard_map/finish/pallas_call | solution.py:507
  (56 shorter events, 10.4 us)
Async XLA Ops:
  0.6 11.2 %copy-start = (bf16[1024,360]{0,1:T(8,128)(2,1)S(1)}, bf16[1024,360]{0,1:T(8,128)(2,1)}, u32[]{:S(2)}) copy-start(bf16[1024,360]{0,1:T(8,128)(2,1)} %param.17) | copy-start | bytes 2211844
  0.6 27.3 %collective-permute-start.3 = (bf16[360,1024]{1,0:T(8,128)(2,1)}, bf16[360,1024]{1,0:T(8,128)(2,1)S(1)}, u32[]{:S(2)}, u32[]{:S(2)}) collective-permute-start(bf16[360,1024]{1,0:T(8,128)(2,1)} %bitcast.9), channel_id=1, source_target_pairs={{0,6},{1,7},{2,3},{3,2},{4,5},{5,4},{6,0},{7,1},{8,14},{9,15},{10,... | collective-permute-start | bytes 2211848 | tf_op jit(solution)/shard_map/ppermute | solution.py:209
  9.9 8.5 %collective-permute-start = (bf16[64,2816]{1,0:T(8,128)(2,1)S(1)}, bf16[64,2816]{1,0:T(8,128)(2,1)S(1)}, u32[]{:S(2)}, u32[]{:S(2)}) collective-permute-start(bf16[64,2816]{1,0:T(8,128)(2,1)S(1)} %get-tuple-element.30), channel_id=1, source_target_pairs={{0,8},{8,0},{16,24},{24,16},{1,9},{9,1},{17,25},{25,17},{2,10},{10... | collective-permute-start | bytes 1081352 | tf_op jit(solution)/shard_map/ppermute | solution.py:193
  10.0 9.1 %collective-permute-start.1 = (bf16[64,1792]{1,0:T(8,128)(2,1)}, bf16[64,1792]{1,0:T(8,128)(2,1)S(1)}, u32[]{:S(2)}, u32[]{:S(2)}) collective-permute-start(bf16[64,1792]{1,0:T(8,128)(2,1)} %get-tuple-element.31), channel_id=1, source_target_pairs={{0,16},{8,24},{16,0},{24,8},{1,17},{9,25},{17,1},{25,9},{2,18},{10... | collective-permute-start | bytes 688136 | tf_op jit(solution)/shard_map/ppermute | solution.py:193
  11.6 11.1 %collective-permute-start.2 = (bf16[64,1792]{1,0:T(8,128)(2,1)S(1)}, bf16[64,1792]{1,0:T(8,128)(2,1)S(1)}, u32[]{:S(2)}, u32[]{:S(2)}) collective-permute-start(bf16[64,1792]{1,0:T(8,128)(2,1)S(1)} %get-tuple-element.32), channel_id=1, source_target_pairs={{0,24},{8,16},{16,8},{24,0},{1,25},{9,17},{17,9},{25,1},{2,26},{10... | collective-permute-start | bytes 688136 | tf_op jit(solution)/shard_map/ppermute | solution.py:193
  12.6 16.9 %collective-permute-start.9 = (bf16[184,1024]{1,0:T(8,128)(2,1)}, bf16[184,1024]{1,0:T(8,128)(2,1)S(1)}, u32[]{:S(2)}, u32[]{:S(2)}) collective-permute-start(bf16[184,1024]{1,0:T(8,128)(2,1)} %slice.22), channel_id=1, source_target_pairs={{0,1},{1,0},{2,4},{3,5},{4,2},{5,3},{6,7},{7,6},{8,9},{9,8},{10,12... | collective-permute-start | bytes 1130504 | tf_op jit(solution)/shard_map/ppermute | solution.py:209
  16.8 1.6 %copy-start.10 = (bf16[176,1024]{1,0:T(8,128)(2,1)S(1)}, bf16[176,1024]{1,0:T(8,128)(2,1)}, u32[]{:S(2)}) copy-start(bf16[176,1024]{1,0:T(8,128)(2,1)} %slice.21) | copy-start | bytes 1081348
  18.4 13.1 %collective-permute-start.8 = (bf16[176,1024]{1,0:T(8,128)(2,1)S(1)}, bf16[176,1024]{1,0:T(8,128)(2,1)S(1)}, u32[]{:S(2)}, u32[]{:S(2)}) collective-permute-start(bf16[176,1024]{1,0:T(8,128)(2,1)S(1)} %copy-done.10), channel_id=1, source_target_pairs={{0,1},{1,0},{2,4},{3,5},{4,2},{5,3},{6,7},{7,6},{8,9},{9,8},{10,12... | collective-permute-start | bytes 1081352 | tf_op jit(solution)/shard_map/ppermute | solution.py:209
  23.3 4.5 %copy-start.5 = (bf16[1,64,1024]{2,1,0:T(8,128)(2,1)S(1)}, bf16[1,64,1024]{2,1,0:T(8,128)(2,1)}, u32[]{:S(2)}) copy-start(bf16[1,64,1024]{2,1,0:T(8,128)(2,1)} %param.11) | copy-start | bytes 393220
  27.9 8.8 %collective-permute-start.4 = (bf16[128,1024]{1,0:T(8,128)(2,1)S(1)}, bf16[128,1024]{1,0:T(8,128)(2,1)S(1)}, u32[]{:S(2)}, u32[]{:S(2)}) collective-permute-start(bf16[128,1024]{1,0:T(8,128)(2,1)S(1)} %pad_maximum_fusion.rest_0_), channel_id=1, source_target_pairs={{0,16},{8,24},{16,0},{24,8},{1,17},{9,25},{17,1},{25,9},{2,18},{10... | collective-permute-start | bytes 786440 | tf_op jit(solution)/shard_map/ppermute | solution.py:193
  29.5 14.1 %collective-permute-start.6 = (bf16[1024,256]{1,0:T(8,128)(2,1)S(1)}, bf16[1024,256]{1,0:T(8,128)(2,1)S(1)}, u32[]{:S(2)}, u32[]{:S(2)}) collective-permute-start(bf16[1024,256]{1,0:T(8,128)(2,1)S(1)} %attention.1.refs_0_), channel_id=1, source_target_pairs={{0,2},{1,3},{2,0},{3,1},{4,6},{5,7},{6,4},{7,5},{8,10},{9,11},{10,... | collective-permute-start | bytes 1572872 | tf_op jit(solution)/shard_map/ppermute | solution.py:195
  29.5 18.8 %collective-permute-start.14 = (bf16[184,1024]{1,0:T(8,128)(2,1)S(1)}, bf16[184,1024]{1,0:T(8,128)(2,1)S(1)}, u32[]{:S(2)}, u32[]{:S(2)}) collective-permute-start(bf16[184,1024]{1,0:T(8,128)(2,1)S(1)} %slice_select_fusion), channel_id=1, source_target_pairs={{0,1},{1,0},{2,3},{3,2},{4,5},{5,4},{6,7},{7,6},{8,9},{9,8},{10,11... | collective-permute-start | bytes 1130504 | tf_op jit(solution)/shard_map/ppermute | solution.py:195
  31.6 16.7 %collective-permute-start.13 = (bf16[176,1024]{1,0:T(8,128)(2,1)S(1)}, bf16[176,1024]{1,0:T(8,128)(2,1)S(1)}, u32[]{:S(2)}, u32[]{:S(2)}) collective-permute-start(bf16[176,1024]{1,0:T(8,128)(2,1)S(1)} %slice_select_fusion.1), channel_id=1, source_target_pairs={{0,1},{1,0},{2,3},{3,2},{4,5},{5,4},{6,7},{7,6},{8,9},{9,8},{10,11... | collective-permute-start | bytes 1081352 | tf_op jit(solution)/shard_map/ppermute | solution.py:195
  37.3 3.3 %copy-start.2 = (bf16[1,8,16,1024]{3,2,1,0:T(8,128)(2,1)S(1)}, bf16[1,8,16,1024]{3,2,1,0:T(8,128)(2,1)}, u32[]{:S(2)}) copy-start(bf16[1,8,16,1024]{3,2,1,0:T(8,128)(2,1)} %param.12) | copy-start | bytes 786436
  37.3 1.5 %collective-permute-start.5 = (bf16[2,360,128]{2,1,0:T(8,128)(2,1)S(1)}, bf16[2,360,128]{2,1,0:T(8,128)(2,1)S(1)}, u32[]{:S(2)}, u32[]{:S(2)}) collective-permute-start(bf16[2,360,128]{2,1,0:T(8,128)(2,1)S(1)} %get-tuple-element.38), channel_id=1, source_target_pairs={{0,8},{8,0},{16,24},{24,16},{1,9},{9,1},{17,25},{25,17},{2,10},{10... | collective-permute-start | bytes 552968 | tf_op jit(solution)/shard_map/ppermute | solution.py:193
  39.0 4.9 %collective-permute-start.7 = (bf16[2,192,128]{2,1,0:T(8,128)(2,1)S(1)}, bf16[2,192,128]{2,1,0:T(8,128)(2,1)S(1)}, u32[]{:S(2)}, u32[]{:S(2)}) collective-permute-start(bf16[2,192,128]{2,1,0:T(8,128)(2,1)S(1)} %get-tuple-element.42), channel_id=1, source_target_pairs={{0,16},{8,24},{16,0},{24,8},{1,17},{9,25},{17,1},{25,9},{2,18},{10... | collective-permute-start | bytes 294920 | tf_op jit(solution)/shard_map/ppermute | solution.py:193
  44.6 4.5 %collective-permute-start.10 = (bf16[3,360,128]{2,1,0:T(8,128)(2,1)S(1)}, bf16[3,360,128]{2,1,0:T(8,128)(2,1)S(1)}, u32[]{:S(2)}, u32[]{:S(2)}) collective-permute-start(bf16[3,360,128]{2,1,0:T(8,128)(2,1)S(1)} %get-tuple-element.46), channel_id=1, source_target_pairs={{0,8},{8,0},{16,24},{24,16},{1,9},{9,1},{17,25},{25,17},{2,10},{10... | collective-permute-start | bytes 829448 | tf_op jit(solution)/shard_map/ppermute | solution.py:193
  49.1 3.0 %collective-permute-start.15 = (bf16[3,360,128]{2,1,0:T(8,128)(2,1)S(1)}, bf16[3,360,128]{2,1,0:T(8,128)(2,1)S(1)}, u32[]{:S(2)}, u32[]{:S(2)}) collective-permute-start(bf16[3,360,128]{2,1,0:T(8,128)(2,1)S(1)} %get-tuple-element.50), channel_id=1, source_target_pairs={{0,8},{8,0},{16,24},{24,16},{1,9},{9,1},{17,25},{25,17},{2,10},{10... | collective-permute-start | bytes 829448 | tf_op jit(solution)/shard_map/ppermute | solution.py:193
  49.3 12.5 %copy-start.6 = (bf16[1,64,2880]{2,1,0:T(8,128)(2,1)S(1)}, bf16[1,64,2880]{2,1,0:T(8,128)(2,1)}, u32[]{:S(2)}) copy-start(bf16[1,64,2880]{2,1,0:T(8,128)(2,1)} %param.9) | copy-start | bytes 1105924
  49.3 12.5 %collective-permute-start.11 = (bf16[3,192,128]{2,1,0:T(8,128)(2,1)S(1)}, bf16[3,192,128]{2,1,0:T(8,128)(2,1)S(1)}, u32[]{:S(2)}, u32[]{:S(2)}) collective-permute-start(bf16[3,192,128]{2,1,0:T(8,128)(2,1)S(1)} %get-tuple-element.47), channel_id=1, source_target_pairs={{0,2},{1,3},{2,0},{3,1},{4,6},{5,7},{6,4},{7,5},{8,10},{9,11},{10,... | collective-permute-start | bytes 442376 | tf_op jit(solution)/shard_map/ppermute | solution.py:195
  51.1 10.7 %collective-permute-start.12 = (bf16[3,192,128]{2,1,0:T(8,128)(2,1)S(1)}, bf16[3,192,128]{2,1,0:T(8,128)(2,1)S(1)}, u32[]{:S(2)}, u32[]{:S(2)}) collective-permute-start(bf16[3,192,128]{2,1,0:T(8,128)(2,1)S(1)} %get-tuple-element.48), channel_id=1, source_target_pairs={{0,18},{1,19},{2,16},{3,17},{4,22},{5,23},{6,20},{7,21},{8,26},{9,... | collective-permute-start | bytes 442376 | tf_op jit(solution)/shard_map/ppermute | solution.py:200
  52.2 9.6 %collective-permute-start.16 = (bf16[2,192,128]{2,1,0:T(8,128)(2,1)S(1)}, bf16[2,192,128]{2,1,0:T(8,128)(2,1)S(1)}, u32[]{:S(2)}, u32[]{:S(2)}) collective-permute-start(bf16[2,192,128]{2,1,0:T(8,128)(2,1)S(1)} %get-tuple-element.52), channel_id=1, source_target_pairs={{0,16},{8,24},{16,0},{24,8},{1,17},{9,25},{17,1},{25,9},{2,18},{10... | collective-permute-start | bytes 294920 | tf_op jit(solution)/shard_map/ppermute | solution.py:193
  53.1 7.2 %collective-permute-start.17 = (bf16[1,192,128]{2,1,0:T(8,128)(2,1)S(1)}, bf16[1,192,128]{2,1,0:T(8,128)(2,1)S(1)}, u32[]{:S(2)}, u32[]{:S(2)}) collective-permute-start(bf16[1,192,128]{2,1,0:T(8,128)(2,1)S(1)} %get-tuple-element.53), channel_id=1, source_target_pairs={{0,2},{1,3},{2,0},{3,1},{4,6},{5,7},{6,4},{7,5},{8,10},{9,11},{10,... | collective-permute-start | bytes 147464 | tf_op jit(solution)/shard_map/ppermute | solution.py:195
  54.9 6.9 %collective-permute-start.18 = (bf16[1,192,128]{2,1,0:T(8,128)(2,1)S(1)}, bf16[1,192,128]{2,1,0:T(8,128)(2,1)S(1)}, u32[]{:S(2)}, u32[]{:S(2)}) collective-permute-start(bf16[1,192,128]{2,1,0:T(8,128)(2,1)S(1)} %get-tuple-element.54), channel_id=1, source_target_pairs={{0,18},{1,19},{2,16},{3,17},{4,22},{5,23},{6,20},{7,21},{8,26},{9,... | collective-permute-start | bytes 147464 | tf_op jit(solution)/shard_map/ppermute | solution.py:200
  (6 other events, 5.8 us)

commit v9 on v8

--- a/solution.py
+++ b/solution.py
@@ -416,37 +416,43 @@
     )(slots, cosine, sine, pool, *pairs)
 
 
-def project_kernel(*refs, n_ctx, counts, pairs):
-    contexts = refs[:n_ctx]
-    weights = refs[n_ctx:-2]
+def project_kernel(ctx_ref, *refs, counts, pairs, tokens):
+    weights = refs[:-2]
     send_ref, keep_ref = refs[-2:]
-    half = contexts[0].shape[1] // 2
-    for n, (i, b) in enumerate(pairs):
+    half = tokens // 2
+    for b in range(len(counts)):
+        used = [(n, i) for n, (i, block) in enumerate(pairs) if block == b]
+        low, high = min(i for _, i in used), max(i for _, i in used) + 1
         at = sum(counts[:b])
         row = 0
         for piece in weights[at : at + counts[b]]:
             rows = slice(row, row + piece.shape[0])
-            terms = jnp.dot(piece[...], contexts[i][...], preferred_element_type=F32).astype(BF16)
-            keep_ref[n, rows, :] = terms[:, :half]
-            send_ref[n, rows, :] = terms[:, half:]
+            terms = jnp.dot(
+                piece[...], ctx_ref[:, low * tokens : high * tokens], preferred_element_type=F32
+            ).astype(BF16)
+            for n, i in used:
+                start = (i - low) * tokens
+                keep_ref[n, rows, :] = terms[:, start : start + half]
+                send_ref[n, rows, :] = terms[:, start + half : start + tokens]
             row += piece.shape[0]
 
 
 def project(contexts, blocks, pairs):
     tokens = contexts[0].shape[1]
+    side_by_side = contexts[0] if len(contexts) == 1 else jnp.concatenate(contexts, axis=1)
     cols = sum(piece.shape[0] for piece in blocks[0])
     shape = jax.ShapeDtypeStruct((len(pairs), cols, tokens // 2), BF16)
     flat = [piece for block in blocks for piece in block]
     counts = tuple(len(block) for block in blocks)
     return pl.pallas_call(
-        functools.partial(project_kernel, n_ctx=len(contexts), counts=counts, pairs=pairs),
+        functools.partial(project_kernel, counts=counts, pairs=pairs, tokens=tokens),
         out_shape=[shape, shape],
-        in_specs=[vmem()] * (len(contexts) + len(flat)),
+        in_specs=[vmem()] * (1 + len(flat)),
         out_specs=[vmem()] * 2,
         compiler_params=params(),
         cost_estimate=FREE,
         name="project",
-    )(*contexts, *flat)
+    )(side_by_side, *flat)
 
 
 def fold_rows(cols):

time: 63.5 us -> 63.5 us (level)
  waiting for transfers between devices: 20.3 us -> 26.1 us
  starting transfers between devices: 21.9 us -> 18.4 us
  other arithmetic: 2.99 us -> 0.99 us
  Pallas kernels: 11.4 us -> 10.7 us
    ppermute x9, waiting for transfers between devices: 8.87 us -> 15.3 us  [swap(): lax.ppermute(values, 'req', [(i, i ^ req_bits) for i in range(lax.axis_si...]
    ppermute x5, starting transfers between devices: 6.66 us -> 5.09 us  [swap(): lax.ppermute(values, 'exp', [(i, i ^ exp_bits) for i in range(lax.axis_si...]
    concatenate x1, other arithmetic: 1.59 us -> 0.27 us  [paired_plan(): cosine = jnp.concatenate([cosine] * 4, axis=1)]
    ppermute x2, starting transfers between devices: 1.84 us -> 0.76 us  [swap(): return lax.ppermute(values, ('req', 'exp'), pairs)]
    slice x1, local copies, waits for them, and re-layouts: 0.77 us -> 1.79 us  [paired_plan(): second += [swap_blocks(weight[cuts[1]], FAR_BIT, NEAR_BIT)]]
    ppermute x9, starting transfers between devices: 6.22 us -> 5.33 us  [swap(): lax.ppermute(values, 'req', [(i, i ^ req_bits) for i in range(lax.axis_si...]
    neg x1, other arithmetic: 1.29 us -> 0.54 us  [paired_plan(): sine = jnp.concatenate([-sine, sine, -sine, sine], axis=1)]
    pallas_call x1, Pallas kernels: 1.24 us -> 0.55 us  [pack(): pl.pallas_call(pack_kernel, out_shape=[jax.ShapeDtypeStruct((tok, w), BF1...]
  transfers between devices with their start and end apart: 19 -> 19, of which waited for: 9 -> 9; matrix products, arithmetic and copies ran while one was open for 7% -> 6% of each run, Pallas kernels for 16% -> 15%
where the time goes in v9:
time: 63.5 us; the launch traced here: 63.2 us
  waiting for transfers between devices  26.1 us (41%)
  starting transfers between devices  18.4 us (29%)
  Pallas kernels  10.7 us (17%)
  local copies, waits for them, and re-layouts  5.48 us (9%)
  between operations  1.52 us (2%)
  other arithmetic  0.99 us (2%)
    ppermute x9, waiting for transfers between devices, swap(): lax.ppermute(values, 'req', [(i, i ^ req_bits) for i in range(lax.axis_si...  15.3 us
    ppermute x5, waiting for transfers between devices, swap(): lax.ppermute(values, 'exp', [(i, i ^ exp_bits) for i in range(lax.axis_si...  9.72 us
    ppermute x3, starting transfers between devices, swap_blocks(): return lax.ppermute(values, 'exp', pairs)  7.21 us
    ppermute x9, starting transfers between devices, swap(): lax.ppermute(values, 'req', [(i, i ^ req_bits) for i in range(lax.axis_si...  5.33 us
    ppermute x5, starting transfers between devices, swap(): lax.ppermute(values, 'exp', [(i, i ^ exp_bits) for i in range(lax.axis_si...  5.09 us
    pallas_call x1, Pallas kernels, attention(): pl.pallas_call(functools.partial(attention_kernel, kv_dev=kv_dev, per_kv=...  4.51 us
    unnamed x18, local copies, waits for them, and re-layouts  2.93 us
    pallas_call x3, Pallas kernels, project(): pl.pallas_call(functools.partial(project_kernel, counts=counts, pairs=pai...  2.07 us
  transfers between devices with their start and end apart: 19, of which 9 were waited for; matrix products, arithmetic and copies ran while one was open for 6% of the time, Pallas kernels for 15%

profile of v9, /device:TPU:0, one launch (start us, length us, event | category | flops | bytes accessed | tf_op | source)
XLA Modules:
  0.0 63.2 jit_solution(2685578495776629320)
XLA Ops:
  0.6 5.1 %collective-permute-start.3 = (bf16[360,1024]{1,0:T(8,128)(2,1)}, bf16[360,1024]{1,0:T(8,128)(2,1)S(1)}, u32[]{:S(2)}, u32[]{:S(2)}) collective-permute-start(bf16[360,1024]{1,0:T(8,128)(2,1)} %bitcast.9), channel_id=1, source_target_pairs={{0,6},{1,7},{2,3},{3,2},{4,5},{5,4},{6,0},{7,1},{8,14},{9,15},{10,... | collective-permute-start | bytes 2211848 | tf_op jit(solution)/shard_map/ppermute | solution.py:209
  5.8 1.8 %slice.22 = bf16[184,1024]{1,0:T(8,128)(2,1)} slice(bf16[360,1024]{1,0:T(8,128)(2,1)} %bitcast.10), slice={[176:360], [0:1024]} | slice | bytes 753664 | tf_op jit(solution)/shard_map/slice | solution.py:544
  7.5 1.5 %collective-permute-start.9 = (bf16[184,1024]{1,0:T(8,128)(2,1)}, bf16[184,1024]{1,0:T(8,128)(2,1)S(1)}, u32[]{:S(2)}, u32[]{:S(2)}) collective-permute-start(bf16[184,1024]{1,0:T(8,128)(2,1)} %slice.22), channel_id=1, source_target_pairs={{0,1},{1,0},{2,4},{3,5},{4,2},{5,3},{6,7},{7,6},{8,9},{9,8},{10,12... | collective-permute-start | bytes 1130504 | tf_op jit(solution)/shard_map/ppermute | solution.py:209
  9.0 0.9 %copy-done.1 = bf16[1,8,16,1024]{3,2,1,0:T(8,128)(2,1)S(1)} copy-done((bf16[1,8,16,1024]{3,2,1,0:T(8,128)(2,1)S(1)}, bf16[1,8,16,1024]{3,2,1,0:T(8,128)(2,1)}, u32[]{:S(2)}) %copy-start.1) | copy-done | bytes 262168
  10.0 1.0 %copy-done.3 = bf16[1,64,4096]{2,1,0:T(8,128)(2,1)S(1)} copy-done((bf16[1,64,4096]{2,1,0:T(8,128)(2,1)S(1)}, bf16[1,64,4096]{2,1,0:T(8,128)(2,1)}, u32[]{:S(2)}) %copy-start.3) | copy-done | bytes 524312
  11.0 0.9 %copy-done.4 = bf16[1,64,1024]{2,1,0:T(8,128)(2,1)S(1)} copy-done((bf16[1,64,1024]{2,1,0:T(8,128)(2,1)S(1)}, bf16[1,64,1024]{2,1,0:T(8,128)(2,1)}, u32[]{:S(2)}) %copy-start.4) | copy-done | bytes 131096
  12.5 1.6 %collective-permute-start.1 = (bf16[64,1792]{1,0:T(8,128)(2,1)S(1)}, bf16[64,1792]{1,0:T(8,128)(2,1)S(1)}, u32[]{:S(2)}, u32[]{:S(2)}) collective-permute-start(bf16[64,1792]{1,0:T(8,128)(2,1)S(1)} %get-tuple-element.31), channel_id=1, source_target_pairs={{0,16},{8,24},{16,0},{24,8},{1,17},{9,25},{17,1},{25,9},{2,18},{10... | collective-permute-start | bytes 688136 | tf_op jit(solution)/shard_map/ppermute | solution.py:193
  15.9 0.8 %slice.21 = bf16[176,1024]{1,0:T(8,128)(2,1)} slice(bf16[360,1024]{1,0:T(8,128)(2,1)S(1)} %bitcast.11), slice={[0:176], [0:1024]} | slice | bytes 720896 | tf_op jit(solution)/shard_map/slice | solution.py:543
  17.6 3.5 %collective-permute-done.1.rest_2_ = bf16[64,1792]{1,0:T(8,128)(2,1)S(1)} collective-permute-done((bf16[64,1792]{1,0:T(8,128)(2,1)S(1)}, bf16[64,1792]{1,0:T(8,128)(2,1)S(1)}, u32[]{:S(2)}, u32[]{:S(2)}) %collective-permute-start.1) | collective-permute-done | bytes 229408 | tf_op jit(solution)/shard_map/ppermute | solution.py:193
  21.1 2.2 %collective-permute-done.2.rest_3_ = bf16[64,1792]{1,0:T(8,128)(2,1)S(1)} collective-permute-done((bf16[64,1792]{1,0:T(8,128)(2,1)S(1)}, bf16[64,1792]{1,0:T(8,128)(2,1)S(1)}, u32[]{:S(2)}, u32[]{:S(2)}) %collective-permute-start.2) | collective-permute-done | bytes 229408 | tf_op jit(solution)/shard_map/ppermute | solution.py:193
  23.3 4.5 %attention.1.ctx_ref = bf16[1024,256]{1,0:T(8,128)(2,1)S(1)} custom-call(s32[1]{0:T(128)S(6)} %copy.12.pages_ref, s32[1,16]{1,0:T(1,128)S(1)} %copy-done.7, f32[64]{0:T(128)S(1)} %copy-done.8, f32[256,128]{1,0:T(8,128)S(1)} %get-tuple-element.59.cos_ref, f32[256,128]{1,0:T(8,128)S(1)} %get-tuple-element.60.sin_ref, ...), custom_call_target="tpu_custom_call" | custom-call | tf_op jit(solution)/shard_map/attention/pallas_call | solution.py:361
  27.9 0.8 %collective-permute-start.4 = (bf16[128,1024]{1,0:T(8,128)(2,1)S(1)}, bf16[128,1024]{1,0:T(8,128)(2,1)S(1)}, u32[]{:S(2)}, u32[]{:S(2)}) collective-permute-start(bf16[128,1024]{1,0:T(8,128)(2,1)S(1)} %pad_maximum_fusion.1.rest_0_), channel_id=1, source_target_pairs={{0,16},{8,24},{16,0},{24,8},{1,17},{9,25},{17,1},{25,9},{2,18},{10... | collective-permute-start | bytes 786440 | tf_op jit(solution)/shard_map/ppermute | solution.py:193
  29.3 7.7 %collective-permute-done.4.rest_1_ = bf16[128,1024]{1,0:T(8,128)(2,1)S(1)} collective-permute-done((bf16[128,1024]{1,0:T(8,128)(2,1)S(1)}, bf16[128,1024]{1,0:T(8,128)(2,1)S(1)}, u32[]{:S(2)}, u32[]{:S(2)}) %collective-permute-start.4) | collective-permute-done | bytes 262176 | tf_op jit(solution)/shard_map/ppermute | solution.py:193
  39.9 1.7 %write_pool.1 = bf16[8,16,1024]{2,1,0:T(8,128)(2,1)} custom-call(s32[1,16]{1,0:T(1,128)S(1)} %copy-done.6, f32[256,128]{1,0:T(8,128)S(1)} %get-tuple-element.59.cos_ref, f32[256,128]{1,0:T(8,128)S(1)} %get-tuple-element.60.sin_ref, bf16[8,16,1024]{2,1,0:T(8,128)(2,1)S(1)} %bitcast.15, bf16[128,1024]{1,0:T(8,128)(2,1)S(1)} %pad_maximum_fusion.1.rest_0_, ...), custom_call_target="tpu_custom_call" | custom-call | tf_op jit(solution)/shard_map/write_pool/pallas_call | solution.py:407
  41.6 1.3 %collective-permute-done.6.ctx_ref = bf16[1024,256]{1,0:T(8,128)(2,1)S(1)} collective-permute-done((bf16[1024,256]{1,0:T(8,128)(2,1)S(1)}, bf16[1024,256]{1,0:T(8,128)(2,1)S(1)}, u32[]{:S(2)}, u32[]{:S(2)}) %collective-permute-start.6) | collective-permute-done | bytes 524320 | tf_op jit(solution)/shard_map/ppermute | solution.py:195
  42.9 1.3 %collective-permute-done.7.rest_1_ = bf16[2,192,128]{2,1,0:T(8,128)(2,1)S(1)} collective-permute-done((bf16[2,192,128]{2,1,0:T(8,128)(2,1)S(1)}, bf16[2,192,128]{2,1,0:T(8,128)(2,1)S(1)}, u32[]{:S(2)}, u32[]{:S(2)}) %collective-permute-start.7) | collective-permute-done | bytes 98336 | tf_op jit(solution)/shard_map/ppermute | solution.py:193
  45.1 3.5 %collective-permute-done.13.refs_2_ = bf16[176,1024]{1,0:T(8,128)(2,1)S(1)} collective-permute-done((bf16[176,1024]{1,0:T(8,128)(2,1)S(1)}, bf16[176,1024]{1,0:T(8,128)(2,1)S(1)}, u32[]{:S(2)}, u32[]{:S(2)}) %collective-permute-start.13) | collective-permute-done | bytes 360480 | tf_op jit(solution)/shard_map/ppermute | solution.py:195
  48.6 0.8 %project.5 = (bf16[3,360,128]{2,1,0:T(8,128)(2,1)S(1)}, bf16[3,360,128]{2,1,0:T(8,128)(2,1)S(1)}) custom-call(bf16[1024,512]{1,0:T(8,128)(2,1)S(1)} %pad_maximum_fusion.ctx_ref, bf16[176,1024]{1,0:T(8,128)(2,1)S(1)} %collective-permute-done.8.refs_2_.refs_0_, bf16[184,1024]{1,0:T(8,128)(2,1)S(1)} %collective-permute-done.9.refs_3_.refs_1_, ...), custom_call_target="tpu_custom_call" | custom-call | tf_op jit(solution)/shard_map/project/pallas_call | solution.py:447
  49.6 2.0 %collective-permute-start.11 = (bf16[3,192,128]{2,1,0:T(8,128)(2,1)S(1)}, bf16[3,192,128]{2,1,0:T(8,128)(2,1)S(1)}, u32[]{:S(2)}, u32[]{:S(2)}) collective-permute-start(bf16[3,192,128]{2,1,0:T(8,128)(2,1)S(1)} %get-tuple-element.47), channel_id=1, source_target_pairs={{0,2},{1,3},{2,0},{3,1},{4,6},{5,7},{6,4},{7,5},{8,10},{9,11},{10,... | collective-permute-start | bytes 442376 | tf_op jit(solution)/shard_map/ppermute | solution.py:195
  52.2 1.3 %collective-permute-start.16 = (bf16[2,192,128]{2,1,0:T(8,128)(2,1)S(1)}, bf16[2,192,128]{2,1,0:T(8,128)(2,1)S(1)}, u32[]{:S(2)}, u32[]{:S(2)}) collective-permute-start(bf16[2,192,128]{2,1,0:T(8,128)(2,1)S(1)} %get-tuple-element.52), channel_id=1, source_target_pairs={{0,16},{8,24},{16,0},{24,8},{1,17},{9,25},{17,1},{25,9},{2,18},{10... | collective-permute-start | bytes 294920 | tf_op jit(solution)/shard_map/ppermute | solution.py:193
  53.4 1.9 %collective-permute-start.17 = (bf16[1,192,128]{2,1,0:T(8,128)(2,1)S(1)}, bf16[1,192,128]{2,1,0:T(8,128)(2,1)S(1)}, u32[]{:S(2)}, u32[]{:S(2)}) collective-permute-start(bf16[1,192,128]{2,1,0:T(8,128)(2,1)S(1)} %get-tuple-element.53), channel_id=1, source_target_pairs={{0,2},{1,3},{2,0},{3,1},{4,6},{5,7},{6,4},{7,5},{8,10},{9,11},{10,... | collective-permute-start | bytes 147464 | tf_op jit(solution)/shard_map/ppermute | solution.py:195
  55.7 5.0 %collective-permute-done.17.rest_6_ = bf16[1,192,128]{2,1,0:T(8,128)(2,1)S(1)} collective-permute-done((bf16[1,192,128]{2,1,0:T(8,128)(2,1)S(1)}, bf16[1,192,128]{2,1,0:T(8,128)(2,1)S(1)}, u32[]{:S(2)}, u32[]{:S(2)}) %collective-permute-start.17) | collective-permute-done | bytes 49184 | tf_op jit(solution)/shard_map/ppermute | solution.py:195
  60.7 1.0 %collective-permute-done.18.rest_7_ = bf16[1,192,128]{2,1,0:T(8,128)(2,1)S(1)} collective-permute-done((bf16[1,192,128]{2,1,0:T(8,128)(2,1)S(1)}, bf16[1,192,128]{2,1,0:T(8,128)(2,1)S(1)}, u32[]{:S(2)}, u32[]{:S(2)}) %collective-permute-start.18) | collective-permute-done | bytes 49184 | tf_op jit(solution)/shard_map/ppermute | solution.py:200
  61.8 1.4 %finish.1 = bf16[64,2880]{1,0:T(8,128)(2,1)} custom-call(bf16[64,2880]{1,0:T(8,128)(2,1)S(1)} %bitcast.19, f32[2,192,128]{2,1,0:T(8,128)S(1)} %get-tuple-element.39.rest_0_, bf16[2,192,128]{2,1,0:T(8,128)(2,1)S(1)} %collective-permute-done.7.rest_1_, bf16[3,192,128]{2,1,0:T(8,128)(2,1)S(1)} %collective-permute-done.11.rest_2_, ...), custom_call_target="tpu_custom_call" | custom-call | tf_op jit(solution)/shard_map/finish/pallas_call | solution.py:513
  (53 shorter events, 8.2 us)
Async XLA Ops:
  0.6 15.3 %copy-start = (bf16[1024,360]{0,1:T(8,128)(2,1)S(1)}, bf16[1024,360]{0,1:T(8,128)(2,1)}, u32[]{:S(2)}) copy-start(bf16[1024,360]{0,1:T(8,128)(2,1)} %param.17) | copy-start | bytes 2211844
  0.6 27.2 %collective-permute-start.3 = (bf16[360,1024]{1,0:T(8,128)(2,1)}, bf16[360,1024]{1,0:T(8,128)(2,1)S(1)}, u32[]{:S(2)}, u32[]{:S(2)}) collective-permute-start(bf16[360,1024]{1,0:T(8,128)(2,1)} %bitcast.9), channel_id=1, source_target_pairs={{0,6},{1,7},{2,3},{3,2},{4,5},{5,4},{6,0},{7,1},{8,14},{9,15},{10,... | collective-permute-start | bytes 2211848 | tf_op jit(solution)/shard_map/ppermute | solution.py:209
  7.5 21.1 %collective-permute-start.9 = (bf16[184,1024]{1,0:T(8,128)(2,1)}, bf16[184,1024]{1,0:T(8,128)(2,1)S(1)}, u32[]{:S(2)}, u32[]{:S(2)}) collective-permute-start(bf16[184,1024]{1,0:T(8,128)(2,1)} %slice.22), channel_id=1, source_target_pairs={{0,1},{1,0},{2,4},{3,5},{4,2},{5,3},{6,7},{7,6},{8,9},{9,8},{10,12... | collective-permute-start | bytes 1130504 | tf_op jit(solution)/shard_map/ppermute | solution.py:209
  12.5 10.8 %copy-start.7 = (s32[1,16]{1,0:T(1,128)S(1)}, s32[1,16]{1,0:T(1,128)}, u32[]{:S(2)}) copy-start(s32[1,16]{1,0:T(1,128)} %table_ref.1) | copy-start | bytes 196
  12.5 10.8 %copy-start.8 = (f32[64]{0:T(128)S(1)}, f32[64]{0:T(128)}, u32[]{:S(2)}) copy-start(f32[64]{0:T(128)} %sink_ref.1) | copy-start | bytes 772
  12.5 8.6 %collective-permute-start.1 = (bf16[64,1792]{1,0:T(8,128)(2,1)S(1)}, bf16[64,1792]{1,0:T(8,128)(2,1)S(1)}, u32[]{:S(2)}, u32[]{:S(2)}) collective-permute-start(bf16[64,1792]{1,0:T(8,128)(2,1)S(1)} %get-tuple-element.31), channel_id=1, source_target_pairs={{0,16},{8,24},{16,0},{24,8},{1,17},{9,25},{17,1},{25,9},{2,18},{10... | collective-permute-start | bytes 688136 | tf_op jit(solution)/shard_map/ppermute | solution.py:193
  14.1 9.2 %collective-permute-start.2 = (bf16[64,1792]{1,0:T(8,128)(2,1)S(1)}, bf16[64,1792]{1,0:T(8,128)(2,1)S(1)}, u32[]{:S(2)}, u32[]{:S(2)}) collective-permute-start(bf16[64,1792]{1,0:T(8,128)(2,1)S(1)} %get-tuple-element.32), channel_id=1, source_target_pairs={{0,24},{8,16},{16,8},{24,0},{1,25},{9,17},{17,9},{25,1},{2,26},{10... | collective-permute-start | bytes 688136 | tf_op jit(solution)/shard_map/ppermute | solution.py:193
  14.1 2.9 %collective-permute-start = (bf16[64,2816]{1,0:T(8,128)(2,1)S(1)}, bf16[64,2816]{1,0:T(8,128)(2,1)S(1)}, u32[]{:S(2)}, u32[]{:S(2)}) collective-permute-start(bf16[64,2816]{1,0:T(8,128)(2,1)S(1)} %get-tuple-element.30), channel_id=1, source_target_pairs={{0,8},{8,0},{16,24},{24,16},{1,9},{9,1},{17,25},{25,17},{2,10},{10... | collective-permute-start | bytes 1081352 | tf_op jit(solution)/shard_map/ppermute | solution.py:193
  17.0 20.9 %collective-permute-start.8 = (bf16[176,1024]{1,0:T(8,128)(2,1)}, bf16[176,1024]{1,0:T(8,128)(2,1)S(1)}, u32[]{:S(2)}, u32[]{:S(2)}) collective-permute-start(bf16[176,1024]{1,0:T(8,128)(2,1)} %slice.21), channel_id=1, source_target_pairs={{0,1},{1,0},{2,4},{3,5},{4,2},{5,3},{6,7},{7,6},{8,9},{9,8},{10,12... | collective-permute-start | bytes 1081352 | tf_op jit(solution)/shard_map/ppermute | solution.py:209
  27.9 9.1 %collective-permute-start.4 = (bf16[128,1024]{1,0:T(8,128)(2,1)S(1)}, bf16[128,1024]{1,0:T(8,128)(2,1)S(1)}, u32[]{:S(2)}, u32[]{:S(2)}) collective-permute-start(bf16[128,1024]{1,0:T(8,128)(2,1)S(1)} %pad_maximum_fusion.1.rest_0_), channel_id=1, source_target_pairs={{0,16},{8,24},{16,0},{24,8},{1,17},{9,25},{17,1},{25,9},{2,18},{10... | collective-permute-start | bytes 786440 | tf_op jit(solution)/shard_map/ppermute | solution.py:193
  28.7 14.2 %collective-permute-start.6 = (bf16[1024,256]{1,0:T(8,128)(2,1)S(1)}, bf16[1024,256]{1,0:T(8,128)(2,1)S(1)}, u32[]{:S(2)}, u32[]{:S(2)}) collective-permute-start(bf16[1024,256]{1,0:T(8,128)(2,1)S(1)} %attention.1.ctx_ref), channel_id=1, source_target_pairs={{0,2},{1,3},{2,0},{3,1},{4,6},{5,7},{6,4},{7,5},{8,10},{9,11},{10,... | collective-permute-start | bytes 1572872 | tf_op jit(solution)/shard_map/ppermute | solution.py:195
  28.7 19.9 %collective-permute-start.14 = (bf16[184,1024]{1,0:T(8,128)(2,1)S(1)}, bf16[184,1024]{1,0:T(8,128)(2,1)S(1)}, u32[]{:S(2)}, u32[]{:S(2)}) collective-permute-start(bf16[184,1024]{1,0:T(8,128)(2,1)S(1)} %slice_select_fusion), channel_id=1, source_target_pairs={{0,1},{1,0},{2,3},{3,2},{4,5},{5,4},{6,7},{7,6},{8,9},{9,8},{10,11... | collective-permute-start | bytes 1130504 | tf_op jit(solution)/shard_map/ppermute | solution.py:195
  37.6 2.3 %copy-start.2 = (bf16[1,8,16,1024]{3,2,1,0:T(8,128)(2,1)S(1)}, bf16[1,8,16,1024]{3,2,1,0:T(8,128)(2,1)}, u32[]{:S(2)}) copy-start(bf16[1,8,16,1024]{3,2,1,0:T(8,128)(2,1)} %param.12) | copy-start | bytes 786436
  37.6 1.5 %collective-permute-start.5 = (bf16[2,360,128]{2,1,0:T(8,128)(2,1)S(1)}, bf16[2,360,128]{2,1,0:T(8,128)(2,1)S(1)}, u32[]{:S(2)}, u32[]{:S(2)}) collective-permute-start(bf16[2,360,128]{2,1,0:T(8,128)(2,1)S(1)} %get-tuple-element.38), channel_id=1, source_target_pairs={{0,8},{8,0},{16,24},{24,16},{1,9},{9,1},{17,25},{25,17},{2,10},{10... | collective-permute-start | bytes 552968 | tf_op jit(solution)/shard_map/ppermute | solution.py:193
  37.9 10.7 %collective-permute-start.13 = (bf16[176,1024]{1,0:T(8,128)(2,1)S(1)}, bf16[176,1024]{1,0:T(8,128)(2,1)S(1)}, u32[]{:S(2)}, u32[]{:S(2)}) collective-permute-start(bf16[176,1024]{1,0:T(8,128)(2,1)S(1)} %slice_select_fusion.1), channel_id=1, source_target_pairs={{0,1},{1,0},{2,3},{3,2},{4,5},{5,4},{6,7},{7,6},{8,9},{9,8},{10,11... | collective-permute-start | bytes 1081352 | tf_op jit(solution)/shard_map/ppermute | solution.py:195
  39.2 5.0 %collective-permute-start.7 = (bf16[2,192,128]{2,1,0:T(8,128)(2,1)S(1)}, bf16[2,192,128]{2,1,0:T(8,128)(2,1)S(1)}, u32[]{:S(2)}, u32[]{:S(2)}) collective-permute-start(bf16[2,192,128]{2,1,0:T(8,128)(2,1)S(1)} %get-tuple-element.42), channel_id=1, source_target_pairs={{0,16},{8,24},{16,0},{24,8},{1,17},{9,25},{17,1},{25,9},{2,18},{10... | collective-permute-start | bytes 294920 | tf_op jit(solution)/shard_map/ppermute | solution.py:193
  45.0 4.5 %collective-permute-start.10 = (bf16[3,360,128]{2,1,0:T(8,128)(2,1)S(1)}, bf16[3,360,128]{2,1,0:T(8,128)(2,1)S(1)}, u32[]{:S(2)}, u32[]{:S(2)}) collective-permute-start(bf16[3,360,128]{2,1,0:T(8,128)(2,1)S(1)} %get-tuple-element.46), channel_id=1, source_target_pairs={{0,8},{8,0},{16,24},{24,16},{1,9},{9,1},{17,25},{25,17},{2,10},{10... | collective-permute-start | bytes 829448 | tf_op jit(solution)/shard_map/ppermute | solution.py:193
  49.4 12.4 %copy-start.5 = (bf16[1,64,2880]{2,1,0:T(8,128)(2,1)S(1)}, bf16[1,64,2880]{2,1,0:T(8,128)(2,1)}, u32[]{:S(2)}) copy-start(bf16[1,64,2880]{2,1,0:T(8,128)(2,1)} %param.9) | copy-start | bytes 1105924
  49.4 2.6 %collective-permute-start.15 = (bf16[3,360,128]{2,1,0:T(8,128)(2,1)S(1)}, bf16[3,360,128]{2,1,0:T(8,128)(2,1)S(1)}, u32[]{:S(2)}, u32[]{:S(2)}) collective-permute-start(bf16[3,360,128]{2,1,0:T(8,128)(2,1)S(1)} %get-tuple-element.50), channel_id=1, source_target_pairs={{0,8},{8,0},{16,24},{24,16},{1,9},{9,1},{17,25},{25,17},{2,10},{10... | collective-permute-start | bytes 829448 | tf_op jit(solution)/shard_map/ppermute | solution.py:193
  49.6 12.1 %collective-permute-start.11 = (bf16[3,192,128]{2,1,0:T(8,128)(2,1)S(1)}, bf16[3,192,128]{2,1,0:T(8,128)(2,1)S(1)}, u32[]{:S(2)}, u32[]{:S(2)}) collective-permute-start(bf16[3,192,128]{2,1,0:T(8,128)(2,1)S(1)} %get-tuple-element.47), channel_id=1, source_target_pairs={{0,2},{1,3},{2,0},{3,1},{4,6},{5,7},{6,4},{7,5},{8,10},{9,11},{10,... | collective-permute-start | bytes 442376 | tf_op jit(solution)/shard_map/ppermute | solution.py:195
  51.6 10.1 %collective-permute-start.12 = (bf16[3,192,128]{2,1,0:T(8,128)(2,1)S(1)}, bf16[3,192,128]{2,1,0:T(8,128)(2,1)S(1)}, u32[]{:S(2)}, u32[]{:S(2)}) collective-permute-start(bf16[3,192,128]{2,1,0:T(8,128)(2,1)S(1)} %get-tuple-element.48), channel_id=1, source_target_pairs={{0,18},{1,19},{2,16},{3,17},{4,22},{5,23},{6,20},{7,21},{8,26},{9,... | collective-permute-start | bytes 442376 | tf_op jit(solution)/shard_map/ppermute | solution.py:200
  52.2 9.6 %collective-permute-start.16 = (bf16[2,192,128]{2,1,0:T(8,128)(2,1)S(1)}, bf16[2,192,128]{2,1,0:T(8,128)(2,1)S(1)}, u32[]{:S(2)}, u32[]{:S(2)}) collective-permute-start(bf16[2,192,128]{2,1,0:T(8,128)(2,1)S(1)} %get-tuple-element.52), channel_id=1, source_target_pairs={{0,16},{8,24},{16,0},{24,8},{1,17},{9,25},{17,1},{25,9},{2,18},{10... | collective-permute-start | bytes 294920 | tf_op jit(solution)/shard_map/ppermute | solution.py:193
  53.4 7.2 %collective-permute-start.17 = (bf16[1,192,128]{2,1,0:T(8,128)(2,1)S(1)}, bf16[1,192,128]{2,1,0:T(8,128)(2,1)S(1)}, u32[]{:S(2)}, u32[]{:S(2)}) collective-permute-start(bf16[1,192,128]{2,1,0:T(8,128)(2,1)S(1)} %get-tuple-element.53), channel_id=1, source_target_pairs={{0,2},{1,3},{2,0},{3,1},{4,6},{5,7},{6,4},{7,5},{8,10},{9,11},{10,... | collective-permute-start | bytes 147464 | tf_op jit(solution)/shard_map/ppermute | solution.py:195
  55.3 6.4 %collective-permute-start.18 = (bf16[1,192,128]{2,1,0:T(8,128)(2,1)S(1)}, bf16[1,192,128]{2,1,0:T(8,128)(2,1)S(1)}, u32[]{:S(2)}, u32[]{:S(2)}) collective-permute-start(bf16[1,192,128]{2,1,0:T(8,128)(2,1)S(1)} %get-tuple-element.54), channel_id=1, source_target_pairs={{0,18},{1,19},{2,16},{3,17},{4,22},{5,23},{6,20},{7,21},{8,26},{9,... | collective-permute-start | bytes 147464 | tf_op jit(solution)/shard_map/ppermute | solution.py:200
  (4 other events, 5.2 us)

commit v10 on v8

--- a/solution.py
+++ b/solution.py
@@ -565,12 +565,11 @@
     ctx, fresh = lax.optimization_barrier((ctx, fresh))
     own_part, over_y = both_sides([ctx], [[weight], [first]], ((0, 0), (0, 1)), True)
     parts += [own_part, swap(over_y, 2, 0)]
-    pool_out = write_pool(new_slots, cosine, sine, kv_pool[0], [chip_rows, fresh])
-    ctx_mate, pool_out = lax.optimization_barrier((ctx_mate, pool_out))
     ctx_mate, parts[1] = lax.optimization_barrier((ctx_mate, parts[1]))
     over_pair, over_both = both_sides([ctx_mate], [[weight], [first], second], ((0, 0), (0, 1), (0, 2)), False)
     parts += [swap(over_pair, 0, PAIR_BIT), swap(over_both, 2, PAIR_BIT)]
     own_part, over_y, over_pair, over_both = both_sides([ctx, ctx_mate], [second, both], ((0, 0), (0, 1), (1, 1)), True)
+    own_part, fresh = lax.optimization_barrier((own_part, fresh))
     parts += [own_part, swap(over_y, 2, 0)]
     parts += [swap(over_pair, 0, PAIR_BIT), swap(over_both, 2, PAIR_BIT)]
     own_bits, first_bits, second_bits, both_bits = (
@@ -586,7 +585,9 @@
         (second_bits, both_bits),
         (of_mate(both_bits),),
     )
-    layer_out = finish(hidden_in[0], parts, places)
+    pool_out = write_pool(new_slots, cosine, sine, kv_pool[0], [chip_rows, fresh])
+    hidden, pool_out = lax.optimization_barrier((hidden_in[0], pool_out))
+    layer_out = finish(hidden, parts, places)
     return (layer_out[None], pool_out[None])
 
 

time: 63.5 us -> 63.5 us (level)
  waiting for transfers between devices: 20.3 us -> 19.6 us
  local copies, waits for them, and re-layouts: 5.13 us -> 5.77 us
    unnamed x22, local copies, waits for them, and re-layouts: 3.59 us -> 4.24 us
where the time goes in v10:
time: 63.5 us; the launch traced here: 63.2 us
  starting transfers between devices  21.9 us (34%)
  waiting for transfers between devices  19.6 us (31%)
  Pallas kernels  11.4 us (18%)
  local copies, waits for them, and re-layouts  5.77 us (9%)
  other arithmetic  2.99 us (5%)
  between operations  1.5 us (2%)
    ppermute x9, waiting for transfers between devices, swap(): lax.ppermute(values, 'req', [(i, i ^ req_bits) for i in range(lax.axis_si...  8.86 us
    ppermute x5, waiting for transfers between devices, swap(): lax.ppermute(values, 'exp', [(i, i ^ exp_bits) for i in range(lax.axis_si...  8.86 us
    ppermute x3, starting transfers between devices, swap_blocks(): return lax.ppermute(values, 'exp', pairs)  7.21 us
    ppermute x5, starting transfers between devices, swap(): lax.ppermute(values, 'exp', [(i, i ^ exp_bits) for i in range(lax.axis_si...  6.68 us
    ppermute x9, starting transfers between devices, swap(): lax.ppermute(values, 'req', [(i, i ^ req_bits) for i in range(lax.axis_si...  6.23 us
    pallas_call x1, Pallas kernels, attention(): pl.pallas_call(functools.partial(attention_kernel, kv_dev=kv_dev, per_kv=...  4.52 us
    unnamed x22, local copies, waits for them, and re-layouts  4.24 us
    pallas_call x3, Pallas kernels, project(): pl.pallas_call(functools.partial(project_kernel, n_ctx=len(contexts), cou...  2.07 us
  transfers between devices with their start and end apart: 19, of which 9 were waited for; matrix products, arithmetic and copies ran while one was open for 7% of the time, Pallas kernels for 16%

profile of v10, /device:TPU:0, one launch (start us, length us, event | category | flops | bytes accessed | tf_op | source)
XLA Modules:
  0.0 63.2 jit_solution(2654533487411880290)
XLA Ops:
  0.6 5.1 %collective-permute-start.3 = (bf16[360,1024]{1,0:T(8,128)(2,1)}, bf16[360,1024]{1,0:T(8,128)(2,1)S(1)}, u32[]{:S(2)}, u32[]{:S(2)}) collective-permute-start(bf16[360,1024]{1,0:T(8,128)(2,1)} %bitcast.9), channel_id=1, source_target_pairs={{0,6},{1,7},{2,3},{3,2},{4,5},{5,4},{6,0},{7,1},{8,14},{9,15},{10,... | collective-permute-start | bytes 2211848 | tf_op jit(solution)/shard_map/ppermute | solution.py:209
  5.8 0.9 %copy-done.1 = bf16[1,8,16,1024]{3,2,1,0:T(8,128)(2,1)S(1)} copy-done((bf16[1,8,16,1024]{3,2,1,0:T(8,128)(2,1)S(1)}, bf16[1,8,16,1024]{3,2,1,0:T(8,128)(2,1)}, u32[]{:S(2)}) %copy-start.1) | copy-done | bytes 262168
  6.7 1.0 %copy-done.3 = bf16[1,64,4096]{2,1,0:T(8,128)(2,1)S(1)} copy-done((bf16[1,64,4096]{2,1,0:T(8,128)(2,1)S(1)}, bf16[1,64,4096]{2,1,0:T(8,128)(2,1)}, u32[]{:S(2)}) %copy-start.3) | copy-done | bytes 524312
  8.7 1.2 %pack.1 = (bf16[64,1792]{1,0:T(8,128)(2,1)S(1)}, bf16[64,2816]{1,0:T(8,128)(2,1)S(1)}, bf16[64,1792]{1,0:T(8,128)(2,1)}, bf16[64,1792]{1,0:T(8,128)(2,1)S(1)}) custom-call(bf16[64,4096]{1,0:T(8,128)(2,1)S(1)} %bitcast.16, bf16[64,1024]{1,0:T(8,128)(2,1)S(1)} %bitcast.17, bf16[128,1024]{1,0:T(8,128)(2,1)S(1)} %bitcast.14), custom_call_target="tpu_custom_call" | custom-call | tf_op jit(solution)/shard_map/pack/pallas_call | solution.py:253
  10.0 1.6 %collective-permute-start.1 = (bf16[64,1792]{1,0:T(8,128)(2,1)}, bf16[64,1792]{1,0:T(8,128)(2,1)S(1)}, u32[]{:S(2)}, u32[]{:S(2)}) collective-permute-start(bf16[64,1792]{1,0:T(8,128)(2,1)} %get-tuple-element.33), channel_id=1, source_target_pairs={{0,16},{8,24},{16,0},{24,8},{1,17},{9,25},{17,1},{25,9},{2,18},{10... | collective-permute-start | bytes 688136 | tf_op jit(solution)/shard_map/ppermute | solution.py:193
  12.6 1.5 %collective-permute-start.9 = (bf16[184,1024]{1,0:T(8,128)(2,1)}, bf16[184,1024]{1,0:T(8,128)(2,1)S(1)}, u32[]{:S(2)}, u32[]{:S(2)}) collective-permute-start(bf16[184,1024]{1,0:T(8,128)(2,1)} %slice.22), channel_id=1, source_target_pairs={{0,1},{1,0},{2,4},{3,5},{4,2},{5,3},{6,7},{7,6},{8,9},{9,8},{10,12... | collective-permute-start | bytes 1130504 | tf_op jit(solution)/shard_map/ppermute | solution.py:209
  14.8 1.3 %fusion = (f32[256,32]{1,0:T(8,128)}, f32[256,32]{1,0:T(8,128)}, f32[256,32]{1,0:T(8,128)}) fusion(f32[32]{0:T(128)S(1)} %multiply_power_fusion, f32[256]{0:T(256)S(1)} %add_convert_fusion), kind=kLoop, calls=%fused_computation.7 | loop fusion | flops 16384 | bytes 99456 | tf_op jit(solution)/shard_map/neg | solution.py:545
  16.8 1.6 %pad_maximum_fusion.1 = (f32[256,128]{1,0:T(8,128)S(1)}, f32[256,128]{1,0:T(8,128)S(1)}) fusion(f32[256,32]{1,0:T(8,128)} %get-tuple-element.62, f32[256,32]{1,0:T(8,128)} %get-tuple-element.61, f32[256,32]{1,0:T(8,128)} %get-tuple-element.60), kind=kLoop, calls=%fused_computation.5 | loop fusion | flops 196608 | bytes 360448 | tf_op jit(solution)/shard_map/concatenate | solution.py:544
  19.1 3.6 %collective-permute-done.2.rest_3_ = bf16[64,1792]{1,0:T(8,128)(2,1)S(1)} collective-permute-done((bf16[64,1792]{1,0:T(8,128)(2,1)S(1)}, bf16[64,1792]{1,0:T(8,128)(2,1)S(1)}, u32[]{:S(2)}, u32[]{:S(2)}) %collective-permute-start.2) | collective-permute-done | bytes 229408 | tf_op jit(solution)/shard_map/ppermute | solution.py:193
  23.3 4.5 %attention.1.refs_0_ = bf16[1024,256]{1,0:T(8,128)(2,1)S(1)} custom-call(s32[1]{0:T(128)S(6)} %copy.12.pages_ref, s32[1,16]{1,0:T(1,128)S(1)} %copy-done.8, f32[64]{0:T(128)S(1)} %copy-done.9, f32[256,128]{1,0:T(8,128)S(1)} %get-tuple-element.63.cos_ref, f32[256,128]{1,0:T(8,128)S(1)} %get-tuple-element.64.sin_ref, ...), custom_call_target="tpu_custom_call" | custom-call | tf_op jit(solution)/shard_map/attention/pallas_call | solution.py:361
  27.9 1.6 %collective-permute-start.4 = (bf16[128,1024]{1,0:T(8,128)(2,1)S(1)}, bf16[128,1024]{1,0:T(8,128)(2,1)S(1)}, u32[]{:S(2)}, u32[]{:S(2)}) collective-permute-start(bf16[128,1024]{1,0:T(8,128)(2,1)S(1)} %pad_maximum_fusion.rest_0_), channel_id=1, source_target_pairs={{0,16},{8,24},{16,0},{24,8},{1,17},{9,25},{17,1},{25,9},{2,18},{10... | collective-permute-start | bytes 786440 | tf_op jit(solution)/shard_map/ppermute | solution.py:193
  29.6 1.6 %collective-permute-start.11 = (bf16[184,1024]{1,0:T(8,128)(2,1)S(1)}, bf16[184,1024]{1,0:T(8,128)(2,1)S(1)}, u32[]{:S(2)}, u32[]{:S(2)}) collective-permute-start(bf16[184,1024]{1,0:T(8,128)(2,1)S(1)} %slice_select_fusion), channel_id=1, source_target_pairs={{0,1},{1,0},{2,3},{3,2},{4,5},{5,4},{6,7},{7,6},{8,9},{9,8},{10,11... | collective-permute-start | bytes 1130504 | tf_op jit(solution)/shard_map/ppermute | solution.py:195
  31.6 1.6 %collective-permute-start.10 = (bf16[176,1024]{1,0:T(8,128)(2,1)S(1)}, bf16[176,1024]{1,0:T(8,128)(2,1)S(1)}, u32[]{:S(2)}, u32[]{:S(2)}) collective-permute-start(bf16[176,1024]{1,0:T(8,128)(2,1)S(1)} %slice_select_fusion.1), channel_id=1, source_target_pairs={{0,1},{1,0},{2,3},{3,2},{4,5},{5,4},{6,7},{7,6},{8,9},{9,8},{10,11... | collective-permute-start | bytes 1081352 | tf_op jit(solution)/shard_map/ppermute | solution.py:195
  33.2 3.6 %collective-permute-done.4.rest_1_ = bf16[128,1024]{1,0:T(8,128)(2,1)S(1)} collective-permute-done((bf16[128,1024]{1,0:T(8,128)(2,1)S(1)}, bf16[128,1024]{1,0:T(8,128)(2,1)S(1)}, u32[]{:S(2)}, u32[]{:S(2)}) %collective-permute-start.4) | collective-permute-done | bytes 262176 | tf_op jit(solution)/shard_map/ppermute | solution.py:193
  37.4 1.4 %collective-permute-done.6.got_ref = bf16[2,360,128]{2,1,0:T(8,128)(2,1)S(1)} collective-permute-done((bf16[2,360,128]{2,1,0:T(8,128)(2,1)S(1)}, bf16[2,360,128]{2,1,0:T(8,128)(2,1)S(1)}, u32[]{:S(2)}, u32[]{:S(2)}) %collective-permute-start.6) | collective-permute-done | bytes 184352 | tf_op jit(solution)/shard_map/ppermute | solution.py:193
  39.0 1.6 %collective-permute-start.7 = (bf16[2,192,128]{2,1,0:T(8,128)(2,1)S(1)}, bf16[2,192,128]{2,1,0:T(8,128)(2,1)S(1)}, u32[]{:S(2)}, u32[]{:S(2)}) collective-permute-start(bf16[2,192,128]{2,1,0:T(8,128)(2,1)S(1)} %get-tuple-element.41), channel_id=1, source_target_pairs={{0,16},{8,24},{16,0},{24,8},{1,17},{9,25},{17,1},{25,9},{2,18},{10... | collective-permute-start | bytes 294920 | tf_op jit(solution)/shard_map/ppermute | solution.py:193
  40.6 3.1 %collective-permute-done.5.refs_1_.refs_0_ = bf16[1024,256]{1,0:T(8,128)(2,1)S(1)} collective-permute-done((bf16[1024,256]{1,0:T(8,128)(2,1)S(1)}, bf16[1024,256]{1,0:T(8,128)(2,1)S(1)}, u32[]{:S(2)}, u32[]{:S(2)}) %collective-permute-start.5) | collective-permute-done | bytes 524320 | tf_op jit(solution)/shard_map/ppermute | solution.py:195
  44.7 3.6 %collective-permute-done.10.refs_4_ = bf16[176,1024]{1,0:T(8,128)(2,1)S(1)} collective-permute-done((bf16[176,1024]{1,0:T(8,128)(2,1)S(1)}, bf16[176,1024]{1,0:T(8,128)(2,1)S(1)}, u32[]{:S(2)}, u32[]{:S(2)}) %collective-permute-start.10) | collective-permute-done | bytes 360480 | tf_op jit(solution)/shard_map/ppermute | solution.py:195
  49.3 1.8 %collective-permute-start.14 = (bf16[3,192,128]{2,1,0:T(8,128)(2,1)S(1)}, bf16[3,192,128]{2,1,0:T(8,128)(2,1)S(1)}, u32[]{:S(2)}, u32[]{:S(2)}) collective-permute-start(bf16[3,192,128]{2,1,0:T(8,128)(2,1)S(1)} %get-tuple-element.53), channel_id=1, source_target_pairs={{0,2},{1,3},{2,0},{3,1},{4,6},{5,7},{6,4},{7,5},{8,10},{9,11},{10,... | collective-permute-start | bytes 442376 | tf_op jit(solution)/shard_map/ppermute | solution.py:195
  53.1 1.7 %collective-permute-start.17 = (bf16[1,192,128]{2,1,0:T(8,128)(2,1)S(1)}, bf16[1,192,128]{2,1,0:T(8,128)(2,1)S(1)}, u32[]{:S(2)}, u32[]{:S(2)}) collective-permute-start(bf16[1,192,128]{2,1,0:T(8,128)(2,1)S(1)} %get-tuple-element.57), channel_id=1, source_target_pairs={{0,2},{1,3},{2,0},{3,1},{4,6},{5,7},{6,4},{7,5},{8,10},{9,11},{10,... | collective-permute-start | bytes 147464 | tf_op jit(solution)/shard_map/ppermute | solution.py:195
  56.4 1.7 %write_pool.1 = bf16[8,16,1024]{2,1,0:T(8,128)(2,1)} custom-call(s32[1,16]{1,0:T(1,128)S(1)} %copy-done.7, f32[256,128]{1,0:T(8,128)S(1)} %get-tuple-element.63.cos_ref, f32[256,128]{1,0:T(8,128)S(1)} %get-tuple-element.64.sin_ref, bf16[8,16,1024]{2,1,0:T(8,128)(2,1)S(1)} %bitcast.15, bf16[128,1024]{1,0:T(8,128)(2,1)S(1)} %pad_maximum_fusion.rest_0_, ...), custom_call_target="tpu_custom_call" | custom-call | tf_op jit(solution)/shard_map/write_pool/pallas_call | solution.py:407
  58.1 2.2 %collective-permute-done.17.rest_6_ = bf16[1,192,128]{2,1,0:T(8,128)(2,1)S(1)} collective-permute-done((bf16[1,192,128]{2,1,0:T(8,128)(2,1)S(1)}, bf16[1,192,128]{2,1,0:T(8,128)(2,1)S(1)}, u32[]{:S(2)}, u32[]{:S(2)}) %collective-permute-start.17) | collective-permute-done | bytes 49184 | tf_op jit(solution)/shard_map/ppermute | solution.py:195
  60.3 1.5 %collective-permute-done.18.rest_7_ = bf16[1,192,128]{2,1,0:T(8,128)(2,1)S(1)} collective-permute-done((bf16[1,192,128]{2,1,0:T(8,128)(2,1)S(1)}, bf16[1,192,128]{2,1,0:T(8,128)(2,1)S(1)}, u32[]{:S(2)}, u32[]{:S(2)}) %collective-permute-start.18) | collective-permute-done | bytes 49184 | tf_op jit(solution)/shard_map/ppermute | solution.py:200
  61.8 1.5 %finish.1 = bf16[64,2880]{1,0:T(8,128)(2,1)} custom-call(bf16[64,2880]{1,0:T(8,128)(2,1)S(1)} %bitcast.19, f32[2,192,128]{2,1,0:T(8,128)S(1)} %get-tuple-element.49.rest_0_, bf16[2,192,128]{2,1,0:T(8,128)(2,1)S(1)} %collective-permute-done.7.rest_1_, bf16[3,192,128]{2,1,0:T(8,128)(2,1)S(1)} %collective-permute-done.14.rest_2_, ...), custom_call_target="tpu_custom_call" | custom-call | tf_op jit(solution)/shard_map/finish/pallas_call | solution.py:507
  (56 shorter events, 11.0 us)
Async XLA Ops:
  0.6 11.2 %copy-start = (bf16[1024,360]{0,1:T(8,128)(2,1)S(1)}, bf16[1024,360]{0,1:T(8,128)(2,1)}, u32[]{:S(2)}) copy-start(bf16[1024,360]{0,1:T(8,128)(2,1)} %param.17) | copy-start | bytes 2211844
  0.6 27.3 %collective-permute-start.3 = (bf16[360,1024]{1,0:T(8,128)(2,1)}, bf16[360,1024]{1,0:T(8,128)(2,1)S(1)}, u32[]{:S(2)}, u32[]{:S(2)}) collective-permute-start(bf16[360,1024]{1,0:T(8,128)(2,1)} %bitcast.9), channel_id=1, source_target_pairs={{0,6},{1,7},{2,3},{3,2},{4,5},{5,4},{6,0},{7,1},{8,14},{9,15},{10,... | collective-permute-start | bytes 2211848 | tf_op jit(solution)/shard_map/ppermute | solution.py:209
  9.9 8.5 %collective-permute-start = (bf16[64,2816]{1,0:T(8,128)(2,1)S(1)}, bf16[64,2816]{1,0:T(8,128)(2,1)S(1)}, u32[]{:S(2)}, u32[]{:S(2)}) collective-permute-start(bf16[64,2816]{1,0:T(8,128)(2,1)S(1)} %get-tuple-element.32), channel_id=1, source_target_pairs={{0,8},{8,0},{16,24},{24,16},{1,9},{9,1},{17,25},{25,17},{2,10},{10... | collective-permute-start | bytes 1081352 | tf_op jit(solution)/shard_map/ppermute | solution.py:193
  10.0 9.1 %collective-permute-start.1 = (bf16[64,1792]{1,0:T(8,128)(2,1)}, bf16[64,1792]{1,0:T(8,128)(2,1)S(1)}, u32[]{:S(2)}, u32[]{:S(2)}) collective-permute-start(bf16[64,1792]{1,0:T(8,128)(2,1)} %get-tuple-element.33), channel_id=1, source_target_pairs={{0,16},{8,24},{16,0},{24,8},{1,17},{9,25},{17,1},{25,9},{2,18},{10... | collective-permute-start | bytes 688136 | tf_op jit(solution)/shard_map/ppermute | solution.py:193
  11.6 11.1 %collective-permute-start.2 = (bf16[64,1792]{1,0:T(8,128)(2,1)S(1)}, bf16[64,1792]{1,0:T(8,128)(2,1)S(1)}, u32[]{:S(2)}, u32[]{:S(2)}) collective-permute-start(bf16[64,1792]{1,0:T(8,128)(2,1)S(1)} %get-tuple-element.34), channel_id=1, source_target_pairs={{0,24},{8,16},{16,8},{24,0},{1,25},{9,17},{17,9},{25,1},{2,26},{10... | collective-permute-start | bytes 688136 | tf_op jit(solution)/shard_map/ppermute | solution.py:193
  12.6 16.9 %collective-permute-start.9 = (bf16[184,1024]{1,0:T(8,128)(2,1)}, bf16[184,1024]{1,0:T(8,128)(2,1)S(1)}, u32[]{:S(2)}, u32[]{:S(2)}) collective-permute-start(bf16[184,1024]{1,0:T(8,128)(2,1)} %slice.22), channel_id=1, source_target_pairs={{0,1},{1,0},{2,4},{3,5},{4,2},{5,3},{6,7},{7,6},{8,9},{9,8},{10,12... | collective-permute-start | bytes 1130504 | tf_op jit(solution)/shard_map/ppermute | solution.py:209
  16.8 1.6 %copy-start.10 = (bf16[176,1024]{1,0:T(8,128)(2,1)S(1)}, bf16[176,1024]{1,0:T(8,128)(2,1)}, u32[]{:S(2)}) copy-start(bf16[176,1024]{1,0:T(8,128)(2,1)} %slice.21) | copy-start | bytes 1081348
  18.4 13.1 %collective-permute-start.8 = (bf16[176,1024]{1,0:T(8,128)(2,1)S(1)}, bf16[176,1024]{1,0:T(8,128)(2,1)S(1)}, u32[]{:S(2)}, u32[]{:S(2)}) collective-permute-start(bf16[176,1024]{1,0:T(8,128)(2,1)S(1)} %copy-done.10), channel_id=1, source_target_pairs={{0,1},{1,0},{2,4},{3,5},{4,2},{5,3},{6,7},{7,6},{8,9},{9,8},{10,12... | collective-permute-start | bytes 1081352 | tf_op jit(solution)/shard_map/ppermute | solution.py:209
  23.3 4.5 %copy-start.5 = (bf16[1,64,1024]{2,1,0:T(8,128)(2,1)S(1)}, bf16[1,64,1024]{2,1,0:T(8,128)(2,1)}, u32[]{:S(2)}) copy-start(bf16[1,64,1024]{2,1,0:T(8,128)(2,1)} %param.11) | copy-start | bytes 393220
  27.9 8.8 %collective-permute-start.4 = (bf16[128,1024]{1,0:T(8,128)(2,1)S(1)}, bf16[128,1024]{1,0:T(8,128)(2,1)S(1)}, u32[]{:S(2)}, u32[]{:S(2)}) collective-permute-start(bf16[128,1024]{1,0:T(8,128)(2,1)S(1)} %pad_maximum_fusion.rest_0_), channel_id=1, source_target_pairs={{0,16},{8,24},{16,0},{24,8},{1,17},{9,25},{17,1},{25,9},{2,18},{10... | collective-permute-start | bytes 786440 | tf_op jit(solution)/shard_map/ppermute | solution.py:193
  29.5 14.1 %collective-permute-start.5 = (bf16[1024,256]{1,0:T(8,128)(2,1)S(1)}, bf16[1024,256]{1,0:T(8,128)(2,1)S(1)}, u32[]{:S(2)}, u32[]{:S(2)}) collective-permute-start(bf16[1024,256]{1,0:T(8,128)(2,1)S(1)} %attention.1.refs_0_), channel_id=1, source_target_pairs={{0,2},{1,3},{2,0},{3,1},{4,6},{5,7},{6,4},{7,5},{8,10},{9,11},{10,... | collective-permute-start | bytes 1572872 | tf_op jit(solution)/shard_map/ppermute | solution.py:195
  29.6 18.8 %collective-permute-start.11 = (bf16[184,1024]{1,0:T(8,128)(2,1)S(1)}, bf16[184,1024]{1,0:T(8,128)(2,1)S(1)}, u32[]{:S(2)}, u32[]{:S(2)}) collective-permute-start(bf16[184,1024]{1,0:T(8,128)(2,1)S(1)} %slice_select_fusion), channel_id=1, source_target_pairs={{0,1},{1,0},{2,3},{3,2},{4,5},{5,4},{6,7},{7,6},{8,9},{9,8},{10,11... | collective-permute-start | bytes 1130504 | tf_op jit(solution)/shard_map/ppermute | solution.py:195
  31.6 16.7 %collective-permute-start.10 = (bf16[176,1024]{1,0:T(8,128)(2,1)S(1)}, bf16[176,1024]{1,0:T(8,128)(2,1)S(1)}, u32[]{:S(2)}, u32[]{:S(2)}) collective-permute-start(bf16[176,1024]{1,0:T(8,128)(2,1)S(1)} %slice_select_fusion.1), channel_id=1, source_target_pairs={{0,1},{1,0},{2,3},{3,2},{4,5},{5,4},{6,7},{7,6},{8,9},{9,8},{10,11... | collective-permute-start | bytes 1081352 | tf_op jit(solution)/shard_map/ppermute | solution.py:195
  37.3 1.5 %collective-permute-start.6 = (bf16[2,360,128]{2,1,0:T(8,128)(2,1)S(1)}, bf16[2,360,128]{2,1,0:T(8,128)(2,1)S(1)}, u32[]{:S(2)}, u32[]{:S(2)}) collective-permute-start(bf16[2,360,128]{2,1,0:T(8,128)(2,1)S(1)} %get-tuple-element.40), channel_id=1, source_target_pairs={{0,8},{8,0},{16,24},{24,16},{1,9},{9,1},{17,25},{25,17},{2,10},{10... | collective-permute-start | bytes 552968 | tf_op jit(solution)/shard_map/ppermute | solution.py:193
  39.0 4.9 %collective-permute-start.7 = (bf16[2,192,128]{2,1,0:T(8,128)(2,1)S(1)}, bf16[2,192,128]{2,1,0:T(8,128)(2,1)S(1)}, u32[]{:S(2)}, u32[]{:S(2)}) collective-permute-start(bf16[2,192,128]{2,1,0:T(8,128)(2,1)S(1)} %get-tuple-element.41), channel_id=1, source_target_pairs={{0,16},{8,24},{16,0},{24,8},{1,17},{9,25},{17,1},{25,9},{2,18},{10... | collective-permute-start | bytes 294920 | tf_op jit(solution)/shard_map/ppermute | solution.py:193
  44.6 4.5 %collective-permute-start.13 = (bf16[3,360,128]{2,1,0:T(8,128)(2,1)S(1)}, bf16[3,360,128]{2,1,0:T(8,128)(2,1)S(1)}, u32[]{:S(2)}, u32[]{:S(2)}) collective-permute-start(bf16[3,360,128]{2,1,0:T(8,128)(2,1)S(1)} %get-tuple-element.52), channel_id=1, source_target_pairs={{0,8},{8,0},{16,24},{24,16},{1,9},{9,1},{17,25},{25,17},{2,10},{10... | collective-permute-start | bytes 829448 | tf_op jit(solution)/shard_map/ppermute | solution.py:193
  49.1 3.0 %collective-permute-start.12 = (bf16[3,360,128]{2,1,0:T(8,128)(2,1)S(1)}, bf16[3,360,128]{2,1,0:T(8,128)(2,1)S(1)}, u32[]{:S(2)}, u32[]{:S(2)}) collective-permute-start(bf16[3,360,128]{2,1,0:T(8,128)(2,1)S(1)} %get-tuple-element.44), channel_id=1, source_target_pairs={{0,8},{8,0},{16,24},{24,16},{1,9},{9,1},{17,25},{25,17},{2,10},{10... | collective-permute-start | bytes 829448 | tf_op jit(solution)/shard_map/ppermute | solution.py:193
  49.3 12.5 %collective-permute-start.14 = (bf16[3,192,128]{2,1,0:T(8,128)(2,1)S(1)}, bf16[3,192,128]{2,1,0:T(8,128)(2,1)S(1)}, u32[]{:S(2)}, u32[]{:S(2)}) collective-permute-start(bf16[3,192,128]{2,1,0:T(8,128)(2,1)S(1)} %get-tuple-element.53), channel_id=1, source_target_pairs={{0,2},{1,3},{2,0},{3,1},{4,6},{5,7},{6,4},{7,5},{8,10},{9,11},{10,... | collective-permute-start | bytes 442376 | tf_op jit(solution)/shard_map/ppermute | solution.py:195
  51.1 10.6 %collective-permute-start.15 = (bf16[3,192,128]{2,1,0:T(8,128)(2,1)S(1)}, bf16[3,192,128]{2,1,0:T(8,128)(2,1)S(1)}, u32[]{:S(2)}, u32[]{:S(2)}) collective-permute-start(bf16[3,192,128]{2,1,0:T(8,128)(2,1)S(1)} %get-tuple-element.54), channel_id=1, source_target_pairs={{0,18},{1,19},{2,16},{3,17},{4,22},{5,23},{6,20},{7,21},{8,26},{9,... | collective-permute-start | bytes 442376 | tf_op jit(solution)/shard_map/ppermute | solution.py:200
  52.0 3.7 %copy-start.2 = (bf16[1,8,16,1024]{3,2,1,0:T(8,128)(2,1)S(1)}, bf16[1,8,16,1024]{3,2,1,0:T(8,128)(2,1)}, u32[]{:S(2)}) copy-start(bf16[1,8,16,1024]{3,2,1,0:T(8,128)(2,1)} %param.12) | copy-start | bytes 786436
  52.2 9.6 %collective-permute-start.16 = (bf16[2,192,128]{2,1,0:T(8,128)(2,1)S(1)}, bf16[2,192,128]{2,1,0:T(8,128)(2,1)S(1)}, u32[]{:S(2)}, u32[]{:S(2)}) collective-permute-start(bf16[2,192,128]{2,1,0:T(8,128)(2,1)S(1)} %get-tuple-element.56), channel_id=1, source_target_pairs={{0,16},{8,24},{16,0},{24,8},{1,17},{9,25},{17,1},{25,9},{2,18},{10... | collective-permute-start | bytes 294920 | tf_op jit(solution)/shard_map/ppermute | solution.py:193
  53.1 7.2 %collective-permute-start.17 = (bf16[1,192,128]{2,1,0:T(8,128)(2,1)S(1)}, bf16[1,192,128]{2,1,0:T(8,128)(2,1)S(1)}, u32[]{:S(2)}, u32[]{:S(2)}) collective-permute-start(bf16[1,192,128]{2,1,0:T(8,128)(2,1)S(1)} %get-tuple-element.57), channel_id=1, source_target_pairs={{0,2},{1,3},{2,0},{3,1},{4,6},{5,7},{6,4},{7,5},{8,10},{9,11},{10,... | collective-permute-start | bytes 147464 | tf_op jit(solution)/shard_map/ppermute | solution.py:195
  54.9 6.9 %collective-permute-start.18 = (bf16[1,192,128]{2,1,0:T(8,128)(2,1)S(1)}, bf16[1,192,128]{2,1,0:T(8,128)(2,1)S(1)}, u32[]{:S(2)}, u32[]{:S(2)}) collective-permute-start(bf16[1,192,128]{2,1,0:T(8,128)(2,1)S(1)} %get-tuple-element.58), channel_id=1, source_target_pairs={{0,18},{1,19},{2,16},{3,17},{4,22},{5,23},{6,20},{7,21},{8,26},{9,... | collective-permute-start | bytes 147464 | tf_op jit(solution)/shard_map/ppermute | solution.py:200
  56.4 5.4 %copy-start.6 = (bf16[1,64,2880]{2,1,0:T(8,128)(2,1)S(1)}, bf16[1,64,2880]{2,1,0:T(8,128)(2,1)}, u32[]{:S(2)}) copy-start(bf16[1,64,2880]{2,1,0:T(8,128)(2,1)} %param.9) | copy-start | bytes 1105924
  (6 other events, 4.9 us)
